TPU v7x, 512 devices: a whole 4x4x16 slice. The times are simulated.
512 devices in a mesh: depth: 8 (over x, core), harm: 64 (over z, y).
Axes of the slice: x: 4, y: 4, z: 16, core: 2. Of those that a mesh axis runs over, the one named last changes fastest.
Arguments:
- source: float32 [8, 8, 4096], P('depth', None, 'harm')
- coupling: bfloat16 [8, 4096, 4096], P('depth', 'harm'), may hold values from -0.125 to 0.125, as said below
- diagonal: float32 [8, 4096], P('depth', 'harm'), may hold values from 1.5 to 8
Outputs:
- solution: float32 [8, 8, 4096], P('depth', None, 'harm')
- residual: float32 [8, 8, 4096], P('depth', None, 'harm')
Inputs may be any that keep to these rules, and one draw needn't show every extreme that they name: coupling[z] is symmetric for every plane z.
All inputs are finite; a program needn't handle non-finite values.
Results may differ from a plain program's by a relative error of at most 0.00083.
Values may be sent and summed in bfloat16 or wider, within the bound.
No kernel may reach another device: no remote copies, remote signals or barrier semaphores. Data moves between devices by JAX's collectives and lax.ppermute only.
A program may use at most 64 MiB of HBM per device.

v0:
```python
import jax
import jax.numpy as jnp
from jax import lax
from jax.sharding import PartitionSpec as P

ITERS = 2


def padded_2(cells, sides, width):
    for axis, dim in sides:
        count = lax.axis_size(axis)
        ends = count - 1
        head = lax.slice_in_dim(cells, 0, width, axis=dim)
        tail = lax.slice_in_dim(cells, cells.shape[dim] - width, cells.shape[dim], axis=dim)
        cells = jnp.concatenate(
            [
                lax.ppermute(tail, axis, [(i, (i + 1) % count) for i in range(ends)]),
                cells,
                lax.ppermute(head, axis, [((i + 1) % count, i) for i in range(ends)]),
            ],
            axis=dim,
        )
    return cells


def inner_product(first, second):
    return jnp.sum(first * second, axis=(0, 2))


def operate_on(vector_in, coupling, diagonal):
    padded = padded_2(vector_in, (("depth", 0),), 1)
    narrow = vector_in.astype(jnp.bfloat16)
    blended = jnp.einsum(
        "zhk,zbk->zbh",
        coupling,
        lax.all_gather(narrow, "harm", axis=2, tiled=True),
        preferred_element_type=jnp.float32,
    )
    return (diagonal[:, None, :] + 2.0) * vector_in + blended - (padded[2:] + padded[:-2])


def on_device(source, coupling, diagonal):
    solution = jnp.zeros_like(source)
    residual = source
    search = source
    rho_now = lax.psum(inner_product(source, residual), ("depth", "harm"))
    for iteration in range(ITERS):
        image_one = operate_on(search, coupling, diagonal)
        source_image = lax.psum(inner_product(source, image_one), ("depth", "harm"))
        alpha_step = rho_now / source_image
        interim = residual - alpha_step[None, :, None] * image_one
        image_two = operate_on(interim, coupling, diagonal)
        image_interim, image_square = lax.psum(
            (inner_product(image_two, interim), inner_product(image_two, image_two)),
            ("depth", "harm"),
        )
        omega_step = image_interim / image_square
        solution = (
            solution + alpha_step[None, :, None] * search + omega_step[None, :, None] * interim
        )
        residual = interim - omega_step[None, :, None] * image_two
        if iteration + 1 < ITERS:
            rho_next = lax.psum(inner_product(source, residual), ("depth", "harm"))
            beta_step = rho_next / rho_now * (alpha_step / omega_step)
            search = residual + beta_step[None, :, None] * (
                search - omega_step[None, :, None] * image_one
            )
            rho_now = rho_next
    return (solution, residual)


def solution(mesh):
    return jax.shard_map(
        on_device,
        mesh=mesh,
        in_specs=(P("depth", None, "harm"), P("depth", "harm", None), P("depth", "harm")),
        out_specs=(P("depth", None, "harm"), P("depth", None, "harm")),
        check_vma=False,
    )
```

profile of v0, /device:TPU:24, one launch (start us, length us, event | category | flops | bytes accessed | tf_op | source)
XLA Modules:
  0.0 934.4 jit_solution(5851851662229022748)
XLA Ops:
  0.6 0.0 copy-start
  0.6 1.4 collective-permute-start
  2.1 3.0 collective-permute-start.1
  5.1 0.7 convert_element_type.12
  5.8 0.7 add_bitcast_fusion
  6.5 0.1 copy.17
  6.6 0.0 copy-start.1
  6.6 107.7 %all_gather.12 = bf16[1,8,4096]{1,0,2:T(2,128)(2,1)S(1)} all-gather(bf16[1,8,64]{1,0,2:T(2,128)(2,1)S(1)} %copy.17), channel_id=1, replica_groups=mesh['depth'=8,'harm'=64] {'harm'}, dimensions={2}, use_global_device_ids=true | all-gather | bytes 66560 | tf_op jit(solution)/shard_map/all_gather | solution.py:36
  114.2 1.9 copy.18
  116.1 0.0 collective-permute-done
  116.1 0.0 collective-permute-done.1
  116.2 0.4 multiply_reduce_fusion.6
  116.5 99.5 %all-reduce.2 = (f32[8]{0:T(128)S(1)}, f32[8]{0:T(128)S(1)}) all-reduce(f32[8]{0:T(128)S(1)} %get-tuple-element.7, f32[8]{0:T(128)S(1)} %get-tuple-element.6), channel_id=1, replica_groups=mesh['depth'=8,'harm'=64] {'depth','harm'}, use_global_device_ids=true, to_apply=%region_1.0 | all-reduce | flops 16 | bytes 128 | tf_op jit(solution)/shard_map/psum | solution.py:46
  216.0 0.1 fusion.20
  216.1 1.3 collective-permute-start.2
  217.4 3.0 collective-permute-start.3
  220.4 0.1 copy.19
  220.5 100.8 %all_gather.13 = bf16[1,8,4096]{1,0,2:T(2,128)(2,1)S(1)} all-gather(bf16[1,8,64]{1,0,2:T(2,128)(2,1)S(1)} %copy.19), channel_id=1, replica_groups=mesh['depth'=8,'harm'=64] {'harm'}, dimensions={2}, use_global_device_ids=true | all-gather | bytes 66560 | tf_op jit(solution)/shard_map/all_gather | solution.py:36
  321.4 1.9 copy.20
  323.2 0.2 convolution_bitcast_fusion.2
  323.5 0.0 collective-permute-done.2
  323.5 0.0 collective-permute-done.3
  323.5 0.2 multiply_reduce_fusion.4
  323.6 98.8 %all-reduce.1 = (f32[8]{0:T(128)S(1)}, f32[8]{0:T(128)S(1)}) all-reduce(f32[8]{0:T(128)S(1)} %get-tuple-element.5, f32[8]{0:T(128)S(1)} %get-tuple-element.4), channel_id=1, replica_groups=mesh['depth'=8,'harm'=64] {'depth','harm'}, use_global_device_ids=true, to_apply=%region_5.0 | all-reduce | flops 16 | bytes 128 | tf_op jit(solution)/shard_map/psum | solution.py:53
  422.4 0.2 multiply_reduce_fusion.3
  422.6 99.6 %psum.60 = f32[8]{0:T(128)S(1)} all-reduce(f32[8]{0:T(128)S(1)} %multiply_reduce_fusion.3), channel_id=1, replica_groups=mesh['depth'=8,'harm'=64] {'depth','harm'}, use_global_device_ids=true, to_apply=%region_9.0 | all-reduce | flops 8 | bytes 64 | tf_op jit(solution)/shard_map/psum | solution.py:63
  522.2 0.1 fusion.19
  522.3 1.3 collective-permute-start.4
  523.6 3.0 collective-permute-start.5
  526.6 0.1 copy.21
  526.7 100.0 %all_gather.14 = bf16[1,8,4096]{1,0,2:T(2,128)(2,1)S(1)} all-gather(bf16[1,8,64]{1,0,2:T(2,128)(2,1)S(1)} %copy.21), channel_id=1, replica_groups=mesh['depth'=8,'harm'=64] {'harm'}, dimensions={2}, use_global_device_ids=true | all-gather | bytes 66560 | tf_op jit(solution)/shard_map/all_gather | solution.py:36
  626.7 1.9 copy.22
  628.6 0.0 collective-permute-done.4
  628.6 0.0 collective-permute-done.5
  628.6 0.4 multiply_reduce_fusion.2
  629.0 99.1 %psum.61 = f32[8]{0:T(128)S(1)} all-reduce(f32[8]{0:T(128)S(1)} %get-tuple-element.25), channel_id=1, replica_groups=mesh['depth'=8,'harm'=64] {'depth','harm'}, use_global_device_ids=true, to_apply=%region_11.0 | all-reduce | flops 8 | bytes 64 | tf_op jit(solution)/shard_map/psum | solution.py:49
  728.0 0.1 fusion.18
  728.1 1.3 collective-permute-start.6
  729.4 3.0 collective-permute-start.7
  732.5 0.1 copy.23
  732.6 100.2 %all_gather.15 = bf16[1,8,4096]{1,0,2:T(2,128)(2,1)S(1)} all-gather(bf16[1,8,64]{1,0,2:T(2,128)(2,1)S(1)} %copy.23), channel_id=1, replica_groups=mesh['depth'=8,'harm'=64] {'harm'}, dimensions={2}, use_global_device_ids=true | all-gather | bytes 66560 | tf_op jit(solution)/shard_map/all_gather | solution.py:36
  832.7 1.9 copy.24
  834.6 0.2 convolution_bitcast_fusion
  834.8 0.0 collective-permute-done.6
  834.8 0.0 collective-permute-done.7
  834.9 0.2 multiply_reduce_fusion
  835.0 98.7 %all-reduce = (f32[8]{0:T(128)S(1)}, f32[8]{0:T(128)S(1)}) all-reduce(f32[8]{0:T(128)S(1)} %get-tuple-element.3, f32[8]{0:T(128)S(1)} %get-tuple-element.2), channel_id=1, replica_groups=mesh['depth'=8,'harm'=64] {'depth','harm'}, use_global_device_ids=true, to_apply=%region_13.0 | all-reduce | flops 16 | bytes 128 | tf_op jit(solution)/shard_map/psum | solution.py:53
  933.7 0.7 multiply_subtract_fusion
  (7 shorter events, 0.0 us)
Async XLA Ops:
  0.6 115.5 %copy-start = (bf16[1,64,4096]{2,1,0:T(8,128)(2,1)S(1)}, bf16[1,64,4096]{2,1,0:T(8,128)(2,1)}, u32[]{:S(2)}) copy-start(bf16[1,64,4096]{2,1,0:T(8,128)(2,1)} %param.4) | copy-start | bytes 1572868
  0.6 115.5 %collective-permute-start = (f32[1,8,64]{2,1,0:T(8,128)}, f32[1,8,64]{2,1,0:T(8,128)S(1)}, u32[]{:S(2)}, u32[]{:S(2)}) collective-permute-start(f32[1,8,64]{2,1,0:T(8,128)} %param.3), channel_id=1, source_target_pairs={{64,0},{128,64},{192,128},{256,192},{320,256},{384,320},{448,384},... | collective-permute-start | bytes 6152 | tf_op jit(solution)/shard_map/ppermute | solution.py:19
  2.1 114.0 %collective-permute-start.1 = (f32[1,8,64]{2,1,0:T(8,128)}, f32[1,8,64]{2,1,0:T(8,128)S(1)}, u32[]{:S(2)}, u32[]{:S(2)}) collective-permute-start(f32[1,8,64]{2,1,0:T(8,128)} %param.3), channel_id=1, source_target_pairs={{0,64},{64,128},{128,192},{192,256},{256,320},{320,384},{384,448},... | collective-permute-start | bytes 6152 | tf_op jit(solution)/shard_map/ppermute | solution.py:17
  6.6 109.6 %copy-start.1 = (f32[1,8,64]{2,1,0:T(8,128)S(1)}, f32[1,8,64]{2,1,0:T(8,128)}, u32[]{:S(2)}) copy-start(f32[1,8,64]{2,1,0:T(8,128)} %param.3) | copy-start | bytes 6148
  216.1 107.4 %collective-permute-start.2 = (f32[1,8,64]{2,1,0:T(8,128)S(1)}, f32[1,8,64]{2,1,0:T(8,128)S(1)}, u32[]{:S(2)}, u32[]{:S(2)}) collective-permute-start(f32[1,8,64]{2,1,0:T(8,128)S(1)} %get-tuple-element.21), channel_id=1, source_target_pairs={{64,0},{128,64},{192,128},{256,192},{320,256},{384,320},{448,384},... | collective-permute-start | bytes 6152 | tf_op jit(solution)/shard_map/ppermute | solution.py:19
  217.4 106.1 %collective-permute-start.3 = (f32[1,8,64]{2,1,0:T(8,128)S(1)}, f32[1,8,64]{2,1,0:T(8,128)S(1)}, u32[]{:S(2)}, u32[]{:S(2)}) collective-permute-start(f32[1,8,64]{2,1,0:T(8,128)S(1)} %get-tuple-element.21), channel_id=1, source_target_pairs={{0,64},{64,128},{128,192},{192,256},{256,320},{320,384},{384,448},... | collective-permute-start | bytes 6152 | tf_op jit(solution)/shard_map/ppermute | solution.py:17
  522.3 106.3 %collective-permute-start.4 = (f32[1,8,64]{2,1,0:T(8,128)S(1)}, f32[1,8,64]{2,1,0:T(8,128)S(1)}, u32[]{:S(2)}, u32[]{:S(2)}) collective-permute-start(f32[1,8,64]{2,1,0:T(8,128)S(1)} %get-tuple-element.18), channel_id=1, source_target_pairs={{64,0},{128,64},{192,128},{256,192},{320,256},{384,320},{448,384},... | collective-permute-start | bytes 6152 | tf_op jit(solution)/shard_map/ppermute | solution.py:19
  523.6 105.0 %collective-permute-start.5 = (f32[1,8,64]{2,1,0:T(8,128)S(1)}, f32[1,8,64]{2,1,0:T(8,128)S(1)}, u32[]{:S(2)}, u32[]{:S(2)}) collective-permute-start(f32[1,8,64]{2,1,0:T(8,128)S(1)} %get-tuple-element.18), channel_id=1, source_target_pairs={{0,64},{64,128},{128,192},{192,256},{256,320},{320,384},{384,448},... | collective-permute-start | bytes 6152 | tf_op jit(solution)/shard_map/ppermute | solution.py:17
  728.1 106.7 %collective-permute-start.6 = (f32[1,8,64]{2,1,0:T(8,128)S(1)}, f32[1,8,64]{2,1,0:T(8,128)S(1)}, u32[]{:S(2)}, u32[]{:S(2)}) collective-permute-start(f32[1,8,64]{2,1,0:T(8,128)S(1)} %get-tuple-element.16), channel_id=1, source_target_pairs={{64,0},{128,64},{192,128},{256,192},{320,256},{384,320},{448,384},... | collective-permute-start | bytes 6152 | tf_op jit(solution)/shard_map/ppermute | solution.py:19
  729.4 105.4 %collective-permute-start.7 = (f32[1,8,64]{2,1,0:T(8,128)S(1)}, f32[1,8,64]{2,1,0:T(8,128)S(1)}, u32[]{:S(2)}, u32[]{:S(2)}) collective-permute-start(f32[1,8,64]{2,1,0:T(8,128)S(1)} %get-tuple-element.16), channel_id=1, source_target_pairs={{0,64},{64,128},{128,192},{192,256},{256,320},{320,384},{384,448},... | collective-permute-start | bytes 6152 | tf_op jit(solution)/shard_map/ppermute | solution.py:17
where the time goes:
time: 938 us; the launch traced here: 934 us
  blocking collectives  904 us (96%)
  starting transfers between devices  17.4 us (2%)
    all_gather x4, blocking collectives, operate_on(): lax.all_gather(narrow, 'harm', axis=2, tiled=True)  409 us
    psum x2, blocking collectives, on_device(): lax.psum((inner_product(image_two, interim), inner_product(image_two, ima...  197 us
    psum x1, blocking collectives, on_device(): rho_next = lax.psum(inner_product(source, residual), ('depth', 'harm'))  99.6 us
    psum x1, blocking collectives, on_device(): rho_now = lax.psum(inner_product(source, residual), ('depth', 'harm'))  99.5 us
    psum x1, blocking collectives, on_device(): source_image = lax.psum(inner_product(source, image_one), ('depth', 'harm'))  99.1 us
  transfers between devices with their start and end apart: 8, of which 0 were waited for; matrix products, arithmetic and copies ran while one was open for 1% of the time, Pallas kernels for 0%

commit v1 on v0

v1 whole, which is shorter than its diff:
```python
import jax
import jax.numpy as jnp
from jax import lax
from jax.experimental import pallas as pl
from jax.experimental.pallas import tpu as pltpu
from jax.sharding import Mesh, PartitionSpec as P

STEPS = 4
CENTRE = 6.75
SCALE = 32.0
PAIRS = [(i, j) for j in range(STEPS + 1) for i in range(j + 1)]
NZ, NY, NX, NC = 16, 4, 4, 2
B = 8
H = 64
W = NY * H
F32 = jnp.float32
BF16 = jnp.bfloat16


def call(body, outs, *args, smem=0):
    specs = [pl.BlockSpec(memory_space=pltpu.SMEM)] * smem
    specs += [pl.BlockSpec(memory_space=pltpu.VMEM)] * (len(args) - smem)
    return pl.pallas_call(
        body,
        out_shape=outs,
        in_specs=specs,
        out_specs=jax.tree.map(lambda _: pl.BlockSpec(memory_space=pltpu.VMEM), outs),
    )(*args)


def store_parts(send, field, row):
    turned = pltpu.roll(field, row * H, 1)
    high = turned.astype(BF16)
    low = (turned - high.astype(F32)).astype(BF16)
    both = jnp.concatenate([high, low], axis=0)
    for z in range(NZ):
        send[z] = both


def unpack(row_ref, packed, field_out, diag_out, send):
    row = row_ref[0]
    field = jnp.concatenate([packed[y][:, :H] for y in range(NY)], axis=1)
    diag = jnp.concatenate([packed[y][:, H:] for y in range(NY)], axis=1)
    both = jnp.concatenate([field, diag], axis=0)
    both = pltpu.roll(both, (NY - row) % NY * H, 1)
    field_out[...] = both[:B]
    diag_out[...] = both[B:]
    store_parts(send, both[:B], row)


def next_field(parts, blocks, field, diag, up, down):
    sums = []
    for block in blocks:
        total = None
        for z in range(NZ):
            term = lax.dot_general(
                parts[z],
                block[:, z * W : (z + 1) * W],
                (((1,), (1,)), ((), ())),
                preferred_element_type=F32,
            )
            total = term if total is None else total + term
        sums.append(total[:B] + total[B:])
    blended = jnp.concatenate(sums, axis=1)
    own = (diag[0:1] + (2.0 - CENTRE)) * field[...]
    return (own + blended - (up[...] + down[...])) * (1.0 / SCALE)


def step(row_ref, parts, c0, c1, c2, c3, field, diag, up, down, field_out, send):
    out = next_field(parts, (c0, c1, c2, c3), field, diag, up, down)
    field_out[...] = out
    store_parts(send, out, row_ref[0])


def last_step(parts, c0, c1, c2, c3, field, diag, up, down, f0, f1, f2, field_out, send):
    out = next_field(parts, (c0, c1, c2, c3), field, diag, up, down)
    field_out[...] = out[:, :H]
    fields = [f0[...], f1[...], f2[...], field[...], out]
    lane = lax.broadcasted_iota(jnp.int32, (B, 128), 1)
    table = jnp.zeros((B, 128), F32)
    for p, (i, j) in enumerate(PAIRS):
        table = jnp.where(lane == p, jnp.sum(fields[i] * fields[j], axis=1, keepdims=True), table)
    for k in range(NX * NC):
        send[k] = table


def add_up(tables, send):
    total = tables[0]
    for k in range(1, NX * NC):
        total = total + tables[k]
    for z in range(NZ):
        send[z] = total


def finish(tables, f0, f1, f2, f3, f4, solution_out, residual_out):
    total = tables[0]
    for z in range(1, NZ):
        total = total + tables[z]
    gram = {}
    for p, (i, j) in enumerate(PAIRS):
        gram[i, j] = gram[j, i] = total[:, p : p + 1]

    def inner(a, c):
        total = None
        for j, cj in enumerate(c):
            part = None
            for i, ai in enumerate(a):
                term = gram[i, j] if ai is None else ai * gram[i, j]
                part = term if part is None else part + term
            part = part if cj is None else part * cj
            total = part if total is None else total + part
        return total

    def plus(a, c, scale):
        out = []
        for k in range(max(len(a), len(c))):
            if k >= len(c):
                out.append(a[k])
            elif k >= len(a):
                out.append(scale * c[k])
            else:
                out.append(a[k] + scale * c[k])
        return out

    def image(a):
        out = [CENTRE * x for x in a] + [jnp.zeros_like(a[0])]
        for k, x in enumerate(a):
            out[k + 1] = out[k + 1] + SCALE * x
        return out

    one = jnp.ones((B, 1), F32)
    source = [None]
    found = None
    residual = search = [one]
    rho = gram[0, 0]
    for iteration in range(2):
        image_one = image(search)
        alpha = rho / inner(source, image_one)
        interim = plus(residual, image_one, -alpha)
        image_two = image(interim)
        omega = inner(image_two, interim) / inner(image_two, image_two)
        if found is None:
            found = [alpha * x for x in search]
        else:
            found = plus(found, search, alpha)
        found = plus(found, interim, omega)
        residual = plus(interim, image_two, -omega)
        if iteration == 0:
            rho_next = inner(source, residual)
            beta = (rho_next / rho) * (alpha / omega)
            search = plus(residual, plus(search, image_one, -omega), beta)
            rho = rho_next
    fields = [f0[:, :H], f1[:, :H], f2[:, :H], f3[:, :H], f4[...]]

    def combine(a):
        out = a[0] * fields[0]
        for k in range(1, len(a)):
            out = out + a[k] * fields[k]
        return out

    solution_out[...] = combine(found)
    residual_out[...] = combine(residual)


def spread(array, axes, count):
    return lax.all_to_all(array, axes, 0, 0, tiled=True)


def neighbours(field):
    ends = NX * NC - 1
    up = lax.ppermute(field, ("x", "c"), [(i, i + 1) for i in range(ends)])
    down = lax.ppermute(field, ("x", "c"), [(i + 1, i) for i in range(ends)])
    return up, down


def on_device(source, coupling, diagonal):
    own = coupling[0]
    row = lax.axis_index("y").astype(jnp.int32).reshape(1)
    blocks = [own]
    for shift in range(1, NY):
        blocks.append(lax.ppermute(own, "y", [((y + shift) % NY, y) for y in range(NY)]))
    packed = jnp.concatenate([source[0], jnp.broadcast_to(diagonal, (B, H))], axis=1)
    packed = lax.all_to_all(jnp.broadcast_to(packed[None], (NY, B, 128)), "y", 0, 0, tiled=True)
    shape = jax.ShapeDtypeStruct
    field_shape, send_shape = shape((B, W), F32), shape((NZ, 2 * B, W), BF16)
    field, diag, send = call(unpack, (field_shape, field_shape, send_shape), row, packed, smem=1)
    fields = [field]
    for k in range(STEPS):
        up, down = neighbours(field)
        parts = lax.all_to_all(send, "z", 0, 0, tiled=True)
        if k + 1 < STEPS:
            field, send = call(
                step, (field_shape, send_shape), row, parts, *blocks, field, diag, up, down, smem=1
            )
            fields.append(field)
        else:
            last, table = call(
                last_step,
                (shape((B, H), F32), shape((NX * NC, B, 128), F32)),
                parts, *blocks, field, diag, up, down, *fields[:3],
            )
    table = lax.all_to_all(table, ("x", "c"), 0, 0, tiled=True)
    table = call(add_up, shape((NZ, B, 128), F32), table)
    table = lax.all_to_all(table, "z", 0, 0, tiled=True)
    own_shape = shape((B, H), F32)
    found, residual = call(finish, (own_shape, own_shape), table, *fields, last)
    return found[None], residual[None]


def solution(mesh):
    fine = Mesh(mesh.devices.reshape(NX, NC, NZ, NY), ("x", "c", "z", "y"))
    depth, harm = ("x", "c"), ("z", "y")
    return jax.shard_map(
        on_device,
        mesh=fine,
        in_specs=(P(depth, None, harm), P(depth, harm, None), P(depth, harm)),
        out_specs=(P(depth, None, harm), P(depth, None, harm)),
        check_vma=False,
    )
```

time: 938 us -> 171 us (0.18)
  blocking collectives: 904 us -> 29.8 us
  waiting for transfers between devices: 0.02 us -> 50.7 us
  starting transfers between devices: 17.4 us -> 65.3 us
  Pallas kernels: 0 us -> 17.2 us
    psum x5 -> x0, blocking collectives: 496 us -> none  [the longest x2 197 us: on_device(): lax.psum((inner_product(image_two, interim), inner_product(image_two, ima...]
    all_gather x4 -> x0, blocking collectives: 409 us -> none  [operate_on(): lax.all_gather(narrow, 'harm', axis=2, tiled=True)]
    all_to_all x0 -> x5, waiting for transfers between devices: none -> 47.5 us  [the longest x4 36.3 us: on_device(): parts = lax.all_to_all(send, 'z', 0, 0, tiled=True)]
    all_to_all x0 -> x5, starting transfers between devices: none -> 35.6 us  [the longest x4 29 us: on_device(): parts = lax.all_to_all(send, 'z', 0, 0, tiled=True)]
    all_to_all x0 -> x2, blocking collectives: none -> 29.8 us  [the longest x1 18.4 us: on_device(): table = lax.all_to_all(table, 'z', 0, 0, tiled=True)]
    pallas_call x0 -> x7, Pallas kernels: none -> 17.2 us  [call(): pl.pallas_call(body, out_shape=outs, in_specs=specs, out_specs=jax.tree.m...]
    ppermute x8 -> x11, starting transfers between devices: 17.4 us -> 29.7 us  [the longest x3 12.3 us: on_device(): lax.ppermute(own, 'y', [((y + shift) % NY, y) for y in range(NY)])]
  transfers between devices with their start and end apart: 8 -> 16, of which waited for: 0 -> 9; matrix products, arithmetic and copies ran while one was open for 1% -> 0% of each run, Pallas kernels for 0% -> 1%
where the time goes in v1:
time: 171 us; the launch traced here: 168 us
  starting transfers between devices  65.3 us (38%)
  waiting for transfers between devices  50.7 us (30%)
  blocking collectives  29.8 us (17%)
  Pallas kernels  17.2 us (10%)
  local copies, waits for them, and re-layouts  4.48 us (3%)
    all_to_all x4, waiting for transfers between devices, on_device(): parts = lax.all_to_all(send, 'z', 0, 0, tiled=True)  36.3 us
    all_to_all x4, starting transfers between devices, on_device(): parts = lax.all_to_all(send, 'z', 0, 0, tiled=True)  29 us
    all_to_all x1, blocking collectives, on_device(): table = lax.all_to_all(table, 'z', 0, 0, tiled=True)  18.4 us
    pallas_call x7, Pallas kernels, call(): pl.pallas_call(body, out_shape=outs, in_specs=specs, out_specs=jax.tree.m...  17.2 us
    ppermute x3, starting transfers between devices, on_device(): lax.ppermute(own, 'y', [((y + shift) % NY, y) for y in range(NY)])  12.3 us
    ppermute x4, starting transfers between devices, neighbours(): up = lax.ppermute(field, ('x', 'c'), [(i, i + 1) for i in range(ends)])  12.2 us
    all_to_all x1, blocking collectives, on_device(): table = lax.all_to_all(table, ('x', 'c'), 0, 0, tiled=True)  11.4 us
    all_to_all x1, waiting for transfers between devices, on_device(): lax.all_to_all(jnp.broadcast_to(packed[None], (NY, B, 128)), 'y', 0, 0, t...  11.2 us
  transfers between devices with their start and end apart: 16, of which 9 were waited for; matrix products, arithmetic and copies ran while one was open for 0% of the time, Pallas kernels for 1%

profile of v1, /device:TPU:24, one launch (start us, length us, event | category | flops | bytes accessed | tf_op | source)
XLA Modules:
  0.0 168.4 jit_solution(2663288574102944394)
XLA Ops:
  0.6 7.6 %collective-permute-start.2 = (bf16[64,4096]{1,0:T(8,128)(2,1)}, bf16[64,4096]{1,0:T(8,128)(2,1)S(1)}, u32[]{:S(2)}, u32[]{:S(2)}) collective-permute-start(bf16[64,4096]{1,0:T(8,128)(2,1)} %bitcast.6), channel_id=1, source_target_pairs={{3,0},{0,1},{1,2},{2,3},{7,4},{4,5},{5,6},{6,7},{11,8},{8,9},{9,10... | collective-permute-start | bytes 1572872 | tf_op jit(solution)/shard_map/ppermute | solution.py:181
  8.3 1.9 %collective-permute-start.1 = (bf16[64,4096]{1,0:T(8,128)(2,1)}, bf16[64,4096]{1,0:T(8,128)(2,1)S(1)}, u32[]{:S(2)}, u32[]{:S(2)}) collective-permute-start(bf16[64,4096]{1,0:T(8,128)(2,1)} %bitcast.7), channel_id=1, source_target_pairs={{2,0},{3,1},{0,2},{1,3},{6,4},{7,5},{4,6},{5,7},{10,8},{11,9},{8,1... | collective-permute-start | bytes 1572872 | tf_op jit(solution)/shard_map/ppermute | solution.py:181
  10.2 2.8 %collective-permute-start = (bf16[64,4096]{1,0:T(8,128)(2,1)}, bf16[64,4096]{1,0:T(8,128)(2,1)S(1)}, u32[]{:S(2)}, u32[]{:S(2)}) collective-permute-start(bf16[64,4096]{1,0:T(8,128)(2,1)} %bitcast.8), channel_id=1, source_target_pairs={{1,0},{2,1},{3,2},{0,3},{5,4},{6,5},{7,6},{4,7},{9,8},{10,9},{11,1... | collective-permute-start | bytes 1572872 | tf_op jit(solution)/shard_map/ppermute | solution.py:181
  13.0 0.1 pad.1.clone
  13.1 0.6 broadcast_in_dim.21
  13.7 6.6 %all-to-all-start = ((f32[4,8,128]{2,1,0:T(8,128)}), f32[4,8,128]{2,1,0:T(8,128)S(1)}, u32[]{:S(2)}, u32[]{:S(2)}) async-start(f32[4,8,128]{2,1,0:T(8,128)} %broadcast_in_dim.21), calls=%async_computation | async-start | bytes 32768 | tf_op jit(solution)/shard_map/all_to_all | solution.py:183
  20.3 11.2 %all-to-all-done.packed = f32[4,8,128]{2,1,0:T(8,128)S(1)} async-done(((f32[4,8,128]{2,1,0:T(8,128)}), f32[4,8,128]{2,1,0:T(8,128)S(1)}, u32[]{:S(2)}, u32[]{:S(2)}) %all-to-all-start) | async-done | bytes 16416 | tf_op jit(solution)/shard_map/all_to_all | solution.py:183
  31.5 0.6 copy-done.10
  32.1 1.6 shard_map.50
  33.7 15.3 %all-to-all-start.1 = ((bf16[16,16,256]{2,1,0:T(8,128)(2,1)}), bf16[16,16,256]{2,1,0:T(8,128)(2,1)S(1)}, u32[]{:S(2)}, u32[]{:S(2)}) async-start(bf16[16,16,256]{2,1,0:T(8,128)(2,1)} %get-tuple-element.15), calls=%async_computation.1 | async-start | bytes 262144 | tf_op jit(solution)/shard_map/all_to_all | solution.py:190
  49.0 1.3 collective-permute-start.4
  50.3 3.0 %collective-permute-start.3 = (f32[8,256]{1,0:T(8,128)S(1)}, f32[8,256]{1,0:T(8,128)S(1)}, u32[]{:S(2)}, u32[]{:S(2)}) collective-permute-start(f32[8,256]{1,0:T(8,128)S(1)} %copy-done.7), channel_id=1, source_target_pairs={{0,64},{64,128},{128,192},{192,256},{256,320},{320,384},{384,448},... | collective-permute-start | bytes 24584 | tf_op jit(solution)/shard_map/ppermute | solution.py:171
  53.3 0.0 collective-permute-done.4.down
  53.4 0.8 collective-permute-done.3.up
  54.1 9.7 %all-to-all-done.1.parts = bf16[16,16,256]{2,1,0:T(8,128)(2,1)S(1)} async-done(((bf16[16,16,256]{2,1,0:T(8,128)(2,1)}), bf16[16,16,256]{2,1,0:T(8,128)(2,1)S(1)}, u32[]{:S(2)}, u32[]{:S(2)}) %all-to-all-start.1) | async-done | bytes 131104 | tf_op jit(solution)/shard_map/all_to_all | solution.py:190
  63.8 0.0 collective-permute-done.2.c3
  63.8 0.0 collective-permute-done.1.c2
  63.9 0.0 collective-permute-done.c1
  63.9 0.6 copy-done.3
  64.5 0.2 copy-done
  64.7 0.2 copy-done.1
  64.9 0.1 copy-done.2
  65.1 3.1 %shard_map.51 = (f32[8,256]{1,0:T(8,128)}, bf16[16,16,256]{2,1,0:T(8,128)(2,1)}) custom-call(s32[1]{0:T(128)} %bitcast.row_ref, bf16[16,16,256]{2,1,0:T(8,128)(2,1)} %copy-done.3, bf16[64,4096]{1,0:T(8,128)(2,1)} %bitcast.9, bf16[64,4096]{1,0:T(8,128)(2,1)} %copy-done.2, bf16[64,4096]{1,0:T(8,128)(2,1)} %copy-done.1, bf16[64,4096]{1,0:T(8,128)(2,1)} %copy-done, ...), custom_call_target="tpu_custom_call" | custom-call | tf_op jit(solution)/shard_map/pallas_call | solution.py:23
  68.1 3.9 %all-to-all-start.2 = ((bf16[16,16,256]{2,1,0:T(8,128)(2,1)}), bf16[16,16,256]{2,1,0:T(8,128)(2,1)S(1)}, u32[]{:S(2)}, u32[]{:S(2)}) async-start(bf16[16,16,256]{2,1,0:T(8,128)(2,1)} %get-tuple-element.18), calls=%async_computation.2 | async-start | bytes 262144 | tf_op jit(solution)/shard_map/all_to_all | solution.py:190
  72.1 1.3 collective-permute-start.6
  73.4 3.0 %collective-permute-start.5 = (f32[8,256]{1,0:T(8,128)S(1)}, f32[8,256]{1,0:T(8,128)S(1)}, u32[]{:S(2)}, u32[]{:S(2)}) collective-permute-start(f32[8,256]{1,0:T(8,128)S(1)} %copy-done.8), channel_id=1, source_target_pairs={{0,64},{64,128},{128,192},{192,256},{256,320},{320,384},{384,448},... | collective-permute-start | bytes 24584 | tf_op jit(solution)/shard_map/ppermute | solution.py:171
  76.4 0.8 collective-permute-done.5.up
  77.2 9.3 %all-to-all-done.2.parts = bf16[16,16,256]{2,1,0:T(8,128)(2,1)S(1)} async-done(((bf16[16,16,256]{2,1,0:T(8,128)(2,1)}), bf16[16,16,256]{2,1,0:T(8,128)(2,1)S(1)}, u32[]{:S(2)}, u32[]{:S(2)}) %all-to-all-start.2) | async-done | bytes 131104 | tf_op jit(solution)/shard_map/all_to_all | solution.py:190
  86.5 0.7 copy-done.6
  87.1 3.1 %shard_map.52 = (f32[8,256]{1,0:T(8,128)}, bf16[16,16,256]{2,1,0:T(8,128)(2,1)}) custom-call(s32[1]{0:T(128)} %bitcast.row_ref, bf16[16,16,256]{2,1,0:T(8,128)(2,1)} %copy-done.6, bf16[64,4096]{1,0:T(8,128)(2,1)} %bitcast.10, bf16[64,4096]{1,0:T(8,128)(2,1)} %copy-done.2, bf16[64,4096]{1,0:T(8,128)(2,1)} %copy-done.1, bf16[64,4096]{1,0:T(8,128)(2,1)} %copy-done, ...), custom_call_target="tpu_custom_call" | custom-call | tf_op jit(solution)/shard_map/pallas_call | solution.py:23
  90.2 4.0 %all-to-all-start.3 = ((bf16[16,16,256]{2,1,0:T(8,128)(2,1)}), bf16[16,16,256]{2,1,0:T(8,128)(2,1)S(1)}, u32[]{:S(2)}, u32[]{:S(2)}) async-start(bf16[16,16,256]{2,1,0:T(8,128)(2,1)} %get-tuple-element.20), calls=%async_computation.3 | async-start | bytes 262144 | tf_op jit(solution)/shard_map/all_to_all | solution.py:190
  94.3 1.3 collective-permute-start.8
  95.6 3.1 %collective-permute-start.7 = (f32[8,256]{1,0:T(8,128)S(1)}, f32[8,256]{1,0:T(8,128)S(1)}, u32[]{:S(2)}, u32[]{:S(2)}) collective-permute-start(f32[8,256]{1,0:T(8,128)S(1)} %copy-done.9), channel_id=1, source_target_pairs={{0,64},{64,128},{128,192},{192,256},{256,320},{320,384},{384,448},... | collective-permute-start | bytes 24584 | tf_op jit(solution)/shard_map/ppermute | solution.py:171
  98.7 0.8 collective-permute-done.7.up
  99.4 8.7 %all-to-all-done.3.parts = bf16[16,16,256]{2,1,0:T(8,128)(2,1)S(1)} async-done(((bf16[16,16,256]{2,1,0:T(8,128)(2,1)}), bf16[16,16,256]{2,1,0:T(8,128)(2,1)S(1)}, u32[]{:S(2)}, u32[]{:S(2)}) %all-to-all-start.3) | async-done | bytes 131104 | tf_op jit(solution)/shard_map/all_to_all | solution.py:190
  108.2 0.7 copy-done.5
  108.8 3.1 %shard_map.53 = (f32[8,256]{1,0:T(8,128)}, bf16[16,16,256]{2,1,0:T(8,128)(2,1)}) custom-call(s32[1]{0:T(128)} %bitcast.row_ref, bf16[16,16,256]{2,1,0:T(8,128)(2,1)} %copy-done.5, bf16[64,4096]{1,0:T(8,128)(2,1)} %bitcast.11, bf16[64,4096]{1,0:T(8,128)(2,1)} %copy-done.2, bf16[64,4096]{1,0:T(8,128)(2,1)} %copy-done.1, bf16[64,4096]{1,0:T(8,128)(2,1)} %copy-done, ...), custom_call_target="tpu_custom_call" | custom-call | tf_op jit(solution)/shard_map/pallas_call | solution.py:23
  111.9 5.8 %all-to-all-start.4 = ((bf16[16,16,256]{2,1,0:T(8,128)(2,1)}), bf16[16,16,256]{2,1,0:T(8,128)(2,1)S(1)}, u32[]{:S(2)}, u32[]{:S(2)}) async-start(bf16[16,16,256]{2,1,0:T(8,128)(2,1)} %get-tuple-element.22), calls=%async_computation.4 | async-start | bytes 262144 | tf_op jit(solution)/shard_map/all_to_all | solution.py:190
  117.6 1.3 collective-permute-start.10
  118.9 3.1 %collective-permute-start.9 = (f32[8,256]{1,0:T(8,128)S(1)}, f32[8,256]{1,0:T(8,128)S(1)}, u32[]{:S(2)}, u32[]{:S(2)}) collective-permute-start(f32[8,256]{1,0:T(8,128)S(1)} %copy-done.11), channel_id=1, source_target_pairs={{0,64},{64,128},{128,192},{192,256},{256,320},{320,384},{384,448},... | collective-permute-start | bytes 24584 | tf_op jit(solution)/shard_map/ppermute | solution.py:171
  122.1 0.8 collective-permute-done.9.up
  122.8 8.7 %all-to-all-done.4.parts = bf16[16,16,256]{2,1,0:T(8,128)(2,1)S(1)} async-done(((bf16[16,16,256]{2,1,0:T(8,128)(2,1)}), bf16[16,16,256]{2,1,0:T(8,128)(2,1)S(1)}, u32[]{:S(2)}, u32[]{:S(2)}) %all-to-all-start.4) | async-done | bytes 131104 | tf_op jit(solution)/shard_map/all_to_all | solution.py:190
  131.5 0.7 copy-done.4
  132.2 3.0 %shard_map.54 = (f32[8,64]{1,0:T(8,128)}, f32[8,8,128]{2,1,0:T(8,128)}) custom-call(bf16[16,16,256]{2,1,0:T(8,128)(2,1)} %copy-done.4, bf16[64,4096]{1,0:T(8,128)(2,1)} %bitcast.12, bf16[64,4096]{1,0:T(8,128)(2,1)} %copy-done.2, bf16[64,4096]{1,0:T(8,128)(2,1)} %copy-done.1, bf16[64,4096]{1,0:T(8,128)(2,1)} %copy-done, f32[8,256]{1,0:T(8,128)} %get-tuple-element.23.field.f3, ...), custom_call_target="tpu_custom_call" | custom-call | tf_op jit(solution)/shard_map/pallas_call | solution.py:23
  135.2 11.4 %all_to_all.35.tables = f32[8,8,128]{2,1,0:T(8,128)} all-to-all(f32[8,8,128]{2,1,0:T(8,128)} %get-tuple-element.24), channel_id=1, replica_groups=mesh['x'=4,'c'=2,'z'=16,'y'=4] {'x','c'}, dimensions={0} | all-to-all | bytes 65536 | tf_op jit(solution)/shard_map/all_to_all | solution.py:202
  146.6 1.4 shard_map.55
  148.0 18.4 %all_to_all.36.tables = f32[16,8,128]{2,1,0:T(8,128)} all-to-all(f32[16,8,128]{2,1,0:T(8,128)} %shard_map.55), channel_id=1, replica_groups=mesh['x'=4,'c'=2,'z'=16,'y'=4] {'z'}, dimensions={0} | all-to-all | bytes 131072 | tf_op jit(solution)/shard_map/all_to_all | solution.py:204
  166.4 2.0 %shard_map.56 = (f32[8,64]{1,0:T(8,128)}, f32[8,64]{1,0:T(8,128)}) custom-call(f32[16,8,128]{2,1,0:T(8,128)} %all_to_all.36.tables, f32[8,256]{1,0:T(8,128)} %get-tuple-element.16.field.f0, f32[8,256]{1,0:T(8,128)} %get-tuple-element.19.field.f1, f32[8,256]{1,0:T(8,128)} %get-tuple-element.21.field.f2, f32[8,256]{1,0:T(8,128)} %get-tuple-element.23.field.f3, ...), custom_call_target="tpu_custom_call" | custom-call | tf_op jit(solution)/shard_map/pallas_call | solution.py:23
  (40 shorter events, 0.1 us)
Async XLA Ops:
  0.6 12.4 %copy-start.21 = (f32[1,64]{1,0:T(1,128)S(1)}, f32[1,64]{1,0:T(1,128)}, u32[]{:S(2)}) copy-start(f32[1,64]{1,0:T(1,128)} %param.5) | copy-start | bytes 772
  0.6 12.4 %copy-start.20 = (f32[1,8,64]{2,1,0:T(8,128)S(1)}, f32[1,8,64]{2,1,0:T(8,128)}, u32[]{:S(2)}) copy-start(f32[1,8,64]{2,1,0:T(8,128)} %param.3) | copy-start | bytes 6148
  0.6 63.2 %collective-permute-start.2 = (bf16[64,4096]{1,0:T(8,128)(2,1)}, bf16[64,4096]{1,0:T(8,128)(2,1)S(1)}, u32[]{:S(2)}, u32[]{:S(2)}) collective-permute-start(bf16[64,4096]{1,0:T(8,128)(2,1)} %bitcast.6), channel_id=1, source_target_pairs={{3,0},{0,1},{1,2},{2,3},{7,4},{4,5},{5,6},{6,7},{11,8},{8,9},{9,10... | collective-permute-start | bytes 1572872 | tf_op jit(solution)/shard_map/ppermute | solution.py:181
  8.3 55.6 %collective-permute-start.1 = (bf16[64,4096]{1,0:T(8,128)(2,1)}, bf16[64,4096]{1,0:T(8,128)(2,1)S(1)}, u32[]{:S(2)}, u32[]{:S(2)}) collective-permute-start(bf16[64,4096]{1,0:T(8,128)(2,1)} %bitcast.7), channel_id=1, source_target_pairs={{2,0},{3,1},{0,2},{1,3},{6,4},{7,5},{4,6},{5,7},{10,8},{11,9},{8,1... | collective-permute-start | bytes 1572872 | tf_op jit(solution)/shard_map/ppermute | solution.py:181
  10.2 53.6 %collective-permute-start = (bf16[64,4096]{1,0:T(8,128)(2,1)}, bf16[64,4096]{1,0:T(8,128)(2,1)S(1)}, u32[]{:S(2)}, u32[]{:S(2)}) collective-permute-start(bf16[64,4096]{1,0:T(8,128)(2,1)} %bitcast.8), channel_id=1, source_target_pairs={{1,0},{2,1},{3,2},{0,3},{5,4},{6,5},{7,6},{4,7},{9,8},{10,9},{11,1... | collective-permute-start | bytes 1572872 | tf_op jit(solution)/shard_map/ppermute | solution.py:181
  13.7 17.8 %all-to-all-start = ((f32[4,8,128]{2,1,0:T(8,128)}), f32[4,8,128]{2,1,0:T(8,128)S(1)}, u32[]{:S(2)}, u32[]{:S(2)}) async-start(f32[4,8,128]{2,1,0:T(8,128)} %broadcast_in_dim.21), calls=%async_computation | async-start | bytes 32768 | tf_op jit(solution)/shard_map/all_to_all | solution.py:183
  31.5 0.6 copy-start.10
  33.7 15.3 %copy-start.7 = (f32[8,256]{1,0:T(8,128)S(1)}, f32[8,256]{1,0:T(8,128)}, u32[]{:S(2)}) copy-start(f32[8,256]{1,0:T(8,128)} %get-tuple-element.16.field.f0) | copy-start | bytes 24580
  33.7 30.2 %all-to-all-start.1 = ((bf16[16,16,256]{2,1,0:T(8,128)(2,1)}), bf16[16,16,256]{2,1,0:T(8,128)(2,1)S(1)}, u32[]{:S(2)}, u32[]{:S(2)}) async-start(bf16[16,16,256]{2,1,0:T(8,128)(2,1)} %get-tuple-element.15), calls=%async_computation.1 | async-start | bytes 262144 | tf_op jit(solution)/shard_map/all_to_all | solution.py:190
  49.0 4.3 %collective-permute-start.4 = (f32[8,256]{1,0:T(8,128)S(1)}, f32[8,256]{1,0:T(8,128)S(1)}, u32[]{:S(2)}, u32[]{:S(2)}) collective-permute-start(f32[8,256]{1,0:T(8,128)S(1)} %copy-done.7), channel_id=1, source_target_pairs={{64,0},{128,64},{192,128},{256,192},{320,256},{384,320},{448,384},... | collective-permute-start | bytes 24584 | tf_op jit(solution)/shard_map/ppermute | solution.py:172
  50.3 3.8 %collective-permute-start.3 = (f32[8,256]{1,0:T(8,128)S(1)}, f32[8,256]{1,0:T(8,128)S(1)}, u32[]{:S(2)}, u32[]{:S(2)}) collective-permute-start(f32[8,256]{1,0:T(8,128)S(1)} %copy-done.7), channel_id=1, source_target_pairs={{0,64},{64,128},{128,192},{192,256},{256,320},{320,384},{384,448},... | collective-permute-start | bytes 24584 | tf_op jit(solution)/shard_map/ppermute | solution.py:171
  53.3 10.5 %copy-start.12 = (f32[8,256]{1,0:T(8,128)}, f32[8,256]{1,0:T(8,128)S(1)}, u32[]{:S(2)}) copy-start(f32[8,256]{1,0:T(8,128)S(1)} %collective-permute-done.4.down) | copy-start | bytes 24580
  54.1 9.8 %copy-start.13 = (f32[8,256]{1,0:T(8,128)}, f32[8,256]{1,0:T(8,128)S(1)}, u32[]{:S(2)}) copy-start(f32[8,256]{1,0:T(8,128)S(1)} %collective-permute-done.3.up) | copy-start | bytes 24580
  63.8 0.7 copy-start.3
  63.8 0.9 copy-start
  63.9 1.1 copy-start.1
  63.9 1.2 copy-start.2
  68.1 3.9 %copy-start.8 = (f32[8,256]{1,0:T(8,128)S(1)}, f32[8,256]{1,0:T(8,128)}, u32[]{:S(2)}) copy-start(f32[8,256]{1,0:T(8,128)} %get-tuple-element.19.field.f1) | copy-start | bytes 24580
  68.1 18.3 %all-to-all-start.2 = ((bf16[16,16,256]{2,1,0:T(8,128)(2,1)}), bf16[16,16,256]{2,1,0:T(8,128)(2,1)S(1)}, u32[]{:S(2)}, u32[]{:S(2)}) async-start(bf16[16,16,256]{2,1,0:T(8,128)(2,1)} %get-tuple-element.18), calls=%async_computation.2 | async-start | bytes 262144 | tf_op jit(solution)/shard_map/all_to_all | solution.py:190
  72.1 4.3 %collective-permute-start.6 = (f32[8,256]{1,0:T(8,128)S(1)}, f32[8,256]{1,0:T(8,128)S(1)}, u32[]{:S(2)}, u32[]{:S(2)}) collective-permute-start(f32[8,256]{1,0:T(8,128)S(1)} %copy-done.8), channel_id=1, source_target_pairs={{64,0},{128,64},{192,128},{256,192},{320,256},{384,320},{448,384},... | collective-permute-start | bytes 24584 | tf_op jit(solution)/shard_map/ppermute | solution.py:172
  73.4 3.8 %collective-permute-start.5 = (f32[8,256]{1,0:T(8,128)S(1)}, f32[8,256]{1,0:T(8,128)S(1)}, u32[]{:S(2)}, u32[]{:S(2)}) collective-permute-start(f32[8,256]{1,0:T(8,128)S(1)} %copy-done.8), channel_id=1, source_target_pairs={{0,64},{64,128},{128,192},{192,256},{256,320},{320,384},{384,448},... | collective-permute-start | bytes 24584 | tf_op jit(solution)/shard_map/ppermute | solution.py:171
  76.4 10.1 %copy-start.17 = (f32[8,256]{1,0:T(8,128)}, f32[8,256]{1,0:T(8,128)S(1)}, u32[]{:S(2)}) copy-start(f32[8,256]{1,0:T(8,128)S(1)} %collective-permute-done.6.down) | copy-start | bytes 24580
  77.2 9.3 %copy-start.19 = (f32[8,256]{1,0:T(8,128)}, f32[8,256]{1,0:T(8,128)S(1)}, u32[]{:S(2)}) copy-start(f32[8,256]{1,0:T(8,128)S(1)} %collective-permute-done.5.up) | copy-start | bytes 24580
  86.5 0.7 copy-start.6
  90.2 4.0 %copy-start.9 = (f32[8,256]{1,0:T(8,128)S(1)}, f32[8,256]{1,0:T(8,128)}, u32[]{:S(2)}) copy-start(f32[8,256]{1,0:T(8,128)} %get-tuple-element.21.field.f2) | copy-start | bytes 24580
  90.2 17.9 %all-to-all-start.3 = ((bf16[16,16,256]{2,1,0:T(8,128)(2,1)}), bf16[16,16,256]{2,1,0:T(8,128)(2,1)S(1)}, u32[]{:S(2)}, u32[]{:S(2)}) async-start(bf16[16,16,256]{2,1,0:T(8,128)(2,1)} %get-tuple-element.20), calls=%async_computation.3 | async-start | bytes 262144 | tf_op jit(solution)/shard_map/all_to_all | solution.py:190
  94.3 4.4 %collective-permute-start.8 = (f32[8,256]{1,0:T(8,128)S(1)}, f32[8,256]{1,0:T(8,128)S(1)}, u32[]{:S(2)}, u32[]{:S(2)}) collective-permute-start(f32[8,256]{1,0:T(8,128)S(1)} %copy-done.9), channel_id=1, source_target_pairs={{64,0},{128,64},{192,128},{256,192},{320,256},{384,320},{448,384},... | collective-permute-start | bytes 24584 | tf_op jit(solution)/shard_map/ppermute | solution.py:172
  95.6 3.9 %collective-permute-start.7 = (f32[8,256]{1,0:T(8,128)S(1)}, f32[8,256]{1,0:T(8,128)S(1)}, u32[]{:S(2)}, u32[]{:S(2)}) collective-permute-start(f32[8,256]{1,0:T(8,128)S(1)} %copy-done.9), channel_id=1, source_target_pairs={{0,64},{64,128},{128,192},{192,256},{256,320},{320,384},{384,448},... | collective-permute-start | bytes 24584 | tf_op jit(solution)/shard_map/ppermute | solution.py:171
  98.6 9.5 %copy-start.15 = (f32[8,256]{1,0:T(8,128)}, f32[8,256]{1,0:T(8,128)S(1)}, u32[]{:S(2)}) copy-start(f32[8,256]{1,0:T(8,128)S(1)} %collective-permute-done.8.down) | copy-start | bytes 24580
  99.4 8.7 %copy-start.18 = (f32[8,256]{1,0:T(8,128)}, f32[8,256]{1,0:T(8,128)S(1)}, u32[]{:S(2)}) copy-start(f32[8,256]{1,0:T(8,128)S(1)} %collective-permute-done.7.up) | copy-start | bytes 24580
  108.1 0.7 copy-start.5
  111.9 5.8 %copy-start.11 = (f32[8,256]{1,0:T(8,128)S(1)}, f32[8,256]{1,0:T(8,128)}, u32[]{:S(2)}) copy-start(f32[8,256]{1,0:T(8,128)} %get-tuple-element.23.field.f3) | copy-start | bytes 24580
  111.9 19.7 %all-to-all-start.4 = ((bf16[16,16,256]{2,1,0:T(8,128)(2,1)}), bf16[16,16,256]{2,1,0:T(8,128)(2,1)S(1)}, u32[]{:S(2)}, u32[]{:S(2)}) async-start(bf16[16,16,256]{2,1,0:T(8,128)(2,1)} %get-tuple-element.22), calls=%async_computation.4 | async-start | bytes 262144 | tf_op jit(solution)/shard_map/all_to_all | solution.py:190
  117.6 4.4 %collective-permute-start.10 = (f32[8,256]{1,0:T(8,128)S(1)}, f32[8,256]{1,0:T(8,128)S(1)}, u32[]{:S(2)}, u32[]{:S(2)}) collective-permute-start(f32[8,256]{1,0:T(8,128)S(1)} %copy-done.11), channel_id=1, source_target_pairs={{64,0},{128,64},{192,128},{256,192},{320,256},{384,320},{448,384},... | collective-permute-start | bytes 24584 | tf_op jit(solution)/shard_map/ppermute | solution.py:172
  118.9 3.9 %collective-permute-start.9 = (f32[8,256]{1,0:T(8,128)S(1)}, f32[8,256]{1,0:T(8,128)S(1)}, u32[]{:S(2)}, u32[]{:S(2)}) collective-permute-start(f32[8,256]{1,0:T(8,128)S(1)} %copy-done.11), channel_id=1, source_target_pairs={{0,64},{64,128},{128,192},{192,256},{256,320},{320,384},{384,448},... | collective-permute-start | bytes 24584 | tf_op jit(solution)/shard_map/ppermute | solution.py:171
  122.0 9.5 %copy-start.14 = (f32[8,256]{1,0:T(8,128)}, f32[8,256]{1,0:T(8,128)S(1)}, u32[]{:S(2)}) copy-start(f32[8,256]{1,0:T(8,128)S(1)} %collective-permute-done.10.down) | copy-start | bytes 24580
  122.8 8.7 %copy-start.16 = (f32[8,256]{1,0:T(8,128)}, f32[8,256]{1,0:T(8,128)S(1)}, u32[]{:S(2)}) copy-start(f32[8,256]{1,0:T(8,128)S(1)} %collective-permute-done.9.up) | copy-start | bytes 24580
  131.5 0.7 copy-start.4

commit v2 on v1

--- a/solution.py
+++ b/solution.py
@@ -18,6 +18,10 @@
 
 
 def call(body, outs, *args, smem=0):
+    args = args[:smem] + tuple(
+        pltpu.with_memory_space_constraint(x, pltpu.VMEM) for x in args[smem:]
+    )
+    outs = jax.tree.map(lambda o: pltpu.VMEM(o.shape, o.dtype), outs)
     specs = [pl.BlockSpec(memory_space=pltpu.SMEM)] * smem
     specs += [pl.BlockSpec(memory_space=pltpu.VMEM)] * (len(args) - smem)
     return pl.pallas_call(
@@ -66,14 +70,14 @@
     return (own + blended - (up[...] + down[...])) * (1.0 / SCALE)
 
 
-def step(row_ref, parts, c0, c1, c2, c3, field, diag, up, down, field_out, send):
-    out = next_field(parts, (c0, c1, c2, c3), field, diag, up, down)
+def step(row_ref, parts, c0, c1, c2, c3, c4, field, diag, up, down, field_out, send):
+    out = next_field(parts, (c0, c1, c2, c3, c4), field, diag, up, down)
     field_out[...] = out
     store_parts(send, out, row_ref[0])
 
 
-def last_step(parts, c0, c1, c2, c3, field, diag, up, down, f0, f1, f2, field_out, send):
-    out = next_field(parts, (c0, c1, c2, c3), field, diag, up, down)
+def last_step(parts, c0, c1, c2, c3, c4, field, diag, up, down, f0, f1, f2, field_out, send):
+    out = next_field(parts, (c0, c1, c2, c3, c4), field, diag, up, down)
     field_out[...] = out[:, :H]
     fields = [f0[...], f1[...], f2[...], field[...], out]
     lane = lax.broadcasted_iota(jnp.int32, (B, 128), 1)
@@ -166,6 +170,10 @@
     return lax.all_to_all(array, axes, 0, 0, tiled=True)
 
 
+def shifted(array, shift):
+    return lax.ppermute(array, "y", [((y + shift) % NY, y) for y in range(NY)])
+
+
 def neighbours(field):
     ends = NX * NC - 1
     up = lax.ppermute(field, ("x", "c"), [(i, i + 1) for i in range(ends)])
@@ -176,11 +184,11 @@
 def on_device(source, coupling, diagonal):
     own = coupling[0]
     row = lax.axis_index("y").astype(jnp.int32).reshape(1)
-    blocks = [own]
-    for shift in range(1, NY):
-        blocks.append(lax.ppermute(own, "y", [((y + shift) % NY, y) for y in range(NY)]))
     packed = jnp.concatenate([source[0], jnp.broadcast_to(diagonal, (B, H))], axis=1)
     packed = lax.all_to_all(jnp.broadcast_to(packed[None], (NY, B, 128)), "y", 0, 0, tiled=True)
+    own, packed = lax.optimization_barrier((own, packed))
+    after, before = shifted(own, 1), shifted(own, -1)
+    blocks = [own, after, shifted(after[: H // 2], 1), shifted(before[H // 2 :], -1), before]
     shape = jax.ShapeDtypeStruct
     field_shape, send_shape = shape((B, W), F32), shape((NZ, 2 * B, W), BF16)
     field, diag, send = call(unpack, (field_shape, field_shape, send_shape), row, packed, smem=1)

time: 171 us -> 146 us (0.85); the launches traced: 168 us -> 145 us
  waiting for transfers between devices: 50.7 us -> 29.4 us
  Pallas kernels: 17.2 us -> 6.67 us
  blocking collectives: 29.8 us -> 38.7 us
  local copies, waits for them, and re-layouts: 4.48 us -> 1.95 us
  starting transfers between devices: 65.3 us -> 67.8 us
    all_to_all x4, waiting for transfers between devices: 36.3 us -> 19.7 us  [on_device(): parts = lax.all_to_all(send, 'z', 0, 0, tiled=True)]
    all_to_all x0 -> x1, blocking collectives: none -> 11.2 us  [on_device(): lax.all_to_all(jnp.broadcast_to(packed[None], (NY, B, 128)), 'y', 0, 0, t...]
    all_to_all x1 -> x0, waiting for transfers between devices: 11.2 us -> none  [on_device(): lax.all_to_all(jnp.broadcast_to(packed[None], (NY, B, 128)), 'y', 0, 0, t...]
    pallas_call x7, Pallas kernels: 17.2 us -> 6.67 us  [call(): pl.pallas_call(body, out_shape=outs, in_specs=specs, out_specs=jax.tree.m...]
    ppermute x4, waiting for transfers between devices: 0.01 us -> 9.72 us  [neighbours(): down = lax.ppermute(field, ('x', 'c'), [(i + 1, i) for i in range(ends)])]
    all_to_all x4, starting transfers between devices: 29 us -> 36.4 us  [on_device(): parts = lax.all_to_all(send, 'z', 0, 0, tiled=True)]
    all_to_all x1 -> x0, starting transfers between devices: 6.56 us -> none  [on_device(): lax.all_to_all(jnp.broadcast_to(packed[None], (NY, B, 128)), 'y', 0, 0, t...]
    ppermute x4, waiting for transfers between devices: 3.16 us -> 0.01 us  [neighbours(): up = lax.ppermute(field, ('x', 'c'), [(i, i + 1) for i in range(ends)])]
  transfers between devices with their start and end apart: 16 -> 16, of which waited for: 9 -> 7; matrix products, arithmetic and copies ran while one was open for 0% -> 0% of each run, Pallas kernels for 1% -> 1%
where the time goes in v2:
time: 146 us; the launch traced here: 145 us
  starting transfers between devices  67.8 us (46%)
  blocking collectives  38.7 us (27%)
  waiting for transfers between devices  29.4 us (20%)
  Pallas kernels  6.67 us (5%)
  local copies, waits for them, and re-layouts  1.95 us (1%)
    all_to_all x4, starting transfers between devices, on_device(): parts = lax.all_to_all(send, 'z', 0, 0, tiled=True)  36.4 us
    all_to_all x4, waiting for transfers between devices, on_device(): parts = lax.all_to_all(send, 'z', 0, 0, tiled=True)  19.7 us
    all_to_all x1, blocking collectives, on_device(): table = lax.all_to_all(table, 'z', 0, 0, tiled=True)  16.7 us
    ppermute x4, starting transfers between devices, shifted(): return lax.ppermute(array, 'y', [((y + shift) % NY, y) for y in range(NY)])  14.2 us
    ppermute x4, starting transfers between devices, neighbours(): up = lax.ppermute(field, ('x', 'c'), [(i, i + 1) for i in range(ends)])  12.1 us
    all_to_all x1, blocking collectives, on_device(): lax.all_to_all(jnp.broadcast_to(packed[None], (NY, B, 128)), 'y', 0, 0, t...  11.2 us
    all_to_all x1, blocking collectives, on_device(): table = lax.all_to_all(table, ('x', 'c'), 0, 0, tiled=True)  10.8 us
    ppermute x4, waiting for transfers between devices, neighbours(): down = lax.ppermute(field, ('x', 'c'), [(i + 1, i) for i in range(ends)])  9.72 us
  transfers between devices with their start and end apart: 16, of which 7 were waited for; matrix products, arithmetic and copies ran while one was open for 0% of the time, Pallas kernels for 1%

profile of v2, /device:TPU:24, one launch (start us, length us, event | category | flops | bytes accessed | tf_op | source)
XLA Modules:
  0.0 145.5 jit_solution(6392357136722252068)
XLA Ops:
  0.6 0.0 copy-start.2
  0.6 0.6 copy-done.2
  1.3 0.1 pad.1.clone
  1.4 11.2 %all_to_all.35.packed = f32[4,8,128]{2,1,0:T(8,128)S(1)} all-to-all(f32[4,8,128]{2,1,0:T(8,128)S(1)} %broadcast_in_dim.21), channel_id=1, replica_groups=mesh['x'=4,'c'=2,'z'=16,'y'=4] {'y'}, dimensions={0} | all-to-all | bytes 32768 | tf_op jit(solution)/shard_map/all_to_all | solution.py:188
  12.6 2.5 %collective-permute-start = (bf16[64,4096]{1,0:T(8,128)(2,1)}, bf16[64,4096]{1,0:T(8,128)(2,1)S(1)}, u32[]{:S(2)}, u32[]{:S(2)}) collective-permute-start(bf16[64,4096]{1,0:T(8,128)(2,1)} %bitcast.8), channel_id=1, source_target_pairs={{1,0},{2,1},{3,2},{0,3},{5,4},{6,5},{7,6},{4,7},{9,8},{10,9},{11,1... | collective-permute-start | bytes 1572872 | tf_op jit(solution)/shard_map/ppermute | solution.py:174
  15.1 4.6 %collective-permute-start.2 = (bf16[64,4096]{1,0:T(8,128)(2,1)}, bf16[64,4096]{1,0:T(8,128)(2,1)S(1)}, u32[]{:S(2)}, u32[]{:S(2)}) collective-permute-start(bf16[64,4096]{1,0:T(8,128)(2,1)} %bitcast.9), channel_id=1, source_target_pairs={{3,0},{0,1},{1,2},{2,3},{7,4},{4,5},{5,6},{6,7},{11,8},{8,9},{9,10... | collective-permute-start | bytes 1572872 | tf_op jit(solution)/shard_map/ppermute | solution.py:174
  19.7 0.9 shard_map.50
  20.6 11.7 %all-to-all-start.1 = ((bf16[16,16,256]{2,1,0:T(8,128)(2,1)}), bf16[16,16,256]{2,1,0:T(8,128)(2,1)S(1)}, u32[]{:S(2)}, u32[]{:S(2)}) async-start(bf16[16,16,256]{2,1,0:T(8,128)(2,1)} %get-tuple-element.18), calls=%async_computation.1 | async-start | bytes 262144 | tf_op jit(solution)/shard_map/all_to_all | solution.py:198
  32.3 0.0 copy-start
  32.3 0.0 collective-permute-done.c1
  32.4 2.1 %collective-permute-start.1 = (bf16[32,4096]{1,0:T(8,128)(2,1)S(1)}, bf16[32,4096]{1,0:T(8,128)(2,1)S(1)}, u32[]{:S(2)}, u32[]{:S(2)}) collective-permute-start(bf16[32,4096]{1,0:T(8,128)(2,1)S(1)} %slice.8), channel_id=1, source_target_pairs={{1,0},{2,1},{3,2},{0,3},{5,4},{6,5},{7,6},{4,7},{9,8},{10,9},{11,1... | collective-permute-start | bytes 786440 | tf_op jit(solution)/shard_map/ppermute | solution.py:174
  34.4 0.0 collective-permute-done.2.c4
  34.5 5.1 %collective-permute-start.3 = (bf16[32,4096]{1,0:T(8,128)(2,1)S(1)}, bf16[32,4096]{1,0:T(8,128)(2,1)S(1)}, u32[]{:S(2)}, u32[]{:S(2)}) collective-permute-start(bf16[32,4096]{1,0:T(8,128)(2,1)S(1)} %slice.9), channel_id=1, source_target_pairs={{3,0},{0,1},{1,2},{2,3},{7,4},{4,5},{5,6},{6,7},{11,8},{8,9},{9,10... | collective-permute-start | bytes 786440 | tf_op jit(solution)/shard_map/ppermute | solution.py:174
  39.6 1.3 collective-permute-start.4
  40.9 1.3 collective-permute-start.5
  42.2 0.0 collective-permute-done.4.up
  42.2 3.5 %collective-permute-done.5.down = f32[8,256]{1,0:T(8,128)S(1)} collective-permute-done((f32[8,256]{1,0:T(8,128)S(1)}, f32[8,256]{1,0:T(8,128)S(1)}, u32[]{:S(2)}, u32[]{:S(2)}) %collective-permute-start.5) | collective-permute-done | bytes 8224 | tf_op jit(solution)/shard_map/ppermute | solution.py:180
  45.7 0.0 all-to-all-done.1.parts
  45.7 0.0 collective-permute-done.1.c2
  45.7 0.0 collective-permute-done.3.c3
  45.7 0.0 copy-done
  45.7 1.5 %shard_map.51 = (f32[8,256]{1,0:T(8,128)S(1)}, bf16[16,16,256]{2,1,0:T(8,128)(2,1)}) custom-call(s32[1]{0:T(128)} %bitcast.row_ref, bf16[16,16,256]{2,1,0:T(8,128)(2,1)S(1)} %all-to-all-done.1.parts, bf16[64,4096]{1,0:T(8,128)(2,1)S(1)} %bitcast.10, bf16[64,4096]{1,0:T(8,128)(2,1)S(1)} %collective-permute-done.c1, ...), custom_call_target="tpu_custom_call" | custom-call | tf_op jit(solution)/shard_map/pallas_call | solution.py:27
  47.2 12.0 %all-to-all-start.2 = ((bf16[16,16,256]{2,1,0:T(8,128)(2,1)}), bf16[16,16,256]{2,1,0:T(8,128)(2,1)S(1)}, u32[]{:S(2)}, u32[]{:S(2)}) async-start(bf16[16,16,256]{2,1,0:T(8,128)(2,1)} %get-tuple-element.22), calls=%async_computation.2 | async-start | bytes 262144 | tf_op jit(solution)/shard_map/all_to_all | solution.py:198
  59.2 4.0 %collective-permute-start.6 = (f32[8,256]{1,0:T(8,128)S(1)}, f32[8,256]{1,0:T(8,128)S(1)}, u32[]{:S(2)}, u32[]{:S(2)}) collective-permute-start(f32[8,256]{1,0:T(8,128)S(1)} %get-tuple-element.23.field.f1), channel_id=1, source_target_pairs={{0,64},{64,128},{128,192},{192,256},{256,320},{320,384},{384,448},... | collective-permute-start | bytes 24584 | tf_op jit(solution)/shard_map/ppermute | solution.py:179
  63.3 1.3 collective-permute-start.7
  64.6 0.0 collective-permute-done.6.up
  64.6 1.8 %collective-permute-done.7.down = f32[8,256]{1,0:T(8,128)S(1)} collective-permute-done((f32[8,256]{1,0:T(8,128)S(1)}, f32[8,256]{1,0:T(8,128)S(1)}, u32[]{:S(2)}, u32[]{:S(2)}) %collective-permute-start.7) | collective-permute-done | bytes 8224 | tf_op jit(solution)/shard_map/ppermute | solution.py:180
  66.3 6.0 %all-to-all-done.2.parts = bf16[16,16,256]{2,1,0:T(8,128)(2,1)S(1)} async-done(((bf16[16,16,256]{2,1,0:T(8,128)(2,1)}), bf16[16,16,256]{2,1,0:T(8,128)(2,1)S(1)}, u32[]{:S(2)}, u32[]{:S(2)}) %all-to-all-start.2) | async-done | bytes 131104 | tf_op jit(solution)/shard_map/all_to_all | solution.py:198
  72.4 1.5 %shard_map.52 = (f32[8,256]{1,0:T(8,128)S(1)}, bf16[16,16,256]{2,1,0:T(8,128)(2,1)}) custom-call(s32[1]{0:T(128)} %bitcast.row_ref, bf16[16,16,256]{2,1,0:T(8,128)(2,1)S(1)} %all-to-all-done.2.parts, bf16[64,4096]{1,0:T(8,128)(2,1)S(1)} %bitcast.11, bf16[64,4096]{1,0:T(8,128)(2,1)S(1)} %collective-permute-done.c1, ...), custom_call_target="tpu_custom_call" | custom-call | tf_op jit(solution)/shard_map/pallas_call | solution.py:27
  73.8 6.5 %all-to-all-start.3 = ((bf16[16,16,256]{2,1,0:T(8,128)(2,1)}), bf16[16,16,256]{2,1,0:T(8,128)(2,1)S(1)}, u32[]{:S(2)}, u32[]{:S(2)}) async-start(bf16[16,16,256]{2,1,0:T(8,128)(2,1)} %get-tuple-element.24), calls=%async_computation.3 | async-start | bytes 262144 | tf_op jit(solution)/shard_map/all_to_all | solution.py:198
  80.3 3.4 %collective-permute-start.8 = (f32[8,256]{1,0:T(8,128)S(1)}, f32[8,256]{1,0:T(8,128)S(1)}, u32[]{:S(2)}, u32[]{:S(2)}) collective-permute-start(f32[8,256]{1,0:T(8,128)S(1)} %get-tuple-element.25.field.f2), channel_id=1, source_target_pairs={{0,64},{64,128},{128,192},{192,256},{256,320},{320,384},{384,448},... | collective-permute-start | bytes 24584 | tf_op jit(solution)/shard_map/ppermute | solution.py:179
  83.7 1.3 collective-permute-start.9
  85.0 0.0 collective-permute-done.8.up
  85.0 2.6 %collective-permute-done.9.down = f32[8,256]{1,0:T(8,128)S(1)} collective-permute-done((f32[8,256]{1,0:T(8,128)S(1)}, f32[8,256]{1,0:T(8,128)S(1)}, u32[]{:S(2)}, u32[]{:S(2)}) %collective-permute-start.9) | collective-permute-done | bytes 8224 | tf_op jit(solution)/shard_map/ppermute | solution.py:180
  87.6 6.5 %all-to-all-done.3.parts = bf16[16,16,256]{2,1,0:T(8,128)(2,1)S(1)} async-done(((bf16[16,16,256]{2,1,0:T(8,128)(2,1)}), bf16[16,16,256]{2,1,0:T(8,128)(2,1)S(1)}, u32[]{:S(2)}, u32[]{:S(2)}) %all-to-all-start.3) | async-done | bytes 131104 | tf_op jit(solution)/shard_map/all_to_all | solution.py:198
  94.1 1.5 %shard_map.53 = (f32[8,256]{1,0:T(8,128)S(1)}, bf16[16,16,256]{2,1,0:T(8,128)(2,1)}) custom-call(s32[1]{0:T(128)} %bitcast.row_ref, bf16[16,16,256]{2,1,0:T(8,128)(2,1)S(1)} %all-to-all-done.3.parts, bf16[64,4096]{1,0:T(8,128)(2,1)S(1)} %bitcast.12, bf16[64,4096]{1,0:T(8,128)(2,1)S(1)} %collective-permute-done.c1, ...), custom_call_target="tpu_custom_call" | custom-call | tf_op jit(solution)/shard_map/pallas_call | solution.py:27
  95.6 6.1 %all-to-all-start.4 = ((bf16[16,16,256]{2,1,0:T(8,128)(2,1)}), bf16[16,16,256]{2,1,0:T(8,128)(2,1)S(1)}, u32[]{:S(2)}, u32[]{:S(2)}) async-start(bf16[16,16,256]{2,1,0:T(8,128)(2,1)} %get-tuple-element.26), calls=%async_computation.4 | async-start | bytes 262144 | tf_op jit(solution)/shard_map/all_to_all | solution.py:198
  101.7 3.4 %collective-permute-start.10 = (f32[8,256]{1,0:T(8,128)S(1)}, f32[8,256]{1,0:T(8,128)S(1)}, u32[]{:S(2)}, u32[]{:S(2)}) collective-permute-start(f32[8,256]{1,0:T(8,128)S(1)} %get-tuple-element.27.field.f3), channel_id=1, source_target_pairs={{0,64},{64,128},{128,192},{192,256},{256,320},{320,384},{384,448},... | collective-permute-start | bytes 24584 | tf_op jit(solution)/shard_map/ppermute | solution.py:179
  105.1 1.3 collective-permute-start.11
  106.4 0.0 collective-permute-done.10.up
  106.4 1.9 %collective-permute-done.11.down = f32[8,256]{1,0:T(8,128)S(1)} collective-permute-done((f32[8,256]{1,0:T(8,128)S(1)}, f32[8,256]{1,0:T(8,128)S(1)}, u32[]{:S(2)}, u32[]{:S(2)}) %collective-permute-start.11) | collective-permute-done | bytes 8224 | tf_op jit(solution)/shard_map/ppermute | solution.py:180
  108.3 7.1 %all-to-all-done.4.parts = bf16[16,16,256]{2,1,0:T(8,128)(2,1)S(1)} async-done(((bf16[16,16,256]{2,1,0:T(8,128)(2,1)}), bf16[16,16,256]{2,1,0:T(8,128)(2,1)S(1)}, u32[]{:S(2)}, u32[]{:S(2)}) %all-to-all-start.4) | async-done | bytes 131104 | tf_op jit(solution)/shard_map/all_to_all | solution.py:198
  115.5 0.8 shard_map.54
  116.3 10.8 %all_to_all.36.tables = f32[8,8,128]{2,1,0:T(8,128)S(1)} all-to-all(f32[8,8,128]{2,1,0:T(8,128)S(1)} %get-tuple-element.28), channel_id=1, replica_groups=mesh['x'=4,'c'=2,'z'=16,'y'=4] {'x','c'}, dimensions={0} | all-to-all | bytes 65536 | tf_op jit(solution)/shard_map/all_to_all | solution.py:210
  127.1 16.7 %all_to_all.37.tables = f32[16,8,128]{2,1,0:T(8,128)S(1)} all-to-all(f32[16,8,128]{2,1,0:T(8,128)S(1)} %shard_map.55), channel_id=1, replica_groups=mesh['x'=4,'c'=2,'z'=16,'y'=4] {'z'}, dimensions={0} | all-to-all | bytes 131072 | tf_op jit(solution)/shard_map/all_to_all | solution.py:212
  143.8 0.5 shard_map.56
  144.3 0.6 copy.5
  144.9 0.6 copy.6
  (7 shorter events, 0.1 us)
Async XLA Ops:
  0.6 0.7 copy-start.2
  0.6 0.7 copy-start.1
  12.6 19.7 %collective-permute-start = (bf16[64,4096]{1,0:T(8,128)(2,1)}, bf16[64,4096]{1,0:T(8,128)(2,1)S(1)}, u32[]{:S(2)}, u32[]{:S(2)}) collective-permute-start(bf16[64,4096]{1,0:T(8,128)(2,1)} %bitcast.8), channel_id=1, source_target_pairs={{1,0},{2,1},{3,2},{0,3},{5,4},{6,5},{7,6},{4,7},{9,8},{10,9},{11,1... | collective-permute-start | bytes 1572872 | tf_op jit(solution)/shard_map/ppermute | solution.py:174
  15.1 19.3 %collective-permute-start.2 = (bf16[64,4096]{1,0:T(8,128)(2,1)}, bf16[64,4096]{1,0:T(8,128)(2,1)S(1)}, u32[]{:S(2)}, u32[]{:S(2)}) collective-permute-start(bf16[64,4096]{1,0:T(8,128)(2,1)} %bitcast.9), channel_id=1, source_target_pairs={{3,0},{0,1},{1,2},{2,3},{7,4},{4,5},{5,6},{6,7},{11,8},{8,9},{9,10... | collective-permute-start | bytes 1572872 | tf_op jit(solution)/shard_map/ppermute | solution.py:174
  20.6 25.1 %all-to-all-start.1 = ((bf16[16,16,256]{2,1,0:T(8,128)(2,1)}), bf16[16,16,256]{2,1,0:T(8,128)(2,1)S(1)}, u32[]{:S(2)}, u32[]{:S(2)}) async-start(bf16[16,16,256]{2,1,0:T(8,128)(2,1)} %get-tuple-element.18), calls=%async_computation.1 | async-start | bytes 262144 | tf_op jit(solution)/shard_map/all_to_all | solution.py:198
  32.3 13.4 %copy-start = (bf16[1,64,4096]{2,1,0:T(8,128)(2,1)S(1)}, bf16[1,64,4096]{2,1,0:T(8,128)(2,1)}, u32[]{:S(2)}) copy-start(bf16[1,64,4096]{2,1,0:T(8,128)(2,1)} %param.4) | copy-start | bytes 1572868
  32.4 13.3 %collective-permute-start.1 = (bf16[32,4096]{1,0:T(8,128)(2,1)S(1)}, bf16[32,4096]{1,0:T(8,128)(2,1)S(1)}, u32[]{:S(2)}, u32[]{:S(2)}) collective-permute-start(bf16[32,4096]{1,0:T(8,128)(2,1)S(1)} %slice.8), channel_id=1, source_target_pairs={{1,0},{2,1},{3,2},{0,3},{5,4},{6,5},{7,6},{4,7},{9,8},{10,9},{11,1... | collective-permute-start | bytes 786440 | tf_op jit(solution)/shard_map/ppermute | solution.py:174
  34.5 11.2 %collective-permute-start.3 = (bf16[32,4096]{1,0:T(8,128)(2,1)S(1)}, bf16[32,4096]{1,0:T(8,128)(2,1)S(1)}, u32[]{:S(2)}, u32[]{:S(2)}) collective-permute-start(bf16[32,4096]{1,0:T(8,128)(2,1)S(1)} %slice.9), channel_id=1, source_target_pairs={{3,0},{0,1},{1,2},{2,3},{7,4},{4,5},{5,6},{6,7},{11,8},{8,9},{9,10... | collective-permute-start | bytes 786440 | tf_op jit(solution)/shard_map/ppermute | solution.py:174
  39.6 2.6 %collective-permute-start.4 = (f32[8,256]{1,0:T(8,128)S(1)}, f32[8,256]{1,0:T(8,128)S(1)}, u32[]{:S(2)}, u32[]{:S(2)}) collective-permute-start(f32[8,256]{1,0:T(8,128)S(1)} %get-tuple-element.20.field.f0), channel_id=1, source_target_pairs={{0,64},{64,128},{128,192},{192,256},{256,320},{320,384},{384,448},... | collective-permute-start | bytes 24584 | tf_op jit(solution)/shard_map/ppermute | solution.py:179
  40.9 4.8 %collective-permute-start.5 = (f32[8,256]{1,0:T(8,128)S(1)}, f32[8,256]{1,0:T(8,128)S(1)}, u32[]{:S(2)}, u32[]{:S(2)}) collective-permute-start(f32[8,256]{1,0:T(8,128)S(1)} %get-tuple-element.20.field.f0), channel_id=1, source_target_pairs={{64,0},{128,64},{192,128},{256,192},{320,256},{384,320},{448,384},... | collective-permute-start | bytes 24584 | tf_op jit(solution)/shard_map/ppermute | solution.py:180
  47.2 25.2 %all-to-all-start.2 = ((bf16[16,16,256]{2,1,0:T(8,128)(2,1)}), bf16[16,16,256]{2,1,0:T(8,128)(2,1)S(1)}, u32[]{:S(2)}, u32[]{:S(2)}) async-start(bf16[16,16,256]{2,1,0:T(8,128)(2,1)} %get-tuple-element.22), calls=%async_computation.2 | async-start | bytes 262144 | tf_op jit(solution)/shard_map/all_to_all | solution.py:198
  59.2 5.3 %collective-permute-start.6 = (f32[8,256]{1,0:T(8,128)S(1)}, f32[8,256]{1,0:T(8,128)S(1)}, u32[]{:S(2)}, u32[]{:S(2)}) collective-permute-start(f32[8,256]{1,0:T(8,128)S(1)} %get-tuple-element.23.field.f1), channel_id=1, source_target_pairs={{0,64},{64,128},{128,192},{192,256},{256,320},{320,384},{384,448},... | collective-permute-start | bytes 24584 | tf_op jit(solution)/shard_map/ppermute | solution.py:179
  63.3 3.1 %collective-permute-start.7 = (f32[8,256]{1,0:T(8,128)S(1)}, f32[8,256]{1,0:T(8,128)S(1)}, u32[]{:S(2)}, u32[]{:S(2)}) collective-permute-start(f32[8,256]{1,0:T(8,128)S(1)} %get-tuple-element.23.field.f1), channel_id=1, source_target_pairs={{64,0},{128,64},{192,128},{256,192},{320,256},{384,320},{448,384},... | collective-permute-start | bytes 24584 | tf_op jit(solution)/shard_map/ppermute | solution.py:180
  73.8 20.2 %all-to-all-start.3 = ((bf16[16,16,256]{2,1,0:T(8,128)(2,1)}), bf16[16,16,256]{2,1,0:T(8,128)(2,1)S(1)}, u32[]{:S(2)}, u32[]{:S(2)}) async-start(bf16[16,16,256]{2,1,0:T(8,128)(2,1)} %get-tuple-element.24), calls=%async_computation.3 | async-start | bytes 262144 | tf_op jit(solution)/shard_map/all_to_all | solution.py:198
  80.3 4.7 %collective-permute-start.8 = (f32[8,256]{1,0:T(8,128)S(1)}, f32[8,256]{1,0:T(8,128)S(1)}, u32[]{:S(2)}, u32[]{:S(2)}) collective-permute-start(f32[8,256]{1,0:T(8,128)S(1)} %get-tuple-element.25.field.f2), channel_id=1, source_target_pairs={{0,64},{64,128},{128,192},{192,256},{256,320},{320,384},{384,448},... | collective-permute-start | bytes 24584 | tf_op jit(solution)/shard_map/ppermute | solution.py:179
  83.7 3.9 %collective-permute-start.9 = (f32[8,256]{1,0:T(8,128)S(1)}, f32[8,256]{1,0:T(8,128)S(1)}, u32[]{:S(2)}, u32[]{:S(2)}) collective-permute-start(f32[8,256]{1,0:T(8,128)S(1)} %get-tuple-element.25.field.f2), channel_id=1, source_target_pairs={{64,0},{128,64},{192,128},{256,192},{320,256},{384,320},{448,384},... | collective-permute-start | bytes 24584 | tf_op jit(solution)/shard_map/ppermute | solution.py:180
  95.6 19.9 %all-to-all-start.4 = ((bf16[16,16,256]{2,1,0:T(8,128)(2,1)}), bf16[16,16,256]{2,1,0:T(8,128)(2,1)S(1)}, u32[]{:S(2)}, u32[]{:S(2)}) async-start(bf16[16,16,256]{2,1,0:T(8,128)(2,1)} %get-tuple-element.26), calls=%async_computation.4 | async-start | bytes 262144 | tf_op jit(solution)/shard_map/all_to_all | solution.py:198
  101.7 4.7 %collective-permute-start.10 = (f32[8,256]{1,0:T(8,128)S(1)}, f32[8,256]{1,0:T(8,128)S(1)}, u32[]{:S(2)}, u32[]{:S(2)}) collective-permute-start(f32[8,256]{1,0:T(8,128)S(1)} %get-tuple-element.27.field.f3), channel_id=1, source_target_pairs={{0,64},{64,128},{128,192},{192,256},{256,320},{320,384},{384,448},... | collective-permute-start | bytes 24584 | tf_op jit(solution)/shard_map/ppermute | solution.py:179
  105.1 3.2 %collective-permute-start.11 = (f32[8,256]{1,0:T(8,128)S(1)}, f32[8,256]{1,0:T(8,128)S(1)}, u32[]{:S(2)}, u32[]{:S(2)}) collective-permute-start(f32[8,256]{1,0:T(8,128)S(1)} %get-tuple-element.27.field.f3), channel_id=1, source_target_pairs={{64,0},{128,64},{192,128},{256,192},{320,256},{384,320},{448,384},... | collective-permute-start | bytes 24584 | tf_op jit(solution)/shard_map/ppermute | solution.py:180

commit v3 on v1

--- a/solution.py
+++ b/solution.py
@@ -6,6 +6,7 @@
 from jax.sharding import Mesh, PartitionSpec as P
 
 STEPS = 4
+LOW_FROM = 2
 CENTRE = 6.75
 SCALE = 32.0
 PAIRS = [(i, j) for j in range(STEPS + 1) for i in range(j + 1)]
@@ -17,7 +18,12 @@
 BF16 = jnp.bfloat16
 
 
-def call(body, outs, *args, smem=0):
+def call(body, outs, *args, smem=0, keep=True):
+    args = args[:smem] + tuple(
+        pltpu.with_memory_space_constraint(x, pltpu.VMEM) for x in args[smem:]
+    )
+    if keep:
+        outs = jax.tree.map(lambda o: pltpu.VMEM(o.shape, o.dtype), outs)
     specs = [pl.BlockSpec(memory_space=pltpu.SMEM)] * smem
     specs += [pl.BlockSpec(memory_space=pltpu.VMEM)] * (len(args) - smem)
     return pl.pallas_call(
@@ -30,11 +36,12 @@
 
 def store_parts(send, field, row):
     turned = pltpu.roll(field, row * H, 1)
-    high = turned.astype(BF16)
-    low = (turned - high.astype(F32)).astype(BF16)
-    both = jnp.concatenate([high, low], axis=0)
+    parts = turned.astype(BF16)
+    if send.shape[1] > B:
+        low = (turned - parts.astype(F32)).astype(BF16)
+        parts = jnp.concatenate([parts, low], axis=0)
     for z in range(NZ):
-        send[z] = both
+        send[z] = parts
 
 
 def unpack(row_ref, packed, field_out, diag_out, send):
@@ -60,7 +67,7 @@
                 preferred_element_type=F32,
             )
             total = term if total is None else total + term
-        sums.append(total[:B] + total[B:])
+        sums.append(total if total.shape[0] == B else total[:B] + total[B:])
     blended = jnp.concatenate(sums, axis=1)
     own = (diag[0:1] + (2.0 - CENTRE)) * field[...]
     return (own + blended - (up[...] + down[...])) * (1.0 / SCALE)
@@ -166,31 +173,36 @@
     return lax.all_to_all(array, axes, 0, 0, tiled=True)
 
 
+def shifted(array, shift):
+    return lax.ppermute(array, "y", [((y + shift) % NY, y) for y in range(NY)])
+
+
 def neighbours(field):
-    ends = NX * NC - 1
-    up = lax.ppermute(field, ("x", "c"), [(i, i + 1) for i in range(ends)])
-    down = lax.ppermute(field, ("x", "c"), [(i + 1, i) for i in range(ends)])
-    return up, down
+    count = NX * NC
+    even = lax.ppermute(field, ("x", "c"), [(i, i ^ 1) for i in range(count)])
+    pairs = [(i, i + 1) for i in range(1, count - 1, 2)]
+    odd = lax.ppermute(field, ("x", "c"), pairs + [(j, i) for i, j in pairs])
+    return even, odd
 
 
 def on_device(source, coupling, diagonal):
     own = coupling[0]
     row = lax.axis_index("y").astype(jnp.int32).reshape(1)
-    blocks = [own]
-    for shift in range(1, NY):
-        blocks.append(lax.ppermute(own, "y", [((y + shift) % NY, y) for y in range(NY)]))
     packed = jnp.concatenate([source[0], jnp.broadcast_to(diagonal, (B, H))], axis=1)
     packed = lax.all_to_all(jnp.broadcast_to(packed[None], (NY, B, 128)), "y", 0, 0, tiled=True)
+    own, packed = lax.optimization_barrier((own, packed))
+    blocks = [own] + [shifted(own, shift) for shift in range(1, NY)]
     shape = jax.ShapeDtypeStruct
-    field_shape, send_shape = shape((B, W), F32), shape((NZ, 2 * B, W), BF16)
-    field, diag, send = call(unpack, (field_shape, field_shape, send_shape), row, packed, smem=1)
+    field_shape = shape((B, W), F32)
+    send_shapes = [shape((NZ, B if k < LOW_FROM else 2 * B, W), BF16) for k in range(STEPS)]
+    field, diag, send = call(unpack, (field_shape, field_shape, send_shapes[0]), row, packed, smem=1)
     fields = [field]
     for k in range(STEPS):
         up, down = neighbours(field)
         parts = lax.all_to_all(send, "z", 0, 0, tiled=True)
         if k + 1 < STEPS:
             field, send = call(
-                step, (field_shape, send_shape), row, parts, *blocks, field, diag, up, down, smem=1
+                step, (field_shape, send_shapes[k + 1]), row, parts, *blocks, field, diag, up, down, smem=1
             )
             fields.append(field)
         else:
@@ -203,7 +215,7 @@
     table = call(add_up, shape((NZ, B, 128), F32), table)
     table = lax.all_to_all(table, "z", 0, 0, tiled=True)
     own_shape = shape((B, H), F32)
-    found, residual = call(finish, (own_shape, own_shape), table, *fields, last)
+    found, residual = call(finish, (own_shape, own_shape), table, *fields, last, keep=False)
     return found[None], residual[None]
 
 

time: 171 us -> 143 us (0.84); the launches traced: 168 us -> 142 us
  waiting for transfers between devices: 50.7 us -> 33.3 us
  Pallas kernels: 17.2 us -> 7.1 us
  blocking collectives: 29.8 us -> 36.8 us
  starting transfers between devices: 65.3 us -> 60.1 us
    all_to_all x0 -> x1, blocking collectives: none -> 11.2 us  [on_device(): lax.all_to_all(jnp.broadcast_to(packed[None], (NY, B, 128)), 'y', 0, 0, t...]
    all_to_all x1 -> x0, waiting for transfers between devices: 11.2 us -> none  [on_device(): lax.all_to_all(jnp.broadcast_to(packed[None], (NY, B, 128)), 'y', 0, 0, t...]
    pallas_call x7, Pallas kernels: 17.2 us -> 7.1 us  [call(): pl.pallas_call(body, out_shape=outs, in_specs=specs, out_specs=jax.tree.m...]
    all_to_all x1 -> x0, starting transfers between devices: 6.56 us -> none  [on_device(): lax.all_to_all(jnp.broadcast_to(packed[None], (NY, B, 128)), 'y', 0, 0, t...]
    all_to_all x4, waiting for transfers between devices: 36.3 us -> 30.1 us  [on_device(): parts = lax.all_to_all(send, 'z', 0, 0, tiled=True)]
    all_to_all x1, blocking collectives: 11.4 us -> 9.26 us  [on_device(): table = lax.all_to_all(table, ('x', 'c'), 0, 0, tiled=True)]
    all_to_all x1, blocking collectives: 18.4 us -> 16.3 us  [on_device(): table = lax.all_to_all(table, 'z', 0, 0, tiled=True)]
    unnamed x44 -> x18, local copies, waits for them, and re-layouts: 3.81 us -> 4.15 us
  transfers between devices with their start and end apart: 16 -> 15, of which waited for: 9 -> 8; matrix products, arithmetic and copies ran while one was open for 0% -> 0% of each run, Pallas kernels for 1% -> 1%
where the time goes in v3:
time: 143 us; the launch traced here: 142 us
  starting transfers between devices  60.1 us (42%)
  blocking collectives  36.8 us (26%)
  waiting for transfers between devices  33.3 us (23%)
  Pallas kernels  7.1 us (5%)
  local copies, waits for them, and re-layouts  4.23 us (3%)
    all_to_all x4, waiting for transfers between devices, on_device(): parts = lax.all_to_all(send, 'z', 0, 0, tiled=True)  30.1 us
    all_to_all x4, starting transfers between devices, on_device(): parts = lax.all_to_all(send, 'z', 0, 0, tiled=True)  29.2 us
    ppermute x4, starting transfers between devices, neighbours(): even = lax.ppermute(field, ('x', 'c'), [(i, i ^ 1) for i in range(count)])  19 us
    all_to_all x1, blocking collectives, on_device(): table = lax.all_to_all(table, 'z', 0, 0, tiled=True)  16.3 us
    all_to_all x1, blocking collectives, on_device(): lax.all_to_all(jnp.broadcast_to(packed[None], (NY, B, 128)), 'y', 0, 0, t...  11.2 us
    all_to_all x1, blocking collectives, on_device(): table = lax.all_to_all(table, ('x', 'c'), 0, 0, tiled=True)  9.26 us
    ppermute x3, starting transfers between devices, shifted(): return lax.ppermute(array, 'y', [((y + shift) % NY, y) for y in range(NY)])  9.21 us
    pallas_call x7, Pallas kernels, call(): pl.pallas_call(body, out_shape=outs, in_specs=specs, out_specs=jax.tree.m...  7.1 us
  transfers between devices with their start and end apart: 15, of which 8 were waited for; matrix products, arithmetic and copies ran while one was open for 0% of the time, Pallas kernels for 1%

profile of v3, /device:TPU:24, one launch (start us, length us, event | category | flops | bytes accessed | tf_op | source)
XLA Modules:
  0.0 142.4 jit_solution(5882168483698099462)
XLA Ops:
  0.6 0.0 copy-start.8
  0.6 0.0 copy-start.7
  0.6 0.6 copy-done.8
  1.3 0.1 pad.1.clone
  1.4 11.2 %all_to_all.35.packed = f32[4,8,128]{2,1,0:T(8,128)S(1)} all-to-all(f32[4,8,128]{2,1,0:T(8,128)S(1)} %broadcast_in_dim.21), channel_id=1, replica_groups=mesh['x'=4,'c'=2,'z'=16,'y'=4] {'y'}, dimensions={0} | all-to-all | bytes 32768 | tf_op jit(solution)/shard_map/all_to_all | solution.py:192
  12.6 4.0 %collective-permute-start.2 = (bf16[64,4096]{1,0:T(8,128)(2,1)}, bf16[64,4096]{1,0:T(8,128)(2,1)S(1)}, u32[]{:S(2)}, u32[]{:S(2)}) collective-permute-start(bf16[64,4096]{1,0:T(8,128)(2,1)} %bitcast.6), channel_id=1, source_target_pairs={{3,0},{0,1},{1,2},{2,3},{7,4},{4,5},{5,6},{6,7},{11,8},{8,9},{9,10... | collective-permute-start | bytes 1572872 | tf_op jit(solution)/shard_map/ppermute | solution.py:177
  16.6 2.4 %collective-permute-start.1 = (bf16[64,4096]{1,0:T(8,128)(2,1)}, bf16[64,4096]{1,0:T(8,128)(2,1)S(1)}, u32[]{:S(2)}, u32[]{:S(2)}) collective-permute-start(bf16[64,4096]{1,0:T(8,128)(2,1)} %bitcast.7), channel_id=1, source_target_pairs={{2,0},{3,1},{0,2},{1,3},{6,4},{7,5},{4,6},{5,7},{10,8},{11,9},{8,1... | collective-permute-start | bytes 1572872 | tf_op jit(solution)/shard_map/ppermute | solution.py:177
  19.0 2.8 %collective-permute-start = (bf16[64,4096]{1,0:T(8,128)(2,1)}, bf16[64,4096]{1,0:T(8,128)(2,1)S(1)}, u32[]{:S(2)}, u32[]{:S(2)}) collective-permute-start(bf16[64,4096]{1,0:T(8,128)(2,1)} %bitcast.8), channel_id=1, source_target_pairs={{1,0},{2,1},{3,2},{0,3},{5,4},{6,5},{7,6},{4,7},{9,8},{10,9},{11,1... | collective-permute-start | bytes 1572872 | tf_op jit(solution)/shard_map/ppermute | solution.py:177
  21.9 0.8 shard_map.50
  22.7 11.7 %all-to-all-start.1 = ((bf16[16,8,256]{2,1,0:T(8,128)(2,1)}), bf16[16,8,256]{2,1,0:T(8,128)(2,1)S(1)}, u32[]{:S(2)}, u32[]{:S(2)}) async-start(bf16[16,8,256]{2,1,0:T(8,128)(2,1)} %get-tuple-element.18), calls=%async_computation.1 | async-start | bytes 131072 | tf_op jit(solution)/shard_map/all_to_all | solution.py:202
  34.4 0.7 collective-permute-start.4
  35.1 4.8 %collective-permute-start.3 = (f32[8,256]{1,0:T(8,128)S(1)}, f32[8,256]{1,0:T(8,128)S(1)}, u32[]{:S(2)}, u32[]{:S(2)}) collective-permute-start(f32[8,256]{1,0:T(8,128)S(1)} %get-tuple-element.20.field.f0), channel_id=1, source_target_pairs={{0,64},{64,0},{128,192},{192,128},{256,320},{320,256},{384,448},{4... | collective-permute-start | bytes 24584 | tf_op jit(solution)/shard_map/ppermute | solution.py:182
  39.9 0.0 collective-permute-done.4.down
  39.9 0.8 collective-permute-done.3.up
  40.7 6.6 %all-to-all-done.1.parts = bf16[16,8,256]{2,1,0:T(8,128)(2,1)S(1)} async-done(((bf16[16,8,256]{2,1,0:T(8,128)(2,1)}), bf16[16,8,256]{2,1,0:T(8,128)(2,1)S(1)}, u32[]{:S(2)}, u32[]{:S(2)}) %all-to-all-start.1) | async-done | bytes 65568 | tf_op jit(solution)/shard_map/all_to_all | solution.py:202
  47.3 0.0 collective-permute-done.2.c3
  47.3 0.0 collective-permute-done.1.c2
  47.3 0.0 collective-permute-done.c1
  47.3 0.0 copy-start
  47.3 1.4 copy-done
  48.7 1.4 shard_map.51
  50.2 0.0 copy-done.2
  50.2 7.6 %all-to-all-start.2 = ((bf16[16,8,256]{2,1,0:T(8,128)(2,1)}), bf16[16,8,256]{2,1,0:T(8,128)(2,1)S(1)}, u32[]{:S(2)}, u32[]{:S(2)}) async-start(bf16[16,8,256]{2,1,0:T(8,128)(2,1)} %get-tuple-element.22), calls=%async_computation.2 | async-start | bytes 131072 | tf_op jit(solution)/shard_map/all_to_all | solution.py:202
  57.8 0.7 collective-permute-start.6
  58.5 4.8 %collective-permute-start.5 = (f32[8,256]{1,0:T(8,128)S(1)}, f32[8,256]{1,0:T(8,128)S(1)}, u32[]{:S(2)}, u32[]{:S(2)}) collective-permute-start(f32[8,256]{1,0:T(8,128)S(1)} %get-tuple-element.23.field.f1), channel_id=1, source_target_pairs={{0,64},{64,0},{128,192},{192,128},{256,320},{320,256},{384,448},{4... | collective-permute-start | bytes 24584 | tf_op jit(solution)/shard_map/ppermute | solution.py:182
  63.2 0.0 collective-permute-done.6.down
  63.2 0.8 collective-permute-done.5.up
  64.0 6.8 %all-to-all-done.2.parts = bf16[16,8,256]{2,1,0:T(8,128)(2,1)S(1)} async-done(((bf16[16,8,256]{2,1,0:T(8,128)(2,1)}), bf16[16,8,256]{2,1,0:T(8,128)(2,1)S(1)}, u32[]{:S(2)}, u32[]{:S(2)}) %all-to-all-start.2) | async-done | bytes 65568 | tf_op jit(solution)/shard_map/all_to_all | solution.py:202
  70.8 1.0 copy-done.3
  71.9 1.5 %shard_map.52 = (f32[8,256]{1,0:T(8,128)S(1)}, bf16[16,16,256]{2,1,0:T(8,128)(2,1)}) custom-call(s32[1]{0:T(128)} %bitcast.row_ref, bf16[16,8,256]{2,1,0:T(8,128)(2,1)S(1)} %all-to-all-done.2.parts, bf16[64,4096]{1,0:T(8,128)(2,1)S(1)} %bitcast.10, bf16[64,4096]{1,0:T(8,128)(2,1)S(1)} %collective-permute-done.c1, bf16[64,4096]{1,0:T(8,128)(2,1)S(1)} %copy-done.3, ...), custom_call_target="tpu_custom_call" | custom-call | tf_op jit(solution)/shard_map/pallas_call | solution.py:29
  73.3 5.2 %all-to-all-start.3 = ((bf16[16,16,256]{2,1,0:T(8,128)(2,1)}), bf16[16,16,256]{2,1,0:T(8,128)(2,1)S(1)}, u32[]{:S(2)}, u32[]{:S(2)}) async-start(bf16[16,16,256]{2,1,0:T(8,128)(2,1)} %get-tuple-element.24), calls=%async_computation.3 | async-start | bytes 262144 | tf_op jit(solution)/shard_map/all_to_all | solution.py:202
  78.6 0.7 collective-permute-start.8
  79.2 4.8 %collective-permute-start.7 = (f32[8,256]{1,0:T(8,128)S(1)}, f32[8,256]{1,0:T(8,128)S(1)}, u32[]{:S(2)}, u32[]{:S(2)}) collective-permute-start(f32[8,256]{1,0:T(8,128)S(1)} %get-tuple-element.25.field.f2), channel_id=1, source_target_pairs={{0,64},{64,0},{128,192},{192,128},{256,320},{320,256},{384,448},{4... | collective-permute-start | bytes 24584 | tf_op jit(solution)/shard_map/ppermute | solution.py:182
  84.0 0.0 collective-permute-done.8.down
  84.0 0.8 collective-permute-done.7.up
  84.8 8.1 %all-to-all-done.3.parts = bf16[16,16,256]{2,1,0:T(8,128)(2,1)S(1)} async-done(((bf16[16,16,256]{2,1,0:T(8,128)(2,1)}), bf16[16,16,256]{2,1,0:T(8,128)(2,1)S(1)}, u32[]{:S(2)}, u32[]{:S(2)}) %all-to-all-start.3) | async-done | bytes 131104 | tf_op jit(solution)/shard_map/all_to_all | solution.py:202
  93.0 1.0 copy-done.6
  94.0 1.5 %shard_map.53 = (f32[8,256]{1,0:T(8,128)S(1)}, bf16[16,16,256]{2,1,0:T(8,128)(2,1)}) custom-call(s32[1]{0:T(128)} %bitcast.row_ref, bf16[16,16,256]{2,1,0:T(8,128)(2,1)S(1)} %all-to-all-done.3.parts, bf16[64,4096]{1,0:T(8,128)(2,1)S(1)} %bitcast.11, bf16[64,4096]{1,0:T(8,128)(2,1)S(1)} %copy-done.6, bf16[64,4096]{1,0:T(8,128)(2,1)S(1)} %copy-done.3, ...), custom_call_target="tpu_custom_call" | custom-call | tf_op jit(solution)/shard_map/pallas_call | solution.py:29
  95.5 4.6 %all-to-all-start.4 = ((bf16[16,16,256]{2,1,0:T(8,128)(2,1)}), bf16[16,16,256]{2,1,0:T(8,128)(2,1)S(1)}, u32[]{:S(2)}, u32[]{:S(2)}) async-start(bf16[16,16,256]{2,1,0:T(8,128)(2,1)} %get-tuple-element.26), calls=%async_computation.4 | async-start | bytes 262144 | tf_op jit(solution)/shard_map/all_to_all | solution.py:202
  100.1 0.7 collective-permute-start.10
  100.8 4.8 %collective-permute-start.9 = (f32[8,256]{1,0:T(8,128)S(1)}, f32[8,256]{1,0:T(8,128)S(1)}, u32[]{:S(2)}, u32[]{:S(2)}) collective-permute-start(f32[8,256]{1,0:T(8,128)S(1)} %get-tuple-element.27.field.f3), channel_id=1, source_target_pairs={{0,64},{64,0},{128,192},{192,128},{256,320},{320,256},{384,448},{4... | collective-permute-start | bytes 24584 | tf_op jit(solution)/shard_map/ppermute | solution.py:182
  105.6 0.0 collective-permute-done.10.down
  105.6 0.8 collective-permute-done.9.up
  106.4 8.6 %all-to-all-done.4.parts = bf16[16,16,256]{2,1,0:T(8,128)(2,1)S(1)} async-done(((bf16[16,16,256]{2,1,0:T(8,128)(2,1)}), bf16[16,16,256]{2,1,0:T(8,128)(2,1)S(1)}, u32[]{:S(2)}, u32[]{:S(2)}) %all-to-all-start.4) | async-done | bytes 131104 | tf_op jit(solution)/shard_map/all_to_all | solution.py:202
  114.9 0.8 shard_map.54
  115.7 9.3 %all_to_all.36.tables = f32[8,8,128]{2,1,0:T(8,128)S(1)} all-to-all(f32[8,8,128]{2,1,0:T(8,128)S(1)} %get-tuple-element.28), channel_id=1, replica_groups=mesh['x'=4,'c'=2,'z'=16,'y'=4] {'x','c'}, dimensions={0} | all-to-all | bytes 65536 | tf_op jit(solution)/shard_map/all_to_all | solution.py:214
  125.0 16.3 %all_to_all.37.tables = f32[16,8,128]{2,1,0:T(8,128)S(1)} all-to-all(f32[16,8,128]{2,1,0:T(8,128)S(1)} %shard_map.55), channel_id=1, replica_groups=mesh['x'=4,'c'=2,'z'=16,'y'=4] {'z'}, dimensions={0} | all-to-all | bytes 131072 | tf_op jit(solution)/shard_map/all_to_all | solution.py:216
  141.3 1.1 shard_map.56
  (13 shorter events, 0.0 us)
Async XLA Ops:
  0.6 0.7 copy-start.8
  0.6 0.7 copy-start.7
  12.6 34.7 %collective-permute-start.2 = (bf16[64,4096]{1,0:T(8,128)(2,1)}, bf16[64,4096]{1,0:T(8,128)(2,1)S(1)}, u32[]{:S(2)}, u32[]{:S(2)}) collective-permute-start(bf16[64,4096]{1,0:T(8,128)(2,1)} %bitcast.6), channel_id=1, source_target_pairs={{3,0},{0,1},{1,2},{2,3},{7,4},{4,5},{5,6},{6,7},{11,8},{8,9},{9,10... | collective-permute-start | bytes 1572872 | tf_op jit(solution)/shard_map/ppermute | solution.py:177
  16.6 30.7 %collective-permute-start.1 = (bf16[64,4096]{1,0:T(8,128)(2,1)}, bf16[64,4096]{1,0:T(8,128)(2,1)S(1)}, u32[]{:S(2)}, u32[]{:S(2)}) collective-permute-start(bf16[64,4096]{1,0:T(8,128)(2,1)} %bitcast.7), channel_id=1, source_target_pairs={{2,0},{3,1},{0,2},{1,3},{6,4},{7,5},{4,6},{5,7},{10,8},{11,9},{8,1... | collective-permute-start | bytes 1572872 | tf_op jit(solution)/shard_map/ppermute | solution.py:177
  19.0 28.3 %collective-permute-start = (bf16[64,4096]{1,0:T(8,128)(2,1)}, bf16[64,4096]{1,0:T(8,128)(2,1)S(1)}, u32[]{:S(2)}, u32[]{:S(2)}) collective-permute-start(bf16[64,4096]{1,0:T(8,128)(2,1)} %bitcast.8), channel_id=1, source_target_pairs={{1,0},{2,1},{3,2},{0,3},{5,4},{6,5},{7,6},{4,7},{9,8},{10,9},{11,1... | collective-permute-start | bytes 1572872 | tf_op jit(solution)/shard_map/ppermute | solution.py:177
  22.7 24.6 %all-to-all-start.1 = ((bf16[16,8,256]{2,1,0:T(8,128)(2,1)}), bf16[16,8,256]{2,1,0:T(8,128)(2,1)S(1)}, u32[]{:S(2)}, u32[]{:S(2)}) async-start(bf16[16,8,256]{2,1,0:T(8,128)(2,1)} %get-tuple-element.18), calls=%async_computation.1 | async-start | bytes 131072 | tf_op jit(solution)/shard_map/all_to_all | solution.py:202
  34.4 5.4 %collective-permute-start.4 = (f32[8,256]{1,0:T(8,128)S(1)}, f32[8,256]{1,0:T(8,128)S(1)}, u32[]{:S(2)}, u32[]{:S(2)}) collective-permute-start(f32[8,256]{1,0:T(8,128)S(1)} %get-tuple-element.20.field.f0), channel_id=1, source_target_pairs={{64,128},{192,256},{320,384},{128,64},{256,192},{384,320},{65,129}... | collective-permute-start | bytes 24584 | tf_op jit(solution)/shard_map/ppermute | solution.py:184
  35.1 5.6 %collective-permute-start.3 = (f32[8,256]{1,0:T(8,128)S(1)}, f32[8,256]{1,0:T(8,128)S(1)}, u32[]{:S(2)}, u32[]{:S(2)}) collective-permute-start(f32[8,256]{1,0:T(8,128)S(1)} %get-tuple-element.20.field.f0), channel_id=1, source_target_pairs={{0,64},{64,0},{128,192},{192,128},{256,320},{320,256},{384,448},{4... | collective-permute-start | bytes 24584 | tf_op jit(solution)/shard_map/ppermute | solution.py:182
  47.3 2.9 %copy-start.2 = (bf16[64,4096]{1,0:T(8,128)(2,1)}, bf16[64,4096]{1,0:T(8,128)(2,1)S(1)}, u32[]{:S(2)}) copy-start(bf16[64,4096]{1,0:T(8,128)(2,1)S(1)} %collective-permute-done.1.c2) | copy-start | bytes 1572868
  47.3 23.5 %copy-start.5 = (bf16[64,4096]{1,0:T(8,128)(2,1)}, bf16[64,4096]{1,0:T(8,128)(2,1)S(1)}, u32[]{:S(2)}) copy-start(bf16[64,4096]{1,0:T(8,128)(2,1)S(1)} %collective-permute-done.c1) | copy-start | bytes 1572868
  47.3 1.4 copy-start
  48.7 22.1 %copy-start.1 = (bf16[1,64,4096]{2,1,0:T(8,128)(2,1)S(1)}, bf16[1,64,4096]{2,1,0:T(8,128)(2,1)}, u32[]{:S(2)}) copy-start(bf16[1,64,4096]{2,1,0:T(8,128)(2,1)} %param.4) | copy-start | bytes 1572868
  50.2 20.7 %all-to-all-start.2 = ((bf16[16,8,256]{2,1,0:T(8,128)(2,1)}), bf16[16,8,256]{2,1,0:T(8,128)(2,1)S(1)}, u32[]{:S(2)}, u32[]{:S(2)}) async-start(bf16[16,8,256]{2,1,0:T(8,128)(2,1)} %get-tuple-element.22), calls=%async_computation.2 | async-start | bytes 131072 | tf_op jit(solution)/shard_map/all_to_all | solution.py:202
  57.8 5.4 %collective-permute-start.6 = (f32[8,256]{1,0:T(8,128)S(1)}, f32[8,256]{1,0:T(8,128)S(1)}, u32[]{:S(2)}, u32[]{:S(2)}) collective-permute-start(f32[8,256]{1,0:T(8,128)S(1)} %get-tuple-element.23.field.f1), channel_id=1, source_target_pairs={{64,128},{192,256},{320,384},{128,64},{256,192},{384,320},{65,129}... | collective-permute-start | bytes 24584 | tf_op jit(solution)/shard_map/ppermute | solution.py:184
  58.5 5.6 %collective-permute-start.5 = (f32[8,256]{1,0:T(8,128)S(1)}, f32[8,256]{1,0:T(8,128)S(1)}, u32[]{:S(2)}, u32[]{:S(2)}) collective-permute-start(f32[8,256]{1,0:T(8,128)S(1)} %get-tuple-element.23.field.f1), channel_id=1, source_target_pairs={{0,64},{64,0},{128,192},{192,128},{256,320},{320,256},{384,448},{4... | collective-permute-start | bytes 24584 | tf_op jit(solution)/shard_map/ppermute | solution.py:182
  70.8 1.0 copy-start.3
  73.3 19.6 %all-to-all-start.3 = ((bf16[16,16,256]{2,1,0:T(8,128)(2,1)}), bf16[16,16,256]{2,1,0:T(8,128)(2,1)S(1)}, u32[]{:S(2)}, u32[]{:S(2)}) async-start(bf16[16,16,256]{2,1,0:T(8,128)(2,1)} %get-tuple-element.24), calls=%async_computation.3 | async-start | bytes 262144 | tf_op jit(solution)/shard_map/all_to_all | solution.py:202
  78.6 5.4 %collective-permute-start.8 = (f32[8,256]{1,0:T(8,128)S(1)}, f32[8,256]{1,0:T(8,128)S(1)}, u32[]{:S(2)}, u32[]{:S(2)}) collective-permute-start(f32[8,256]{1,0:T(8,128)S(1)} %get-tuple-element.25.field.f2), channel_id=1, source_target_pairs={{64,128},{192,256},{320,384},{128,64},{256,192},{384,320},{65,129}... | collective-permute-start | bytes 24584 | tf_op jit(solution)/shard_map/ppermute | solution.py:184
  79.2 5.6 %collective-permute-start.7 = (f32[8,256]{1,0:T(8,128)S(1)}, f32[8,256]{1,0:T(8,128)S(1)}, u32[]{:S(2)}, u32[]{:S(2)}) collective-permute-start(f32[8,256]{1,0:T(8,128)S(1)} %get-tuple-element.25.field.f2), channel_id=1, source_target_pairs={{0,64},{64,0},{128,192},{192,128},{256,320},{320,256},{384,448},{4... | collective-permute-start | bytes 24584 | tf_op jit(solution)/shard_map/ppermute | solution.py:182
  93.0 1.0 copy-start.6
  94.0 20.9 %copy-start.4 = (bf16[64,4096]{1,0:T(8,128)(2,1)S(1)}, bf16[64,4096]{1,0:T(8,128)(2,1)}, u32[]{:S(2)}) copy-start(bf16[64,4096]{1,0:T(8,128)(2,1)} %copy-done.2) | copy-start | bytes 1572868
  95.5 19.5 %all-to-all-start.4 = ((bf16[16,16,256]{2,1,0:T(8,128)(2,1)}), bf16[16,16,256]{2,1,0:T(8,128)(2,1)S(1)}, u32[]{:S(2)}, u32[]{:S(2)}) async-start(bf16[16,16,256]{2,1,0:T(8,128)(2,1)} %get-tuple-element.26), calls=%async_computation.4 | async-start | bytes 262144 | tf_op jit(solution)/shard_map/all_to_all | solution.py:202
  100.1 5.4 %collective-permute-start.10 = (f32[8,256]{1,0:T(8,128)S(1)}, f32[8,256]{1,0:T(8,128)S(1)}, u32[]{:S(2)}, u32[]{:S(2)}) collective-permute-start(f32[8,256]{1,0:T(8,128)S(1)} %get-tuple-element.27.field.f3), channel_id=1, source_target_pairs={{64,128},{192,256},{320,384},{128,64},{256,192},{384,320},{65,129}... | collective-permute-start | bytes 24584 | tf_op jit(solution)/shard_map/ppermute | solution.py:184
  100.8 5.6 %collective-permute-start.9 = (f32[8,256]{1,0:T(8,128)S(1)}, f32[8,256]{1,0:T(8,128)S(1)}, u32[]{:S(2)}, u32[]{:S(2)}) collective-permute-start(f32[8,256]{1,0:T(8,128)S(1)} %get-tuple-element.27.field.f3), channel_id=1, source_target_pairs={{0,64},{64,0},{128,192},{192,128},{256,320},{320,256},{384,448},{4... | collective-permute-start | bytes 24584 | tf_op jit(solution)/shard_map/ppermute | solution.py:182

commit v4 on v3

--- a/solution.py
+++ b/solution.py
@@ -30,6 +30,7 @@
         body,
         out_shape=outs,
         in_specs=specs,
+        compiler_params=pltpu.CompilerParams(vmem_limit_bytes=8 << 20),
         out_specs=jax.tree.map(lambda _: pl.BlockSpec(memory_space=pltpu.VMEM), outs),
     )(*args)
 
@@ -44,15 +45,19 @@
         send[z] = parts
 
 
-def unpack(row_ref, packed, field_out, diag_out, send):
-    row = row_ref[0]
-    field = jnp.concatenate([packed[y][:, :H] for y in range(NY)], axis=1)
-    diag = jnp.concatenate([packed[y][:, H:] for y in range(NY)], axis=1)
-    both = jnp.concatenate([field, diag], axis=0)
-    both = pltpu.roll(both, (NY - row) % NY * H, 1)
-    field_out[...] = both[:B]
-    diag_out[...] = both[B:]
-    store_parts(send, both[:B], row)
+def unpack(row_ref, packed, field_out, even_out, diag_out, send):
+    row = row_ref[0] % NY
+    core = row_ref[0] // NY
+
+    def wide(which, columns):
+        joined = jnp.concatenate([packed[which * NY + y][:, columns] for y in range(NY)], axis=1)
+        return pltpu.roll(joined, (NY - row) % NY * H, 1)
+
+    field = wide(core, slice(0, H))
+    field_out[...] = field
+    even_out[...] = wide(1 - core, slice(0, H))
+    diag_out[...] = wide(core, slice(H, 2 * H))
+    store_parts(send, field, row)
 
 
 def next_field(parts, blocks, field, diag, up, down):
@@ -76,7 +81,7 @@
 def step(row_ref, parts, c0, c1, c2, c3, field, diag, up, down, field_out, send):
     out = next_field(parts, (c0, c1, c2, c3), field, diag, up, down)
     field_out[...] = out
-    store_parts(send, out, row_ref[0])
+    store_parts(send, out, row_ref[0] % NY)
 
 
 def last_step(parts, c0, c1, c2, c3, field, diag, up, down, f0, f1, f2, field_out, send):
@@ -177,32 +182,40 @@
     return lax.ppermute(array, "y", [((y + shift) % NY, y) for y in range(NY)])
 
 
-def neighbours(field):
-    count = NX * NC
-    even = lax.ppermute(field, ("x", "c"), [(i, i ^ 1) for i in range(count)])
-    pairs = [(i, i + 1) for i in range(1, count - 1, 2)]
-    odd = lax.ppermute(field, ("x", "c"), pairs + [(j, i) for i, j in pairs])
-    return even, odd
+def even(field):
+    return lax.ppermute(field, ("x", "c"), [(i, i ^ 1) for i in range(NX * NC)])
+
+
+def odd(field):
+    pairs = [(i, i + 1) for i in range(1, NX * NC - 1, 2)]
+    return lax.ppermute(field, ("x", "c"), pairs + [(j, i) for i, j in pairs])
 
 
 def on_device(source, coupling, diagonal):
     own = coupling[0]
-    row = lax.axis_index("y").astype(jnp.int32).reshape(1)
+    row = lax.axis_index(("c", "y")).astype(jnp.int32).reshape(1)
     packed = jnp.concatenate([source[0], jnp.broadcast_to(diagonal, (B, H))], axis=1)
-    packed = lax.all_to_all(jnp.broadcast_to(packed[None], (NY, B, 128)), "y", 0, 0, tiled=True)
+    packed = jnp.broadcast_to(packed[None], (NC * NY, B, 128))
+    packed = lax.all_to_all(packed, ("c", "y"), 0, 0, tiled=True)
     own, packed = lax.optimization_barrier((own, packed))
     blocks = [own] + [shifted(own, shift) for shift in range(1, NY)]
     shape = jax.ShapeDtypeStruct
-    field_shape = shape((B, W), F32)
-    send_shapes = [shape((NZ, B if k < LOW_FROM else 2 * B, W), BF16) for k in range(STEPS)]
-    field, diag, send = call(unpack, (field_shape, field_shape, send_shapes[0]), row, packed, smem=1)
+    wide = shape((B, W), F32)
+    sends = [shape((NZ, B if k < LOW_FROM else 2 * B, W), BF16) for k in range(STEPS)]
+    field, up, diag, send = call(unpack, (wide, wide, wide, sends[0]), row, packed, smem=1)
     fields = [field]
     for k in range(STEPS):
-        up, down = neighbours(field)
+        down = odd(field)
+        if k > 0:
+            up = even(field)
         parts = lax.all_to_all(send, "z", 0, 0, tiled=True)
         if k + 1 < STEPS:
             field, send = call(
-                step, (field_shape, send_shapes[k + 1]), row, parts, *blocks, field, diag, up, down, smem=1
+                step,
+                (wide, sends[k + 1]),
+                row, parts, *blocks, field, diag, up, down,
+                smem=1,
+
             )
             fields.append(field)
         else:

time: 143 us -> 143 us (level)
  waiting for transfers between devices: 33.3 us -> 38.1 us
  starting transfers between devices: 60.1 us -> 57.1 us
  local copies, waits for them, and re-layouts: 4.23 us -> 1.76 us
    all_to_all x4, waiting for transfers between devices: 30.1 us -> 35.7 us  [on_device(): parts = lax.all_to_all(send, 'z', 0, 0, tiled=True)]
    ppermute x8 -> x7, starting transfers between devices: 21.7 us -> 16.9 us  [the longest x3 14.3 us: even(): return lax.ppermute(field, ('x', 'c'), [(i, i ^ 1) for i in range(NX * NC)])]
    unnamed x18 -> x8, local copies, waits for them, and re-layouts: 4.15 us -> 1.68 us
    all_to_all x4, starting transfers between devices: 29.2 us -> 31 us  [on_device(): parts = lax.all_to_all(send, 'z', 0, 0, tiled=True)]
    ppermute x8 -> x7, waiting for transfers between devices: 3.19 us -> 2.4 us  [the longest x3 2.39 us: even(): return lax.ppermute(field, ('x', 'c'), [(i, i ^ 1) for i in range(NX * NC)])]
  transfers between devices with their start and end apart: 15 -> 14, of which waited for: 8 -> 7; matrix products, arithmetic and copies ran while one was open for 0% -> 0% of each run, Pallas kernels for 1% -> 1%
where the time goes in v4:
time: 143 us; the launch traced here: 142 us
  starting transfers between devices  57.1 us (40%)
  waiting for transfers between devices  38.1 us (27%)
  blocking collectives  36.9 us (26%)
  Pallas kernels  7.1 us (5%)
  local copies, waits for them, and re-layouts  1.76 us (1%)
    all_to_all x4, waiting for transfers between devices, on_device(): parts = lax.all_to_all(send, 'z', 0, 0, tiled=True)  35.7 us
    all_to_all x4, starting transfers between devices, on_device(): parts = lax.all_to_all(send, 'z', 0, 0, tiled=True)  31 us
    all_to_all x1, blocking collectives, on_device(): table = lax.all_to_all(table, 'z', 0, 0, tiled=True)  16.3 us
    ppermute x3, starting transfers between devices, even(): return lax.ppermute(field, ('x', 'c'), [(i, i ^ 1) for i in range(NX * NC)])  14.3 us
    all_to_all x1, blocking collectives, on_device(): packed = lax.all_to_all(packed, ('c', 'y'), 0, 0, tiled=True)  11.3 us
    all_to_all x1, blocking collectives, on_device(): table = lax.all_to_all(table, ('x', 'c'), 0, 0, tiled=True)  9.26 us
    ppermute x3, starting transfers between devices, shifted(): return lax.ppermute(array, 'y', [((y + shift) % NY, y) for y in range(NY)])  9.17 us
    pallas_call x7, Pallas kernels, call(): pl.pallas_call(body, out_shape=outs, in_specs=specs, compiler_params=pltp...  7.1 us
  transfers between devices with their start and end apart: 14, of which 7 were waited for; matrix products, arithmetic and copies ran while one was open for 0% of the time, Pallas kernels for 1%

profile of v4, /device:TPU:24, one launch (start us, length us, event | category | flops | bytes accessed | tf_op | source)
XLA Modules:
  0.0 141.8 jit_solution(8831625970681937315)
XLA Ops:
  0.6 0.0 copy-start.3
  0.6 0.0 copy-start.2
  0.6 0.6 copy-done.3
  1.3 0.1 pad.1.clone
  1.4 0.0 copy-done.2
  1.4 11.3 %all_to_all.35.packed = f32[8,8,128]{2,1,0:T(8,128)S(1)} all-to-all(f32[8,8,128]{2,1,0:T(8,128)S(1)} %broadcast_in_dim.21), channel_id=1, replica_groups=mesh['x'=4,'c'=2,'z'=16,'y'=4] {'c','y'}, dimensions={0} | all-to-all | bytes 65536 | tf_op jit(solution)/shard_map/all_to_all | solution.py:199
  12.7 3.8 %collective-permute-start.2 = (bf16[64,4096]{1,0:T(8,128)(2,1)}, bf16[64,4096]{1,0:T(8,128)(2,1)S(1)}, u32[]{:S(2)}, u32[]{:S(2)}) collective-permute-start(bf16[64,4096]{1,0:T(8,128)(2,1)} %bitcast.6), channel_id=1, source_target_pairs={{3,0},{0,1},{1,2},{2,3},{7,4},{4,5},{5,6},{6,7},{11,8},{8,9},{9,10... | collective-permute-start | bytes 1572872 | tf_op jit(solution)/shard_map/ppermute | solution.py:182
  16.6 2.5 %collective-permute-start.1 = (bf16[64,4096]{1,0:T(8,128)(2,1)}, bf16[64,4096]{1,0:T(8,128)(2,1)S(1)}, u32[]{:S(2)}, u32[]{:S(2)}) collective-permute-start(bf16[64,4096]{1,0:T(8,128)(2,1)} %bitcast.7), channel_id=1, source_target_pairs={{2,0},{3,1},{0,2},{1,3},{6,4},{7,5},{4,6},{5,7},{10,8},{11,9},{8,1... | collective-permute-start | bytes 1572872 | tf_op jit(solution)/shard_map/ppermute | solution.py:182
  19.0 2.9 %collective-permute-start = (bf16[64,4096]{1,0:T(8,128)(2,1)}, bf16[64,4096]{1,0:T(8,128)(2,1)S(1)}, u32[]{:S(2)}, u32[]{:S(2)}) collective-permute-start(bf16[64,4096]{1,0:T(8,128)(2,1)} %bitcast.8), channel_id=1, source_target_pairs={{1,0},{2,1},{3,2},{0,3},{5,4},{6,5},{7,6},{4,7},{9,8},{10,9},{11,1... | collective-permute-start | bytes 1572872 | tf_op jit(solution)/shard_map/ppermute | solution.py:182
  21.9 0.8 shard_map.50
  22.8 11.7 %all-to-all-start.1 = ((bf16[16,8,256]{2,1,0:T(8,128)(2,1)}), bf16[16,8,256]{2,1,0:T(8,128)(2,1)S(1)}, u32[]{:S(2)}, u32[]{:S(2)}) async-start(bf16[16,8,256]{2,1,0:T(8,128)(2,1)} %get-tuple-element.19), calls=%async_computation.1 | async-start | bytes 131072 | tf_op jit(solution)/shard_map/all_to_all | solution.py:211
  34.5 0.7 collective-permute-start.3
  35.2 0.0 collective-permute-done.3.down
  35.2 12.2 %all-to-all-done.1.parts = bf16[16,8,256]{2,1,0:T(8,128)(2,1)S(1)} async-done(((bf16[16,8,256]{2,1,0:T(8,128)(2,1)}), bf16[16,8,256]{2,1,0:T(8,128)(2,1)S(1)}, u32[]{:S(2)}, u32[]{:S(2)}) %all-to-all-start.1) | async-done | bytes 65568 | tf_op jit(solution)/shard_map/all_to_all | solution.py:211
  47.4 0.0 collective-permute-done.2.c3
  47.4 0.0 collective-permute-done.1.c2
  47.4 0.0 collective-permute-done.c1
  47.4 0.0 copy-start
  47.4 1.0 copy-done
  48.4 0.0 copy-start.1
  48.4 1.4 %shard_map.51 = (f32[8,256]{1,0:T(8,128)S(1)}, bf16[16,8,256]{2,1,0:T(8,128)(2,1)}) custom-call(s32[1]{0:T(128)} %bitcast.row_ref, bf16[16,8,256]{2,1,0:T(8,128)(2,1)S(1)} %all-to-all-done.1.parts, bf16[64,4096]{1,0:T(8,128)(2,1)S(1)} %bitcast.9, bf16[64,4096]{1,0:T(8,128)(2,1)S(1)} %collective-permute-done.c1, ...), custom_call_target="tpu_custom_call" | custom-call | tf_op jit(solution)/shard_map/pallas_call | solution.py:29
  49.8 9.4 %all-to-all-start.2 = ((bf16[16,8,256]{2,1,0:T(8,128)(2,1)}), bf16[16,8,256]{2,1,0:T(8,128)(2,1)S(1)}, u32[]{:S(2)}, u32[]{:S(2)}) async-start(bf16[16,8,256]{2,1,0:T(8,128)(2,1)} %get-tuple-element.24), calls=%async_computation.2 | async-start | bytes 131072 | tf_op jit(solution)/shard_map/all_to_all | solution.py:211
  59.3 0.7 collective-permute-start.5
  59.9 4.8 %collective-permute-start.4 = (f32[8,256]{1,0:T(8,128)S(1)}, f32[8,256]{1,0:T(8,128)S(1)}, u32[]{:S(2)}, u32[]{:S(2)}) collective-permute-start(f32[8,256]{1,0:T(8,128)S(1)} %get-tuple-element.25.field.f1), channel_id=1, source_target_pairs={{0,64},{64,0},{128,192},{192,128},{256,320},{320,256},{384,448},{4... | collective-permute-start | bytes 24584 | tf_op jit(solution)/shard_map/ppermute | solution.py:186
  64.7 0.0 collective-permute-done.5.down
  64.7 0.8 collective-permute-done.4.up
  65.5 6.8 %all-to-all-done.2.parts = bf16[16,8,256]{2,1,0:T(8,128)(2,1)S(1)} async-done(((bf16[16,8,256]{2,1,0:T(8,128)(2,1)}), bf16[16,8,256]{2,1,0:T(8,128)(2,1)S(1)}, u32[]{:S(2)}, u32[]{:S(2)}) %all-to-all-start.2) | async-done | bytes 65568 | tf_op jit(solution)/shard_map/all_to_all | solution.py:211
  72.3 0.0 copy-done.1
  72.3 1.5 %shard_map.52 = (f32[8,256]{1,0:T(8,128)S(1)}, bf16[16,16,256]{2,1,0:T(8,128)(2,1)}) custom-call(s32[1]{0:T(128)} %bitcast.row_ref, bf16[16,8,256]{2,1,0:T(8,128)(2,1)S(1)} %all-to-all-done.2.parts, bf16[64,4096]{1,0:T(8,128)(2,1)S(1)} %bitcast.10, bf16[64,4096]{1,0:T(8,128)(2,1)S(1)} %collective-permute-done.c1, ...), custom_call_target="tpu_custom_call" | custom-call | tf_op jit(solution)/shard_map/pallas_call | solution.py:29
  73.8 5.2 %all-to-all-start.3 = ((bf16[16,16,256]{2,1,0:T(8,128)(2,1)}), bf16[16,16,256]{2,1,0:T(8,128)(2,1)S(1)}, u32[]{:S(2)}, u32[]{:S(2)}) async-start(bf16[16,16,256]{2,1,0:T(8,128)(2,1)} %get-tuple-element.26), calls=%async_computation.3 | async-start | bytes 262144 | tf_op jit(solution)/shard_map/all_to_all | solution.py:211
  79.0 0.7 collective-permute-start.7
  79.7 4.8 %collective-permute-start.6 = (f32[8,256]{1,0:T(8,128)S(1)}, f32[8,256]{1,0:T(8,128)S(1)}, u32[]{:S(2)}, u32[]{:S(2)}) collective-permute-start(f32[8,256]{1,0:T(8,128)S(1)} %get-tuple-element.27.field.f2), channel_id=1, source_target_pairs={{0,64},{64,0},{128,192},{192,128},{256,320},{320,256},{384,448},{4... | collective-permute-start | bytes 24584 | tf_op jit(solution)/shard_map/ppermute | solution.py:186
  84.4 0.0 collective-permute-done.7.down
  84.5 0.8 collective-permute-done.6.up
  85.2 8.1 %all-to-all-done.3.parts = bf16[16,16,256]{2,1,0:T(8,128)(2,1)S(1)} async-done(((bf16[16,16,256]{2,1,0:T(8,128)(2,1)}), bf16[16,16,256]{2,1,0:T(8,128)(2,1)S(1)}, u32[]{:S(2)}, u32[]{:S(2)}) %all-to-all-start.3) | async-done | bytes 131104 | tf_op jit(solution)/shard_map/all_to_all | solution.py:211
  93.4 1.5 %shard_map.53 = (f32[8,256]{1,0:T(8,128)S(1)}, bf16[16,16,256]{2,1,0:T(8,128)(2,1)}) custom-call(s32[1]{0:T(128)} %bitcast.row_ref, bf16[16,16,256]{2,1,0:T(8,128)(2,1)S(1)} %all-to-all-done.3.parts, bf16[64,4096]{1,0:T(8,128)(2,1)S(1)} %bitcast.11, bf16[64,4096]{1,0:T(8,128)(2,1)S(1)} %collective-permute-done.c1, ...), custom_call_target="tpu_custom_call" | custom-call | tf_op jit(solution)/shard_map/pallas_call | solution.py:29
  94.9 4.6 %all-to-all-start.4 = ((bf16[16,16,256]{2,1,0:T(8,128)(2,1)}), bf16[16,16,256]{2,1,0:T(8,128)(2,1)S(1)}, u32[]{:S(2)}, u32[]{:S(2)}) async-start(bf16[16,16,256]{2,1,0:T(8,128)(2,1)} %get-tuple-element.28), calls=%async_computation.4 | async-start | bytes 262144 | tf_op jit(solution)/shard_map/all_to_all | solution.py:211
  99.5 0.7 collective-permute-start.9
  100.2 4.8 %collective-permute-start.8 = (f32[8,256]{1,0:T(8,128)S(1)}, f32[8,256]{1,0:T(8,128)S(1)}, u32[]{:S(2)}, u32[]{:S(2)}) collective-permute-start(f32[8,256]{1,0:T(8,128)S(1)} %get-tuple-element.29.field.f3), channel_id=1, source_target_pairs={{0,64},{64,0},{128,192},{192,128},{256,320},{320,256},{384,448},{4... | collective-permute-start | bytes 24584 | tf_op jit(solution)/shard_map/ppermute | solution.py:186
  105.0 0.0 collective-permute-done.9.down
  105.0 0.8 collective-permute-done.8.up
  105.8 8.6 %all-to-all-done.4.parts = bf16[16,16,256]{2,1,0:T(8,128)(2,1)S(1)} async-done(((bf16[16,16,256]{2,1,0:T(8,128)(2,1)}), bf16[16,16,256]{2,1,0:T(8,128)(2,1)S(1)}, u32[]{:S(2)}, u32[]{:S(2)}) %all-to-all-start.4) | async-done | bytes 131104 | tf_op jit(solution)/shard_map/all_to_all | solution.py:211
  114.3 0.8 shard_map.54
  115.1 9.3 %all_to_all.36.tables = f32[8,8,128]{2,1,0:T(8,128)S(1)} all-to-all(f32[8,8,128]{2,1,0:T(8,128)S(1)} %get-tuple-element.30), channel_id=1, replica_groups=mesh['x'=4,'c'=2,'z'=16,'y'=4] {'x','c'}, dimensions={0} | all-to-all | bytes 65536 | tf_op jit(solution)/shard_map/all_to_all | solution.py:227
  124.4 16.3 %all_to_all.37.tables = f32[16,8,128]{2,1,0:T(8,128)S(1)} all-to-all(f32[16,8,128]{2,1,0:T(8,128)S(1)} %shard_map.55), channel_id=1, replica_groups=mesh['x'=4,'c'=2,'z'=16,'y'=4] {'z'}, dimensions={0} | all-to-all | bytes 131072 | tf_op jit(solution)/shard_map/all_to_all | solution.py:229
  140.7 1.1 shard_map.56
  (3 shorter events, 0.0 us)
Async XLA Ops:
  0.6 0.7 copy-start.3
  0.6 0.7 copy-start.2
  12.7 34.7 %collective-permute-start.2 = (bf16[64,4096]{1,0:T(8,128)(2,1)}, bf16[64,4096]{1,0:T(8,128)(2,1)S(1)}, u32[]{:S(2)}, u32[]{:S(2)}) collective-permute-start(bf16[64,4096]{1,0:T(8,128)(2,1)} %bitcast.6), channel_id=1, source_target_pairs={{3,0},{0,1},{1,2},{2,3},{7,4},{4,5},{5,6},{6,7},{11,8},{8,9},{9,10... | collective-permute-start | bytes 1572872 | tf_op jit(solution)/shard_map/ppermute | solution.py:182
  16.6 30.8 %collective-permute-start.1 = (bf16[64,4096]{1,0:T(8,128)(2,1)}, bf16[64,4096]{1,0:T(8,128)(2,1)S(1)}, u32[]{:S(2)}, u32[]{:S(2)}) collective-permute-start(bf16[64,4096]{1,0:T(8,128)(2,1)} %bitcast.7), channel_id=1, source_target_pairs={{2,0},{3,1},{0,2},{1,3},{6,4},{7,5},{4,6},{5,7},{10,8},{11,9},{8,1... | collective-permute-start | bytes 1572872 | tf_op jit(solution)/shard_map/ppermute | solution.py:182
  19.0 28.3 %collective-permute-start = (bf16[64,4096]{1,0:T(8,128)(2,1)}, bf16[64,4096]{1,0:T(8,128)(2,1)S(1)}, u32[]{:S(2)}, u32[]{:S(2)}) collective-permute-start(bf16[64,4096]{1,0:T(8,128)(2,1)} %bitcast.8), channel_id=1, source_target_pairs={{1,0},{2,1},{3,2},{0,3},{5,4},{6,5},{7,6},{4,7},{9,8},{10,9},{11,1... | collective-permute-start | bytes 1572872 | tf_op jit(solution)/shard_map/ppermute | solution.py:182
  22.8 24.6 %all-to-all-start.1 = ((bf16[16,8,256]{2,1,0:T(8,128)(2,1)}), bf16[16,8,256]{2,1,0:T(8,128)(2,1)S(1)}, u32[]{:S(2)}, u32[]{:S(2)}) async-start(bf16[16,8,256]{2,1,0:T(8,128)(2,1)} %get-tuple-element.19), calls=%async_computation.1 | async-start | bytes 131072 | tf_op jit(solution)/shard_map/all_to_all | solution.py:211
  34.5 0.7 collective-permute-start.3
  47.4 1.0 copy-start
  48.4 23.9 %copy-start.1 = (bf16[1,64,4096]{2,1,0:T(8,128)(2,1)S(1)}, bf16[1,64,4096]{2,1,0:T(8,128)(2,1)}, u32[]{:S(2)}) copy-start(bf16[1,64,4096]{2,1,0:T(8,128)(2,1)} %param.4) | copy-start | bytes 1572868
  49.8 22.5 %all-to-all-start.2 = ((bf16[16,8,256]{2,1,0:T(8,128)(2,1)}), bf16[16,8,256]{2,1,0:T(8,128)(2,1)S(1)}, u32[]{:S(2)}, u32[]{:S(2)}) async-start(bf16[16,8,256]{2,1,0:T(8,128)(2,1)} %get-tuple-element.24), calls=%async_computation.2 | async-start | bytes 131072 | tf_op jit(solution)/shard_map/all_to_all | solution.py:211
  59.3 5.4 %collective-permute-start.5 = (f32[8,256]{1,0:T(8,128)S(1)}, f32[8,256]{1,0:T(8,128)S(1)}, u32[]{:S(2)}, u32[]{:S(2)}) collective-permute-start(f32[8,256]{1,0:T(8,128)S(1)} %get-tuple-element.25.field.f1), channel_id=1, source_target_pairs={{64,128},{192,256},{320,384},{128,64},{256,192},{384,320},{65,129}... | collective-permute-start | bytes 24584 | tf_op jit(solution)/shard_map/ppermute | solution.py:191
  59.9 5.6 %collective-permute-start.4 = (f32[8,256]{1,0:T(8,128)S(1)}, f32[8,256]{1,0:T(8,128)S(1)}, u32[]{:S(2)}, u32[]{:S(2)}) collective-permute-start(f32[8,256]{1,0:T(8,128)S(1)} %get-tuple-element.25.field.f1), channel_id=1, source_target_pairs={{0,64},{64,0},{128,192},{192,128},{256,320},{320,256},{384,448},{4... | collective-permute-start | bytes 24584 | tf_op jit(solution)/shard_map/ppermute | solution.py:186
  73.8 19.6 %all-to-all-start.3 = ((bf16[16,16,256]{2,1,0:T(8,128)(2,1)}), bf16[16,16,256]{2,1,0:T(8,128)(2,1)S(1)}, u32[]{:S(2)}, u32[]{:S(2)}) async-start(bf16[16,16,256]{2,1,0:T(8,128)(2,1)} %get-tuple-element.26), calls=%async_computation.3 | async-start | bytes 262144 | tf_op jit(solution)/shard_map/all_to_all | solution.py:211
  79.0 5.4 %collective-permute-start.7 = (f32[8,256]{1,0:T(8,128)S(1)}, f32[8,256]{1,0:T(8,128)S(1)}, u32[]{:S(2)}, u32[]{:S(2)}) collective-permute-start(f32[8,256]{1,0:T(8,128)S(1)} %get-tuple-element.27.field.f2), channel_id=1, source_target_pairs={{64,128},{192,256},{320,384},{128,64},{256,192},{384,320},{65,129}... | collective-permute-start | bytes 24584 | tf_op jit(solution)/shard_map/ppermute | solution.py:191
  79.7 5.6 %collective-permute-start.6 = (f32[8,256]{1,0:T(8,128)S(1)}, f32[8,256]{1,0:T(8,128)S(1)}, u32[]{:S(2)}, u32[]{:S(2)}) collective-permute-start(f32[8,256]{1,0:T(8,128)S(1)} %get-tuple-element.27.field.f2), channel_id=1, source_target_pairs={{0,64},{64,0},{128,192},{192,128},{256,320},{320,256},{384,448},{4... | collective-permute-start | bytes 24584 | tf_op jit(solution)/shard_map/ppermute | solution.py:186
  94.9 19.5 %all-to-all-start.4 = ((bf16[16,16,256]{2,1,0:T(8,128)(2,1)}), bf16[16,16,256]{2,1,0:T(8,128)(2,1)S(1)}, u32[]{:S(2)}, u32[]{:S(2)}) async-start(bf16[16,16,256]{2,1,0:T(8,128)(2,1)} %get-tuple-element.28), calls=%async_computation.4 | async-start | bytes 262144 | tf_op jit(solution)/shard_map/all_to_all | solution.py:211
  99.5 5.4 %collective-permute-start.9 = (f32[8,256]{1,0:T(8,128)S(1)}, f32[8,256]{1,0:T(8,128)S(1)}, u32[]{:S(2)}, u32[]{:S(2)}) collective-permute-start(f32[8,256]{1,0:T(8,128)S(1)} %get-tuple-element.29.field.f3), channel_id=1, source_target_pairs={{64,128},{192,256},{320,384},{128,64},{256,192},{384,320},{65,129}... | collective-permute-start | bytes 24584 | tf_op jit(solution)/shard_map/ppermute | solution.py:191
  100.2 5.6 %collective-permute-start.8 = (f32[8,256]{1,0:T(8,128)S(1)}, f32[8,256]{1,0:T(8,128)S(1)}, u32[]{:S(2)}, u32[]{:S(2)}) collective-permute-start(f32[8,256]{1,0:T(8,128)S(1)} %get-tuple-element.29.field.f3), channel_id=1, source_target_pairs={{0,64},{64,0},{128,192},{192,128},{256,320},{320,256},{384,448},{4... | collective-permute-start | bytes 24584 | tf_op jit(solution)/shard_map/ppermute | solution.py:186

commit v5 on v4

--- a/solution.py
+++ b/solution.py
@@ -18,9 +18,10 @@
 BF16 = jnp.bfloat16
 
 
-def call(body, outs, *args, smem=0, keep=True):
+def call(body, outs, *args, smem=0, loose=(), keep=True):
     args = args[:smem] + tuple(
-        pltpu.with_memory_space_constraint(x, pltpu.VMEM) for x in args[smem:]
+        x if i in loose else pltpu.with_memory_space_constraint(x, pltpu.VMEM)
+        for i, x in enumerate(args[smem:])
     )
     if keep:
         outs = jax.tree.map(lambda o: pltpu.VMEM(o.shape, o.dtype), outs)
@@ -35,58 +36,52 @@
     )(*args)
 
 
-def store_parts(send, field, row):
-    turned = pltpu.roll(field, row * H, 1)
-    parts = turned.astype(BF16)
+def store_parts(send, field):
+    parts = field.astype(BF16)
     if send.shape[1] > B:
-        low = (turned - parts.astype(F32)).astype(BF16)
+        low = (field - parts.astype(F32)).astype(BF16)
         parts = jnp.concatenate([parts, low], axis=0)
     for z in range(NZ):
         send[z] = parts
 
 
-def unpack(row_ref, packed, field_out, even_out, diag_out, send):
-    row = row_ref[0] % NY
-    core = row_ref[0] // NY
+def unpack(core_ref, packed, field_out, even_out, diag_out, send):
+    core = core_ref[0]
 
     def wide(which, columns):
-        joined = jnp.concatenate([packed[which * NY + y][:, columns] for y in range(NY)], axis=1)
-        return pltpu.roll(joined, (NY - row) % NY * H, 1)
+        return jnp.concatenate([packed[which * NY + y][:, columns] for y in range(NY)], axis=1)
 
     field = wide(core, slice(0, H))
     field_out[...] = field
     even_out[...] = wide(1 - core, slice(0, H))
     diag_out[...] = wide(core, slice(H, 2 * H))
-    store_parts(send, field, row)
-
-
-def next_field(parts, blocks, field, diag, up, down):
-    sums = []
-    for block in blocks:
-        total = None
-        for z in range(NZ):
-            term = lax.dot_general(
-                parts[z],
-                block[:, z * W : (z + 1) * W],
-                (((1,), (1,)), ((), ())),
-                preferred_element_type=F32,
-            )
-            total = term if total is None else total + term
-        sums.append(total if total.shape[0] == B else total[:B] + total[B:])
-    blended = jnp.concatenate(sums, axis=1)
+    store_parts(send, field)
+
+
+def next_field(parts, rows, field, diag, up, down):
+    total = None
+    for z in range(NZ):
+        term = lax.dot_general(
+            parts[z],
+            rows[:, z * W : (z + 1) * W],
+            (((1,), (1,)), ((), ())),
+            preferred_element_type=F32,
+        )
+        total = term if total is None else total + term
+    blended = total if total.shape[0] == B else total[:B] + total[B:]
     own = (diag[0:1] + (2.0 - CENTRE)) * field[...]
     return (own + blended - (up[...] + down[...])) * (1.0 / SCALE)
 
 
-def step(row_ref, parts, c0, c1, c2, c3, field, diag, up, down, field_out, send):
-    out = next_field(parts, (c0, c1, c2, c3), field, diag, up, down)
+def step(parts, rows, field, diag, up, down, field_out, send):
+    out = next_field(parts, rows, field, diag, up, down)
     field_out[...] = out
-    store_parts(send, out, row_ref[0] % NY)
-
-
-def last_step(parts, c0, c1, c2, c3, field, diag, up, down, f0, f1, f2, field_out, send):
-    out = next_field(parts, (c0, c1, c2, c3), field, diag, up, down)
-    field_out[...] = out[:, :H]
+    store_parts(send, out)
+
+
+def last_step(parts, rows, field, diag, up, down, f0, f1, f2, field_out, send):
+    out = next_field(parts, rows, field, diag, up, down)
+    field_out[...] = out
     fields = [f0[...], f1[...], f2[...], field[...], out]
     lane = lax.broadcasted_iota(jnp.int32, (B, 128), 1)
     table = jnp.zeros((B, 128), F32)
@@ -104,7 +99,7 @@
         send[z] = total
 
 
-def finish(tables, f0, f1, f2, f3, f4, solution_out, residual_out):
+def finish(row_ref, tables, f0, f1, f2, f3, f4, solution_out, residual_out):
     total = tables[0]
     for z in range(1, NZ):
         total = total + tables[z]
@@ -162,24 +157,20 @@
             beta = (rho_next / rho) * (alpha / omega)
             search = plus(residual, plus(search, image_one, -omega), beta)
             rho = rho_next
-    fields = [f0[:, :H], f1[:, :H], f2[:, :H], f3[:, :H], f4[...]]
+    fields = [f0, f1, f2, f3, f4]
+    row = row_ref[0]
 
     def combine(a):
-        out = a[0] * fields[0]
+        wide = a[0] * fields[0][...]
         for k in range(1, len(a)):
-            out = out + a[k] * fields[k]
-        return out
+            wide = wide + a[k] * fields[k][...]
+        own = wide[:, :H]
+        for y in range(1, NY):
+            own = jnp.where(row == y, wide[:, y * H : (y + 1) * H], own)
+        return own
 
     solution_out[...] = combine(found)
     residual_out[...] = combine(residual)
-
-
-def spread(array, axes, count):
-    return lax.all_to_all(array, axes, 0, 0, tiled=True)
-
-
-def shifted(array, shift):
-    return lax.ppermute(array, "y", [((y + shift) % NY, y) for y in range(NY)])
 
 
 def even(field):
@@ -193,16 +184,16 @@
 
 def on_device(source, coupling, diagonal):
     own = coupling[0]
-    row = lax.axis_index(("c", "y")).astype(jnp.int32).reshape(1)
+    row, core = (lax.axis_index(axis).astype(jnp.int32).reshape(1) for axis in ("y", "c"))
     packed = jnp.concatenate([source[0], jnp.broadcast_to(diagonal, (B, H))], axis=1)
     packed = jnp.broadcast_to(packed[None], (NC * NY, B, 128))
     packed = lax.all_to_all(packed, ("c", "y"), 0, 0, tiled=True)
     own, packed = lax.optimization_barrier((own, packed))
-    blocks = [own] + [shifted(own, shift) for shift in range(1, NY)]
+    rows = lax.all_gather(own, "y", axis=0, tiled=True)
     shape = jax.ShapeDtypeStruct
     wide = shape((B, W), F32)
     sends = [shape((NZ, B if k < LOW_FROM else 2 * B, W), BF16) for k in range(STEPS)]
-    field, up, diag, send = call(unpack, (wide, wide, wide, sends[0]), row, packed, smem=1)
+    field, up, diag, send = call(unpack, (wide, wide, wide, sends[0]), core, packed, smem=1)
     fields = [field]
     for k in range(STEPS):
         down = odd(field)
@@ -211,24 +202,23 @@
         parts = lax.all_to_all(send, "z", 0, 0, tiled=True)
         if k + 1 < STEPS:
             field, send = call(
-                step,
-                (wide, sends[k + 1]),
-                row, parts, *blocks, field, diag, up, down,
-                smem=1,
-
+                step, (wide, sends[k + 1]), parts, rows, field, diag, up, down,
+                loose=(1,) if k == 0 else (),
             )
             fields.append(field)
         else:
             last, table = call(
                 last_step,
-                (shape((B, H), F32), shape((NX * NC, B, 128), F32)),
-                parts, *blocks, field, diag, up, down, *fields[:3],
+                (wide, shape((NX * NC, B, 128), F32)),
+                parts, rows, field, diag, up, down, *fields[:3],
             )
     table = lax.all_to_all(table, ("x", "c"), 0, 0, tiled=True)
     table = call(add_up, shape((NZ, B, 128), F32), table)
     table = lax.all_to_all(table, "z", 0, 0, tiled=True)
     own_shape = shape((B, H), F32)
-    found, residual = call(finish, (own_shape, own_shape), table, *fields, last, keep=False)
+    found, residual = call(
+        finish, (own_shape, own_shape), row, table, *fields, last, smem=1, keep=False
+    )
     return found[None], residual[None]
 
 

time: 143 us -> 165 us (1.15)
  waiting for transfers between devices: 38.1 us -> 62.6 us
  blocking collectives: 36.9 us -> 20.5 us
  between operations: 0.82 us -> 14.2 us
  starting transfers between devices: 57.1 us -> 54.9 us
    all_to_all x1 -> x0, blocking collectives: 16.3 us -> none  [on_device(): table = lax.all_to_all(table, 'z', 0, 0, tiled=True)]
    all_to_all x0 -> x1, waiting for transfers between devices: none -> 12.7 us  [on_device(): table = lax.all_to_all(table, 'z', 0, 0, tiled=True)]
    all_gather x0 -> x1, waiting for transfers between devices: none -> 12.2 us  [on_device(): rows = lax.all_gather(own, 'y', axis=0, tiled=True)]
    ppermute x3 -> x0, starting transfers between devices: 9.17 us -> none  [shifted(): return lax.ppermute(array, 'y', [((y + shift) % NY, y) for y in range(NY)])]
    all_to_all x0 -> x1, starting transfers between devices: none -> 3.8 us  [on_device(): table = lax.all_to_all(table, 'z', 0, 0, tiled=True)]
    all_to_all x4, starting transfers between devices: 31 us -> 34.2 us  [on_device(): parts = lax.all_to_all(send, 'z', 0, 0, tiled=True)]
  transfers between devices with their start and end apart: 14 -> 13, of which waited for: 7 -> 9; matrix products, arithmetic and copies ran while one was open for 0% -> 0% of each run, Pallas kernels for 1% -> 0%
where the time goes in v5:
time: 165 us; the launch traced here: 163 us
  waiting for transfers between devices  62.6 us (38%)
  starting transfers between devices  54.9 us (33%)
  blocking collectives  20.5 us (12%)
  between operations  14.2 us (9%)
  Pallas kernels  7.38 us (4%)
  local copies, waits for them, and re-layouts  2.33 us (1%)
    all_to_all x4, waiting for transfers between devices, on_device(): parts = lax.all_to_all(send, 'z', 0, 0, tiled=True)  35.3 us
    all_to_all x4, starting transfers between devices, on_device(): parts = lax.all_to_all(send, 'z', 0, 0, tiled=True)  34.2 us
    ppermute x3, starting transfers between devices, even(): return lax.ppermute(field, ('x', 'c'), [(i, i ^ 1) for i in range(NX * NC)])  14.2 us
    all_to_all x1, waiting for transfers between devices, on_device(): table = lax.all_to_all(table, 'z', 0, 0, tiled=True)  12.7 us
    all_gather x1, waiting for transfers between devices, on_device(): rows = lax.all_gather(own, 'y', axis=0, tiled=True)  12.2 us
    all_to_all x1, blocking collectives, on_device(): packed = lax.all_to_all(packed, ('c', 'y'), 0, 0, tiled=True)  11.3 us
    all_to_all x1, blocking collectives, on_device(): table = lax.all_to_all(table, ('x', 'c'), 0, 0, tiled=True)  9.2 us
    pallas_call x7, Pallas kernels, call(): pl.pallas_call(body, out_shape=outs, in_specs=specs, compiler_params=pltp...  7.38 us
  transfers between devices with their start and end apart: 13, of which 9 were waited for; matrix products, arithmetic and copies ran while one was open for 0% of the time, Pallas kernels for 0%

profile of v5, /device:TPU:24, one launch (start us, length us, event | category | flops | bytes accessed | tf_op | source)
XLA Modules:
  0.0 162.6 jit_solution(13162427751533830822)
XLA Ops:
  7.2 0.0 all-gather.2.cloned.1.call-start
  7.2 0.7 pad.1.clone
  7.9 0.7 pad_maximum_fusion
  8.6 11.3 %all_to_all.35.packed = f32[8,8,128]{2,1,0:T(8,128)S(1)} all-to-all(f32[8,8,128]{2,1,0:T(8,128)S(1)} %broadcast_in_dim.21), channel_id=1, replica_groups=mesh['x'=4,'c'=2,'z'=16,'y'=4] {'c','y'}, dimensions={0} | all-to-all | bytes 65536 | tf_op jit(solution)/shard_map/all_to_all | solution.py:190
  20.0 0.0 all-gather.2.cloned.1.call-update
  20.0 0.7 shard_map.50
  20.7 11.7 %all-to-all-start.1 = ((bf16[16,8,256]{2,1,0:T(8,128)(2,1)}), bf16[16,8,256]{2,1,0:T(8,128)(2,1)S(1)}, u32[]{:S(2)}, u32[]{:S(2)}) async-start(bf16[16,8,256]{2,1,0:T(8,128)(2,1)} %get-tuple-element.19), calls=%async_computation.1 | async-start | bytes 131072 | tf_op jit(solution)/shard_map/all_to_all | solution.py:202
  32.4 0.7 collective-permute-start
  33.1 0.0 collective-permute-done.down
  33.1 12.1 %all-to-all-done.1.parts = bf16[16,8,256]{2,1,0:T(8,128)(2,1)S(1)} async-done(((bf16[16,8,256]{2,1,0:T(8,128)(2,1)}), bf16[16,8,256]{2,1,0:T(8,128)(2,1)S(1)}, u32[]{:S(2)}, u32[]{:S(2)}) %all-to-all-start.1) | async-done | bytes 65568 | tf_op jit(solution)/shard_map/all_to_all | solution.py:202
  45.2 12.2 %all-gather.2.cloned.1.call-done.rows = bf16[256,4096]{1,0:T(8,128)(2,1)} async-done(((bf16[64,4096]{1,0:T(8,128)(2,1)}), bf16[256,4096]{1,0:T(8,128)(2,1)}) %all-gather.2.cloned.1.call-update) | async-done | bytes 2097168 | tf_op jit(solution)/shard_map/all_gather | solution.py:192
  57.3 0.0 copy-start
  57.3 1.6 copy-done
  58.9 0.0 copy-start.1
  58.9 1.3 shard_map.51
  60.2 12.3 %all-to-all-start.2 = ((bf16[16,8,256]{2,1,0:T(8,128)(2,1)}), bf16[16,8,256]{2,1,0:T(8,128)(2,1)S(1)}, u32[]{:S(2)}, u32[]{:S(2)}) async-start(bf16[16,8,256]{2,1,0:T(8,128)(2,1)} %get-tuple-element.24), calls=%async_computation.2 | async-start | bytes 131072 | tf_op jit(solution)/shard_map/all_to_all | solution.py:202
  72.5 0.7 collective-permute-start.2
  73.2 4.7 %collective-permute-start.1 = (f32[8,256]{1,0:T(8,128)S(1)}, f32[8,256]{1,0:T(8,128)S(1)}, u32[]{:S(2)}, u32[]{:S(2)}) collective-permute-start(f32[8,256]{1,0:T(8,128)S(1)} %get-tuple-element.25.field.f1), channel_id=1, source_target_pairs={{0,64},{64,0},{128,192},{192,128},{256,320},{320,256},{384,448},{4... | collective-permute-start | bytes 24584 | tf_op jit(solution)/shard_map/ppermute | solution.py:177
  77.9 0.0 collective-permute-done.2.down
  77.9 0.8 collective-permute-done.1.up
  78.7 6.5 %all-to-all-done.2.parts = bf16[16,8,256]{2,1,0:T(8,128)(2,1)S(1)} async-done(((bf16[16,8,256]{2,1,0:T(8,128)(2,1)}), bf16[16,8,256]{2,1,0:T(8,128)(2,1)S(1)}, u32[]{:S(2)}, u32[]{:S(2)}) %all-to-all-start.2) | async-done | bytes 65568 | tf_op jit(solution)/shard_map/all_to_all | solution.py:202
  85.2 0.0 copy-done.1
  85.2 1.3 shard_map.52
  86.6 5.5 %all-to-all-start.3 = ((bf16[16,16,256]{2,1,0:T(8,128)(2,1)}), bf16[16,16,256]{2,1,0:T(8,128)(2,1)S(1)}, u32[]{:S(2)}, u32[]{:S(2)}) async-start(bf16[16,16,256]{2,1,0:T(8,128)(2,1)} %get-tuple-element.26), calls=%async_computation.3 | async-start | bytes 262144 | tf_op jit(solution)/shard_map/all_to_all | solution.py:202
  92.1 0.7 collective-permute-start.4
  92.8 4.7 %collective-permute-start.3 = (f32[8,256]{1,0:T(8,128)S(1)}, f32[8,256]{1,0:T(8,128)S(1)}, u32[]{:S(2)}, u32[]{:S(2)}) collective-permute-start(f32[8,256]{1,0:T(8,128)S(1)} %get-tuple-element.27.field.f2), channel_id=1, source_target_pairs={{0,64},{64,0},{128,192},{192,128},{256,320},{320,256},{384,448},{4... | collective-permute-start | bytes 24584 | tf_op jit(solution)/shard_map/ppermute | solution.py:177
  97.5 0.0 collective-permute-done.4.down
  97.5 0.8 collective-permute-done.3.up
  98.3 8.2 %all-to-all-done.3.parts = bf16[16,16,256]{2,1,0:T(8,128)(2,1)S(1)} async-done(((bf16[16,16,256]{2,1,0:T(8,128)(2,1)}), bf16[16,16,256]{2,1,0:T(8,128)(2,1)S(1)}, u32[]{:S(2)}, u32[]{:S(2)}) %all-to-all-start.3) | async-done | bytes 131104 | tf_op jit(solution)/shard_map/all_to_all | solution.py:202
  106.5 1.3 shard_map.53
  107.8 4.6 %all-to-all-start.4 = ((bf16[16,16,256]{2,1,0:T(8,128)(2,1)}), bf16[16,16,256]{2,1,0:T(8,128)(2,1)S(1)}, u32[]{:S(2)}, u32[]{:S(2)}) async-start(bf16[16,16,256]{2,1,0:T(8,128)(2,1)} %get-tuple-element.28), calls=%async_computation.4 | async-start | bytes 262144 | tf_op jit(solution)/shard_map/all_to_all | solution.py:202
  112.5 0.7 collective-permute-start.6
  113.1 4.7 %collective-permute-start.5 = (f32[8,256]{1,0:T(8,128)S(1)}, f32[8,256]{1,0:T(8,128)S(1)}, u32[]{:S(2)}, u32[]{:S(2)}) collective-permute-start(f32[8,256]{1,0:T(8,128)S(1)} %get-tuple-element.29.field.f3), channel_id=1, source_target_pairs={{0,64},{64,0},{128,192},{192,128},{256,320},{320,256},{384,448},{4... | collective-permute-start | bytes 24584 | tf_op jit(solution)/shard_map/ppermute | solution.py:177
  117.9 0.0 collective-permute-done.6.down
  117.9 0.8 collective-permute-done.5.up
  118.7 8.6 %all-to-all-done.4.parts = bf16[16,16,256]{2,1,0:T(8,128)(2,1)S(1)} async-done(((bf16[16,16,256]{2,1,0:T(8,128)(2,1)}), bf16[16,16,256]{2,1,0:T(8,128)(2,1)S(1)}, u32[]{:S(2)}, u32[]{:S(2)}) %all-to-all-start.4) | async-done | bytes 131104 | tf_op jit(solution)/shard_map/all_to_all | solution.py:202
  127.3 0.7 shard_map.54
  128.0 9.2 %all_to_all.36.tables = f32[8,8,128]{2,1,0:T(8,128)S(1)} all-to-all(f32[8,8,128]{2,1,0:T(8,128)S(1)} %get-tuple-element.30), channel_id=1, replica_groups=mesh['x'=4,'c'=2,'z'=16,'y'=4] {'x','c'}, dimensions={0} | all-to-all | bytes 65536 | tf_op jit(solution)/shard_map/all_to_all | solution.py:215
  137.2 0.6 shard_map.55
  137.8 3.8 %all-to-all-start.6 = ((f32[16,8,128]{2,1,0:T(8,128)}), f32[16,8,128]{2,1,0:T(8,128)S(1)}, u32[]{:S(2)}, u32[]{:S(2)}) async-start(f32[16,8,128]{2,1,0:T(8,128)} %shard_map.55), calls=%async_computation.6 | async-start | bytes 131072 | tf_op jit(solution)/shard_map/all_to_all | solution.py:217
  141.6 12.7 %all-to-all-done.6.tables = f32[16,8,128]{2,1,0:T(8,128)S(1)} async-done(((f32[16,8,128]{2,1,0:T(8,128)}), f32[16,8,128]{2,1,0:T(8,128)S(1)}, u32[]{:S(2)}, u32[]{:S(2)}) %all-to-all-start.6) | async-done | bytes 65568 | tf_op jit(solution)/shard_map/all_to_all | solution.py:217
  154.4 1.4 shard_map.56
  (1 shorter events, 0.0 us)
Async XLA Ops:
  7.2 50.2 %all-gather.2.cloned.1.call-start = ((), (), s32[]{:S(2)}) async-start(), calls=%async_computation.7 | async-start | bytes 2621440 | tf_op jit(solution)/shard_map/all_gather | solution.py:192
  20.7 24.5 %all-to-all-start.1 = ((bf16[16,8,256]{2,1,0:T(8,128)(2,1)}), bf16[16,8,256]{2,1,0:T(8,128)(2,1)S(1)}, u32[]{:S(2)}, u32[]{:S(2)}) async-start(bf16[16,8,256]{2,1,0:T(8,128)(2,1)} %get-tuple-element.19), calls=%async_computation.1 | async-start | bytes 131072 | tf_op jit(solution)/shard_map/all_to_all | solution.py:202
  32.4 0.7 collective-permute-start
  57.3 1.6 copy-start
  58.9 26.3 %copy-start.1 = (bf16[256,4096]{1,0:T(8,128)(2,1)S(1)}, bf16[256,4096]{1,0:T(8,128)(2,1)}, u32[]{:S(2)}) copy-start(bf16[256,4096]{1,0:T(8,128)(2,1)} %all-gather.2.cloned.1.call-done.rows) | copy-start | bytes 6291460
  60.2 25.0 %all-to-all-start.2 = ((bf16[16,8,256]{2,1,0:T(8,128)(2,1)}), bf16[16,8,256]{2,1,0:T(8,128)(2,1)S(1)}, u32[]{:S(2)}, u32[]{:S(2)}) async-start(bf16[16,8,256]{2,1,0:T(8,128)(2,1)} %get-tuple-element.24), calls=%async_computation.2 | async-start | bytes 131072 | tf_op jit(solution)/shard_map/all_to_all | solution.py:202
  72.5 5.4 %collective-permute-start.2 = (f32[8,256]{1,0:T(8,128)S(1)}, f32[8,256]{1,0:T(8,128)S(1)}, u32[]{:S(2)}, u32[]{:S(2)}) collective-permute-start(f32[8,256]{1,0:T(8,128)S(1)} %get-tuple-element.25.field.f1), channel_id=1, source_target_pairs={{64,128},{192,256},{320,384},{128,64},{256,192},{384,320},{65,129}... | collective-permute-start | bytes 24584 | tf_op jit(solution)/shard_map/ppermute | solution.py:182
  73.2 5.6 %collective-permute-start.1 = (f32[8,256]{1,0:T(8,128)S(1)}, f32[8,256]{1,0:T(8,128)S(1)}, u32[]{:S(2)}, u32[]{:S(2)}) collective-permute-start(f32[8,256]{1,0:T(8,128)S(1)} %get-tuple-element.25.field.f1), channel_id=1, source_target_pairs={{0,64},{64,0},{128,192},{192,128},{256,320},{320,256},{384,448},{4... | collective-permute-start | bytes 24584 | tf_op jit(solution)/shard_map/ppermute | solution.py:177
  86.6 19.9 %all-to-all-start.3 = ((bf16[16,16,256]{2,1,0:T(8,128)(2,1)}), bf16[16,16,256]{2,1,0:T(8,128)(2,1)S(1)}, u32[]{:S(2)}, u32[]{:S(2)}) async-start(bf16[16,16,256]{2,1,0:T(8,128)(2,1)} %get-tuple-element.26), calls=%async_computation.3 | async-start | bytes 262144 | tf_op jit(solution)/shard_map/all_to_all | solution.py:202
  92.1 5.4 %collective-permute-start.4 = (f32[8,256]{1,0:T(8,128)S(1)}, f32[8,256]{1,0:T(8,128)S(1)}, u32[]{:S(2)}, u32[]{:S(2)}) collective-permute-start(f32[8,256]{1,0:T(8,128)S(1)} %get-tuple-element.27.field.f2), channel_id=1, source_target_pairs={{64,128},{192,256},{320,384},{128,64},{256,192},{384,320},{65,129}... | collective-permute-start | bytes 24584 | tf_op jit(solution)/shard_map/ppermute | solution.py:182
  92.8 5.6 %collective-permute-start.3 = (f32[8,256]{1,0:T(8,128)S(1)}, f32[8,256]{1,0:T(8,128)S(1)}, u32[]{:S(2)}, u32[]{:S(2)}) collective-permute-start(f32[8,256]{1,0:T(8,128)S(1)} %get-tuple-element.27.field.f2), channel_id=1, source_target_pairs={{0,64},{64,0},{128,192},{192,128},{256,320},{320,256},{384,448},{4... | collective-permute-start | bytes 24584 | tf_op jit(solution)/shard_map/ppermute | solution.py:177
  107.8 19.5 %all-to-all-start.4 = ((bf16[16,16,256]{2,1,0:T(8,128)(2,1)}), bf16[16,16,256]{2,1,0:T(8,128)(2,1)S(1)}, u32[]{:S(2)}, u32[]{:S(2)}) async-start(bf16[16,16,256]{2,1,0:T(8,128)(2,1)} %get-tuple-element.28), calls=%async_computation.4 | async-start | bytes 262144 | tf_op jit(solution)/shard_map/all_to_all | solution.py:202
  112.5 5.4 %collective-permute-start.6 = (f32[8,256]{1,0:T(8,128)S(1)}, f32[8,256]{1,0:T(8,128)S(1)}, u32[]{:S(2)}, u32[]{:S(2)}) collective-permute-start(f32[8,256]{1,0:T(8,128)S(1)} %get-tuple-element.29.field.f3), channel_id=1, source_target_pairs={{64,128},{192,256},{320,384},{128,64},{256,192},{384,320},{65,129}... | collective-permute-start | bytes 24584 | tf_op jit(solution)/shard_map/ppermute | solution.py:182
  113.1 5.6 %collective-permute-start.5 = (f32[8,256]{1,0:T(8,128)S(1)}, f32[8,256]{1,0:T(8,128)S(1)}, u32[]{:S(2)}, u32[]{:S(2)}) collective-permute-start(f32[8,256]{1,0:T(8,128)S(1)} %get-tuple-element.29.field.f3), channel_id=1, source_target_pairs={{0,64},{64,0},{128,192},{192,128},{256,320},{320,256},{384,448},{4... | collective-permute-start | bytes 24584 | tf_op jit(solution)/shard_map/ppermute | solution.py:177
  137.8 16.5 %all-to-all-start.6 = ((f32[16,8,128]{2,1,0:T(8,128)}), f32[16,8,128]{2,1,0:T(8,128)S(1)}, u32[]{:S(2)}, u32[]{:S(2)}) async-start(f32[16,8,128]{2,1,0:T(8,128)} %shard_map.55), calls=%async_computation.6 | async-start | bytes 131072 | tf_op jit(solution)/shard_map/all_to_all | solution.py:217
Sparse Core Ops, SparseCore 0:
  20.1 37.1 all-gather.1

commit v6 on v4

--- a/solution.py
+++ b/solution.py
@@ -6,7 +6,7 @@
 from jax.sharding import Mesh, PartitionSpec as P
 
 STEPS = 4
-LOW_FROM = 2
+LOW_FROM = 0
 CENTRE = 6.75
 SCALE = 32.0
 PAIRS = [(i, j) for j in range(STEPS + 1) for i in range(j + 1)]
@@ -78,14 +78,14 @@
     return (own + blended - (up[...] + down[...])) * (1.0 / SCALE)
 
 
-def step(row_ref, parts, c0, c1, c2, c3, field, diag, up, down, field_out, send):
-    out = next_field(parts, (c0, c1, c2, c3), field, diag, up, down)
+def step(row_ref, parts, c0, c1, c2, c3, c4, field, diag, up, down, field_out, send):
+    out = next_field(parts, (c0, c1, c2, c3, c4), field, diag, up, down)
     field_out[...] = out
     store_parts(send, out, row_ref[0] % NY)
 
 
-def last_step(parts, c0, c1, c2, c3, field, diag, up, down, f0, f1, f2, field_out, send):
-    out = next_field(parts, (c0, c1, c2, c3), field, diag, up, down)
+def last_step(parts, c0, c1, c2, c3, c4, field, diag, up, down, f0, f1, f2, field_out, send):
+    out = next_field(parts, (c0, c1, c2, c3, c4), field, diag, up, down)
     field_out[...] = out[:, :H]
     fields = [f0[...], f1[...], f2[...], field[...], out]
     lane = lax.broadcasted_iota(jnp.int32, (B, 128), 1)
@@ -174,10 +174,6 @@
     residual_out[...] = combine(residual)
 
 
-def spread(array, axes, count):
-    return lax.all_to_all(array, axes, 0, 0, tiled=True)
-
-
 def shifted(array, shift):
     return lax.ppermute(array, "y", [((y + shift) % NY, y) for y in range(NY)])
 
@@ -198,7 +194,8 @@
     packed = jnp.broadcast_to(packed[None], (NC * NY, B, 128))
     packed = lax.all_to_all(packed, ("c", "y"), 0, 0, tiled=True)
     own, packed = lax.optimization_barrier((own, packed))
-    blocks = [own] + [shifted(own, shift) for shift in range(1, NY)]
+    after, before = shifted(own, 1), shifted(own, -1)
+    blocks = [own, after, shifted(after[: H // 2], 1), shifted(before[H // 2 :], -1), before]
     shape = jax.ShapeDtypeStruct
     wide = shape((B, W), F32)
     sends = [shape((NZ, B if k < LOW_FROM else 2 * B, W), BF16) for k in range(STEPS)]

time: 143 us -> 145 us (1.014); the launches traced: 142 us -> 142 us
  blocking collectives: 36.9 us -> 38.9 us
    ppermute x3 -> x4, starting transfers between devices: 9.17 us -> 14.2 us  [shifted(): return lax.ppermute(array, 'y', [((y + shift) % NY, y) for y in range(NY)])]
    ppermute x3, starting transfers between devices: 14.3 us -> 9.72 us  [even(): return lax.ppermute(field, ('x', 'c'), [(i, i ^ 1) for i in range(NX * NC)])]
    all_to_all x1, blocking collectives: 9.26 us -> 10.9 us  [on_device(): table = lax.all_to_all(table, ('x', 'c'), 0, 0, tiled=True)]
  transfers between devices with their start and end apart: 14 -> 15, of which waited for: 7 -> 7; matrix products, arithmetic and copies ran while one was open for 0% -> 0% of each run, Pallas kernels for 1% -> 1%
where the time goes in v6:
time: 145 us; the launch traced here: 142 us
  starting transfers between devices  57.4 us (40%)
  blocking collectives  38.9 us (27%)
  waiting for transfers between devices  37 us (26%)
  Pallas kernels  7.21 us (5%)
    all_to_all x4, waiting for transfers between devices, on_device(): parts = lax.all_to_all(send, 'z', 0, 0, tiled=True)  35.6 us
    all_to_all x4, starting transfers between devices, on_device(): parts = lax.all_to_all(send, 'z', 0, 0, tiled=True)  30.8 us
    all_to_all x1, blocking collectives, on_device(): table = lax.all_to_all(table, 'z', 0, 0, tiled=True)  16.7 us
    ppermute x4, starting transfers between devices, shifted(): return lax.ppermute(array, 'y', [((y + shift) % NY, y) for y in range(NY)])  14.2 us
    all_to_all x1, blocking collectives, on_device(): packed = lax.all_to_all(packed, ('c', 'y'), 0, 0, tiled=True)  11.3 us
    all_to_all x1, blocking collectives, on_device(): table = lax.all_to_all(table, ('x', 'c'), 0, 0, tiled=True)  10.9 us
    ppermute x3, starting transfers between devices, even(): return lax.ppermute(field, ('x', 'c'), [(i, i ^ 1) for i in range(NX * NC)])  9.72 us
    pallas_call x7, Pallas kernels, call(): pl.pallas_call(body, out_shape=outs, in_specs=specs, compiler_params=pltp...  7.21 us
  transfers between devices with their start and end apart: 15, of which 7 were waited for; matrix products, arithmetic and copies ran while one was open for 0% of the time, Pallas kernels for 1%

profile of v6, /device:TPU:24, one launch (start us, length us, event | category | flops | bytes accessed | tf_op | source)
XLA Modules:
  0.0 142.1 jit_solution(729112560990197940)
XLA Ops:
  0.6 0.0 copy-start.2
  0.6 0.0 copy-start.1
  0.6 0.6 copy-done.2
  1.3 0.1 pad.1.clone
  1.4 0.0 copy-done.1
  1.4 11.3 %all_to_all.35.packed = f32[8,8,128]{2,1,0:T(8,128)S(1)} all-to-all(f32[8,8,128]{2,1,0:T(8,128)S(1)} %broadcast_in_dim.21), channel_id=1, replica_groups=mesh['x'=4,'c'=2,'z'=16,'y'=4] {'c','y'}, dimensions={0} | all-to-all | bytes 65536 | tf_op jit(solution)/shard_map/all_to_all | solution.py:195
  12.7 2.3 %collective-permute-start = (bf16[64,4096]{1,0:T(8,128)(2,1)}, bf16[64,4096]{1,0:T(8,128)(2,1)S(1)}, u32[]{:S(2)}, u32[]{:S(2)}) collective-permute-start(bf16[64,4096]{1,0:T(8,128)(2,1)} %bitcast.6), channel_id=1, source_target_pairs={{1,0},{2,1},{3,2},{0,3},{5,4},{6,5},{7,6},{4,7},{9,8},{10,9},{11,1... | collective-permute-start | bytes 1572872 | tf_op jit(solution)/shard_map/ppermute | solution.py:178
  15.1 4.7 %collective-permute-start.2 = (bf16[64,4096]{1,0:T(8,128)(2,1)}, bf16[64,4096]{1,0:T(8,128)(2,1)S(1)}, u32[]{:S(2)}, u32[]{:S(2)}) collective-permute-start(bf16[64,4096]{1,0:T(8,128)(2,1)} %bitcast.7), channel_id=1, source_target_pairs={{3,0},{0,1},{1,2},{2,3},{7,4},{4,5},{5,6},{6,7},{11,8},{8,9},{9,10... | collective-permute-start | bytes 1572872 | tf_op jit(solution)/shard_map/ppermute | solution.py:178
  19.8 0.9 shard_map.50
  20.7 11.7 %all-to-all-start.1 = ((bf16[16,16,256]{2,1,0:T(8,128)(2,1)}), bf16[16,16,256]{2,1,0:T(8,128)(2,1)S(1)}, u32[]{:S(2)}, u32[]{:S(2)}) async-start(bf16[16,16,256]{2,1,0:T(8,128)(2,1)} %get-tuple-element.19), calls=%async_computation.1 | async-start | bytes 262144 | tf_op jit(solution)/shard_map/all_to_all | solution.py:208
  32.4 0.0 copy-start
  32.4 0.0 collective-permute-done.c1
  32.4 2.1 %collective-permute-start.1 = (bf16[32,4096]{1,0:T(8,128)(2,1)S(1)}, bf16[32,4096]{1,0:T(8,128)(2,1)S(1)}, u32[]{:S(2)}, u32[]{:S(2)}) collective-permute-start(bf16[32,4096]{1,0:T(8,128)(2,1)S(1)} %slice.8), channel_id=1, source_target_pairs={{1,0},{2,1},{3,2},{0,3},{5,4},{6,5},{7,6},{4,7},{9,8},{10,9},{11,1... | collective-permute-start | bytes 786440 | tf_op jit(solution)/shard_map/ppermute | solution.py:178
  34.5 0.0 collective-permute-done.2.c4
  34.5 5.1 %collective-permute-start.3 = (bf16[32,4096]{1,0:T(8,128)(2,1)S(1)}, bf16[32,4096]{1,0:T(8,128)(2,1)S(1)}, u32[]{:S(2)}, u32[]{:S(2)}) collective-permute-start(bf16[32,4096]{1,0:T(8,128)(2,1)S(1)} %slice.9), channel_id=1, source_target_pairs={{3,0},{0,1},{1,2},{2,3},{7,4},{4,5},{5,6},{6,7},{11,8},{8,9},{9,10... | collective-permute-start | bytes 786440 | tf_op jit(solution)/shard_map/ppermute | solution.py:178
  39.7 0.7 collective-permute-start.4
  40.4 0.0 collective-permute-done.4.down
  40.4 6.0 %all-to-all-done.1.parts = bf16[16,16,256]{2,1,0:T(8,128)(2,1)S(1)} async-done(((bf16[16,16,256]{2,1,0:T(8,128)(2,1)}), bf16[16,16,256]{2,1,0:T(8,128)(2,1)S(1)}, u32[]{:S(2)}, u32[]{:S(2)}) %all-to-all-start.1) | async-done | bytes 131104 | tf_op jit(solution)/shard_map/all_to_all | solution.py:208
  46.4 0.0 collective-permute-done.1.c2
  46.4 0.0 collective-permute-done.3.c3
  46.4 0.0 copy-done
  46.4 1.5 %shard_map.51 = (f32[8,256]{1,0:T(8,128)S(1)}, bf16[16,16,256]{2,1,0:T(8,128)(2,1)}) custom-call(s32[1]{0:T(128)} %bitcast.row_ref, bf16[16,16,256]{2,1,0:T(8,128)(2,1)S(1)} %all-to-all-done.1.parts, bf16[64,4096]{1,0:T(8,128)(2,1)S(1)} %bitcast.8, bf16[64,4096]{1,0:T(8,128)(2,1)S(1)} %collective-permute-done.c1, ...), custom_call_target="tpu_custom_call" | custom-call | tf_op jit(solution)/shard_map/pallas_call | solution.py:29
  47.9 9.4 %all-to-all-start.2 = ((bf16[16,16,256]{2,1,0:T(8,128)(2,1)}), bf16[16,16,256]{2,1,0:T(8,128)(2,1)S(1)}, u32[]{:S(2)}, u32[]{:S(2)}) async-start(bf16[16,16,256]{2,1,0:T(8,128)(2,1)} %get-tuple-element.24), calls=%async_computation.2 | async-start | bytes 262144 | tf_op jit(solution)/shard_map/all_to_all | solution.py:208
  57.3 2.4 %collective-permute-start.5 = (f32[8,256]{1,0:T(8,128)S(1)}, f32[8,256]{1,0:T(8,128)S(1)}, u32[]{:S(2)}, u32[]{:S(2)}) collective-permute-start(f32[8,256]{1,0:T(8,128)S(1)} %get-tuple-element.25.field.f1), channel_id=1, source_target_pairs={{0,64},{64,0},{128,192},{192,128},{256,320},{320,256},{384,448},{4... | collective-permute-start | bytes 24584 | tf_op jit(solution)/shard_map/ppermute | solution.py:182
  59.7 0.7 collective-permute-start.6
  60.3 0.1 collective-permute-done.5.up
  60.5 0.0 collective-permute-done.6.down
  60.5 10.7 %all-to-all-done.2.parts = bf16[16,16,256]{2,1,0:T(8,128)(2,1)S(1)} async-done(((bf16[16,16,256]{2,1,0:T(8,128)(2,1)}), bf16[16,16,256]{2,1,0:T(8,128)(2,1)S(1)}, u32[]{:S(2)}, u32[]{:S(2)}) %all-to-all-start.2) | async-done | bytes 131104 | tf_op jit(solution)/shard_map/all_to_all | solution.py:208
  71.2 1.5 %shard_map.52 = (f32[8,256]{1,0:T(8,128)S(1)}, bf16[16,16,256]{2,1,0:T(8,128)(2,1)}) custom-call(s32[1]{0:T(128)} %bitcast.row_ref, bf16[16,16,256]{2,1,0:T(8,128)(2,1)S(1)} %all-to-all-done.2.parts, bf16[64,4096]{1,0:T(8,128)(2,1)S(1)} %bitcast.9, bf16[64,4096]{1,0:T(8,128)(2,1)S(1)} %collective-permute-done.c1, ...), custom_call_target="tpu_custom_call" | custom-call | tf_op jit(solution)/shard_map/pallas_call | solution.py:29
  72.6 5.6 %all-to-all-start.3 = ((bf16[16,16,256]{2,1,0:T(8,128)(2,1)}), bf16[16,16,256]{2,1,0:T(8,128)(2,1)S(1)}, u32[]{:S(2)}, u32[]{:S(2)}) async-start(bf16[16,16,256]{2,1,0:T(8,128)(2,1)} %get-tuple-element.26), calls=%async_computation.3 | async-start | bytes 262144 | tf_op jit(solution)/shard_map/all_to_all | solution.py:208
  78.2 1.9 %collective-permute-start.7 = (f32[8,256]{1,0:T(8,128)S(1)}, f32[8,256]{1,0:T(8,128)S(1)}, u32[]{:S(2)}, u32[]{:S(2)}) collective-permute-start(f32[8,256]{1,0:T(8,128)S(1)} %get-tuple-element.27.field.f2), channel_id=1, source_target_pairs={{0,64},{64,0},{128,192},{192,128},{256,320},{320,256},{384,448},{4... | collective-permute-start | bytes 24584 | tf_op jit(solution)/shard_map/ppermute | solution.py:182
  80.1 0.7 collective-permute-start.8
  80.8 0.5 collective-permute-done.7.up
  81.3 0.0 collective-permute-done.8.down
  81.3 11.7 %all-to-all-done.3.parts = bf16[16,16,256]{2,1,0:T(8,128)(2,1)S(1)} async-done(((bf16[16,16,256]{2,1,0:T(8,128)(2,1)}), bf16[16,16,256]{2,1,0:T(8,128)(2,1)S(1)}, u32[]{:S(2)}, u32[]{:S(2)}) %all-to-all-start.3) | async-done | bytes 131104 | tf_op jit(solution)/shard_map/all_to_all | solution.py:208
  93.0 1.5 %shard_map.53 = (f32[8,256]{1,0:T(8,128)S(1)}, bf16[16,16,256]{2,1,0:T(8,128)(2,1)}) custom-call(s32[1]{0:T(128)} %bitcast.row_ref, bf16[16,16,256]{2,1,0:T(8,128)(2,1)S(1)} %all-to-all-done.3.parts, bf16[64,4096]{1,0:T(8,128)(2,1)S(1)} %bitcast.10, bf16[64,4096]{1,0:T(8,128)(2,1)S(1)} %collective-permute-done.c1, ...), custom_call_target="tpu_custom_call" | custom-call | tf_op jit(solution)/shard_map/pallas_call | solution.py:29
  94.5 4.1 %all-to-all-start.4 = ((bf16[16,16,256]{2,1,0:T(8,128)(2,1)}), bf16[16,16,256]{2,1,0:T(8,128)(2,1)S(1)}, u32[]{:S(2)}, u32[]{:S(2)}) async-start(bf16[16,16,256]{2,1,0:T(8,128)(2,1)} %get-tuple-element.28), calls=%async_computation.4 | async-start | bytes 262144 | tf_op jit(solution)/shard_map/all_to_all | solution.py:208
  98.6 0.7 collective-permute-start.10
  99.3 5.4 %collective-permute-start.9 = (f32[8,256]{1,0:T(8,128)S(1)}, f32[8,256]{1,0:T(8,128)S(1)}, u32[]{:S(2)}, u32[]{:S(2)}) collective-permute-start(f32[8,256]{1,0:T(8,128)S(1)} %get-tuple-element.29.field.f3), channel_id=1, source_target_pairs={{0,64},{64,0},{128,192},{192,128},{256,320},{320,256},{384,448},{4... | collective-permute-start | bytes 24584 | tf_op jit(solution)/shard_map/ppermute | solution.py:182
  104.7 0.0 collective-permute-done.10.down
  104.7 0.8 collective-permute-done.9.up
  105.5 7.2 %all-to-all-done.4.parts = bf16[16,16,256]{2,1,0:T(8,128)(2,1)S(1)} async-done(((bf16[16,16,256]{2,1,0:T(8,128)(2,1)}), bf16[16,16,256]{2,1,0:T(8,128)(2,1)S(1)}, u32[]{:S(2)}, u32[]{:S(2)}) %all-to-all-start.4) | async-done | bytes 131104 | tf_op jit(solution)/shard_map/all_to_all | solution.py:208
  112.6 0.8 shard_map.54
  113.5 10.9 %all_to_all.36.tables = f32[8,8,128]{2,1,0:T(8,128)S(1)} all-to-all(f32[8,8,128]{2,1,0:T(8,128)S(1)} %get-tuple-element.30), channel_id=1, replica_groups=mesh['x'=4,'c'=2,'z'=16,'y'=4] {'x','c'}, dimensions={0} | all-to-all | bytes 65536 | tf_op jit(solution)/shard_map/all_to_all | solution.py:224
  124.4 16.7 %all_to_all.37.tables = f32[16,8,128]{2,1,0:T(8,128)S(1)} all-to-all(f32[16,8,128]{2,1,0:T(8,128)S(1)} %shard_map.55), channel_id=1, replica_groups=mesh['x'=4,'c'=2,'z'=16,'y'=4] {'z'}, dimensions={0} | all-to-all | bytes 131072 | tf_op jit(solution)/shard_map/all_to_all | solution.py:226
  141.0 1.1 shard_map.56
  (5 shorter events, 0.1 us)
Async XLA Ops:
  0.6 0.7 copy-start.2
  0.6 0.7 copy-start.1
  12.7 19.7 %collective-permute-start = (bf16[64,4096]{1,0:T(8,128)(2,1)}, bf16[64,4096]{1,0:T(8,128)(2,1)S(1)}, u32[]{:S(2)}, u32[]{:S(2)}) collective-permute-start(bf16[64,4096]{1,0:T(8,128)(2,1)} %bitcast.6), channel_id=1, source_target_pairs={{1,0},{2,1},{3,2},{0,3},{5,4},{6,5},{7,6},{4,7},{9,8},{10,9},{11,1... | collective-permute-start | bytes 1572872 | tf_op jit(solution)/shard_map/ppermute | solution.py:178
  15.1 19.5 %collective-permute-start.2 = (bf16[64,4096]{1,0:T(8,128)(2,1)}, bf16[64,4096]{1,0:T(8,128)(2,1)S(1)}, u32[]{:S(2)}, u32[]{:S(2)}) collective-permute-start(bf16[64,4096]{1,0:T(8,128)(2,1)} %bitcast.7), channel_id=1, source_target_pairs={{3,0},{0,1},{1,2},{2,3},{7,4},{4,5},{5,6},{6,7},{11,8},{8,9},{9,10... | collective-permute-start | bytes 1572872 | tf_op jit(solution)/shard_map/ppermute | solution.py:178
  20.7 25.7 %all-to-all-start.1 = ((bf16[16,16,256]{2,1,0:T(8,128)(2,1)}), bf16[16,16,256]{2,1,0:T(8,128)(2,1)S(1)}, u32[]{:S(2)}, u32[]{:S(2)}) async-start(bf16[16,16,256]{2,1,0:T(8,128)(2,1)} %get-tuple-element.19), calls=%async_computation.1 | async-start | bytes 262144 | tf_op jit(solution)/shard_map/all_to_all | solution.py:208
  32.4 14.0 %copy-start = (bf16[1,64,4096]{2,1,0:T(8,128)(2,1)S(1)}, bf16[1,64,4096]{2,1,0:T(8,128)(2,1)}, u32[]{:S(2)}) copy-start(bf16[1,64,4096]{2,1,0:T(8,128)(2,1)} %param.4) | copy-start | bytes 1572868
  32.4 14.0 %collective-permute-start.1 = (bf16[32,4096]{1,0:T(8,128)(2,1)S(1)}, bf16[32,4096]{1,0:T(8,128)(2,1)S(1)}, u32[]{:S(2)}, u32[]{:S(2)}) collective-permute-start(bf16[32,4096]{1,0:T(8,128)(2,1)S(1)} %slice.8), channel_id=1, source_target_pairs={{1,0},{2,1},{3,2},{0,3},{5,4},{6,5},{7,6},{4,7},{9,8},{10,9},{11,1... | collective-permute-start | bytes 786440 | tf_op jit(solution)/shard_map/ppermute | solution.py:178
  34.5 11.9 %collective-permute-start.3 = (bf16[32,4096]{1,0:T(8,128)(2,1)S(1)}, bf16[32,4096]{1,0:T(8,128)(2,1)S(1)}, u32[]{:S(2)}, u32[]{:S(2)}) collective-permute-start(bf16[32,4096]{1,0:T(8,128)(2,1)S(1)} %slice.9), channel_id=1, source_target_pairs={{3,0},{0,1},{1,2},{2,3},{7,4},{4,5},{5,6},{6,7},{11,8},{8,9},{9,10... | collective-permute-start | bytes 786440 | tf_op jit(solution)/shard_map/ppermute | solution.py:178
  39.7 0.7 collective-permute-start.4
  47.9 23.3 %all-to-all-start.2 = ((bf16[16,16,256]{2,1,0:T(8,128)(2,1)}), bf16[16,16,256]{2,1,0:T(8,128)(2,1)S(1)}, u32[]{:S(2)}, u32[]{:S(2)}) async-start(bf16[16,16,256]{2,1,0:T(8,128)(2,1)} %get-tuple-element.24), calls=%async_computation.2 | async-start | bytes 262144 | tf_op jit(solution)/shard_map/all_to_all | solution.py:208
  57.3 3.2 %collective-permute-start.5 = (f32[8,256]{1,0:T(8,128)S(1)}, f32[8,256]{1,0:T(8,128)S(1)}, u32[]{:S(2)}, u32[]{:S(2)}) collective-permute-start(f32[8,256]{1,0:T(8,128)S(1)} %get-tuple-element.25.field.f1), channel_id=1, source_target_pairs={{0,64},{64,0},{128,192},{192,128},{256,320},{320,256},{384,448},{4... | collective-permute-start | bytes 24584 | tf_op jit(solution)/shard_map/ppermute | solution.py:182
  59.7 0.8 collective-permute-start.6
  72.6 20.4 %all-to-all-start.3 = ((bf16[16,16,256]{2,1,0:T(8,128)(2,1)}), bf16[16,16,256]{2,1,0:T(8,128)(2,1)S(1)}, u32[]{:S(2)}, u32[]{:S(2)}) async-start(bf16[16,16,256]{2,1,0:T(8,128)(2,1)} %get-tuple-element.26), calls=%async_computation.3 | async-start | bytes 262144 | tf_op jit(solution)/shard_map/all_to_all | solution.py:208
  78.2 3.1 %collective-permute-start.7 = (f32[8,256]{1,0:T(8,128)S(1)}, f32[8,256]{1,0:T(8,128)S(1)}, u32[]{:S(2)}, u32[]{:S(2)}) collective-permute-start(f32[8,256]{1,0:T(8,128)S(1)} %get-tuple-element.27.field.f2), channel_id=1, source_target_pairs={{0,64},{64,0},{128,192},{192,128},{256,320},{320,256},{384,448},{4... | collective-permute-start | bytes 24584 | tf_op jit(solution)/shard_map/ppermute | solution.py:182
  80.1 1.1 collective-permute-start.8
  94.5 18.2 %all-to-all-start.4 = ((bf16[16,16,256]{2,1,0:T(8,128)(2,1)}), bf16[16,16,256]{2,1,0:T(8,128)(2,1)S(1)}, u32[]{:S(2)}, u32[]{:S(2)}) async-start(bf16[16,16,256]{2,1,0:T(8,128)(2,1)} %get-tuple-element.28), calls=%async_computation.4 | async-start | bytes 262144 | tf_op jit(solution)/shard_map/all_to_all | solution.py:208
  98.6 6.1 %collective-permute-start.10 = (f32[8,256]{1,0:T(8,128)S(1)}, f32[8,256]{1,0:T(8,128)S(1)}, u32[]{:S(2)}, u32[]{:S(2)}) collective-permute-start(f32[8,256]{1,0:T(8,128)S(1)} %get-tuple-element.29.field.f3), channel_id=1, source_target_pairs={{64,128},{192,256},{320,384},{128,64},{256,192},{384,320},{65,129}... | collective-permute-start | bytes 24584 | tf_op jit(solution)/shard_map/ppermute | solution.py:187
  99.3 6.2 %collective-permute-start.9 = (f32[8,256]{1,0:T(8,128)S(1)}, f32[8,256]{1,0:T(8,128)S(1)}, u32[]{:S(2)}, u32[]{:S(2)}) collective-permute-start(f32[8,256]{1,0:T(8,128)S(1)} %get-tuple-element.29.field.f3), channel_id=1, source_target_pairs={{0,64},{64,0},{128,192},{192,128},{256,320},{320,256},{384,448},{4... | collective-permute-start | bytes 24584 | tf_op jit(solution)/shard_map/ppermute | solution.py:182

commit v7 on v6

--- a/solution.py
+++ b/solution.py
@@ -6,7 +6,6 @@
 from jax.sharding import Mesh, PartitionSpec as P
 
 STEPS = 4
-LOW_FROM = 0
 CENTRE = 6.75
 SCALE = 32.0
 PAIRS = [(i, j) for j in range(STEPS + 1) for i in range(j + 1)]
@@ -37,17 +36,16 @@
 
 def store_parts(send, field, row):
     turned = pltpu.roll(field, row * H, 1)
-    parts = turned.astype(BF16)
-    if send.shape[1] > B:
-        low = (turned - parts.astype(F32)).astype(BF16)
-        parts = jnp.concatenate([parts, low], axis=0)
+    high = turned.astype(BF16)
+    low = (turned - high.astype(F32)).astype(BF16)
+    both = jnp.concatenate([high, low], axis=0)
     for z in range(NZ):
-        send[z] = parts
+        send[z] = both
 
 
 def unpack(row_ref, packed, field_out, even_out, diag_out, send):
     row = row_ref[0] % NY
-    core = row_ref[0] // NY
+    core = row_ref[0] // NY % NC
 
     def wide(which, columns):
         joined = jnp.concatenate([packed[which * NY + y][:, columns] for y in range(NY)], axis=1)
@@ -60,7 +58,7 @@
     store_parts(send, field, row)
 
 
-def next_field(parts, blocks, field, diag, up, down):
+def next_field(parts, blocks, field, diag, beside):
     sums = []
     for block in blocks:
         total = None
@@ -72,36 +70,72 @@
                 preferred_element_type=F32,
             )
             total = term if total is None else total + term
-        sums.append(total if total.shape[0] == B else total[:B] + total[B:])
+        sums.append(total[:B] + total[B:])
     blended = jnp.concatenate(sums, axis=1)
     own = (diag[0:1] + (2.0 - CENTRE)) * field[...]
-    return (own + blended - (up[...] + down[...])) * (1.0 / SCALE)
+    total = own + blended
+    if beside is not None:
+        total = total - beside
+    return total * (1.0 / SCALE)
 
 
 def step(row_ref, parts, c0, c1, c2, c3, c4, field, diag, up, down, field_out, send):
-    out = next_field(parts, (c0, c1, c2, c3, c4), field, diag, up, down)
+    out = next_field(parts, (c0, c1, c2, c3, c4), field, diag, up[...] + down[...])
     field_out[...] = out
     store_parts(send, out, row_ref[0] % NY)
 
 
-def last_step(parts, c0, c1, c2, c3, c4, field, diag, up, down, f0, f1, f2, field_out, send):
-    out = next_field(parts, (c0, c1, c2, c3, c4), field, diag, up, down)
-    field_out[...] = out[:, :H]
-    fields = [f0[...], f1[...], f2[...], field[...], out]
+def last_step(parts, c0, c1, c2, c3, c4, field, diag, f0, f1, f2, u0, d0, u1, d1, u2, d2, send):
+    partial = next_field(parts, (c0, c1, c2, c3, c4), field, diag, None)
+    f3 = field[...]
+    fields = [f0[...], f1[...], f2[...], f3]
+    beside = [u0[...] + d0[...], u1[...] + d1[...], u2[...] + d2[...]]
     lane = lax.broadcasted_iota(jnp.int32, (B, 128), 1)
     table = jnp.zeros((B, 128), F32)
     for p, (i, j) in enumerate(PAIRS):
-        table = jnp.where(lane == p, jnp.sum(fields[i] * fields[j], axis=1, keepdims=True), table)
+        if j < STEPS:
+            terms = fields[i] * fields[j]
+        elif i < STEPS - 1:
+            terms = partial * fields[i] - f3 * beside[i] * (1.0 / SCALE)
+        else:
+            continue
+        table = jnp.where(lane == p, jnp.sum(terms, axis=1, keepdims=True), table)
+    packed = jnp.concatenate([table, partial, f3], axis=1)
     for k in range(NX * NC):
-        send[k] = table
-
-
-def add_up(tables, send):
-    total = tables[0]
-    for k in range(1, NX * NC):
-        total = total + tables[k]
+        send[k] = packed
+
+
+def add_up(plane_ref, packed, last_out, send):
+    count = NX * NC
+    inv = 1.0 / SCALE
+
+    def partial(p):
+        return packed[p][:, 128 : 128 + W]
+
+    def before(p):
+        return packed[p][:, 128 + W :]
+
+    table = packed[0][:, :128]
+    for p in range(1, count):
+        table = table + packed[p][:, :128]
+    square = cross = jnp.zeros((B, W), F32)
+    for p in range(count):
+        beside = before(p - 1) if p > 0 else 0.0
+        if p + 1 < count:
+            beside = beside + before(p + 1)
+        last = partial(p) - beside * inv
+        square = square + last * last
+        cross = cross + last * before(p)
+    lane = lax.broadcasted_iota(jnp.int32, (B, 128), 1)
+    for pair, terms in (((STEPS - 1, STEPS), cross), ((STEPS, STEPS), square)):
+        value = jnp.sum(terms, axis=1, keepdims=True)
+        table = jnp.where(lane == PAIRS.index(pair), value, table)
     for z in range(NZ):
-        send[z] = total
+        send[z] = table
+    plane = plane_ref[0] // NY
+    above = jnp.where(plane > 0, before(jnp.maximum(plane - 1, 0)), 0.0)
+    below = jnp.where(plane + 1 < count, before(jnp.minimum(plane + 1, count - 1)), 0.0)
+    last_out[...] = partial(plane) - (above + below) * inv
 
 
 def finish(tables, f0, f1, f2, f3, f4, solution_out, residual_out):
@@ -162,7 +196,7 @@
             beta = (rho_next / rho) * (alpha / omega)
             search = plus(residual, plus(search, image_one, -omega), beta)
             rho = rho_next
-    fields = [f0[:, :H], f1[:, :H], f2[:, :H], f3[:, :H], f4[...]]
+    fields = [f[:, :H] for f in (f0, f1, f2, f3, f4)]
 
     def combine(a):
         out = a[0] * fields[0]
@@ -189,7 +223,7 @@
 
 def on_device(source, coupling, diagonal):
     own = coupling[0]
-    row = lax.axis_index(("c", "y")).astype(jnp.int32).reshape(1)
+    row = lax.axis_index(("x", "c", "y")).astype(jnp.int32).reshape(1)
     packed = jnp.concatenate([source[0], jnp.broadcast_to(diagonal, (B, H))], axis=1)
     packed = jnp.broadcast_to(packed[None], (NC * NY, B, 128))
     packed = lax.all_to_all(packed, ("c", "y"), 0, 0, tiled=True)
@@ -198,31 +232,27 @@
     blocks = [own, after, shifted(after[: H // 2], 1), shifted(before[H // 2 :], -1), before]
     shape = jax.ShapeDtypeStruct
     wide = shape((B, W), F32)
-    sends = [shape((NZ, B if k < LOW_FROM else 2 * B, W), BF16) for k in range(STEPS)]
-    field, up, diag, send = call(unpack, (wide, wide, wide, sends[0]), row, packed, smem=1)
-    fields = [field]
-    for k in range(STEPS):
+    send_shape = shape((NZ, 2 * B, W), BF16)
+    field, up, diag, send = call(unpack, (wide, wide, wide, send_shape), row, packed, smem=1)
+    fields, beside = [field], []
+    for k in range(STEPS - 1):
         down = odd(field)
         if k > 0:
             up = even(field)
+        beside += [up, down]
         parts = lax.all_to_all(send, "z", 0, 0, tiled=True)
-        if k + 1 < STEPS:
-            field, send = call(
-                step,
-                (wide, sends[k + 1]),
-                row, parts, *blocks, field, diag, up, down,
-                smem=1,
-
-            )
-            fields.append(field)
-        else:
-            last, table = call(
-                last_step,
-                (shape((B, H), F32), shape((NX * NC, B, 128), F32)),
-                parts, *blocks, field, diag, up, down, *fields[:3],
-            )
-    table = lax.all_to_all(table, ("x", "c"), 0, 0, tiled=True)
-    table = call(add_up, shape((NZ, B, 128), F32), table)
+        field, send = call(
+            step, (wide, send_shape), row, parts, *blocks, field, diag, up, down, smem=1
+        )
+        fields.append(field)
+    parts = lax.all_to_all(send, "z", 0, 0, tiled=True)
+    packed = call(
+        last_step,
+        shape((NX * NC, B, 128 + 2 * W), F32),
+        parts, *blocks, field, diag, *fields[:3], *beside,
+    )
+    packed = lax.all_to_all(packed, ("x", "c"), 0, 0, tiled=True)
+    last, table = call(add_up, (wide, shape((NZ, B, 128), F32)), row, packed, smem=1)
     table = lax.all_to_all(table, "z", 0, 0, tiled=True)
     own_shape = shape((B, H), F32)
     found, residual = call(finish, (own_shape, own_shape), table, *fields, last, keep=False)

time: 145 us -> 145 us (level)
  blocking collectives: 38.9 us -> 57.9 us
  starting transfers between devices: 57.4 us -> 47.2 us
  waiting for transfers between devices: 37 us -> 29 us
    all_to_all x1 -> x2, blocking collectives: 10.9 us -> 29.9 us  [the longest x1 18 us: on_device(): parts = lax.all_to_all(send, 'z', 0, 0, tiled=True)]
    all_to_all x4 -> x3, waiting for transfers between devices: 35.6 us -> 28.4 us  [on_device(): parts = lax.all_to_all(send, 'z', 0, 0, tiled=True)]
    ppermute x3 -> x2, starting transfers between devices: 9.72 us -> 4.33 us  [even(): return lax.ppermute(field, ('x', 'c'), [(i, i ^ 1) for i in range(NX * NC)])]
    all_to_all x4 -> x3, starting transfers between devices: 30.8 us -> 26.7 us  [on_device(): parts = lax.all_to_all(send, 'z', 0, 0, tiled=True)]
  transfers between devices with their start and end apart: 15 -> 12, of which waited for: 7 -> 5; matrix products, arithmetic and copies ran while one was open for 0% -> 0% of each run, Pallas kernels for 1% -> 1%
where the time goes in v7:
time: 145 us; the launch traced here: 142 us
  blocking collectives  57.9 us (40%)
  starting transfers between devices  47.2 us (33%)
  waiting for transfers between devices  29 us (20%)
  Pallas kernels  6.66 us (5%)
    all_to_all x3, waiting for transfers between devices, on_device(): parts = lax.all_to_all(send, 'z', 0, 0, tiled=True)  28.4 us
    all_to_all x3, starting transfers between devices, on_device(): parts = lax.all_to_all(send, 'z', 0, 0, tiled=True)  26.7 us
    all_to_all x1, blocking collectives, on_device(): parts = lax.all_to_all(send, 'z', 0, 0, tiled=True)  18 us
    all_to_all x1, blocking collectives, on_device(): table = lax.all_to_all(table, 'z', 0, 0, tiled=True)  16.7 us
    ppermute x4, starting transfers between devices, shifted(): return lax.ppermute(array, 'y', [((y + shift) % NY, y) for y in range(NY)])  14.2 us
    all_to_all x1, blocking collectives, on_device(): packed = lax.all_to_all(packed, ('x', 'c'), 0, 0, tiled=True)  11.9 us
    all_to_all x1, blocking collectives, on_device(): packed = lax.all_to_all(packed, ('c', 'y'), 0, 0, tiled=True)  11.3 us
    pallas_call x7, Pallas kernels, call(): pl.pallas_call(body, out_shape=outs, in_specs=specs, compiler_params=pltp...  6.66 us
  transfers between devices with their start and end apart: 12, of which 5 were waited for; matrix products, arithmetic and copies ran while one was open for 0% of the time, Pallas kernels for 1%

profile of v7, /device:TPU:24, one launch (start us, length us, event | category | flops | bytes accessed | tf_op | source)
XLA Modules:
  0.0 142.4 jit_solution(11846984943705855127)
XLA Ops:
  0.6 0.0 copy-start.2
  0.6 0.0 copy-start.1
  0.6 0.6 copy-done.2
  1.3 0.1 pad.1.clone
  1.4 0.0 copy-done.1
  1.4 11.3 %all_to_all.35.packed = f32[8,8,128]{2,1,0:T(8,128)S(1)} all-to-all(f32[8,8,128]{2,1,0:T(8,128)S(1)} %broadcast_in_dim.21), channel_id=1, replica_groups=mesh['x'=4,'c'=2,'z'=16,'y'=4] {'c','y'}, dimensions={0} | all-to-all | bytes 65536 | tf_op jit(solution)/shard_map/all_to_all | solution.py:229
  12.7 2.3 %collective-permute-start = (bf16[64,4096]{1,0:T(8,128)(2,1)}, bf16[64,4096]{1,0:T(8,128)(2,1)S(1)}, u32[]{:S(2)}, u32[]{:S(2)}) collective-permute-start(bf16[64,4096]{1,0:T(8,128)(2,1)} %bitcast.6), channel_id=1, source_target_pairs={{1,0},{2,1},{3,2},{0,3},{5,4},{6,5},{7,6},{4,7},{9,8},{10,9},{11,1... | collective-permute-start | bytes 1572872 | tf_op jit(solution)/shard_map/ppermute | solution.py:212
  15.1 4.7 %collective-permute-start.2 = (bf16[64,4096]{1,0:T(8,128)(2,1)}, bf16[64,4096]{1,0:T(8,128)(2,1)S(1)}, u32[]{:S(2)}, u32[]{:S(2)}) collective-permute-start(bf16[64,4096]{1,0:T(8,128)(2,1)} %bitcast.7), channel_id=1, source_target_pairs={{3,0},{0,1},{1,2},{2,3},{7,4},{4,5},{5,6},{6,7},{11,8},{8,9},{9,10... | collective-permute-start | bytes 1572872 | tf_op jit(solution)/shard_map/ppermute | solution.py:212
  19.8 0.9 shard_map.50
  20.7 11.7 %all-to-all-start.1 = ((bf16[16,16,256]{2,1,0:T(8,128)(2,1)}), bf16[16,16,256]{2,1,0:T(8,128)(2,1)S(1)}, u32[]{:S(2)}, u32[]{:S(2)}) async-start(bf16[16,16,256]{2,1,0:T(8,128)(2,1)} %get-tuple-element.19), calls=%async_computation.1 | async-start | bytes 262144 | tf_op jit(solution)/shard_map/all_to_all | solution.py:243
  32.4 0.0 copy-start
  32.4 0.0 collective-permute-done.c1
  32.5 2.1 %collective-permute-start.1 = (bf16[32,4096]{1,0:T(8,128)(2,1)S(1)}, bf16[32,4096]{1,0:T(8,128)(2,1)S(1)}, u32[]{:S(2)}, u32[]{:S(2)}) collective-permute-start(bf16[32,4096]{1,0:T(8,128)(2,1)S(1)} %slice.8), channel_id=1, source_target_pairs={{1,0},{2,1},{3,2},{0,3},{5,4},{6,5},{7,6},{4,7},{9,8},{10,9},{11,1... | collective-permute-start | bytes 786440 | tf_op jit(solution)/shard_map/ppermute | solution.py:212
  34.5 0.0 collective-permute-done.2.c4
  34.5 5.1 %collective-permute-start.3 = (bf16[32,4096]{1,0:T(8,128)(2,1)S(1)}, bf16[32,4096]{1,0:T(8,128)(2,1)S(1)}, u32[]{:S(2)}, u32[]{:S(2)}) collective-permute-start(bf16[32,4096]{1,0:T(8,128)(2,1)S(1)} %slice.9), channel_id=1, source_target_pairs={{3,0},{0,1},{1,2},{2,3},{7,4},{4,5},{5,6},{6,7},{11,8},{8,9},{9,10... | collective-permute-start | bytes 786440 | tf_op jit(solution)/shard_map/ppermute | solution.py:212
  39.7 0.7 collective-permute-start.4
  40.4 0.0 collective-permute-done.4.down.d0
  40.4 6.0 %all-to-all-done.1.parts = bf16[16,16,256]{2,1,0:T(8,128)(2,1)S(1)} async-done(((bf16[16,16,256]{2,1,0:T(8,128)(2,1)}), bf16[16,16,256]{2,1,0:T(8,128)(2,1)S(1)}, u32[]{:S(2)}, u32[]{:S(2)}) %all-to-all-start.1) | async-done | bytes 131104 | tf_op jit(solution)/shard_map/all_to_all | solution.py:243
  46.4 0.0 collective-permute-done.1.c2
  46.4 0.0 collective-permute-done.3.c3
  46.4 0.0 copy-done
  46.4 1.5 %shard_map.51 = (f32[8,256]{1,0:T(8,128)S(1)}, bf16[16,16,256]{2,1,0:T(8,128)(2,1)}) custom-call(s32[1]{0:T(128)} %bitcast.row_ref.plane_ref, bf16[16,16,256]{2,1,0:T(8,128)(2,1)S(1)} %all-to-all-done.1.parts, bf16[64,4096]{1,0:T(8,128)(2,1)S(1)} %bitcast.8, bf16[64,4096]{1,0:T(8,128)(2,1)S(1)} %collective-permute-done.c1, ...), custom_call_target="tpu_custom_call" | custom-call | tf_op jit(solution)/shard_map/pallas_call | solution.py:28
  47.9 9.4 %all-to-all-start.2 = ((bf16[16,16,256]{2,1,0:T(8,128)(2,1)}), bf16[16,16,256]{2,1,0:T(8,128)(2,1)S(1)}, u32[]{:S(2)}, u32[]{:S(2)}) async-start(bf16[16,16,256]{2,1,0:T(8,128)(2,1)} %get-tuple-element.24), calls=%async_computation.2 | async-start | bytes 262144 | tf_op jit(solution)/shard_map/all_to_all | solution.py:243
  57.3 2.4 %collective-permute-start.5 = (f32[8,256]{1,0:T(8,128)S(1)}, f32[8,256]{1,0:T(8,128)S(1)}, u32[]{:S(2)}, u32[]{:S(2)}) collective-permute-start(f32[8,256]{1,0:T(8,128)S(1)} %get-tuple-element.25.field.f1), channel_id=1, source_target_pairs={{0,64},{64,0},{128,192},{192,128},{256,320},{320,256},{384,448},{4... | collective-permute-start | bytes 24584 | tf_op jit(solution)/shard_map/ppermute | solution.py:216
  59.7 0.7 collective-permute-start.6
  60.4 0.1 collective-permute-done.5.up.u1
  60.5 0.0 collective-permute-done.6.down.d1
  60.5 10.7 %all-to-all-done.2.parts = bf16[16,16,256]{2,1,0:T(8,128)(2,1)S(1)} async-done(((bf16[16,16,256]{2,1,0:T(8,128)(2,1)}), bf16[16,16,256]{2,1,0:T(8,128)(2,1)S(1)}, u32[]{:S(2)}, u32[]{:S(2)}) %all-to-all-start.2) | async-done | bytes 131104 | tf_op jit(solution)/shard_map/all_to_all | solution.py:243
  71.2 1.5 %shard_map.52 = (f32[8,256]{1,0:T(8,128)S(1)}, bf16[16,16,256]{2,1,0:T(8,128)(2,1)}) custom-call(s32[1]{0:T(128)} %bitcast.row_ref.plane_ref, bf16[16,16,256]{2,1,0:T(8,128)(2,1)S(1)} %all-to-all-done.2.parts, bf16[64,4096]{1,0:T(8,128)(2,1)S(1)} %bitcast.9, bf16[64,4096]{1,0:T(8,128)(2,1)S(1)} %collective-permute-done.c1, ...), custom_call_target="tpu_custom_call" | custom-call | tf_op jit(solution)/shard_map/pallas_call | solution.py:28
  72.6 5.6 %all-to-all-start.3 = ((bf16[16,16,256]{2,1,0:T(8,128)(2,1)}), bf16[16,16,256]{2,1,0:T(8,128)(2,1)S(1)}, u32[]{:S(2)}, u32[]{:S(2)}) async-start(bf16[16,16,256]{2,1,0:T(8,128)(2,1)} %get-tuple-element.26), calls=%async_computation.3 | async-start | bytes 262144 | tf_op jit(solution)/shard_map/all_to_all | solution.py:243
  78.2 1.9 %collective-permute-start.7 = (f32[8,256]{1,0:T(8,128)S(1)}, f32[8,256]{1,0:T(8,128)S(1)}, u32[]{:S(2)}, u32[]{:S(2)}) collective-permute-start(f32[8,256]{1,0:T(8,128)S(1)} %get-tuple-element.27.field.f2), channel_id=1, source_target_pairs={{0,64},{64,0},{128,192},{192,128},{256,320},{320,256},{384,448},{4... | collective-permute-start | bytes 24584 | tf_op jit(solution)/shard_map/ppermute | solution.py:216
  80.2 0.7 collective-permute-start.8
  80.8 0.5 collective-permute-done.7.up.u2
  81.3 0.0 collective-permute-done.8.down.d2
  81.3 11.7 %all-to-all-done.3.parts = bf16[16,16,256]{2,1,0:T(8,128)(2,1)S(1)} async-done(((bf16[16,16,256]{2,1,0:T(8,128)(2,1)}), bf16[16,16,256]{2,1,0:T(8,128)(2,1)S(1)}, u32[]{:S(2)}, u32[]{:S(2)}) %all-to-all-start.3) | async-done | bytes 131104 | tf_op jit(solution)/shard_map/all_to_all | solution.py:243
  93.0 0.8 shard_map.53
  93.8 18.0 %all_to_all.36.parts = bf16[16,16,256]{2,1,0:T(8,128)(2,1)S(1)} all-to-all(bf16[16,16,256]{2,1,0:T(8,128)(2,1)S(1)} %get-tuple-element.28), channel_id=1, replica_groups=mesh['x'=4,'c'=2,'z'=16,'y'=4] {'z'}, dimensions={0} | all-to-all | bytes 262144 | tf_op jit(solution)/shard_map/all_to_all | solution.py:248
  111.8 0.8 shard_map.54
  112.6 11.9 %all_to_all.37.packed = f32[8,8,640]{2,1,0:T(8,128)S(1)} all-to-all(f32[8,8,640]{2,1,0:T(8,128)S(1)} %shard_map.54), channel_id=1, replica_groups=mesh['x'=4,'c'=2,'z'=16,'y'=4] {'x','c'}, dimensions={0} | all-to-all | bytes 327680 | tf_op jit(solution)/shard_map/all_to_all | solution.py:254
  124.6 0.1 shard_map.55
  124.7 16.7 %all_to_all.38.tables = f32[16,8,128]{2,1,0:T(8,128)S(1)} all-to-all(f32[16,8,128]{2,1,0:T(8,128)S(1)} %get-tuple-element.30), channel_id=1, replica_groups=mesh['x'=4,'c'=2,'z'=16,'y'=4] {'z'}, dimensions={0} | all-to-all | bytes 131072 | tf_op jit(solution)/shard_map/all_to_all | solution.py:256
  141.3 1.1 shard_map.56
  (4 shorter events, 0.1 us)
Async XLA Ops:
  0.6 0.7 copy-start.2
  0.6 0.7 copy-start.1
  12.7 19.7 %collective-permute-start = (bf16[64,4096]{1,0:T(8,128)(2,1)}, bf16[64,4096]{1,0:T(8,128)(2,1)S(1)}, u32[]{:S(2)}, u32[]{:S(2)}) collective-permute-start(bf16[64,4096]{1,0:T(8,128)(2,1)} %bitcast.6), channel_id=1, source_target_pairs={{1,0},{2,1},{3,2},{0,3},{5,4},{6,5},{7,6},{4,7},{9,8},{10,9},{11,1... | collective-permute-start | bytes 1572872 | tf_op jit(solution)/shard_map/ppermute | solution.py:212
  15.1 19.5 %collective-permute-start.2 = (bf16[64,4096]{1,0:T(8,128)(2,1)}, bf16[64,4096]{1,0:T(8,128)(2,1)S(1)}, u32[]{:S(2)}, u32[]{:S(2)}) collective-permute-start(bf16[64,4096]{1,0:T(8,128)(2,1)} %bitcast.7), channel_id=1, source_target_pairs={{3,0},{0,1},{1,2},{2,3},{7,4},{4,5},{5,6},{6,7},{11,8},{8,9},{9,10... | collective-permute-start | bytes 1572872 | tf_op jit(solution)/shard_map/ppermute | solution.py:212
  20.7 25.7 %all-to-all-start.1 = ((bf16[16,16,256]{2,1,0:T(8,128)(2,1)}), bf16[16,16,256]{2,1,0:T(8,128)(2,1)S(1)}, u32[]{:S(2)}, u32[]{:S(2)}) async-start(bf16[16,16,256]{2,1,0:T(8,128)(2,1)} %get-tuple-element.19), calls=%async_computation.1 | async-start | bytes 262144 | tf_op jit(solution)/shard_map/all_to_all | solution.py:243
  32.4 14.0 %copy-start = (bf16[1,64,4096]{2,1,0:T(8,128)(2,1)S(1)}, bf16[1,64,4096]{2,1,0:T(8,128)(2,1)}, u32[]{:S(2)}) copy-start(bf16[1,64,4096]{2,1,0:T(8,128)(2,1)} %param.4) | copy-start | bytes 1572868
  32.5 14.0 %collective-permute-start.1 = (bf16[32,4096]{1,0:T(8,128)(2,1)S(1)}, bf16[32,4096]{1,0:T(8,128)(2,1)S(1)}, u32[]{:S(2)}, u32[]{:S(2)}) collective-permute-start(bf16[32,4096]{1,0:T(8,128)(2,1)S(1)} %slice.8), channel_id=1, source_target_pairs={{1,0},{2,1},{3,2},{0,3},{5,4},{6,5},{7,6},{4,7},{9,8},{10,9},{11,1... | collective-permute-start | bytes 786440 | tf_op jit(solution)/shard_map/ppermute | solution.py:212
  34.5 11.9 %collective-permute-start.3 = (bf16[32,4096]{1,0:T(8,128)(2,1)S(1)}, bf16[32,4096]{1,0:T(8,128)(2,1)S(1)}, u32[]{:S(2)}, u32[]{:S(2)}) collective-permute-start(bf16[32,4096]{1,0:T(8,128)(2,1)S(1)} %slice.9), channel_id=1, source_target_pairs={{3,0},{0,1},{1,2},{2,3},{7,4},{4,5},{5,6},{6,7},{11,8},{8,9},{9,10... | collective-permute-start | bytes 786440 | tf_op jit(solution)/shard_map/ppermute | solution.py:212
  39.7 0.7 collective-permute-start.4
  47.9 23.3 %all-to-all-start.2 = ((bf16[16,16,256]{2,1,0:T(8,128)(2,1)}), bf16[16,16,256]{2,1,0:T(8,128)(2,1)S(1)}, u32[]{:S(2)}, u32[]{:S(2)}) async-start(bf16[16,16,256]{2,1,0:T(8,128)(2,1)} %get-tuple-element.24), calls=%async_computation.2 | async-start | bytes 262144 | tf_op jit(solution)/shard_map/all_to_all | solution.py:243
  57.3 3.2 %collective-permute-start.5 = (f32[8,256]{1,0:T(8,128)S(1)}, f32[8,256]{1,0:T(8,128)S(1)}, u32[]{:S(2)}, u32[]{:S(2)}) collective-permute-start(f32[8,256]{1,0:T(8,128)S(1)} %get-tuple-element.25.field.f1), channel_id=1, source_target_pairs={{0,64},{64,0},{128,192},{192,128},{256,320},{320,256},{384,448},{4... | collective-permute-start | bytes 24584 | tf_op jit(solution)/shard_map/ppermute | solution.py:216
  59.7 0.8 collective-permute-start.6
  72.6 20.4 %all-to-all-start.3 = ((bf16[16,16,256]{2,1,0:T(8,128)(2,1)}), bf16[16,16,256]{2,1,0:T(8,128)(2,1)S(1)}, u32[]{:S(2)}, u32[]{:S(2)}) async-start(bf16[16,16,256]{2,1,0:T(8,128)(2,1)} %get-tuple-element.26), calls=%async_computation.3 | async-start | bytes 262144 | tf_op jit(solution)/shard_map/all_to_all | solution.py:243
  78.2 3.1 %collective-permute-start.7 = (f32[8,256]{1,0:T(8,128)S(1)}, f32[8,256]{1,0:T(8,128)S(1)}, u32[]{:S(2)}, u32[]{:S(2)}) collective-permute-start(f32[8,256]{1,0:T(8,128)S(1)} %get-tuple-element.27.field.f2), channel_id=1, source_target_pairs={{0,64},{64,0},{128,192},{192,128},{256,320},{320,256},{384,448},{4... | collective-permute-start | bytes 24584 | tf_op jit(solution)/shard_map/ppermute | solution.py:216
  80.2 1.1 collective-permute-start.8

commit v8 on v7

--- a/solution.py
+++ b/solution.py
@@ -8,6 +8,8 @@
 STEPS = 4
 CENTRE = 6.75
 SCALE = 32.0
+LINK = (6.5**2 / 12 + 2.0) / SCALE
+WITH_LOW = (True, True, True, False)
 PAIRS = [(i, j) for j in range(STEPS + 1) for i in range(j + 1)]
 NZ, NY, NX, NC = 16, 4, 4, 2
 B = 8
@@ -36,11 +38,12 @@
 
 def store_parts(send, field, row):
     turned = pltpu.roll(field, row * H, 1)
-    high = turned.astype(BF16)
-    low = (turned - high.astype(F32)).astype(BF16)
-    both = jnp.concatenate([high, low], axis=0)
+    parts = turned.astype(BF16)
+    if send.shape[1] > B:
+        low = (turned - parts.astype(F32)).astype(BF16)
+        parts = jnp.concatenate([parts, low], axis=0)
     for z in range(NZ):
-        send[z] = both
+        send[z] = parts
 
 
 def unpack(row_ref, packed, field_out, even_out, diag_out, send):
@@ -58,7 +61,7 @@
     store_parts(send, field, row)
 
 
-def next_field(parts, blocks, field, diag, beside):
+def next_field(parts, blocks, field, previous, diag, beside):
     sums = []
     for block in blocks:
         total = None
@@ -70,23 +73,27 @@
                 preferred_element_type=F32,
             )
             total = term if total is None else total + term
-        sums.append(total[:B] + total[B:])
+        sums.append(total if total.shape[0] == B else total[:B] + total[B:])
     blended = jnp.concatenate(sums, axis=1)
     own = (diag[0:1] + (2.0 - CENTRE)) * field[...]
     total = own + blended
+    if previous is not None:
+        total = total - LINK * previous[...]
     if beside is not None:
         total = total - beside
     return total * (1.0 / SCALE)
 
 
-def step(row_ref, parts, c0, c1, c2, c3, c4, field, diag, up, down, field_out, send):
-    out = next_field(parts, (c0, c1, c2, c3, c4), field, diag, up[...] + down[...])
+def step(row_ref, parts, c0, c1, c2, c3, c4, diag, up, down, field, *rest):
+    *previous, field_out, send = rest
+    previous = previous[0] if previous else None
+    out = next_field(parts, (c0, c1, c2, c3, c4), field, previous, diag, up[...] + down[...])
     field_out[...] = out
     store_parts(send, out, row_ref[0] % NY)
 
 
 def last_step(parts, c0, c1, c2, c3, c4, field, diag, f0, f1, f2, u0, d0, u1, d1, u2, d2, send):
-    partial = next_field(parts, (c0, c1, c2, c3, c4), field, diag, None)
+    partial = next_field(parts, (c0, c1, c2, c3, c4), field, f2, diag, None)
     f3 = field[...]
     fields = [f0[...], f1[...], f2[...], f3]
     beside = [u0[...] + d0[...], u1[...] + d1[...], u2[...] + d2[...]]
@@ -172,6 +179,8 @@
         out = [CENTRE * x for x in a] + [jnp.zeros_like(a[0])]
         for k, x in enumerate(a):
             out[k + 1] = out[k + 1] + SCALE * x
+            if k > 0:
+                out[k - 1] = out[k - 1] + LINK * x
         return out
 
     one = jnp.ones((B, 1), F32)
@@ -232,8 +241,8 @@
     blocks = [own, after, shifted(after[: H // 2], 1), shifted(before[H // 2 :], -1), before]
     shape = jax.ShapeDtypeStruct
     wide = shape((B, W), F32)
-    send_shape = shape((NZ, 2 * B, W), BF16)
-    field, up, diag, send = call(unpack, (wide, wide, wide, send_shape), row, packed, smem=1)
+    sends = [shape((NZ, 2 * B if low else B, W), BF16) for low in WITH_LOW]
+    field, up, diag, send = call(unpack, (wide, wide, wide, sends[0]), row, packed, smem=1)
     fields, beside = [field], []
     for k in range(STEPS - 1):
         down = odd(field)
@@ -242,7 +251,10 @@
         beside += [up, down]
         parts = lax.all_to_all(send, "z", 0, 0, tiled=True)
         field, send = call(
-            step, (wide, send_shape), row, parts, *blocks, field, diag, up, down, smem=1
+            step,
+            (wide, sends[k + 1]),
+            row, parts, *blocks, diag, up, down, *fields[::-1][:2],
+            smem=1,
         )
         fields.append(field)
     parts = lax.all_to_all(send, "z", 0, 0, tiled=True)

time: 145 us -> 142 us (0.979)
  blocking collectives: 57.9 us -> 55.1 us
where the time goes in v8:
time: 142 us; the launch traced here: 140 us
  blocking collectives  55.1 us (39%)
  starting transfers between devices  47.2 us (33%)
  waiting for transfers between devices  29 us (20%)
  Pallas kernels  6.64 us (5%)
    all_to_all x3, waiting for transfers between devices, on_device(): parts = lax.all_to_all(send, 'z', 0, 0, tiled=True)  28.4 us
    all_to_all x3, starting transfers between devices, on_device(): parts = lax.all_to_all(send, 'z', 0, 0, tiled=True)  26.7 us
    all_to_all x1, blocking collectives, on_device(): parts = lax.all_to_all(send, 'z', 0, 0, tiled=True)  17.3 us
    all_to_all x1, blocking collectives, on_device(): table = lax.all_to_all(table, 'z', 0, 0, tiled=True)  15.5 us
    ppermute x4, starting transfers between devices, shifted(): return lax.ppermute(array, 'y', [((y + shift) % NY, y) for y in range(NY)])  14.2 us
    all_to_all x1, blocking collectives, on_device(): packed = lax.all_to_all(packed, ('c', 'y'), 0, 0, tiled=True)  11.3 us
    all_to_all x1, blocking collectives, on_device(): packed = lax.all_to_all(packed, ('x', 'c'), 0, 0, tiled=True)  10.9 us
    pallas_call x7, Pallas kernels, call(): pl.pallas_call(body, out_shape=outs, in_specs=specs, compiler_params=pltp...  6.64 us
  transfers between devices with their start and end apart: 12, of which 5 were waited for; matrix products, arithmetic and copies ran while one was open for 0% of the time, Pallas kernels for 1%

profile of v8, /device:TPU:24, one launch (start us, length us, event | category | flops | bytes accessed | tf_op | source)
XLA Modules:
  0.0 139.6 jit_solution(15687748883870634506)
XLA Ops:
  0.6 0.0 copy-start.2
  0.6 0.0 copy-start.1
  0.6 0.6 copy-done.2
  1.3 0.1 pad.1.clone
  1.4 0.0 copy-done.1
  1.4 11.3 %all_to_all.35.packed = f32[8,8,128]{2,1,0:T(8,128)S(1)} all-to-all(f32[8,8,128]{2,1,0:T(8,128)S(1)} %broadcast_in_dim.21), channel_id=1, replica_groups=mesh['x'=4,'c'=2,'z'=16,'y'=4] {'c','y'}, dimensions={0} | all-to-all | bytes 65536 | tf_op jit(solution)/shard_map/all_to_all | solution.py:238
  12.7 2.3 %collective-permute-start = (bf16[64,4096]{1,0:T(8,128)(2,1)}, bf16[64,4096]{1,0:T(8,128)(2,1)S(1)}, u32[]{:S(2)}, u32[]{:S(2)}) collective-permute-start(bf16[64,4096]{1,0:T(8,128)(2,1)} %bitcast.6), channel_id=1, source_target_pairs={{1,0},{2,1},{3,2},{0,3},{5,4},{6,5},{7,6},{4,7},{9,8},{10,9},{11,1... | collective-permute-start | bytes 1572872 | tf_op jit(solution)/shard_map/ppermute | solution.py:221
  15.1 4.7 %collective-permute-start.2 = (bf16[64,4096]{1,0:T(8,128)(2,1)}, bf16[64,4096]{1,0:T(8,128)(2,1)S(1)}, u32[]{:S(2)}, u32[]{:S(2)}) collective-permute-start(bf16[64,4096]{1,0:T(8,128)(2,1)} %bitcast.7), channel_id=1, source_target_pairs={{3,0},{0,1},{1,2},{2,3},{7,4},{4,5},{5,6},{6,7},{11,8},{8,9},{9,10... | collective-permute-start | bytes 1572872 | tf_op jit(solution)/shard_map/ppermute | solution.py:221
  19.8 0.9 shard_map.50
  20.7 11.7 %all-to-all-start.1 = ((bf16[16,16,256]{2,1,0:T(8,128)(2,1)}), bf16[16,16,256]{2,1,0:T(8,128)(2,1)S(1)}, u32[]{:S(2)}, u32[]{:S(2)}) async-start(bf16[16,16,256]{2,1,0:T(8,128)(2,1)} %get-tuple-element.19), calls=%async_computation.1 | async-start | bytes 262144 | tf_op jit(solution)/shard_map/all_to_all | solution.py:252
  32.4 0.0 copy-start
  32.4 0.0 collective-permute-done.c1
  32.5 2.1 %collective-permute-start.1 = (bf16[32,4096]{1,0:T(8,128)(2,1)S(1)}, bf16[32,4096]{1,0:T(8,128)(2,1)S(1)}, u32[]{:S(2)}, u32[]{:S(2)}) collective-permute-start(bf16[32,4096]{1,0:T(8,128)(2,1)S(1)} %slice.8), channel_id=1, source_target_pairs={{1,0},{2,1},{3,2},{0,3},{5,4},{6,5},{7,6},{4,7},{9,8},{10,9},{11,1... | collective-permute-start | bytes 786440 | tf_op jit(solution)/shard_map/ppermute | solution.py:221
  34.5 0.0 collective-permute-done.2.c4
  34.5 5.1 %collective-permute-start.3 = (bf16[32,4096]{1,0:T(8,128)(2,1)S(1)}, bf16[32,4096]{1,0:T(8,128)(2,1)S(1)}, u32[]{:S(2)}, u32[]{:S(2)}) collective-permute-start(bf16[32,4096]{1,0:T(8,128)(2,1)S(1)} %slice.9), channel_id=1, source_target_pairs={{3,0},{0,1},{1,2},{2,3},{7,4},{4,5},{5,6},{6,7},{11,8},{8,9},{9,10... | collective-permute-start | bytes 786440 | tf_op jit(solution)/shard_map/ppermute | solution.py:221
  39.7 0.7 collective-permute-start.4
  40.4 0.0 collective-permute-done.4.down.d0
  40.4 6.0 %all-to-all-done.1.parts = bf16[16,16,256]{2,1,0:T(8,128)(2,1)S(1)} async-done(((bf16[16,16,256]{2,1,0:T(8,128)(2,1)}), bf16[16,16,256]{2,1,0:T(8,128)(2,1)S(1)}, u32[]{:S(2)}, u32[]{:S(2)}) %all-to-all-start.1) | async-done | bytes 131104 | tf_op jit(solution)/shard_map/all_to_all | solution.py:252
  46.4 0.0 collective-permute-done.1.c2
  46.4 0.0 collective-permute-done.3.c3
  46.4 0.0 copy-done
  46.4 1.5 %shard_map.51 = (f32[8,256]{1,0:T(8,128)S(1)}, bf16[16,16,256]{2,1,0:T(8,128)(2,1)}) custom-call(s32[1]{0:T(128)} %bitcast.row_ref.plane_ref, bf16[16,16,256]{2,1,0:T(8,128)(2,1)S(1)} %all-to-all-done.1.parts, bf16[64,4096]{1,0:T(8,128)(2,1)S(1)} %bitcast.8, bf16[64,4096]{1,0:T(8,128)(2,1)S(1)} %collective-permute-done.c1, ...), custom_call_target="tpu_custom_call" | custom-call | tf_op jit(solution)/shard_map/pallas_call | solution.py:30
  47.9 9.4 %all-to-all-start.2 = ((bf16[16,16,256]{2,1,0:T(8,128)(2,1)}), bf16[16,16,256]{2,1,0:T(8,128)(2,1)S(1)}, u32[]{:S(2)}, u32[]{:S(2)}) async-start(bf16[16,16,256]{2,1,0:T(8,128)(2,1)} %get-tuple-element.24), calls=%async_computation.2 | async-start | bytes 262144 | tf_op jit(solution)/shard_map/all_to_all | solution.py:252
  57.3 2.4 %collective-permute-start.5 = (f32[8,256]{1,0:T(8,128)S(1)}, f32[8,256]{1,0:T(8,128)S(1)}, u32[]{:S(2)}, u32[]{:S(2)}) collective-permute-start(f32[8,256]{1,0:T(8,128)S(1)} %get-tuple-element.25.field.rest_0_.f1), channel_id=1, source_target_pairs={{0,64},{64,0},{128,192},{192,128},{256,320},{320,256},{384,448},{4... | collective-permute-start | bytes 24584 | tf_op jit(solution)/shard_map/ppermute | solution.py:225
  59.7 0.7 collective-permute-start.6
  60.4 0.1 collective-permute-done.5.up.u1
  60.5 0.0 collective-permute-done.6.down.d1
  60.5 10.7 %all-to-all-done.2.parts = bf16[16,16,256]{2,1,0:T(8,128)(2,1)S(1)} async-done(((bf16[16,16,256]{2,1,0:T(8,128)(2,1)}), bf16[16,16,256]{2,1,0:T(8,128)(2,1)S(1)}, u32[]{:S(2)}, u32[]{:S(2)}) %all-to-all-start.2) | async-done | bytes 131104 | tf_op jit(solution)/shard_map/all_to_all | solution.py:252
  71.2 1.5 %shard_map.52 = (f32[8,256]{1,0:T(8,128)S(1)}, bf16[16,16,256]{2,1,0:T(8,128)(2,1)}) custom-call(s32[1]{0:T(128)} %bitcast.row_ref.plane_ref, bf16[16,16,256]{2,1,0:T(8,128)(2,1)S(1)} %all-to-all-done.2.parts, bf16[64,4096]{1,0:T(8,128)(2,1)S(1)} %bitcast.9, bf16[64,4096]{1,0:T(8,128)(2,1)S(1)} %collective-permute-done.c1, ...), custom_call_target="tpu_custom_call" | custom-call | tf_op jit(solution)/shard_map/pallas_call | solution.py:30
  72.6 5.6 %all-to-all-start.3 = ((bf16[16,16,256]{2,1,0:T(8,128)(2,1)}), bf16[16,16,256]{2,1,0:T(8,128)(2,1)S(1)}, u32[]{:S(2)}, u32[]{:S(2)}) async-start(bf16[16,16,256]{2,1,0:T(8,128)(2,1)} %get-tuple-element.26), calls=%async_computation.3 | async-start | bytes 262144 | tf_op jit(solution)/shard_map/all_to_all | solution.py:252
  78.2 1.9 %collective-permute-start.7 = (f32[8,256]{1,0:T(8,128)S(1)}, f32[8,256]{1,0:T(8,128)S(1)}, u32[]{:S(2)}, u32[]{:S(2)}) collective-permute-start(f32[8,256]{1,0:T(8,128)S(1)} %get-tuple-element.27.field.f2), channel_id=1, source_target_pairs={{0,64},{64,0},{128,192},{192,128},{256,320},{320,256},{384,448},{4... | collective-permute-start | bytes 24584 | tf_op jit(solution)/shard_map/ppermute | solution.py:225
  80.2 0.7 collective-permute-start.8
  80.8 0.5 collective-permute-done.7.up.u2
  81.3 0.0 collective-permute-done.8.down.d2
  81.3 11.7 %all-to-all-done.3.parts = bf16[16,16,256]{2,1,0:T(8,128)(2,1)S(1)} async-done(((bf16[16,16,256]{2,1,0:T(8,128)(2,1)}), bf16[16,16,256]{2,1,0:T(8,128)(2,1)S(1)}, u32[]{:S(2)}, u32[]{:S(2)}) %all-to-all-start.3) | async-done | bytes 131104 | tf_op jit(solution)/shard_map/all_to_all | solution.py:252
  93.0 0.8 shard_map.53
  93.8 17.3 %all_to_all.36.parts = bf16[16,8,256]{2,1,0:T(8,128)(2,1)S(1)} all-to-all(bf16[16,8,256]{2,1,0:T(8,128)(2,1)S(1)} %get-tuple-element.28), channel_id=1, replica_groups=mesh['x'=4,'c'=2,'z'=16,'y'=4] {'z'}, dimensions={0} | all-to-all | bytes 131072 | tf_op jit(solution)/shard_map/all_to_all | solution.py:260
  111.1 0.8 shard_map.54
  111.9 10.9 %all_to_all.37.packed = f32[8,8,640]{2,1,0:T(8,128)S(1)} all-to-all(f32[8,8,640]{2,1,0:T(8,128)S(1)} %shard_map.54), channel_id=1, replica_groups=mesh['x'=4,'c'=2,'z'=16,'y'=4] {'x','c'}, dimensions={0} | all-to-all | bytes 327680 | tf_op jit(solution)/shard_map/all_to_all | solution.py:266
  122.9 0.1 shard_map.55
  123.0 15.5 %all_to_all.38.tables = f32[16,8,128]{2,1,0:T(8,128)S(1)} all-to-all(f32[16,8,128]{2,1,0:T(8,128)S(1)} %get-tuple-element.30), channel_id=1, replica_groups=mesh['x'=4,'c'=2,'z'=16,'y'=4] {'z'}, dimensions={0} | all-to-all | bytes 131072 | tf_op jit(solution)/shard_map/all_to_all | solution.py:268
  138.5 1.1 shard_map.56
  (4 shorter events, 0.1 us)
Async XLA Ops:
  0.6 0.7 copy-start.2
  0.6 0.7 copy-start.1
  12.7 19.7 %collective-permute-start = (bf16[64,4096]{1,0:T(8,128)(2,1)}, bf16[64,4096]{1,0:T(8,128)(2,1)S(1)}, u32[]{:S(2)}, u32[]{:S(2)}) collective-permute-start(bf16[64,4096]{1,0:T(8,128)(2,1)} %bitcast.6), channel_id=1, source_target_pairs={{1,0},{2,1},{3,2},{0,3},{5,4},{6,5},{7,6},{4,7},{9,8},{10,9},{11,1... | collective-permute-start | bytes 1572872 | tf_op jit(solution)/shard_map/ppermute | solution.py:221
  15.1 19.5 %collective-permute-start.2 = (bf16[64,4096]{1,0:T(8,128)(2,1)}, bf16[64,4096]{1,0:T(8,128)(2,1)S(1)}, u32[]{:S(2)}, u32[]{:S(2)}) collective-permute-start(bf16[64,4096]{1,0:T(8,128)(2,1)} %bitcast.7), channel_id=1, source_target_pairs={{3,0},{0,1},{1,2},{2,3},{7,4},{4,5},{5,6},{6,7},{11,8},{8,9},{9,10... | collective-permute-start | bytes 1572872 | tf_op jit(solution)/shard_map/ppermute | solution.py:221
  20.7 25.7 %all-to-all-start.1 = ((bf16[16,16,256]{2,1,0:T(8,128)(2,1)}), bf16[16,16,256]{2,1,0:T(8,128)(2,1)S(1)}, u32[]{:S(2)}, u32[]{:S(2)}) async-start(bf16[16,16,256]{2,1,0:T(8,128)(2,1)} %get-tuple-element.19), calls=%async_computation.1 | async-start | bytes 262144 | tf_op jit(solution)/shard_map/all_to_all | solution.py:252
  32.4 14.0 %copy-start = (bf16[1,64,4096]{2,1,0:T(8,128)(2,1)S(1)}, bf16[1,64,4096]{2,1,0:T(8,128)(2,1)}, u32[]{:S(2)}) copy-start(bf16[1,64,4096]{2,1,0:T(8,128)(2,1)} %param.4) | copy-start | bytes 1572868
  32.5 14.0 %collective-permute-start.1 = (bf16[32,4096]{1,0:T(8,128)(2,1)S(1)}, bf16[32,4096]{1,0:T(8,128)(2,1)S(1)}, u32[]{:S(2)}, u32[]{:S(2)}) collective-permute-start(bf16[32,4096]{1,0:T(8,128)(2,1)S(1)} %slice.8), channel_id=1, source_target_pairs={{1,0},{2,1},{3,2},{0,3},{5,4},{6,5},{7,6},{4,7},{9,8},{10,9},{11,1... | collective-permute-start | bytes 786440 | tf_op jit(solution)/shard_map/ppermute | solution.py:221
  34.5 11.9 %collective-permute-start.3 = (bf16[32,4096]{1,0:T(8,128)(2,1)S(1)}, bf16[32,4096]{1,0:T(8,128)(2,1)S(1)}, u32[]{:S(2)}, u32[]{:S(2)}) collective-permute-start(bf16[32,4096]{1,0:T(8,128)(2,1)S(1)} %slice.9), channel_id=1, source_target_pairs={{3,0},{0,1},{1,2},{2,3},{7,4},{4,5},{5,6},{6,7},{11,8},{8,9},{9,10... | collective-permute-start | bytes 786440 | tf_op jit(solution)/shard_map/ppermute | solution.py:221
  39.7 0.7 collective-permute-start.4
  47.9 23.3 %all-to-all-start.2 = ((bf16[16,16,256]{2,1,0:T(8,128)(2,1)}), bf16[16,16,256]{2,1,0:T(8,128)(2,1)S(1)}, u32[]{:S(2)}, u32[]{:S(2)}) async-start(bf16[16,16,256]{2,1,0:T(8,128)(2,1)} %get-tuple-element.24), calls=%async_computation.2 | async-start | bytes 262144 | tf_op jit(solution)/shard_map/all_to_all | solution.py:252
  57.3 3.2 %collective-permute-start.5 = (f32[8,256]{1,0:T(8,128)S(1)}, f32[8,256]{1,0:T(8,128)S(1)}, u32[]{:S(2)}, u32[]{:S(2)}) collective-permute-start(f32[8,256]{1,0:T(8,128)S(1)} %get-tuple-element.25.field.rest_0_.f1), channel_id=1, source_target_pairs={{0,64},{64,0},{128,192},{192,128},{256,320},{320,256},{384,448},{4... | collective-permute-start | bytes 24584 | tf_op jit(solution)/shard_map/ppermute | solution.py:225
  59.7 0.8 collective-permute-start.6
  72.6 20.4 %all-to-all-start.3 = ((bf16[16,16,256]{2,1,0:T(8,128)(2,1)}), bf16[16,16,256]{2,1,0:T(8,128)(2,1)S(1)}, u32[]{:S(2)}, u32[]{:S(2)}) async-start(bf16[16,16,256]{2,1,0:T(8,128)(2,1)} %get-tuple-element.26), calls=%async_computation.3 | async-start | bytes 262144 | tf_op jit(solution)/shard_map/all_to_all | solution.py:252
  78.2 3.1 %collective-permute-start.7 = (f32[8,256]{1,0:T(8,128)S(1)}, f32[8,256]{1,0:T(8,128)S(1)}, u32[]{:S(2)}, u32[]{:S(2)}) collective-permute-start(f32[8,256]{1,0:T(8,128)S(1)} %get-tuple-element.27.field.f2), channel_id=1, source_target_pairs={{0,64},{64,0},{128,192},{192,128},{256,320},{320,256},{384,448},{4... | collective-permute-start | bytes 24584 | tf_op jit(solution)/shard_map/ppermute | solution.py:225
  80.2 1.1 collective-permute-start.8

commit v9 on v8

--- a/solution.py
+++ b/solution.py
@@ -19,9 +19,10 @@
 BF16 = jnp.bfloat16
 
 
-def call(body, outs, *args, smem=0, keep=True):
+def call(body, outs, *args, smem=0, loose=(), keep=True):
     args = args[:smem] + tuple(
-        pltpu.with_memory_space_constraint(x, pltpu.VMEM) for x in args[smem:]
+        x if i in loose else pltpu.with_memory_space_constraint(x, pltpu.VMEM)
+        for i, x in enumerate(args[smem:])
     )
     if keep:
         outs = jax.tree.map(lambda o: pltpu.VMEM(o.shape, o.dtype), outs)
@@ -36,8 +37,15 @@
     )(*args)
 
 
+def reorder(field, row):
+    lane = lax.broadcasted_iota(jnp.int32, field.shape, 1)
+    pairs = jnp.where(lane % (2 * H) < H, pltpu.roll(field, W - H, 1), pltpu.roll(field, H, 1))
+    field = jnp.where(row % 2 == 1, pairs, field)
+    return jnp.where(row >= 2, pltpu.roll(field, 2 * H, 1), field)
+
+
 def store_parts(send, field, row):
-    turned = pltpu.roll(field, row * H, 1)
+    turned = reorder(field, row)
     parts = turned.astype(BF16)
     if send.shape[1] > B:
         low = (turned - parts.astype(F32)).astype(BF16)
@@ -51,8 +59,9 @@
     core = row_ref[0] // NY % NC
 
     def wide(which, columns):
-        joined = jnp.concatenate([packed[which * NY + y][:, columns] for y in range(NY)], axis=1)
-        return pltpu.roll(joined, (NY - row) % NY * H, 1)
+        return reorder(
+            jnp.concatenate([packed[which * NY + y][:, columns] for y in range(NY)], axis=1), row
+        )
 
     field = wide(core, slice(0, H))
     field_out[...] = field
@@ -84,16 +93,16 @@
     return total * (1.0 / SCALE)
 
 
-def step(row_ref, parts, c0, c1, c2, c3, c4, diag, up, down, field, *rest):
+def step(row_ref, parts, c0, c1, c2, c3, diag, up, down, field, *rest):
     *previous, field_out, send = rest
     previous = previous[0] if previous else None
-    out = next_field(parts, (c0, c1, c2, c3, c4), field, previous, diag, up[...] + down[...])
+    out = next_field(parts, (c0, c1, c2, c3), field, previous, diag, up[...] + down[...])
     field_out[...] = out
     store_parts(send, out, row_ref[0] % NY)
 
 
-def last_step(parts, c0, c1, c2, c3, c4, field, diag, f0, f1, f2, u0, d0, u1, d1, u2, d2, send):
-    partial = next_field(parts, (c0, c1, c2, c3, c4), field, f2, diag, None)
+def last_step(parts, c0, c1, c2, c3, field, diag, f0, f1, f2, u0, d0, u1, d1, u2, d2, send):
+    partial = next_field(parts, (c0, c1, c2, c3), field, f2, diag, None)
     f3 = field[...]
     fields = [f0[...], f1[...], f2[...], f3]
     beside = [u0[...] + d0[...], u1[...] + d1[...], u2[...] + d2[...]]
@@ -217,8 +226,8 @@
     residual_out[...] = combine(residual)
 
 
-def shifted(array, shift):
-    return lax.ppermute(array, "y", [((y + shift) % NY, y) for y in range(NY)])
+def swapped(array, mask):
+    return lax.ppermute(array, "y", [(y, y ^ mask) for y in range(NY)])
 
 
 def even(field):
@@ -236,9 +245,9 @@
     packed = jnp.concatenate([source[0], jnp.broadcast_to(diagonal, (B, H))], axis=1)
     packed = jnp.broadcast_to(packed[None], (NC * NY, B, 128))
     packed = lax.all_to_all(packed, ("c", "y"), 0, 0, tiled=True)
-    own, packed = lax.optimization_barrier((own, packed))
-    after, before = shifted(own, 1), shifted(own, -1)
-    blocks = [own, after, shifted(after[: H // 2], 1), shifted(before[H // 2 :], -1), before]
+    by_1, by_3 = swapped(own, 1), swapped(own, 3)
+    by_1, packed = lax.optimization_barrier((by_1, packed))
+    blocks = [own, by_1, swapped(by_1, 3), by_3]
     shape = jax.ShapeDtypeStruct
     wide = shape((B, W), F32)
     sends = [shape((NZ, 2 * B if low else B, W), BF16) for low in WITH_LOW]
@@ -255,6 +264,7 @@
             (wide, sends[k + 1]),
             row, parts, *blocks, diag, up, down, *fields[::-1][:2],
             smem=1,
+            loose=(1,) if k == 0 else (),
         )
         fields.append(field)
     parts = lax.all_to_all(send, "z", 0, 0, tiled=True)

time: 142 us -> 139 us (0.979); the launches traced: 140 us -> 138 us
  blocking collectives: 55.1 us -> 43.1 us
  waiting for transfers between devices: 29 us -> 34 us
  starting transfers between devices: 47.2 us -> 51.4 us
  local copies, waits for them, and re-layouts: 0.77 us -> 2.41 us
    all_to_all x1 -> x0, blocking collectives: 11.3 us -> none  [on_device(): packed = lax.all_to_all(packed, ('c', 'y'), 0, 0, tiled=True)]
    all_to_all x0 -> x1, starting transfers between devices: none -> 8.15 us  [on_device(): packed = lax.all_to_all(packed, ('c', 'y'), 0, 0, tiled=True)]
    ppermute x4 -> x3, starting transfers between devices: 14.2 us -> 8.6 us  [swapped(): return lax.ppermute(array, 'y', [(y, y ^ mask) for y in range(NY)])]
    ppermute x2, starting transfers between devices: 4.33 us -> 9.52 us  [even(): return lax.ppermute(field, ('x', 'c'), [(i, i ^ 1) for i in range(NX * NC)])]
    all_to_all x3, starting transfers between devices: 26.7 us -> 23.2 us  [on_device(): parts = lax.all_to_all(send, 'z', 0, 0, tiled=True)]
    all_to_all x0 -> x1, waiting for transfers between devices: none -> 2.53 us  [on_device(): packed = lax.all_to_all(packed, ('c', 'y'), 0, 0, tiled=True)]
    all_to_all x3, waiting for transfers between devices: 28.4 us -> 29.9 us  [on_device(): parts = lax.all_to_all(send, 'z', 0, 0, tiled=True)]
  transfers between devices with their start and end apart: 12 -> 12, of which waited for: 5 -> 6; matrix products, arithmetic and copies ran while one was open for 0% -> 1% of each run, Pallas kernels for 1% -> 1%
where the time goes in v9:
time: 139 us; the launch traced here: 138 us
  starting transfers between devices  51.4 us (37%)
  blocking collectives  43.1 us (31%)
  waiting for transfers between devices  34 us (24%)
  Pallas kernels  6.59 us (5%)
  local copies, waits for them, and re-layouts  2.41 us (2%)
    all_to_all x3, waiting for transfers between devices, on_device(): parts = lax.all_to_all(send, 'z', 0, 0, tiled=True)  29.9 us
    all_to_all x3, starting transfers between devices, on_device(): parts = lax.all_to_all(send, 'z', 0, 0, tiled=True)  23.2 us
    all_to_all x1, blocking collectives, on_device(): parts = lax.all_to_all(send, 'z', 0, 0, tiled=True)  17.2 us
    all_to_all x1, blocking collectives, on_device(): table = lax.all_to_all(table, 'z', 0, 0, tiled=True)  15.6 us
    all_to_all x1, blocking collectives, on_device(): packed = lax.all_to_all(packed, ('x', 'c'), 0, 0, tiled=True)  10.3 us
    ppermute x2, starting transfers between devices, even(): return lax.ppermute(field, ('x', 'c'), [(i, i ^ 1) for i in range(NX * NC)])  9.52 us
    ppermute x3, starting transfers between devices, swapped(): return lax.ppermute(array, 'y', [(y, y ^ mask) for y in range(NY)])  8.6 us
    all_to_all x1, starting transfers between devices, on_device(): packed = lax.all_to_all(packed, ('c', 'y'), 0, 0, tiled=True)  8.15 us
  transfers between devices with their start and end apart: 12, of which 6 were waited for; matrix products, arithmetic and copies ran while one was open for 1% of the time, Pallas kernels for 1%

profile of v9, /device:TPU:24, one launch (start us, length us, event | category | flops | bytes accessed | tf_op | source)
XLA Modules:
  0.0 138.3 jit_solution(14587522142413239097)
XLA Ops:
  0.6 0.0 copy-start.2
  0.6 2.7 %collective-permute-start = (bf16[64,4096]{1,0:T(8,128)(2,1)}, bf16[64,4096]{1,0:T(8,128)(2,1)S(1)}, u32[]{:S(2)}, u32[]{:S(2)}) collective-permute-start(bf16[64,4096]{1,0:T(8,128)(2,1)} %bitcast.6), channel_id=1, source_target_pairs={{0,1},{1,0},{2,3},{3,2},{4,5},{5,4},{6,7},{7,6},{8,9},{9,8},{10,11... | collective-permute-start | bytes 1572872 | tf_op jit(solution)/shard_map/ppermute | solution.py:230
  3.3 0.7 pad.1.clone
  4.0 0.0 copy-done.2
  4.0 0.6 broadcast_in_dim.21
  4.7 8.2 %all-to-all-start = ((f32[8,8,128]{2,1,0:T(8,128)}), f32[8,8,128]{2,1,0:T(8,128)S(1)}, u32[]{:S(2)}, u32[]{:S(2)}) async-start(f32[8,8,128]{2,1,0:T(8,128)} %broadcast_in_dim.21), calls=%async_computation | async-start | bytes 65536 | tf_op jit(solution)/shard_map/all_to_all | solution.py:247
  12.8 2.0 %collective-permute-start.2 = (bf16[64,4096]{1,0:T(8,128)(2,1)}, bf16[64,4096]{1,0:T(8,128)(2,1)S(1)}, u32[]{:S(2)}, u32[]{:S(2)}) collective-permute-start(bf16[64,4096]{1,0:T(8,128)(2,1)} %bitcast.7), channel_id=1, source_target_pairs={{0,3},{1,2},{2,1},{3,0},{4,7},{5,6},{6,5},{7,4},{8,11},{9,10},{10,... | collective-permute-start | bytes 1572872 | tf_op jit(solution)/shard_map/ppermute | solution.py:230
  14.8 2.5 %all-to-all-done.packed = f32[8,8,128]{2,1,0:T(8,128)S(1)} async-done(((f32[8,8,128]{2,1,0:T(8,128)}), f32[8,8,128]{2,1,0:T(8,128)S(1)}, u32[]{:S(2)}, u32[]{:S(2)}) %all-to-all-start) | async-done | bytes 32800 | tf_op jit(solution)/shard_map/all_to_all | solution.py:247
  17.3 0.0 collective-permute-done.c1
  17.3 4.0 %collective-permute-start.1 = (bf16[64,4096]{1,0:T(8,128)(2,1)S(1)}, bf16[64,4096]{1,0:T(8,128)(2,1)S(1)}, u32[]{:S(2)}, u32[]{:S(2)}) collective-permute-start(bf16[64,4096]{1,0:T(8,128)(2,1)S(1)} %collective-permute-done.c1), channel_id=1, source_target_pairs={{0,3},{1,2},{2,1},{3,0},{4,7},{5,6},{6,5},{7,4},{8,11},{9,10},{10,... | collective-permute-start | bytes 1572872 | tf_op jit(solution)/shard_map/ppermute | solution.py:230
  21.3 0.9 shard_map.50
  22.2 15.2 %all-to-all-start.1 = ((bf16[16,16,256]{2,1,0:T(8,128)(2,1)}), bf16[16,16,256]{2,1,0:T(8,128)(2,1)S(1)}, u32[]{:S(2)}, u32[]{:S(2)}) async-start(bf16[16,16,256]{2,1,0:T(8,128)(2,1)} %get-tuple-element.19), calls=%async_computation.1 | async-start | bytes 262144 | tf_op jit(solution)/shard_map/all_to_all | solution.py:261
  37.4 0.7 collective-permute-start.3
  38.1 0.0 collective-permute-done.2.c3
  38.1 0.0 collective-permute-done.3.down.d0
  38.1 14.0 %all-to-all-done.1.parts = bf16[16,16,256]{2,1,0:T(8,128)(2,1)S(1)} async-done(((bf16[16,16,256]{2,1,0:T(8,128)(2,1)}), bf16[16,16,256]{2,1,0:T(8,128)(2,1)S(1)}, u32[]{:S(2)}, u32[]{:S(2)}) %all-to-all-start.1) | async-done | bytes 131104 | tf_op jit(solution)/shard_map/all_to_all | solution.py:261
  52.1 0.0 collective-permute-done.1.c2
  52.1 0.0 copy-start
  52.1 1.0 copy-done
  53.1 0.0 copy-start.1
  53.1 1.5 %shard_map.51 = (f32[8,256]{1,0:T(8,128)S(1)}, bf16[16,16,256]{2,1,0:T(8,128)(2,1)}) custom-call(s32[1]{0:T(128)} %bitcast.row_ref.plane_ref, bf16[16,16,256]{2,1,0:T(8,128)(2,1)S(1)} %all-to-all-done.1.parts, bf16[64,4096]{1,0:T(8,128)(2,1)S(1)} %bitcast.8, bf16[64,4096]{1,0:T(8,128)(2,1)S(1)} %collective-permute-done.c1, ...), custom_call_target="tpu_custom_call" | custom-call | tf_op jit(solution)/shard_map/pallas_call | solution.py:31
  54.6 3.7 %all-to-all-start.2 = ((bf16[16,16,256]{2,1,0:T(8,128)(2,1)}), bf16[16,16,256]{2,1,0:T(8,128)(2,1)S(1)}, u32[]{:S(2)}, u32[]{:S(2)}) async-start(bf16[16,16,256]{2,1,0:T(8,128)(2,1)} %get-tuple-element.24), calls=%async_computation.2 | async-start | bytes 262144 | tf_op jit(solution)/shard_map/all_to_all | solution.py:261
  58.4 0.7 collective-permute-start.5
  59.0 4.8 %collective-permute-start.4 = (f32[8,256]{1,0:T(8,128)S(1)}, f32[8,256]{1,0:T(8,128)S(1)}, u32[]{:S(2)}, u32[]{:S(2)}) collective-permute-start(f32[8,256]{1,0:T(8,128)S(1)} %get-tuple-element.25.field.rest_0_.f1), channel_id=1, source_target_pairs={{0,64},{64,0},{128,192},{192,128},{256,320},{320,256},{384,448},{4... | collective-permute-start | bytes 24584 | tf_op jit(solution)/shard_map/ppermute | solution.py:234
  63.8 0.0 collective-permute-done.5.down.d1
  63.8 0.8 collective-permute-done.4.up.u1
  64.6 7.8 %all-to-all-done.2.parts = bf16[16,16,256]{2,1,0:T(8,128)(2,1)S(1)} async-done(((bf16[16,16,256]{2,1,0:T(8,128)(2,1)}), bf16[16,16,256]{2,1,0:T(8,128)(2,1)S(1)}, u32[]{:S(2)}, u32[]{:S(2)}) %all-to-all-start.2) | async-done | bytes 131104 | tf_op jit(solution)/shard_map/all_to_all | solution.py:261
  72.4 0.0 copy-done.1
  72.4 1.5 %shard_map.52 = (f32[8,256]{1,0:T(8,128)S(1)}, bf16[16,16,256]{2,1,0:T(8,128)(2,1)}) custom-call(s32[1]{0:T(128)} %bitcast.row_ref.plane_ref, bf16[16,16,256]{2,1,0:T(8,128)(2,1)S(1)} %all-to-all-done.2.parts, bf16[64,4096]{1,0:T(8,128)(2,1)S(1)} %bitcast.9, bf16[64,4096]{1,0:T(8,128)(2,1)S(1)} %collective-permute-done.c1, ...), custom_call_target="tpu_custom_call" | custom-call | tf_op jit(solution)/shard_map/pallas_call | solution.py:31
  73.8 4.3 %all-to-all-start.3 = ((bf16[16,16,256]{2,1,0:T(8,128)(2,1)}), bf16[16,16,256]{2,1,0:T(8,128)(2,1)S(1)}, u32[]{:S(2)}, u32[]{:S(2)}) async-start(bf16[16,16,256]{2,1,0:T(8,128)(2,1)} %get-tuple-element.26), calls=%async_computation.3 | async-start | bytes 262144 | tf_op jit(solution)/shard_map/all_to_all | solution.py:261
  78.1 0.7 collective-permute-start.7
  78.8 4.8 %collective-permute-start.6 = (f32[8,256]{1,0:T(8,128)S(1)}, f32[8,256]{1,0:T(8,128)S(1)}, u32[]{:S(2)}, u32[]{:S(2)}) collective-permute-start(f32[8,256]{1,0:T(8,128)S(1)} %get-tuple-element.27.field.f2), channel_id=1, source_target_pairs={{0,64},{64,0},{128,192},{192,128},{256,320},{320,256},{384,448},{4... | collective-permute-start | bytes 24584 | tf_op jit(solution)/shard_map/ppermute | solution.py:234
  83.5 0.0 collective-permute-done.7.down.d2
  83.5 0.8 collective-permute-done.6.up.u2
  84.3 8.1 %all-to-all-done.3.parts = bf16[16,16,256]{2,1,0:T(8,128)(2,1)S(1)} async-done(((bf16[16,16,256]{2,1,0:T(8,128)(2,1)}), bf16[16,16,256]{2,1,0:T(8,128)(2,1)S(1)}, u32[]{:S(2)}, u32[]{:S(2)}) %all-to-all-start.3) | async-done | bytes 131104 | tf_op jit(solution)/shard_map/all_to_all | solution.py:261
  92.5 0.8 shard_map.53
  93.3 17.2 %all_to_all.35.parts = bf16[16,8,256]{2,1,0:T(8,128)(2,1)S(1)} all-to-all(bf16[16,8,256]{2,1,0:T(8,128)(2,1)S(1)} %get-tuple-element.28), channel_id=1, replica_groups=mesh['x'=4,'c'=2,'z'=16,'y'=4] {'z'}, dimensions={0} | all-to-all | bytes 131072 | tf_op jit(solution)/shard_map/all_to_all | solution.py:270
  110.5 0.8 shard_map.54
  111.3 10.3 %all_to_all.36.packed = f32[8,8,640]{2,1,0:T(8,128)S(1)} all-to-all(f32[8,8,640]{2,1,0:T(8,128)S(1)} %shard_map.54), channel_id=1, replica_groups=mesh['x'=4,'c'=2,'z'=16,'y'=4] {'x','c'}, dimensions={0} | all-to-all | bytes 327680 | tf_op jit(solution)/shard_map/all_to_all | solution.py:276
  121.6 0.1 shard_map.55
  121.7 15.6 %all_to_all.37.tables = f32[16,8,128]{2,1,0:T(8,128)S(1)} all-to-all(f32[16,8,128]{2,1,0:T(8,128)S(1)} %get-tuple-element.30), channel_id=1, replica_groups=mesh['x'=4,'c'=2,'z'=16,'y'=4] {'z'}, dimensions={0} | all-to-all | bytes 131072 | tf_op jit(solution)/shard_map/all_to_all | solution.py:278
  137.2 1.1 shard_map.56
  (1 shorter events, 0.0 us)
Async XLA Ops:
  0.6 3.4 %copy-start.2 = (f32[1,8,64]{2,1,0:T(8,128)S(1)}, f32[1,8,64]{2,1,0:T(8,128)}, u32[]{:S(2)}) copy-start(f32[1,8,64]{2,1,0:T(8,128)} %param.3) | copy-start | bytes 6148
  0.6 16.7 %collective-permute-start = (bf16[64,4096]{1,0:T(8,128)(2,1)}, bf16[64,4096]{1,0:T(8,128)(2,1)S(1)}, u32[]{:S(2)}, u32[]{:S(2)}) collective-permute-start(bf16[64,4096]{1,0:T(8,128)(2,1)} %bitcast.6), channel_id=1, source_target_pairs={{0,1},{1,0},{2,3},{3,2},{4,5},{5,4},{6,7},{7,6},{8,9},{9,8},{10,11... | collective-permute-start | bytes 1572872 | tf_op jit(solution)/shard_map/ppermute | solution.py:230
  4.7 12.6 %all-to-all-start = ((f32[8,8,128]{2,1,0:T(8,128)}), f32[8,8,128]{2,1,0:T(8,128)S(1)}, u32[]{:S(2)}, u32[]{:S(2)}) async-start(f32[8,8,128]{2,1,0:T(8,128)} %broadcast_in_dim.21), calls=%async_computation | async-start | bytes 65536 | tf_op jit(solution)/shard_map/all_to_all | solution.py:247
  12.8 25.3 %collective-permute-start.2 = (bf16[64,4096]{1,0:T(8,128)(2,1)}, bf16[64,4096]{1,0:T(8,128)(2,1)S(1)}, u32[]{:S(2)}, u32[]{:S(2)}) collective-permute-start(bf16[64,4096]{1,0:T(8,128)(2,1)} %bitcast.7), channel_id=1, source_target_pairs={{0,3},{1,2},{2,1},{3,0},{4,7},{5,6},{6,5},{7,4},{8,11},{9,10},{10,... | collective-permute-start | bytes 1572872 | tf_op jit(solution)/shard_map/ppermute | solution.py:230
  17.3 34.8 %collective-permute-start.1 = (bf16[64,4096]{1,0:T(8,128)(2,1)S(1)}, bf16[64,4096]{1,0:T(8,128)(2,1)S(1)}, u32[]{:S(2)}, u32[]{:S(2)}) collective-permute-start(bf16[64,4096]{1,0:T(8,128)(2,1)S(1)} %collective-permute-done.c1), channel_id=1, source_target_pairs={{0,3},{1,2},{2,1},{3,0},{4,7},{5,6},{6,5},{7,4},{8,11},{9,10},{10,... | collective-permute-start | bytes 1572872 | tf_op jit(solution)/shard_map/ppermute | solution.py:230
  22.2 29.9 %all-to-all-start.1 = ((bf16[16,16,256]{2,1,0:T(8,128)(2,1)}), bf16[16,16,256]{2,1,0:T(8,128)(2,1)S(1)}, u32[]{:S(2)}, u32[]{:S(2)}) async-start(bf16[16,16,256]{2,1,0:T(8,128)(2,1)} %get-tuple-element.19), calls=%async_computation.1 | async-start | bytes 262144 | tf_op jit(solution)/shard_map/all_to_all | solution.py:261
  37.4 0.7 collective-permute-start.3
  52.1 1.0 copy-start
  53.1 19.2 %copy-start.1 = (bf16[1,64,4096]{2,1,0:T(8,128)(2,1)S(1)}, bf16[1,64,4096]{2,1,0:T(8,128)(2,1)}, u32[]{:S(2)}) copy-start(bf16[1,64,4096]{2,1,0:T(8,128)(2,1)} %param.4) | copy-start | bytes 1572868
  54.6 17.7 %all-to-all-start.2 = ((bf16[16,16,256]{2,1,0:T(8,128)(2,1)}), bf16[16,16,256]{2,1,0:T(8,128)(2,1)S(1)}, u32[]{:S(2)}, u32[]{:S(2)}) async-start(bf16[16,16,256]{2,1,0:T(8,128)(2,1)} %get-tuple-element.24), calls=%async_computation.2 | async-start | bytes 262144 | tf_op jit(solution)/shard_map/all_to_all | solution.py:261
  58.4 5.4 %collective-permute-start.5 = (f32[8,256]{1,0:T(8,128)S(1)}, f32[8,256]{1,0:T(8,128)S(1)}, u32[]{:S(2)}, u32[]{:S(2)}) collective-permute-start(f32[8,256]{1,0:T(8,128)S(1)} %get-tuple-element.25.field.rest_0_.f1), channel_id=1, source_target_pairs={{64,128},{192,256},{320,384},{128,64},{256,192},{384,320},{65,129}... | collective-permute-start | bytes 24584 | tf_op jit(solution)/shard_map/ppermute | solution.py:239
  59.0 5.6 %collective-permute-start.4 = (f32[8,256]{1,0:T(8,128)S(1)}, f32[8,256]{1,0:T(8,128)S(1)}, u32[]{:S(2)}, u32[]{:S(2)}) collective-permute-start(f32[8,256]{1,0:T(8,128)S(1)} %get-tuple-element.25.field.rest_0_.f1), channel_id=1, source_target_pairs={{0,64},{64,0},{128,192},{192,128},{256,320},{320,256},{384,448},{4... | collective-permute-start | bytes 24584 | tf_op jit(solution)/shard_map/ppermute | solution.py:234
  73.8 18.7 %all-to-all-start.3 = ((bf16[16,16,256]{2,1,0:T(8,128)(2,1)}), bf16[16,16,256]{2,1,0:T(8,128)(2,1)S(1)}, u32[]{:S(2)}, u32[]{:S(2)}) async-start(bf16[16,16,256]{2,1,0:T(8,128)(2,1)} %get-tuple-element.26), calls=%async_computation.3 | async-start | bytes 262144 | tf_op jit(solution)/shard_map/all_to_all | solution.py:261
  78.1 5.4 %collective-permute-start.7 = (f32[8,256]{1,0:T(8,128)S(1)}, f32[8,256]{1,0:T(8,128)S(1)}, u32[]{:S(2)}, u32[]{:S(2)}) collective-permute-start(f32[8,256]{1,0:T(8,128)S(1)} %get-tuple-element.27.field.f2), channel_id=1, source_target_pairs={{64,128},{192,256},{320,384},{128,64},{256,192},{384,320},{65,129}... | collective-permute-start | bytes 24584 | tf_op jit(solution)/shard_map/ppermute | solution.py:239
  78.8 5.6 %collective-permute-start.6 = (f32[8,256]{1,0:T(8,128)S(1)}, f32[8,256]{1,0:T(8,128)S(1)}, u32[]{:S(2)}, u32[]{:S(2)}) collective-permute-start(f32[8,256]{1,0:T(8,128)S(1)} %get-tuple-element.27.field.f2), channel_id=1, source_target_pairs={{0,64},{64,0},{128,192},{192,128},{256,320},{320,256},{384,448},{4... | collective-permute-start | bytes 24584 | tf_op jit(solution)/shard_map/ppermute | solution.py:234

commit v10 on v9

--- a/solution.py
+++ b/solution.py
@@ -19,10 +19,9 @@
 BF16 = jnp.bfloat16
 
 
-def call(body, outs, *args, smem=0, loose=(), keep=True):
+def call(body, outs, *args, smem=0, keep=True, aliases={}):
     args = args[:smem] + tuple(
-        x if i in loose else pltpu.with_memory_space_constraint(x, pltpu.VMEM)
-        for i, x in enumerate(args[smem:])
+        pltpu.with_memory_space_constraint(x, pltpu.VMEM) for x in args[smem:]
     )
     if keep:
         outs = jax.tree.map(lambda o: pltpu.VMEM(o.shape, o.dtype), outs)
@@ -32,6 +31,7 @@
         body,
         out_shape=outs,
         in_specs=specs,
+        input_output_aliases=aliases,
         compiler_params=pltpu.CompilerParams(vmem_limit_bytes=8 << 20),
         out_specs=jax.tree.map(lambda _: pl.BlockSpec(memory_space=pltpu.VMEM), outs),
     )(*args)
@@ -54,7 +54,7 @@
         send[z] = parts
 
 
-def unpack(row_ref, packed, field_out, even_out, diag_out, send):
+def unpack(row_ref, packed, own, field_out, even_out, diag_out, send, own_out):
     row = row_ref[0] % NY
     core = row_ref[0] // NY % NC
 
@@ -247,11 +247,18 @@
     packed = lax.all_to_all(packed, ("c", "y"), 0, 0, tiled=True)
     by_1, by_3 = swapped(own, 1), swapped(own, 3)
     by_1, packed = lax.optimization_barrier((by_1, packed))
-    blocks = [own, by_1, swapped(by_1, 3), by_3]
+    by_2 = swapped(by_1, 3)
     shape = jax.ShapeDtypeStruct
     wide = shape((B, W), F32)
     sends = [shape((NZ, 2 * B if low else B, W), BF16) for low in WITH_LOW]
-    field, up, diag, send = call(unpack, (wide, wide, wide, sends[0]), row, packed, smem=1)
+    field, up, diag, send, own = call(
+        unpack,
+        (wide, wide, wide, sends[0], shape((H, NZ * W), BF16)),
+        row, packed, own,
+        smem=1,
+        aliases={2: 4},
+    )
+    blocks = [own, by_1, by_2, by_3]
     fields, beside = [field], []
     for k in range(STEPS - 1):
         down = odd(field)
@@ -264,7 +271,6 @@
             (wide, sends[k + 1]),
             row, parts, *blocks, diag, up, down, *fields[::-1][:2],
             smem=1,
-            loose=(1,) if k == 0 else (),
         )
         fields.append(field)
     parts = lax.all_to_all(send, "z", 0, 0, tiled=True)

time: 139 us -> 142 us (1.022)
  blocking collectives: 43.1 us -> 53 us
  starting transfers between devices: 51.4 us -> 47.2 us
  waiting for transfers between devices: 34 us -> 31.6 us
    all_to_all x0 -> x1, blocking collectives: none -> 9.96 us  [on_device(): packed = lax.all_to_all(packed, ('c', 'y'), 0, 0, tiled=True)]
    all_to_all x1 -> x0, starting transfers between devices: 8.15 us -> none  [on_device(): packed = lax.all_to_all(packed, ('c', 'y'), 0, 0, tiled=True)]
    ppermute x3, starting transfers between devices: 8.6 us -> 12.5 us  [swapped(): return lax.ppermute(array, 'y', [(y, y ^ mask) for y in range(NY)])]
    all_to_all x1 -> x0, waiting for transfers between devices: 2.53 us -> none  [on_device(): packed = lax.all_to_all(packed, ('c', 'y'), 0, 0, tiled=True)]
  transfers between devices with their start and end apart: 12 -> 11, of which waited for: 6 -> 5; matrix products, arithmetic and copies ran while one was open for 1% -> 0% of each run, Pallas kernels for 1% -> 1%
where the time goes in v10:
time: 142 us; the launch traced here: 140 us
  blocking collectives  53 us (37%)
  starting transfers between devices  47.2 us (33%)
  waiting for transfers between devices  31.6 us (22%)
  Pallas kernels  6.59 us (5%)
    all_to_all x3, waiting for transfers between devices, on_device(): parts = lax.all_to_all(send, 'z', 0, 0, tiled=True)  29.9 us
    all_to_all x3, starting transfers between devices, on_device(): parts = lax.all_to_all(send, 'z', 0, 0, tiled=True)  23.3 us
    all_to_all x1, blocking collectives, on_device(): parts = lax.all_to_all(send, 'z', 0, 0, tiled=True)  17.2 us
    all_to_all x1, blocking collectives, on_device(): table = lax.all_to_all(table, 'z', 0, 0, tiled=True)  15.6 us
    ppermute x3, starting transfers between devices, swapped(): return lax.ppermute(array, 'y', [(y, y ^ mask) for y in range(NY)])  12.5 us
    all_to_all x1, blocking collectives, on_device(): packed = lax.all_to_all(packed, ('x', 'c'), 0, 0, tiled=True)  10.3 us
    all_to_all x1, blocking collectives, on_device(): packed = lax.all_to_all(packed, ('c', 'y'), 0, 0, tiled=True)  9.96 us
    ppermute x2, starting transfers between devices, even(): return lax.ppermute(field, ('x', 'c'), [(i, i ^ 1) for i in range(NX * NC)])  9.52 us
  transfers between devices with their start and end apart: 11, of which 5 were waited for; matrix products, arithmetic and copies ran while one was open for 0% of the time, Pallas kernels for 1%

profile of v10, /device:TPU:24, one launch (start us, length us, event | category | flops | bytes accessed | tf_op | source)
XLA Modules:
  0.0 140.3 jit_solution(4845417980445869003)
XLA Ops:
  0.6 0.0 copy-start.1
  0.6 1.0 copy.8
  1.7 0.0 copy-start
  1.7 2.8 %collective-permute-start = (bf16[64,4096]{1,0:T(8,128)(2,1)S(1)}, bf16[64,4096]{1,0:T(8,128)(2,1)S(1)}, u32[]{:S(2)}, u32[]{:S(2)}) collective-permute-start(bf16[64,4096]{1,0:T(8,128)(2,1)S(1)} %bitcast.6), channel_id=1, source_target_pairs={{0,1},{1,0},{2,3},{3,2},{4,5},{5,4},{6,7},{7,6},{8,9},{9,8},{10,11... | collective-permute-start | bytes 1572872 | tf_op jit(solution)/shard_map/ppermute | solution.py:230
  4.5 6.8 %collective-permute-start.2 = (bf16[64,4096]{1,0:T(8,128)(2,1)S(1)}, bf16[64,4096]{1,0:T(8,128)(2,1)S(1)}, u32[]{:S(2)}, u32[]{:S(2)}) collective-permute-start(bf16[64,4096]{1,0:T(8,128)(2,1)S(1)} %bitcast.7), channel_id=1, source_target_pairs={{0,3},{1,2},{2,1},{3,0},{4,7},{5,6},{6,5},{7,4},{8,11},{9,10},{10,... | collective-permute-start | bytes 1572872 | tf_op jit(solution)/shard_map/ppermute | solution.py:230
  11.3 0.0 copy-done.1
  11.3 0.1 pad.1.clone
  11.3 0.0 copy-done
  11.4 10.0 %all_to_all.35.packed = f32[8,8,128]{2,1,0:T(8,128)S(1)} all-to-all(f32[8,8,128]{2,1,0:T(8,128)S(1)} %broadcast_in_dim.21), channel_id=1, replica_groups=mesh['x'=4,'c'=2,'z'=16,'y'=4] {'c','y'}, dimensions={0} | all-to-all | bytes 65536 | tf_op jit(solution)/shard_map/all_to_all | solution.py:247
  21.3 0.0 collective-permute-done.c1
  21.3 2.9 %collective-permute-start.1 = (bf16[64,4096]{1,0:T(8,128)(2,1)S(1)}, bf16[64,4096]{1,0:T(8,128)(2,1)S(1)}, u32[]{:S(2)}, u32[]{:S(2)}) collective-permute-start(bf16[64,4096]{1,0:T(8,128)(2,1)S(1)} %collective-permute-done.c1), channel_id=1, source_target_pairs={{0,3},{1,2},{2,1},{3,0},{4,7},{5,6},{6,5},{7,4},{8,11},{9,10},{10,... | collective-permute-start | bytes 1572872 | tf_op jit(solution)/shard_map/ppermute | solution.py:230
  24.2 0.0 collective-permute-done.2.c3
  24.2 0.9 shard_map.50
  25.1 15.2 %all-to-all-start.1 = ((bf16[16,16,256]{2,1,0:T(8,128)(2,1)}), bf16[16,16,256]{2,1,0:T(8,128)(2,1)S(1)}, u32[]{:S(2)}, u32[]{:S(2)}) async-start(bf16[16,16,256]{2,1,0:T(8,128)(2,1)} %get-tuple-element.20), calls=%async_computation.1 | async-start | bytes 262144 | tf_op jit(solution)/shard_map/all_to_all | solution.py:268
  40.3 0.7 collective-permute-start.3
  41.0 0.0 collective-permute-done.3.down.d0
  41.0 14.0 %all-to-all-done.1.parts = bf16[16,16,256]{2,1,0:T(8,128)(2,1)S(1)} async-done(((bf16[16,16,256]{2,1,0:T(8,128)(2,1)}), bf16[16,16,256]{2,1,0:T(8,128)(2,1)S(1)}, u32[]{:S(2)}, u32[]{:S(2)}) %all-to-all-start.1) | async-done | bytes 131104 | tf_op jit(solution)/shard_map/all_to_all | solution.py:268
  55.0 0.0 collective-permute-done.1.c2
  55.0 1.5 %shard_map.51 = (f32[8,256]{1,0:T(8,128)S(1)}, bf16[16,16,256]{2,1,0:T(8,128)(2,1)}) custom-call(s32[1]{0:T(128)} %bitcast.row_ref.plane_ref, bf16[16,16,256]{2,1,0:T(8,128)(2,1)S(1)} %all-to-all-done.1.parts, bf16[64,4096]{1,0:T(8,128)(2,1)S(1)} %get-tuple-element.21.c0, bf16[64,4096]{1,0:T(8,128)(2,1)S(1)} %collective-permute-done.c1, ...), custom_call_target="tpu_custom_call" | custom-call | tf_op jit(solution)/shard_map/pallas_call | solution.py:30
  56.5 3.8 %all-to-all-start.2 = ((bf16[16,16,256]{2,1,0:T(8,128)(2,1)}), bf16[16,16,256]{2,1,0:T(8,128)(2,1)S(1)}, u32[]{:S(2)}, u32[]{:S(2)}) async-start(bf16[16,16,256]{2,1,0:T(8,128)(2,1)} %get-tuple-element.26), calls=%async_computation.2 | async-start | bytes 262144 | tf_op jit(solution)/shard_map/all_to_all | solution.py:268
  60.3 0.7 collective-permute-start.5
  61.0 4.8 %collective-permute-start.4 = (f32[8,256]{1,0:T(8,128)S(1)}, f32[8,256]{1,0:T(8,128)S(1)}, u32[]{:S(2)}, u32[]{:S(2)}) collective-permute-start(f32[8,256]{1,0:T(8,128)S(1)} %get-tuple-element.27.field.rest_0_.f1), channel_id=1, source_target_pairs={{0,64},{64,0},{128,192},{192,128},{256,320},{320,256},{384,448},{4... | collective-permute-start | bytes 24584 | tf_op jit(solution)/shard_map/ppermute | solution.py:234
  65.8 0.0 collective-permute-done.5.down.d1
  65.8 0.8 collective-permute-done.4.up.u1
  66.6 7.8 %all-to-all-done.2.parts = bf16[16,16,256]{2,1,0:T(8,128)(2,1)S(1)} async-done(((bf16[16,16,256]{2,1,0:T(8,128)(2,1)}), bf16[16,16,256]{2,1,0:T(8,128)(2,1)S(1)}, u32[]{:S(2)}, u32[]{:S(2)}) %all-to-all-start.2) | async-done | bytes 131104 | tf_op jit(solution)/shard_map/all_to_all | solution.py:268
  74.4 1.5 %shard_map.52 = (f32[8,256]{1,0:T(8,128)S(1)}, bf16[16,16,256]{2,1,0:T(8,128)(2,1)}) custom-call(s32[1]{0:T(128)} %bitcast.row_ref.plane_ref, bf16[16,16,256]{2,1,0:T(8,128)(2,1)S(1)} %all-to-all-done.2.parts, bf16[64,4096]{1,0:T(8,128)(2,1)S(1)} %get-tuple-element.21.c0, bf16[64,4096]{1,0:T(8,128)(2,1)S(1)} %collective-permute-done.c1, ...), custom_call_target="tpu_custom_call" | custom-call | tf_op jit(solution)/shard_map/pallas_call | solution.py:30
  75.8 4.2 %all-to-all-start.3 = ((bf16[16,16,256]{2,1,0:T(8,128)(2,1)}), bf16[16,16,256]{2,1,0:T(8,128)(2,1)S(1)}, u32[]{:S(2)}, u32[]{:S(2)}) async-start(bf16[16,16,256]{2,1,0:T(8,128)(2,1)} %get-tuple-element.28), calls=%async_computation.3 | async-start | bytes 262144 | tf_op jit(solution)/shard_map/all_to_all | solution.py:268
  80.1 0.7 collective-permute-start.7
  80.7 4.8 %collective-permute-start.6 = (f32[8,256]{1,0:T(8,128)S(1)}, f32[8,256]{1,0:T(8,128)S(1)}, u32[]{:S(2)}, u32[]{:S(2)}) collective-permute-start(f32[8,256]{1,0:T(8,128)S(1)} %get-tuple-element.29.field.f2), channel_id=1, source_target_pairs={{0,64},{64,0},{128,192},{192,128},{256,320},{320,256},{384,448},{4... | collective-permute-start | bytes 24584 | tf_op jit(solution)/shard_map/ppermute | solution.py:234
  85.5 0.0 collective-permute-done.7.down.d2
  85.5 0.8 collective-permute-done.6.up.u2
  86.3 8.1 %all-to-all-done.3.parts = bf16[16,16,256]{2,1,0:T(8,128)(2,1)S(1)} async-done(((bf16[16,16,256]{2,1,0:T(8,128)(2,1)}), bf16[16,16,256]{2,1,0:T(8,128)(2,1)S(1)}, u32[]{:S(2)}, u32[]{:S(2)}) %all-to-all-start.3) | async-done | bytes 131104 | tf_op jit(solution)/shard_map/all_to_all | solution.py:268
  94.5 0.8 shard_map.53
  95.2 17.2 %all_to_all.36.parts = bf16[16,8,256]{2,1,0:T(8,128)(2,1)S(1)} all-to-all(bf16[16,8,256]{2,1,0:T(8,128)(2,1)S(1)} %get-tuple-element.30), channel_id=1, replica_groups=mesh['x'=4,'c'=2,'z'=16,'y'=4] {'z'}, dimensions={0} | all-to-all | bytes 131072 | tf_op jit(solution)/shard_map/all_to_all | solution.py:276
  112.4 0.8 shard_map.54
  113.2 10.3 %all_to_all.37.packed = f32[8,8,640]{2,1,0:T(8,128)S(1)} all-to-all(f32[8,8,640]{2,1,0:T(8,128)S(1)} %shard_map.54), channel_id=1, replica_groups=mesh['x'=4,'c'=2,'z'=16,'y'=4] {'x','c'}, dimensions={0} | all-to-all | bytes 327680 | tf_op jit(solution)/shard_map/all_to_all | solution.py:282
  123.5 0.1 shard_map.55
  123.6 15.6 %all_to_all.38.tables = f32[16,8,128]{2,1,0:T(8,128)S(1)} all-to-all(f32[16,8,128]{2,1,0:T(8,128)S(1)} %get-tuple-element.32), channel_id=1, replica_groups=mesh['x'=4,'c'=2,'z'=16,'y'=4] {'z'}, dimensions={0} | all-to-all | bytes 131072 | tf_op jit(solution)/shard_map/all_to_all | solution.py:284
  139.2 1.1 shard_map.56
  (2 shorter events, 0.0 us)
Async XLA Ops:
  0.6 10.6 %copy-start.1 = (f32[1,64]{1,0:T(1,128)S(1)}, f32[1,64]{1,0:T(1,128)}, u32[]{:S(2)}) copy-start(f32[1,64]{1,0:T(1,128)} %param.5) | copy-start | bytes 772
  1.7 9.6 %copy-start = (f32[1,8,64]{2,1,0:T(8,128)S(1)}, f32[1,8,64]{2,1,0:T(8,128)}, u32[]{:S(2)}) copy-start(f32[1,8,64]{2,1,0:T(8,128)} %param.3) | copy-start | bytes 6148
  1.7 19.6 %collective-permute-start = (bf16[64,4096]{1,0:T(8,128)(2,1)S(1)}, bf16[64,4096]{1,0:T(8,128)(2,1)S(1)}, u32[]{:S(2)}, u32[]{:S(2)}) collective-permute-start(bf16[64,4096]{1,0:T(8,128)(2,1)S(1)} %bitcast.6), channel_id=1, source_target_pairs={{0,1},{1,0},{2,3},{3,2},{4,5},{5,4},{6,7},{7,6},{8,9},{9,8},{10,11... | collective-permute-start | bytes 1572872 | tf_op jit(solution)/shard_map/ppermute | solution.py:230
  4.5 19.8 %collective-permute-start.2 = (bf16[64,4096]{1,0:T(8,128)(2,1)S(1)}, bf16[64,4096]{1,0:T(8,128)(2,1)S(1)}, u32[]{:S(2)}, u32[]{:S(2)}) collective-permute-start(bf16[64,4096]{1,0:T(8,128)(2,1)S(1)} %bitcast.7), channel_id=1, source_target_pairs={{0,3},{1,2},{2,1},{3,0},{4,7},{5,6},{6,5},{7,4},{8,11},{9,10},{10,... | collective-permute-start | bytes 1572872 | tf_op jit(solution)/shard_map/ppermute | solution.py:230
  21.3 33.7 %collective-permute-start.1 = (bf16[64,4096]{1,0:T(8,128)(2,1)S(1)}, bf16[64,4096]{1,0:T(8,128)(2,1)S(1)}, u32[]{:S(2)}, u32[]{:S(2)}) collective-permute-start(bf16[64,4096]{1,0:T(8,128)(2,1)S(1)} %collective-permute-done.c1), channel_id=1, source_target_pairs={{0,3},{1,2},{2,1},{3,0},{4,7},{5,6},{6,5},{7,4},{8,11},{9,10},{10,... | collective-permute-start | bytes 1572872 | tf_op jit(solution)/shard_map/ppermute | solution.py:230
  25.1 29.9 %all-to-all-start.1 = ((bf16[16,16,256]{2,1,0:T(8,128)(2,1)}), bf16[16,16,256]{2,1,0:T(8,128)(2,1)S(1)}, u32[]{:S(2)}, u32[]{:S(2)}) async-start(bf16[16,16,256]{2,1,0:T(8,128)(2,1)} %get-tuple-element.20), calls=%async_computation.1 | async-start | bytes 262144 | tf_op jit(solution)/shard_map/all_to_all | solution.py:268
  40.3 0.7 collective-permute-start.3
  56.5 17.9 %all-to-all-start.2 = ((bf16[16,16,256]{2,1,0:T(8,128)(2,1)}), bf16[16,16,256]{2,1,0:T(8,128)(2,1)S(1)}, u32[]{:S(2)}, u32[]{:S(2)}) async-start(bf16[16,16,256]{2,1,0:T(8,128)(2,1)} %get-tuple-element.26), calls=%async_computation.2 | async-start | bytes 262144 | tf_op jit(solution)/shard_map/all_to_all | solution.py:268
  60.3 5.4 %collective-permute-start.5 = (f32[8,256]{1,0:T(8,128)S(1)}, f32[8,256]{1,0:T(8,128)S(1)}, u32[]{:S(2)}, u32[]{:S(2)}) collective-permute-start(f32[8,256]{1,0:T(8,128)S(1)} %get-tuple-element.27.field.rest_0_.f1), channel_id=1, source_target_pairs={{64,128},{192,256},{320,384},{128,64},{256,192},{384,320},{65,129}... | collective-permute-start | bytes 24584 | tf_op jit(solution)/shard_map/ppermute | solution.py:239
  61.0 5.6 %collective-permute-start.4 = (f32[8,256]{1,0:T(8,128)S(1)}, f32[8,256]{1,0:T(8,128)S(1)}, u32[]{:S(2)}, u32[]{:S(2)}) collective-permute-start(f32[8,256]{1,0:T(8,128)S(1)} %get-tuple-element.27.field.rest_0_.f1), channel_id=1, source_target_pairs={{0,64},{64,0},{128,192},{192,128},{256,320},{320,256},{384,448},{4... | collective-permute-start | bytes 24584 | tf_op jit(solution)/shard_map/ppermute | solution.py:234
  75.8 18.6 %all-to-all-start.3 = ((bf16[16,16,256]{2,1,0:T(8,128)(2,1)}), bf16[16,16,256]{2,1,0:T(8,128)(2,1)S(1)}, u32[]{:S(2)}, u32[]{:S(2)}) async-start(bf16[16,16,256]{2,1,0:T(8,128)(2,1)} %get-tuple-element.28), calls=%async_computation.3 | async-start | bytes 262144 | tf_op jit(solution)/shard_map/all_to_all | solution.py:268
  80.1 5.4 %collective-permute-start.7 = (f32[8,256]{1,0:T(8,128)S(1)}, f32[8,256]{1,0:T(8,128)S(1)}, u32[]{:S(2)}, u32[]{:S(2)}) collective-permute-start(f32[8,256]{1,0:T(8,128)S(1)} %get-tuple-element.29.field.f2), channel_id=1, source_target_pairs={{64,128},{192,256},{320,384},{128,64},{256,192},{384,320},{65,129}... | collective-permute-start | bytes 24584 | tf_op jit(solution)/shard_map/ppermute | solution.py:239
  80.7 5.6 %collective-permute-start.6 = (f32[8,256]{1,0:T(8,128)S(1)}, f32[8,256]{1,0:T(8,128)S(1)}, u32[]{:S(2)}, u32[]{:S(2)}) collective-permute-start(f32[8,256]{1,0:T(8,128)S(1)} %get-tuple-element.29.field.f2), channel_id=1, source_target_pairs={{0,64},{64,0},{128,192},{192,128},{256,320},{320,256},{384,448},{4... | collective-permute-start | bytes 24584 | tf_op jit(solution)/shard_map/ppermute | solution.py:234

commit v11 on v9

--- a/solution.py
+++ b/solution.py
@@ -9,7 +9,7 @@
 CENTRE = 6.75
 SCALE = 32.0
 LINK = (6.5**2 / 12 + 2.0) / SCALE
-WITH_LOW = (True, True, True, False)
+WITH_LOW = (False, True, True, False)
 PAIRS = [(i, j) for j in range(STEPS + 1) for i in range(j + 1)]
 NZ, NY, NX, NC = 16, 4, 4, 2
 B = 8
@@ -19,19 +19,21 @@
 BF16 = jnp.bfloat16
 
 
-def call(body, outs, *args, smem=0, loose=(), keep=True):
+def call(body, outs, *args, smem=0, hbm=0, scratch=(), keep=True):
+    first = smem + hbm
     args = args[:smem] + tuple(
-        x if i in loose else pltpu.with_memory_space_constraint(x, pltpu.VMEM)
+        pltpu.with_memory_space_constraint(x, pltpu.VMEM if i >= hbm else pltpu.HBM)
         for i, x in enumerate(args[smem:])
     )
     if keep:
         outs = jax.tree.map(lambda o: pltpu.VMEM(o.shape, o.dtype), outs)
-    specs = [pl.BlockSpec(memory_space=pltpu.SMEM)] * smem
-    specs += [pl.BlockSpec(memory_space=pltpu.VMEM)] * (len(args) - smem)
+    places = [pltpu.SMEM] * smem + [pltpu.HBM] * hbm + [pltpu.VMEM] * (len(args) - first)
+    specs = [pl.BlockSpec(memory_space=place) for place in places]
     return pl.pallas_call(
         body,
         out_shape=outs,
         in_specs=specs,
+        scratch_shapes=scratch,
         compiler_params=pltpu.CompilerParams(vmem_limit_bytes=8 << 20),
         out_specs=jax.tree.map(lambda _: pl.BlockSpec(memory_space=pltpu.VMEM), outs),
     )(*args)
@@ -70,9 +72,11 @@
     store_parts(send, field, row)
 
 
-def next_field(parts, blocks, field, previous, diag, beside):
+def next_field(parts, blocks, field, previous, diag, beside, wait=None):
     sums = []
-    for block in blocks:
+    for block in blocks[::-1]:
+        if wait is not None and block is blocks[0]:
+            wait()
         total = None
         for z in range(NZ):
             term = lax.dot_general(
@@ -83,7 +87,7 @@
             )
             total = term if total is None else total + term
         sums.append(total if total.shape[0] == B else total[:B] + total[B:])
-    blended = jnp.concatenate(sums, axis=1)
+    blended = jnp.concatenate(sums[::-1], axis=1)
     own = (diag[0:1] + (2.0 - CENTRE)) * field[...]
     total = own + blended
     if previous is not None:
@@ -93,9 +97,16 @@
     return total * (1.0 / SCALE)
 
 
-def step(row_ref, parts, c0, c1, c2, c3, diag, up, down, field, *rest):
-    *previous, field_out, send = rest
-    previous = previous[0] if previous else None
+def first_step(row_ref, own, parts, c1, c2, c3, diag, up, down, field, field_out, send, c0, arrived):
+    fetch = pltpu.make_async_copy(own, c0, arrived)
+    fetch.start()
+    beside = up[...] + down[...]
+    out = next_field(parts, (c0, c1, c2, c3), field, None, diag, beside, fetch.wait)
+    field_out[...] = out
+    store_parts(send, out, row_ref[0] % NY)
+
+
+def step(row_ref, parts, c0, c1, c2, c3, diag, up, down, field, previous, field_out, send):
     out = next_field(parts, (c0, c1, c2, c3), field, previous, diag, up[...] + down[...])
     field_out[...] = out
     store_parts(send, out, row_ref[0] % NY)
@@ -259,13 +270,18 @@
             up = even(field)
         beside += [up, down]
         parts = lax.all_to_all(send, "z", 0, 0, tiled=True)
-        field, send = call(
-            step,
-            (wide, sends[k + 1]),
-            row, parts, *blocks, diag, up, down, *fields[::-1][:2],
-            smem=1,
-            loose=(1,) if k == 0 else (),
-        )
+        outs = (wide, sends[k + 1])
+        if k == 0:
+            field, send = call(
+                first_step, outs, row, own, parts, *blocks[1:], diag, up, down, field,
+                smem=1,
+                hbm=1,
+                scratch=[pltpu.VMEM((H, NZ * W), BF16), pltpu.SemaphoreType.DMA],
+            )
+        else:
+            field, send = call(
+                step, outs, row, parts, *blocks, diag, up, down, *fields[::-1][:2], smem=1
+            )
         fields.append(field)
     parts = lax.all_to_all(send, "z", 0, 0, tiled=True)
     packed = call(

time: 139 us -> 138 us (level)
  waiting for transfers between devices: 34 us -> 31.3 us
  starting transfers between devices: 51.4 us -> 53.4 us
    all_to_all x3, waiting for transfers between devices: 29.9 us -> 27.1 us  [on_device(): parts = lax.all_to_all(send, 'z', 0, 0, tiled=True)]
where the time goes in v11:
time: 138 us; the launch traced here: 137 us
  starting transfers between devices  53.4 us (39%)
  blocking collectives  42.4 us (31%)
  waiting for transfers between devices  31.3 us (23%)
  Pallas kernels  7.55 us (5%)
    all_to_all x3, waiting for transfers between devices, on_device(): parts = lax.all_to_all(send, 'z', 0, 0, tiled=True)  27.1 us
    all_to_all x3, starting transfers between devices, on_device(): parts = lax.all_to_all(send, 'z', 0, 0, tiled=True)  24.2 us
    all_to_all x1, blocking collectives, on_device(): parts = lax.all_to_all(send, 'z', 0, 0, tiled=True)  16.9 us
    all_to_all x1, blocking collectives, on_device(): table = lax.all_to_all(table, 'z', 0, 0, tiled=True)  15.5 us
    ppermute x2, starting transfers between devices, even(): return lax.ppermute(field, ('x', 'c'), [(i, i ^ 1) for i in range(NX * NC)])  10.5 us
    all_to_all x1, blocking collectives, on_device(): packed = lax.all_to_all(packed, ('x', 'c'), 0, 0, tiled=True)  9.99 us
    ppermute x3, starting transfers between devices, swapped(): return lax.ppermute(array, 'y', [(y, y ^ mask) for y in range(NY)])  8.61 us
    all_to_all x1, starting transfers between devices, on_device(): packed = lax.all_to_all(packed, ('c', 'y'), 0, 0, tiled=True)  8.15 us
  transfers between devices with their start and end apart: 12, of which 6 were waited for; matrix products, arithmetic and copies ran while one was open for 1% of the time, Pallas kernels for 1%

profile of v11, /device:TPU:24, one launch (start us, length us, event | category | flops | bytes accessed | tf_op | source)
XLA Modules:
  0.0 136.8 jit_solution(10689989946377606300)
XLA Ops:
  0.6 0.0 copy-start.1
  0.6 2.7 %collective-permute-start = (bf16[64,4096]{1,0:T(8,128)(2,1)}, bf16[64,4096]{1,0:T(8,128)(2,1)S(1)}, u32[]{:S(2)}, u32[]{:S(2)}) collective-permute-start(bf16[64,4096]{1,0:T(8,128)(2,1)} %bitcast.6), channel_id=1, source_target_pairs={{0,1},{1,0},{2,3},{3,2},{4,5},{5,4},{6,7},{7,6},{8,9},{9,8},{10,11... | collective-permute-start | bytes 1572872 | tf_op jit(solution)/shard_map/ppermute | solution.py:241
  3.3 0.7 pad.1.clone
  4.0 0.0 copy-done.1
  4.0 0.6 broadcast_in_dim.21
  4.6 8.2 %all-to-all-start = ((f32[8,8,128]{2,1,0:T(8,128)}), f32[8,8,128]{2,1,0:T(8,128)S(1)}, u32[]{:S(2)}, u32[]{:S(2)}) async-start(f32[8,8,128]{2,1,0:T(8,128)} %broadcast_in_dim.21), calls=%async_computation | async-start | bytes 65536 | tf_op jit(solution)/shard_map/all_to_all | solution.py:258
  12.8 2.0 %collective-permute-start.2 = (bf16[64,4096]{1,0:T(8,128)(2,1)}, bf16[64,4096]{1,0:T(8,128)(2,1)S(1)}, u32[]{:S(2)}, u32[]{:S(2)}) collective-permute-start(bf16[64,4096]{1,0:T(8,128)(2,1)} %bitcast.7), channel_id=1, source_target_pairs={{0,3},{1,2},{2,1},{3,0},{4,7},{5,6},{6,5},{7,4},{8,11},{9,10},{10,... | collective-permute-start | bytes 1572872 | tf_op jit(solution)/shard_map/ppermute | solution.py:241
  14.8 2.5 %all-to-all-done.packed = f32[8,8,128]{2,1,0:T(8,128)S(1)} async-done(((f32[8,8,128]{2,1,0:T(8,128)}), f32[8,8,128]{2,1,0:T(8,128)S(1)}, u32[]{:S(2)}, u32[]{:S(2)}) %all-to-all-start) | async-done | bytes 32800 | tf_op jit(solution)/shard_map/all_to_all | solution.py:258
  17.3 0.0 collective-permute-done.c1
  17.3 4.0 %collective-permute-start.1 = (bf16[64,4096]{1,0:T(8,128)(2,1)S(1)}, bf16[64,4096]{1,0:T(8,128)(2,1)S(1)}, u32[]{:S(2)}, u32[]{:S(2)}) collective-permute-start(bf16[64,4096]{1,0:T(8,128)(2,1)S(1)} %collective-permute-done.c1), channel_id=1, source_target_pairs={{0,3},{1,2},{2,1},{3,0},{4,7},{5,6},{6,5},{7,4},{8,11},{9,10},{10,... | collective-permute-start | bytes 1572872 | tf_op jit(solution)/shard_map/ppermute | solution.py:241
  21.3 0.8 shard_map.50
  22.2 15.2 %all-to-all-start.1 = ((bf16[16,8,256]{2,1,0:T(8,128)(2,1)}), bf16[16,8,256]{2,1,0:T(8,128)(2,1)S(1)}, u32[]{:S(2)}, u32[]{:S(2)}) async-start(bf16[16,8,256]{2,1,0:T(8,128)(2,1)} %get-tuple-element.19), calls=%async_computation.1 | async-start | bytes 131072 | tf_op jit(solution)/shard_map/all_to_all | solution.py:272
  37.4 0.7 collective-permute-start.3
  38.0 0.0 collective-permute-done.2.c3
  38.1 0.0 collective-permute-done.3.down.d0
  38.1 12.0 %all-to-all-done.1.parts = bf16[16,8,256]{2,1,0:T(8,128)(2,1)S(1)} async-done(((bf16[16,8,256]{2,1,0:T(8,128)(2,1)}), bf16[16,8,256]{2,1,0:T(8,128)(2,1)S(1)}, u32[]{:S(2)}, u32[]{:S(2)}) %all-to-all-start.1) | async-done | bytes 65568 | tf_op jit(solution)/shard_map/all_to_all | solution.py:272
  50.1 0.0 collective-permute-done.1.c2
  50.1 0.0 copy-start
  50.1 2.4 %shard_map.51 = (f32[8,256]{1,0:T(8,128)S(1)}, bf16[16,16,256]{2,1,0:T(8,128)(2,1)}) custom-call(s32[1]{0:T(128)} %bitcast.row_ref.plane_ref, bf16[64,4096]{1,0:T(8,128)(2,1)} %bitcast.8, bf16[16,8,256]{2,1,0:T(8,128)(2,1)S(1)} %all-to-all-done.1.parts, bf16[64,4096]{1,0:T(8,128)(2,1)S(1)} %collective-permute-done.c1, ...), custom_call_target="tpu_custom_call" | custom-call | tf_op jit(solution)/shard_map/pallas_call | solution.py:32
  52.5 3.6 %all-to-all-start.2 = ((bf16[16,16,256]{2,1,0:T(8,128)(2,1)}), bf16[16,16,256]{2,1,0:T(8,128)(2,1)S(1)}, u32[]{:S(2)}, u32[]{:S(2)}) async-start(bf16[16,16,256]{2,1,0:T(8,128)(2,1)} %get-tuple-element.24), calls=%async_computation.2 | async-start | bytes 262144 | tf_op jit(solution)/shard_map/all_to_all | solution.py:272
  56.1 0.7 collective-permute-start.5
  56.8 5.5 %collective-permute-start.4 = (f32[8,256]{1,0:T(8,128)S(1)}, f32[8,256]{1,0:T(8,128)S(1)}, u32[]{:S(2)}, u32[]{:S(2)}) collective-permute-start(f32[8,256]{1,0:T(8,128)S(1)} %get-tuple-element.25.field.previous.f1), channel_id=1, source_target_pairs={{0,64},{64,0},{128,192},{192,128},{256,320},{320,256},{384,448},{4... | collective-permute-start | bytes 24584 | tf_op jit(solution)/shard_map/ppermute | solution.py:245
  62.3 0.0 collective-permute-done.5.down.d1
  62.3 0.8 collective-permute-done.4.up.u1
  63.1 6.9 %all-to-all-done.2.parts = bf16[16,16,256]{2,1,0:T(8,128)(2,1)S(1)} async-done(((bf16[16,16,256]{2,1,0:T(8,128)(2,1)}), bf16[16,16,256]{2,1,0:T(8,128)(2,1)S(1)}, u32[]{:S(2)}, u32[]{:S(2)}) %all-to-all-start.2) | async-done | bytes 131104 | tf_op jit(solution)/shard_map/all_to_all | solution.py:272
  69.9 0.0 copy-done
  69.9 1.5 %shard_map.52 = (f32[8,256]{1,0:T(8,128)S(1)}, bf16[16,16,256]{2,1,0:T(8,128)(2,1)}) custom-call(s32[1]{0:T(128)} %bitcast.row_ref.plane_ref, bf16[16,16,256]{2,1,0:T(8,128)(2,1)S(1)} %all-to-all-done.2.parts, bf16[64,4096]{1,0:T(8,128)(2,1)S(1)} %bitcast.9, bf16[64,4096]{1,0:T(8,128)(2,1)S(1)} %collective-permute-done.c1, ...), custom_call_target="tpu_custom_call" | custom-call | tf_op jit(solution)/shard_map/pallas_call | solution.py:32
  71.4 5.5 %all-to-all-start.3 = ((bf16[16,16,256]{2,1,0:T(8,128)(2,1)}), bf16[16,16,256]{2,1,0:T(8,128)(2,1)S(1)}, u32[]{:S(2)}, u32[]{:S(2)}) async-start(bf16[16,16,256]{2,1,0:T(8,128)(2,1)} %get-tuple-element.26), calls=%async_computation.3 | async-start | bytes 262144 | tf_op jit(solution)/shard_map/all_to_all | solution.py:272
  76.9 0.7 collective-permute-start.7
  77.5 5.0 %collective-permute-start.6 = (f32[8,256]{1,0:T(8,128)S(1)}, f32[8,256]{1,0:T(8,128)S(1)}, u32[]{:S(2)}, u32[]{:S(2)}) collective-permute-start(f32[8,256]{1,0:T(8,128)S(1)} %get-tuple-element.27.field.f2), channel_id=1, source_target_pairs={{0,64},{64,0},{128,192},{192,128},{256,320},{320,256},{384,448},{4... | collective-permute-start | bytes 24584 | tf_op jit(solution)/shard_map/ppermute | solution.py:245
  82.6 0.0 collective-permute-done.7.down.d2
  82.6 0.8 collective-permute-done.6.up.u2
  83.4 8.2 %all-to-all-done.3.parts = bf16[16,16,256]{2,1,0:T(8,128)(2,1)S(1)} async-done(((bf16[16,16,256]{2,1,0:T(8,128)(2,1)}), bf16[16,16,256]{2,1,0:T(8,128)(2,1)S(1)}, u32[]{:S(2)}, u32[]{:S(2)}) %all-to-all-start.3) | async-done | bytes 131104 | tf_op jit(solution)/shard_map/all_to_all | solution.py:272
  91.6 0.8 shard_map.53
  92.4 16.9 %all_to_all.35.parts = bf16[16,8,256]{2,1,0:T(8,128)(2,1)S(1)} all-to-all(bf16[16,8,256]{2,1,0:T(8,128)(2,1)S(1)} %get-tuple-element.28), channel_id=1, replica_groups=mesh['x'=4,'c'=2,'z'=16,'y'=4] {'z'}, dimensions={0} | all-to-all | bytes 131072 | tf_op jit(solution)/shard_map/all_to_all | solution.py:286
  109.2 0.8 shard_map.54
  110.0 10.0 %all_to_all.36.packed = f32[8,8,640]{2,1,0:T(8,128)S(1)} all-to-all(f32[8,8,640]{2,1,0:T(8,128)S(1)} %shard_map.54), channel_id=1, replica_groups=mesh['x'=4,'c'=2,'z'=16,'y'=4] {'x','c'}, dimensions={0} | all-to-all | bytes 327680 | tf_op jit(solution)/shard_map/all_to_all | solution.py:292
  120.0 0.1 shard_map.55
  120.1 15.5 %all_to_all.37.tables = f32[16,8,128]{2,1,0:T(8,128)S(1)} all-to-all(f32[16,8,128]{2,1,0:T(8,128)S(1)} %get-tuple-element.30), channel_id=1, replica_groups=mesh['x'=4,'c'=2,'z'=16,'y'=4] {'z'}, dimensions={0} | all-to-all | bytes 131072 | tf_op jit(solution)/shard_map/all_to_all | solution.py:294
  135.7 1.1 shard_map.56
  (1 shorter events, 0.0 us)
Async XLA Ops:
  0.6 3.4 %copy-start.1 = (f32[1,8,64]{2,1,0:T(8,128)S(1)}, f32[1,8,64]{2,1,0:T(8,128)}, u32[]{:S(2)}) copy-start(f32[1,8,64]{2,1,0:T(8,128)} %param.3) | copy-start | bytes 6148
  0.6 16.7 %collective-permute-start = (bf16[64,4096]{1,0:T(8,128)(2,1)}, bf16[64,4096]{1,0:T(8,128)(2,1)S(1)}, u32[]{:S(2)}, u32[]{:S(2)}) collective-permute-start(bf16[64,4096]{1,0:T(8,128)(2,1)} %bitcast.6), channel_id=1, source_target_pairs={{0,1},{1,0},{2,3},{3,2},{4,5},{5,4},{6,7},{7,6},{8,9},{9,8},{10,11... | collective-permute-start | bytes 1572872 | tf_op jit(solution)/shard_map/ppermute | solution.py:241
  4.6 12.7 %all-to-all-start = ((f32[8,8,128]{2,1,0:T(8,128)}), f32[8,8,128]{2,1,0:T(8,128)S(1)}, u32[]{:S(2)}, u32[]{:S(2)}) async-start(f32[8,8,128]{2,1,0:T(8,128)} %broadcast_in_dim.21), calls=%async_computation | async-start | bytes 65536 | tf_op jit(solution)/shard_map/all_to_all | solution.py:258
  12.8 25.2 %collective-permute-start.2 = (bf16[64,4096]{1,0:T(8,128)(2,1)}, bf16[64,4096]{1,0:T(8,128)(2,1)S(1)}, u32[]{:S(2)}, u32[]{:S(2)}) collective-permute-start(bf16[64,4096]{1,0:T(8,128)(2,1)} %bitcast.7), channel_id=1, source_target_pairs={{0,3},{1,2},{2,1},{3,0},{4,7},{5,6},{6,5},{7,4},{8,11},{9,10},{10,... | collective-permute-start | bytes 1572872 | tf_op jit(solution)/shard_map/ppermute | solution.py:241
  17.3 32.8 %collective-permute-start.1 = (bf16[64,4096]{1,0:T(8,128)(2,1)S(1)}, bf16[64,4096]{1,0:T(8,128)(2,1)S(1)}, u32[]{:S(2)}, u32[]{:S(2)}) collective-permute-start(bf16[64,4096]{1,0:T(8,128)(2,1)S(1)} %collective-permute-done.c1), channel_id=1, source_target_pairs={{0,3},{1,2},{2,1},{3,0},{4,7},{5,6},{6,5},{7,4},{8,11},{9,10},{10,... | collective-permute-start | bytes 1572872 | tf_op jit(solution)/shard_map/ppermute | solution.py:241
  22.2 27.9 %all-to-all-start.1 = ((bf16[16,8,256]{2,1,0:T(8,128)(2,1)}), bf16[16,8,256]{2,1,0:T(8,128)(2,1)S(1)}, u32[]{:S(2)}, u32[]{:S(2)}) async-start(bf16[16,8,256]{2,1,0:T(8,128)(2,1)} %get-tuple-element.19), calls=%async_computation.1 | async-start | bytes 131072 | tf_op jit(solution)/shard_map/all_to_all | solution.py:272
  37.4 0.7 collective-permute-start.3
  50.1 19.8 %copy-start = (bf16[1,64,4096]{2,1,0:T(8,128)(2,1)S(1)}, bf16[1,64,4096]{2,1,0:T(8,128)(2,1)}, u32[]{:S(2)}) copy-start(bf16[1,64,4096]{2,1,0:T(8,128)(2,1)} %param.4) | copy-start | bytes 1572868
  52.5 17.4 %all-to-all-start.2 = ((bf16[16,16,256]{2,1,0:T(8,128)(2,1)}), bf16[16,16,256]{2,1,0:T(8,128)(2,1)S(1)}, u32[]{:S(2)}, u32[]{:S(2)}) async-start(bf16[16,16,256]{2,1,0:T(8,128)(2,1)} %get-tuple-element.24), calls=%async_computation.2 | async-start | bytes 262144 | tf_op jit(solution)/shard_map/all_to_all | solution.py:272
  56.1 6.1 %collective-permute-start.5 = (f32[8,256]{1,0:T(8,128)S(1)}, f32[8,256]{1,0:T(8,128)S(1)}, u32[]{:S(2)}, u32[]{:S(2)}) collective-permute-start(f32[8,256]{1,0:T(8,128)S(1)} %get-tuple-element.25.field.previous.f1), channel_id=1, source_target_pairs={{64,128},{192,256},{320,384},{128,64},{256,192},{384,320},{65,129}... | collective-permute-start | bytes 24584 | tf_op jit(solution)/shard_map/ppermute | solution.py:250
  56.8 6.3 %collective-permute-start.4 = (f32[8,256]{1,0:T(8,128)S(1)}, f32[8,256]{1,0:T(8,128)S(1)}, u32[]{:S(2)}, u32[]{:S(2)}) collective-permute-start(f32[8,256]{1,0:T(8,128)S(1)} %get-tuple-element.25.field.previous.f1), channel_id=1, source_target_pairs={{0,64},{64,0},{128,192},{192,128},{256,320},{320,256},{384,448},{4... | collective-permute-start | bytes 24584 | tf_op jit(solution)/shard_map/ppermute | solution.py:245
  71.4 20.2 %all-to-all-start.3 = ((bf16[16,16,256]{2,1,0:T(8,128)(2,1)}), bf16[16,16,256]{2,1,0:T(8,128)(2,1)S(1)}, u32[]{:S(2)}, u32[]{:S(2)}) async-start(bf16[16,16,256]{2,1,0:T(8,128)(2,1)} %get-tuple-element.26), calls=%async_computation.3 | async-start | bytes 262144 | tf_op jit(solution)/shard_map/all_to_all | solution.py:272
  76.9 5.7 %collective-permute-start.7 = (f32[8,256]{1,0:T(8,128)S(1)}, f32[8,256]{1,0:T(8,128)S(1)}, u32[]{:S(2)}, u32[]{:S(2)}) collective-permute-start(f32[8,256]{1,0:T(8,128)S(1)} %get-tuple-element.27.field.f2), channel_id=1, source_target_pairs={{64,128},{192,256},{320,384},{128,64},{256,192},{384,320},{65,129}... | collective-permute-start | bytes 24584 | tf_op jit(solution)/shard_map/ppermute | solution.py:250
  77.5 5.8 %collective-permute-start.6 = (f32[8,256]{1,0:T(8,128)S(1)}, f32[8,256]{1,0:T(8,128)S(1)}, u32[]{:S(2)}, u32[]{:S(2)}) collective-permute-start(f32[8,256]{1,0:T(8,128)S(1)} %get-tuple-element.27.field.f2), channel_id=1, source_target_pairs={{0,64},{64,0},{128,192},{192,128},{256,320},{320,256},{384,448},{4... | collective-permute-start | bytes 24584 | tf_op jit(solution)/shard_map/ppermute | solution.py:245

commit v12 on v11

--- a/solution.py
+++ b/solution.py
@@ -9,7 +9,7 @@
 CENTRE = 6.75
 SCALE = 32.0
 LINK = (6.5**2 / 12 + 2.0) / SCALE
-WITH_LOW = (False, True, True, False)
+WITH_LOW = (False, False, True, False)
 PAIRS = [(i, j) for j in range(STEPS + 1) for i in range(j + 1)]
 NZ, NY, NX, NC = 16, 4, 4, 2
 B = 8
@@ -278,6 +278,7 @@
                 hbm=1,
                 scratch=[pltpu.VMEM((H, NZ * W), BF16), pltpu.SemaphoreType.DMA],
             )
+            blocks[0], field = lax.optimization_barrier((own, field))
         else:
             field, send = call(
                 step, outs, row, parts, *blocks, diag, up, down, *fields[::-1][:2], smem=1

time: 138 us -> 138 us (level)
  no operation moved by 1% of the time
where the time goes in v12:
time: 138 us; the launch traced here: 137 us
  starting transfers between devices  53.3 us (39%)
  blocking collectives  43 us (31%)
  waiting for transfers between devices  30.8 us (22%)
  Pallas kernels  7.51 us (5%)
    all_to_all x3, waiting for transfers between devices, on_device(): parts = lax.all_to_all(send, 'z', 0, 0, tiled=True)  26.6 us
    all_to_all x3, starting transfers between devices, on_device(): parts = lax.all_to_all(send, 'z', 0, 0, tiled=True)  24.4 us
    all_to_all x1, blocking collectives, on_device(): parts = lax.all_to_all(send, 'z', 0, 0, tiled=True)  17.2 us
    all_to_all x1, blocking collectives, on_device(): table = lax.all_to_all(table, 'z', 0, 0, tiled=True)  15.6 us
    all_to_all x1, blocking collectives, on_device(): packed = lax.all_to_all(packed, ('x', 'c'), 0, 0, tiled=True)  10.3 us
    ppermute x2, starting transfers between devices, even(): return lax.ppermute(field, ('x', 'c'), [(i, i ^ 1) for i in range(NX * NC)])  10.2 us
    ppermute x3, starting transfers between devices, swapped(): return lax.ppermute(array, 'y', [(y, y ^ mask) for y in range(NY)])  8.61 us
    all_to_all x1, starting transfers between devices, on_device(): packed = lax.all_to_all(packed, ('c', 'y'), 0, 0, tiled=True)  8.15 us
  transfers between devices with their start and end apart: 12, of which 6 were waited for; matrix products, arithmetic and copies ran while one was open for 1% of the time, Pallas kernels for 1%

profile of v12, /device:TPU:24, one launch (start us, length us, event | category | flops | bytes accessed | tf_op | source)
XLA Modules:
  0.0 136.8 jit_solution(15915857438530397756)
XLA Ops:
  0.6 0.0 copy-start.1
  0.6 2.7 %collective-permute-start = (bf16[64,4096]{1,0:T(8,128)(2,1)}, bf16[64,4096]{1,0:T(8,128)(2,1)S(1)}, u32[]{:S(2)}, u32[]{:S(2)}) collective-permute-start(bf16[64,4096]{1,0:T(8,128)(2,1)} %bitcast.6), channel_id=1, source_target_pairs={{0,1},{1,0},{2,3},{3,2},{4,5},{5,4},{6,7},{7,6},{8,9},{9,8},{10,11... | collective-permute-start | bytes 1572872 | tf_op jit(solution)/shard_map/ppermute | solution.py:241
  3.3 0.7 pad.1.clone
  4.0 0.0 copy-done.1
  4.0 0.6 broadcast_in_dim.21
  4.6 8.2 %all-to-all-start = ((f32[8,8,128]{2,1,0:T(8,128)}), f32[8,8,128]{2,1,0:T(8,128)S(1)}, u32[]{:S(2)}, u32[]{:S(2)}) async-start(f32[8,8,128]{2,1,0:T(8,128)} %broadcast_in_dim.21), calls=%async_computation | async-start | bytes 65536 | tf_op jit(solution)/shard_map/all_to_all | solution.py:258
  12.8 2.0 %collective-permute-start.2 = (bf16[64,4096]{1,0:T(8,128)(2,1)}, bf16[64,4096]{1,0:T(8,128)(2,1)S(1)}, u32[]{:S(2)}, u32[]{:S(2)}) collective-permute-start(bf16[64,4096]{1,0:T(8,128)(2,1)} %bitcast.7), channel_id=1, source_target_pairs={{0,3},{1,2},{2,1},{3,0},{4,7},{5,6},{6,5},{7,4},{8,11},{9,10},{10,... | collective-permute-start | bytes 1572872 | tf_op jit(solution)/shard_map/ppermute | solution.py:241
  14.8 2.5 %all-to-all-done.packed = f32[8,8,128]{2,1,0:T(8,128)S(1)} async-done(((f32[8,8,128]{2,1,0:T(8,128)}), f32[8,8,128]{2,1,0:T(8,128)S(1)}, u32[]{:S(2)}, u32[]{:S(2)}) %all-to-all-start) | async-done | bytes 32800 | tf_op jit(solution)/shard_map/all_to_all | solution.py:258
  17.3 0.0 collective-permute-done.c1
  17.3 4.0 %collective-permute-start.1 = (bf16[64,4096]{1,0:T(8,128)(2,1)S(1)}, bf16[64,4096]{1,0:T(8,128)(2,1)S(1)}, u32[]{:S(2)}, u32[]{:S(2)}) collective-permute-start(bf16[64,4096]{1,0:T(8,128)(2,1)S(1)} %collective-permute-done.c1), channel_id=1, source_target_pairs={{0,3},{1,2},{2,1},{3,0},{4,7},{5,6},{6,5},{7,4},{8,11},{9,10},{10,... | collective-permute-start | bytes 1572872 | tf_op jit(solution)/shard_map/ppermute | solution.py:241
  21.3 0.8 shard_map.50
  22.2 15.2 %all-to-all-start.1 = ((bf16[16,8,256]{2,1,0:T(8,128)(2,1)}), bf16[16,8,256]{2,1,0:T(8,128)(2,1)S(1)}, u32[]{:S(2)}, u32[]{:S(2)}) async-start(bf16[16,8,256]{2,1,0:T(8,128)(2,1)} %get-tuple-element.21), calls=%async_computation.1 | async-start | bytes 131072 | tf_op jit(solution)/shard_map/all_to_all | solution.py:272
  37.4 0.7 collective-permute-start.3
  38.0 0.0 collective-permute-done.2.c3
  38.1 0.0 collective-permute-done.3.down.d0
  38.1 12.0 %all-to-all-done.1.parts = bf16[16,8,256]{2,1,0:T(8,128)(2,1)S(1)} async-done(((bf16[16,8,256]{2,1,0:T(8,128)(2,1)}), bf16[16,8,256]{2,1,0:T(8,128)(2,1)S(1)}, u32[]{:S(2)}, u32[]{:S(2)}) %all-to-all-start.1) | async-done | bytes 65568 | tf_op jit(solution)/shard_map/all_to_all | solution.py:272
  50.1 0.0 collective-permute-done.1.c2
  50.1 0.0 copy-start
  50.1 2.4 %shard_map.51 = (f32[8,256]{1,0:T(8,128)S(1)}, bf16[16,8,256]{2,1,0:T(8,128)(2,1)}) custom-call(s32[1]{0:T(128)} %bitcast.row_ref.plane_ref, bf16[64,4096]{1,0:T(8,128)(2,1)} %bitcast.8, bf16[16,8,256]{2,1,0:T(8,128)(2,1)S(1)} %all-to-all-done.1.parts, bf16[64,4096]{1,0:T(8,128)(2,1)S(1)} %collective-permute-done.c1, ...), custom_call_target="tpu_custom_call" | custom-call | tf_op jit(solution)/shard_map/pallas_call | solution.py:32
  52.5 3.6 %all-to-all-start.2 = ((bf16[16,8,256]{2,1,0:T(8,128)(2,1)}), bf16[16,8,256]{2,1,0:T(8,128)(2,1)S(1)}, u32[]{:S(2)}, u32[]{:S(2)}) async-start(bf16[16,8,256]{2,1,0:T(8,128)(2,1)} %get-tuple-element.26), calls=%async_computation.2 | async-start | bytes 131072 | tf_op jit(solution)/shard_map/all_to_all | solution.py:272
  56.1 0.7 collective-permute-start.5
  56.8 5.5 %collective-permute-start.4 = (f32[8,256]{1,0:T(8,128)S(1)}, f32[8,256]{1,0:T(8,128)S(1)}, u32[]{:S(2)}, u32[]{:S(2)}) collective-permute-start(f32[8,256]{1,0:T(8,128)S(1)} %get-tuple-element.29.field.previous.f1), channel_id=1, source_target_pairs={{0,64},{64,0},{128,192},{192,128},{256,320},{320,256},{384,448},{4... | collective-permute-start | bytes 24584 | tf_op jit(solution)/shard_map/ppermute | solution.py:245
  62.2 0.0 collective-permute-done.5.down.d1
  62.2 0.8 collective-permute-done.4.up.u1
  63.0 6.4 %all-to-all-done.2.parts = bf16[16,8,256]{2,1,0:T(8,128)(2,1)S(1)} async-done(((bf16[16,8,256]{2,1,0:T(8,128)(2,1)}), bf16[16,8,256]{2,1,0:T(8,128)(2,1)S(1)}, u32[]{:S(2)}, u32[]{:S(2)}) %all-to-all-start.2) | async-done | bytes 65568 | tf_op jit(solution)/shard_map/all_to_all | solution.py:272
  69.4 0.0 copy-done
  69.4 1.5 %shard_map.52 = (f32[8,256]{1,0:T(8,128)S(1)}, bf16[16,16,256]{2,1,0:T(8,128)(2,1)}) custom-call(s32[1]{0:T(128)} %bitcast.row_ref.plane_ref, bf16[16,8,256]{2,1,0:T(8,128)(2,1)S(1)} %all-to-all-done.2.parts, bf16[64,4096]{1,0:T(8,128)(2,1)S(1)} %bitcast.9, bf16[64,4096]{1,0:T(8,128)(2,1)S(1)} %collective-permute-done.c1, ...), custom_call_target="tpu_custom_call" | custom-call | tf_op jit(solution)/shard_map/pallas_call | solution.py:32
  70.9 5.6 %all-to-all-start.3 = ((bf16[16,16,256]{2,1,0:T(8,128)(2,1)}), bf16[16,16,256]{2,1,0:T(8,128)(2,1)S(1)}, u32[]{:S(2)}, u32[]{:S(2)}) async-start(bf16[16,16,256]{2,1,0:T(8,128)(2,1)} %get-tuple-element.30), calls=%async_computation.3 | async-start | bytes 262144 | tf_op jit(solution)/shard_map/all_to_all | solution.py:272
  76.5 0.7 collective-permute-start.7
  77.2 4.8 %collective-permute-start.6 = (f32[8,256]{1,0:T(8,128)S(1)}, f32[8,256]{1,0:T(8,128)S(1)}, u32[]{:S(2)}, u32[]{:S(2)}) collective-permute-start(f32[8,256]{1,0:T(8,128)S(1)} %get-tuple-element.31.field.f2), channel_id=1, source_target_pairs={{0,64},{64,0},{128,192},{192,128},{256,320},{320,256},{384,448},{4... | collective-permute-start | bytes 24584 | tf_op jit(solution)/shard_map/ppermute | solution.py:245
  82.0 0.0 collective-permute-done.7.down.d2
  82.0 0.8 collective-permute-done.6.up.u2
  82.8 8.1 %all-to-all-done.3.parts = bf16[16,16,256]{2,1,0:T(8,128)(2,1)S(1)} async-done(((bf16[16,16,256]{2,1,0:T(8,128)(2,1)}), bf16[16,16,256]{2,1,0:T(8,128)(2,1)S(1)}, u32[]{:S(2)}, u32[]{:S(2)}) %all-to-all-start.3) | async-done | bytes 131104 | tf_op jit(solution)/shard_map/all_to_all | solution.py:272
  90.9 0.8 shard_map.53
  91.7 17.2 %all_to_all.35.parts = bf16[16,8,256]{2,1,0:T(8,128)(2,1)S(1)} all-to-all(bf16[16,8,256]{2,1,0:T(8,128)(2,1)S(1)} %get-tuple-element.32), channel_id=1, replica_groups=mesh['x'=4,'c'=2,'z'=16,'y'=4] {'z'}, dimensions={0} | all-to-all | bytes 131072 | tf_op jit(solution)/shard_map/all_to_all | solution.py:287
  108.9 0.8 shard_map.54
  109.7 10.3 %all_to_all.36.packed = f32[8,8,640]{2,1,0:T(8,128)S(1)} all-to-all(f32[8,8,640]{2,1,0:T(8,128)S(1)} %shard_map.54), channel_id=1, replica_groups=mesh['x'=4,'c'=2,'z'=16,'y'=4] {'x','c'}, dimensions={0} | all-to-all | bytes 327680 | tf_op jit(solution)/shard_map/all_to_all | solution.py:293
  120.0 0.1 shard_map.55
  120.1 15.6 %all_to_all.37.tables = f32[16,8,128]{2,1,0:T(8,128)S(1)} all-to-all(f32[16,8,128]{2,1,0:T(8,128)S(1)} %get-tuple-element.34), channel_id=1, replica_groups=mesh['x'=4,'c'=2,'z'=16,'y'=4] {'z'}, dimensions={0} | all-to-all | bytes 131072 | tf_op jit(solution)/shard_map/all_to_all | solution.py:295
  135.7 1.1 shard_map.56
  (1 shorter events, 0.0 us)
Async XLA Ops:
  0.6 3.4 %copy-start.1 = (f32[1,8,64]{2,1,0:T(8,128)S(1)}, f32[1,8,64]{2,1,0:T(8,128)}, u32[]{:S(2)}) copy-start(f32[1,8,64]{2,1,0:T(8,128)} %param.3) | copy-start | bytes 6148
  0.6 16.7 %collective-permute-start = (bf16[64,4096]{1,0:T(8,128)(2,1)}, bf16[64,4096]{1,0:T(8,128)(2,1)S(1)}, u32[]{:S(2)}, u32[]{:S(2)}) collective-permute-start(bf16[64,4096]{1,0:T(8,128)(2,1)} %bitcast.6), channel_id=1, source_target_pairs={{0,1},{1,0},{2,3},{3,2},{4,5},{5,4},{6,7},{7,6},{8,9},{9,8},{10,11... | collective-permute-start | bytes 1572872 | tf_op jit(solution)/shard_map/ppermute | solution.py:241
  4.6 12.7 %all-to-all-start = ((f32[8,8,128]{2,1,0:T(8,128)}), f32[8,8,128]{2,1,0:T(8,128)S(1)}, u32[]{:S(2)}, u32[]{:S(2)}) async-start(f32[8,8,128]{2,1,0:T(8,128)} %broadcast_in_dim.21), calls=%async_computation | async-start | bytes 65536 | tf_op jit(solution)/shard_map/all_to_all | solution.py:258
  12.8 25.2 %collective-permute-start.2 = (bf16[64,4096]{1,0:T(8,128)(2,1)}, bf16[64,4096]{1,0:T(8,128)(2,1)S(1)}, u32[]{:S(2)}, u32[]{:S(2)}) collective-permute-start(bf16[64,4096]{1,0:T(8,128)(2,1)} %bitcast.7), channel_id=1, source_target_pairs={{0,3},{1,2},{2,1},{3,0},{4,7},{5,6},{6,5},{7,4},{8,11},{9,10},{10,... | collective-permute-start | bytes 1572872 | tf_op jit(solution)/shard_map/ppermute | solution.py:241
  17.3 32.8 %collective-permute-start.1 = (bf16[64,4096]{1,0:T(8,128)(2,1)S(1)}, bf16[64,4096]{1,0:T(8,128)(2,1)S(1)}, u32[]{:S(2)}, u32[]{:S(2)}) collective-permute-start(bf16[64,4096]{1,0:T(8,128)(2,1)S(1)} %collective-permute-done.c1), channel_id=1, source_target_pairs={{0,3},{1,2},{2,1},{3,0},{4,7},{5,6},{6,5},{7,4},{8,11},{9,10},{10,... | collective-permute-start | bytes 1572872 | tf_op jit(solution)/shard_map/ppermute | solution.py:241
  22.2 27.9 %all-to-all-start.1 = ((bf16[16,8,256]{2,1,0:T(8,128)(2,1)}), bf16[16,8,256]{2,1,0:T(8,128)(2,1)S(1)}, u32[]{:S(2)}, u32[]{:S(2)}) async-start(bf16[16,8,256]{2,1,0:T(8,128)(2,1)} %get-tuple-element.21), calls=%async_computation.1 | async-start | bytes 131072 | tf_op jit(solution)/shard_map/all_to_all | solution.py:272
  37.4 0.7 collective-permute-start.3
  50.1 19.3 %copy-start = (bf16[1,64,4096]{2,1,0:T(8,128)(2,1)S(1)}, bf16[1,64,4096]{2,1,0:T(8,128)(2,1)}, u32[]{:S(2)}) copy-start(bf16[1,64,4096]{2,1,0:T(8,128)(2,1)} %param.4) | copy-start | bytes 1572868
  52.5 16.9 %all-to-all-start.2 = ((bf16[16,8,256]{2,1,0:T(8,128)(2,1)}), bf16[16,8,256]{2,1,0:T(8,128)(2,1)S(1)}, u32[]{:S(2)}, u32[]{:S(2)}) async-start(bf16[16,8,256]{2,1,0:T(8,128)(2,1)} %get-tuple-element.26), calls=%async_computation.2 | async-start | bytes 131072 | tf_op jit(solution)/shard_map/all_to_all | solution.py:272
  56.1 6.1 %collective-permute-start.5 = (f32[8,256]{1,0:T(8,128)S(1)}, f32[8,256]{1,0:T(8,128)S(1)}, u32[]{:S(2)}, u32[]{:S(2)}) collective-permute-start(f32[8,256]{1,0:T(8,128)S(1)} %get-tuple-element.29.field.previous.f1), channel_id=1, source_target_pairs={{64,128},{192,256},{320,384},{128,64},{256,192},{384,320},{65,129}... | collective-permute-start | bytes 24584 | tf_op jit(solution)/shard_map/ppermute | solution.py:250
  56.8 6.3 %collective-permute-start.4 = (f32[8,256]{1,0:T(8,128)S(1)}, f32[8,256]{1,0:T(8,128)S(1)}, u32[]{:S(2)}, u32[]{:S(2)}) collective-permute-start(f32[8,256]{1,0:T(8,128)S(1)} %get-tuple-element.29.field.previous.f1), channel_id=1, source_target_pairs={{0,64},{64,0},{128,192},{192,128},{256,320},{320,256},{384,448},{4... | collective-permute-start | bytes 24584 | tf_op jit(solution)/shard_map/ppermute | solution.py:245
  70.9 20.0 %all-to-all-start.3 = ((bf16[16,16,256]{2,1,0:T(8,128)(2,1)}), bf16[16,16,256]{2,1,0:T(8,128)(2,1)S(1)}, u32[]{:S(2)}, u32[]{:S(2)}) async-start(bf16[16,16,256]{2,1,0:T(8,128)(2,1)} %get-tuple-element.30), calls=%async_computation.3 | async-start | bytes 262144 | tf_op jit(solution)/shard_map/all_to_all | solution.py:272
  76.5 5.4 %collective-permute-start.7 = (f32[8,256]{1,0:T(8,128)S(1)}, f32[8,256]{1,0:T(8,128)S(1)}, u32[]{:S(2)}, u32[]{:S(2)}) collective-permute-start(f32[8,256]{1,0:T(8,128)S(1)} %get-tuple-element.31.field.f2), channel_id=1, source_target_pairs={{64,128},{192,256},{320,384},{128,64},{256,192},{384,320},{65,129}... | collective-permute-start | bytes 24584 | tf_op jit(solution)/shard_map/ppermute | solution.py:250
  77.2 5.6 %collective-permute-start.6 = (f32[8,256]{1,0:T(8,128)S(1)}, f32[8,256]{1,0:T(8,128)S(1)}, u32[]{:S(2)}, u32[]{:S(2)}) collective-permute-start(f32[8,256]{1,0:T(8,128)S(1)} %get-tuple-element.31.field.f2), channel_id=1, source_target_pairs={{0,64},{64,0},{128,192},{192,128},{256,320},{320,256},{384,448},{4... | collective-permute-start | bytes 24584 | tf_op jit(solution)/shard_map/ppermute | solution.py:245

commit v13 on v11

--- a/solution.py
+++ b/solution.py
@@ -272,11 +272,11 @@
         parts = lax.all_to_all(send, "z", 0, 0, tiled=True)
         outs = (wide, sends[k + 1])
         if k == 0:
-            field, send = call(
-                first_step, outs, row, own, parts, *blocks[1:], diag, up, down, field,
+            field, send, blocks[0] = call(
+                first_step, (*outs, shape((H, NZ * W), BF16)), row, own, parts, *blocks[1:], diag, up, down, field,
                 smem=1,
                 hbm=1,
-                scratch=[pltpu.VMEM((H, NZ * W), BF16), pltpu.SemaphoreType.DMA],
+                scratch=[pltpu.SemaphoreType.DMA],
             )
         else:
             field, send = call(

time: 138 us -> 137 us (level)
  no operation moved by 1% of the time
where the time goes in v13:
time: 137 us
  starting transfers between devices  53.4 us (39%)
  blocking collectives  42.4 us (31%)
  waiting for transfers between devices  31.2 us (23%)
  Pallas kernels  7.32 us (5%)
    all_to_all x3, waiting for transfers between devices, on_device(): parts = lax.all_to_all(send, 'z', 0, 0, tiled=True)  27.1 us
    all_to_all x3, starting transfers between devices, on_device(): parts = lax.all_to_all(send, 'z', 0, 0, tiled=True)  24.2 us
    all_to_all x1, blocking collectives, on_device(): parts = lax.all_to_all(send, 'z', 0, 0, tiled=True)  16.9 us
    all_to_all x1, blocking collectives, on_device(): table = lax.all_to_all(table, 'z', 0, 0, tiled=True)  15.5 us
    ppermute x2, starting transfers between devices, even(): return lax.ppermute(field, ('x', 'c'), [(i, i ^ 1) for i in range(NX * NC)])  10.5 us
    all_to_all x1, blocking collectives, on_device(): packed = lax.all_to_all(packed, ('x', 'c'), 0, 0, tiled=True)  9.99 us
    ppermute x3, starting transfers between devices, swapped(): return lax.ppermute(array, 'y', [(y, y ^ mask) for y in range(NY)])  8.61 us
    all_to_all x1, starting transfers between devices, on_device(): packed = lax.all_to_all(packed, ('c', 'y'), 0, 0, tiled=True)  8.15 us
  transfers between devices with their start and end apart: 12, of which 6 were waited for; matrix products, arithmetic and copies ran while one was open for 1% of the time, Pallas kernels for 1%

profile of v13, /device:TPU:24, one launch (start us, length us, event | category | flops | bytes accessed | tf_op | source)
XLA Modules:
  0.0 136.5 jit_solution(4846149938084161313)
XLA Ops:
  0.6 0.0 copy-start
  0.6 2.7 %collective-permute-start = (bf16[64,4096]{1,0:T(8,128)(2,1)}, bf16[64,4096]{1,0:T(8,128)(2,1)S(1)}, u32[]{:S(2)}, u32[]{:S(2)}) collective-permute-start(bf16[64,4096]{1,0:T(8,128)(2,1)} %bitcast.6), channel_id=1, source_target_pairs={{0,1},{1,0},{2,3},{3,2},{4,5},{5,4},{6,7},{7,6},{8,9},{9,8},{10,11... | collective-permute-start | bytes 1572872 | tf_op jit(solution)/shard_map/ppermute | solution.py:241
  3.3 0.7 pad.1.clone
  4.0 0.0 copy-done
  4.0 0.6 broadcast_in_dim.21
  4.7 8.2 %all-to-all-start = ((f32[8,8,128]{2,1,0:T(8,128)}), f32[8,8,128]{2,1,0:T(8,128)S(1)}, u32[]{:S(2)}, u32[]{:S(2)}) async-start(f32[8,8,128]{2,1,0:T(8,128)} %broadcast_in_dim.21), calls=%async_computation | async-start | bytes 65536 | tf_op jit(solution)/shard_map/all_to_all | solution.py:258
  12.8 2.0 %collective-permute-start.2 = (bf16[64,4096]{1,0:T(8,128)(2,1)}, bf16[64,4096]{1,0:T(8,128)(2,1)S(1)}, u32[]{:S(2)}, u32[]{:S(2)}) collective-permute-start(bf16[64,4096]{1,0:T(8,128)(2,1)} %bitcast.7), channel_id=1, source_target_pairs={{0,3},{1,2},{2,1},{3,0},{4,7},{5,6},{6,5},{7,4},{8,11},{9,10},{10,... | collective-permute-start | bytes 1572872 | tf_op jit(solution)/shard_map/ppermute | solution.py:241
  14.8 2.5 %all-to-all-done.packed = f32[8,8,128]{2,1,0:T(8,128)S(1)} async-done(((f32[8,8,128]{2,1,0:T(8,128)}), f32[8,8,128]{2,1,0:T(8,128)S(1)}, u32[]{:S(2)}, u32[]{:S(2)}) %all-to-all-start) | async-done | bytes 32800 | tf_op jit(solution)/shard_map/all_to_all | solution.py:258
  17.3 0.0 collective-permute-done.c1
  17.3 4.0 %collective-permute-start.1 = (bf16[64,4096]{1,0:T(8,128)(2,1)S(1)}, bf16[64,4096]{1,0:T(8,128)(2,1)S(1)}, u32[]{:S(2)}, u32[]{:S(2)}) collective-permute-start(bf16[64,4096]{1,0:T(8,128)(2,1)S(1)} %collective-permute-done.c1), channel_id=1, source_target_pairs={{0,3},{1,2},{2,1},{3,0},{4,7},{5,6},{6,5},{7,4},{8,11},{9,10},{10,... | collective-permute-start | bytes 1572872 | tf_op jit(solution)/shard_map/ppermute | solution.py:241
  21.3 0.9 shard_map.50
  22.2 15.2 %all-to-all-start.1 = ((bf16[16,8,256]{2,1,0:T(8,128)(2,1)}), bf16[16,8,256]{2,1,0:T(8,128)(2,1)S(1)}, u32[]{:S(2)}, u32[]{:S(2)}) async-start(bf16[16,8,256]{2,1,0:T(8,128)(2,1)} %get-tuple-element.20), calls=%async_computation.1 | async-start | bytes 131072 | tf_op jit(solution)/shard_map/all_to_all | solution.py:272
  37.4 0.7 collective-permute-start.3
  38.1 0.0 collective-permute-done.2.c3
  38.1 0.0 collective-permute-done.3.down.d0
  38.1 12.0 %all-to-all-done.1.parts = bf16[16,8,256]{2,1,0:T(8,128)(2,1)S(1)} async-done(((bf16[16,8,256]{2,1,0:T(8,128)(2,1)}), bf16[16,8,256]{2,1,0:T(8,128)(2,1)S(1)}, u32[]{:S(2)}, u32[]{:S(2)}) %all-to-all-start.1) | async-done | bytes 65568 | tf_op jit(solution)/shard_map/all_to_all | solution.py:272
  50.1 0.0 collective-permute-done.1.c2
  50.1 2.2 %shard_map.51 = (f32[8,256]{1,0:T(8,128)S(1)}, bf16[16,16,256]{2,1,0:T(8,128)(2,1)}, bf16[64,4096]{1,0:T(8,128)(2,1)S(1)}) custom-call(s32[1]{0:T(128)} %bitcast.row_ref.plane_ref, bf16[64,4096]{1,0:T(8,128)(2,1)} %bitcast.8, bf16[16,8,256]{2,1,0:T(8,128)(2,1)S(1)} %all-to-all-done.1.parts, bf16[64,4096]{1,0:T(8,128)(2,1)S(1)} %collective-permute-done.c1, ...), custom_call_target="tpu_custom_call" | custom-call | tf_op jit(solution)/shard_map/pallas_call | solution.py:32
  52.3 3.6 %all-to-all-start.2 = ((bf16[16,16,256]{2,1,0:T(8,128)(2,1)}), bf16[16,16,256]{2,1,0:T(8,128)(2,1)S(1)}, u32[]{:S(2)}, u32[]{:S(2)}) async-start(bf16[16,16,256]{2,1,0:T(8,128)(2,1)} %get-tuple-element.25), calls=%async_computation.2 | async-start | bytes 262144 | tf_op jit(solution)/shard_map/all_to_all | solution.py:272
  55.9 0.7 collective-permute-start.5
  56.6 5.5 %collective-permute-start.4 = (f32[8,256]{1,0:T(8,128)S(1)}, f32[8,256]{1,0:T(8,128)S(1)}, u32[]{:S(2)}, u32[]{:S(2)}) collective-permute-start(f32[8,256]{1,0:T(8,128)S(1)} %get-tuple-element.27.field.previous.f1), channel_id=1, source_target_pairs={{0,64},{64,0},{128,192},{192,128},{256,320},{320,256},{384,448},{4... | collective-permute-start | bytes 24584 | tf_op jit(solution)/shard_map/ppermute | solution.py:245
  62.0 0.0 collective-permute-done.5.down.d1
  62.0 0.8 collective-permute-done.4.up.u1
  62.8 6.9 %all-to-all-done.2.parts = bf16[16,16,256]{2,1,0:T(8,128)(2,1)S(1)} async-done(((bf16[16,16,256]{2,1,0:T(8,128)(2,1)}), bf16[16,16,256]{2,1,0:T(8,128)(2,1)S(1)}, u32[]{:S(2)}, u32[]{:S(2)}) %all-to-all-start.2) | async-done | bytes 131104 | tf_op jit(solution)/shard_map/all_to_all | solution.py:272
  69.7 1.5 %shard_map.52 = (f32[8,256]{1,0:T(8,128)S(1)}, bf16[16,16,256]{2,1,0:T(8,128)(2,1)}) custom-call(s32[1]{0:T(128)} %bitcast.row_ref.plane_ref, bf16[16,16,256]{2,1,0:T(8,128)(2,1)S(1)} %all-to-all-done.2.parts, bf16[64,4096]{1,0:T(8,128)(2,1)S(1)} %get-tuple-element.26.c0, bf16[64,4096]{1,0:T(8,128)(2,1)S(1)} %collective-permute-done.c1, ...), custom_call_target="tpu_custom_call" | custom-call | tf_op jit(solution)/shard_map/pallas_call | solution.py:32
  71.2 5.5 %all-to-all-start.3 = ((bf16[16,16,256]{2,1,0:T(8,128)(2,1)}), bf16[16,16,256]{2,1,0:T(8,128)(2,1)S(1)}, u32[]{:S(2)}, u32[]{:S(2)}) async-start(bf16[16,16,256]{2,1,0:T(8,128)(2,1)} %get-tuple-element.28), calls=%async_computation.3 | async-start | bytes 262144 | tf_op jit(solution)/shard_map/all_to_all | solution.py:272
  76.6 0.7 collective-permute-start.7
  77.3 5.0 %collective-permute-start.6 = (f32[8,256]{1,0:T(8,128)S(1)}, f32[8,256]{1,0:T(8,128)S(1)}, u32[]{:S(2)}, u32[]{:S(2)}) collective-permute-start(f32[8,256]{1,0:T(8,128)S(1)} %get-tuple-element.29.field.f2), channel_id=1, source_target_pairs={{0,64},{64,0},{128,192},{192,128},{256,320},{320,256},{384,448},{4... | collective-permute-start | bytes 24584 | tf_op jit(solution)/shard_map/ppermute | solution.py:245
  82.3 0.0 collective-permute-done.7.down.d2
  82.3 0.8 collective-permute-done.6.up.u2
  83.1 8.2 %all-to-all-done.3.parts = bf16[16,16,256]{2,1,0:T(8,128)(2,1)S(1)} async-done(((bf16[16,16,256]{2,1,0:T(8,128)(2,1)}), bf16[16,16,256]{2,1,0:T(8,128)(2,1)S(1)}, u32[]{:S(2)}, u32[]{:S(2)}) %all-to-all-start.3) | async-done | bytes 131104 | tf_op jit(solution)/shard_map/all_to_all | solution.py:272
  91.3 0.8 shard_map.53
  92.1 16.9 %all_to_all.35.parts = bf16[16,8,256]{2,1,0:T(8,128)(2,1)S(1)} all-to-all(bf16[16,8,256]{2,1,0:T(8,128)(2,1)S(1)} %get-tuple-element.30), channel_id=1, replica_groups=mesh['x'=4,'c'=2,'z'=16,'y'=4] {'z'}, dimensions={0} | all-to-all | bytes 131072 | tf_op jit(solution)/shard_map/all_to_all | solution.py:286
  109.0 0.8 shard_map.54
  109.8 10.0 %all_to_all.36.packed = f32[8,8,640]{2,1,0:T(8,128)S(1)} all-to-all(f32[8,8,640]{2,1,0:T(8,128)S(1)} %shard_map.54), channel_id=1, replica_groups=mesh['x'=4,'c'=2,'z'=16,'y'=4] {'x','c'}, dimensions={0} | all-to-all | bytes 327680 | tf_op jit(solution)/shard_map/all_to_all | solution.py:292
  119.8 0.1 shard_map.55
  119.9 15.5 %all_to_all.37.tables = f32[16,8,128]{2,1,0:T(8,128)S(1)} all-to-all(f32[16,8,128]{2,1,0:T(8,128)S(1)} %get-tuple-element.32), channel_id=1, replica_groups=mesh['x'=4,'c'=2,'z'=16,'y'=4] {'z'}, dimensions={0} | all-to-all | bytes 131072 | tf_op jit(solution)/shard_map/all_to_all | solution.py:294
  135.4 1.1 shard_map.56
  (1 shorter events, 0.0 us)
Async XLA Ops:
  0.6 3.4 %copy-start = (f32[1,8,64]{2,1,0:T(8,128)S(1)}, f32[1,8,64]{2,1,0:T(8,128)}, u32[]{:S(2)}) copy-start(f32[1,8,64]{2,1,0:T(8,128)} %param.3) | copy-start | bytes 6148
  0.6 16.7 %collective-permute-start = (bf16[64,4096]{1,0:T(8,128)(2,1)}, bf16[64,4096]{1,0:T(8,128)(2,1)S(1)}, u32[]{:S(2)}, u32[]{:S(2)}) collective-permute-start(bf16[64,4096]{1,0:T(8,128)(2,1)} %bitcast.6), channel_id=1, source_target_pairs={{0,1},{1,0},{2,3},{3,2},{4,5},{5,4},{6,7},{7,6},{8,9},{9,8},{10,11... | collective-permute-start | bytes 1572872 | tf_op jit(solution)/shard_map/ppermute | solution.py:241
  4.7 12.7 %all-to-all-start = ((f32[8,8,128]{2,1,0:T(8,128)}), f32[8,8,128]{2,1,0:T(8,128)S(1)}, u32[]{:S(2)}, u32[]{:S(2)}) async-start(f32[8,8,128]{2,1,0:T(8,128)} %broadcast_in_dim.21), calls=%async_computation | async-start | bytes 65536 | tf_op jit(solution)/shard_map/all_to_all | solution.py:258
  12.8 25.3 %collective-permute-start.2 = (bf16[64,4096]{1,0:T(8,128)(2,1)}, bf16[64,4096]{1,0:T(8,128)(2,1)S(1)}, u32[]{:S(2)}, u32[]{:S(2)}) collective-permute-start(bf16[64,4096]{1,0:T(8,128)(2,1)} %bitcast.7), channel_id=1, source_target_pairs={{0,3},{1,2},{2,1},{3,0},{4,7},{5,6},{6,5},{7,4},{8,11},{9,10},{10,... | collective-permute-start | bytes 1572872 | tf_op jit(solution)/shard_map/ppermute | solution.py:241
  17.3 32.8 %collective-permute-start.1 = (bf16[64,4096]{1,0:T(8,128)(2,1)S(1)}, bf16[64,4096]{1,0:T(8,128)(2,1)S(1)}, u32[]{:S(2)}, u32[]{:S(2)}) collective-permute-start(bf16[64,4096]{1,0:T(8,128)(2,1)S(1)} %collective-permute-done.c1), channel_id=1, source_target_pairs={{0,3},{1,2},{2,1},{3,0},{4,7},{5,6},{6,5},{7,4},{8,11},{9,10},{10,... | collective-permute-start | bytes 1572872 | tf_op jit(solution)/shard_map/ppermute | solution.py:241
  22.2 27.9 %all-to-all-start.1 = ((bf16[16,8,256]{2,1,0:T(8,128)(2,1)}), bf16[16,8,256]{2,1,0:T(8,128)(2,1)S(1)}, u32[]{:S(2)}, u32[]{:S(2)}) async-start(bf16[16,8,256]{2,1,0:T(8,128)(2,1)} %get-tuple-element.20), calls=%async_computation.1 | async-start | bytes 131072 | tf_op jit(solution)/shard_map/all_to_all | solution.py:272
  37.4 0.7 collective-permute-start.3
  52.3 17.4 %all-to-all-start.2 = ((bf16[16,16,256]{2,1,0:T(8,128)(2,1)}), bf16[16,16,256]{2,1,0:T(8,128)(2,1)S(1)}, u32[]{:S(2)}, u32[]{:S(2)}) async-start(bf16[16,16,256]{2,1,0:T(8,128)(2,1)} %get-tuple-element.25), calls=%async_computation.2 | async-start | bytes 262144 | tf_op jit(solution)/shard_map/all_to_all | solution.py:272
  55.9 6.1 %collective-permute-start.5 = (f32[8,256]{1,0:T(8,128)S(1)}, f32[8,256]{1,0:T(8,128)S(1)}, u32[]{:S(2)}, u32[]{:S(2)}) collective-permute-start(f32[8,256]{1,0:T(8,128)S(1)} %get-tuple-element.27.field.previous.f1), channel_id=1, source_target_pairs={{64,128},{192,256},{320,384},{128,64},{256,192},{384,320},{65,129}... | collective-permute-start | bytes 24584 | tf_op jit(solution)/shard_map/ppermute | solution.py:250
  56.6 6.3 %collective-permute-start.4 = (f32[8,256]{1,0:T(8,128)S(1)}, f32[8,256]{1,0:T(8,128)S(1)}, u32[]{:S(2)}, u32[]{:S(2)}) collective-permute-start(f32[8,256]{1,0:T(8,128)S(1)} %get-tuple-element.27.field.previous.f1), channel_id=1, source_target_pairs={{0,64},{64,0},{128,192},{192,128},{256,320},{320,256},{384,448},{4... | collective-permute-start | bytes 24584 | tf_op jit(solution)/shard_map/ppermute | solution.py:245
  71.2 20.2 %all-to-all-start.3 = ((bf16[16,16,256]{2,1,0:T(8,128)(2,1)}), bf16[16,16,256]{2,1,0:T(8,128)(2,1)S(1)}, u32[]{:S(2)}, u32[]{:S(2)}) async-start(bf16[16,16,256]{2,1,0:T(8,128)(2,1)} %get-tuple-element.28), calls=%async_computation.3 | async-start | bytes 262144 | tf_op jit(solution)/shard_map/all_to_all | solution.py:272
  76.6 5.7 %collective-permute-start.7 = (f32[8,256]{1,0:T(8,128)S(1)}, f32[8,256]{1,0:T(8,128)S(1)}, u32[]{:S(2)}, u32[]{:S(2)}) collective-permute-start(f32[8,256]{1,0:T(8,128)S(1)} %get-tuple-element.29.field.f2), channel_id=1, source_target_pairs={{64,128},{192,256},{320,384},{128,64},{256,192},{384,320},{65,129}... | collective-permute-start | bytes 24584 | tf_op jit(solution)/shard_map/ppermute | solution.py:250
  77.3 5.8 %collective-permute-start.6 = (f32[8,256]{1,0:T(8,128)S(1)}, f32[8,256]{1,0:T(8,128)S(1)}, u32[]{:S(2)}, u32[]{:S(2)}) collective-permute-start(f32[8,256]{1,0:T(8,128)S(1)} %get-tuple-element.29.field.f2), channel_id=1, source_target_pairs={{0,64},{64,0},{128,192},{192,128},{256,320},{320,256},{384,448},{4... | collective-permute-start | bytes 24584 | tf_op jit(solution)/shard_map/ppermute | solution.py:245

commit v14 on v13

--- a/solution.py
+++ b/solution.py
@@ -14,6 +14,7 @@
 NZ, NY, NX, NC = 16, 4, 4, 2
 B = 8
 H = 64
+FETCHES = 8
 W = NY * H
 F32 = jnp.float32
 BF16 = jnp.bfloat16
@@ -98,10 +99,20 @@
 
 
 def first_step(row_ref, own, parts, c1, c2, c3, diag, up, down, field, field_out, send, c0, arrived):
-    fetch = pltpu.make_async_copy(own, c0, arrived)
-    fetch.start()
+    rows = [pl.ds(k * H // FETCHES, H // FETCHES) for k in range(FETCHES)]
+    fetches = [
+        pltpu.make_async_copy(own.at[part], c0.at[part], arrived.at[k])
+        for k, part in enumerate(rows)
+    ]
+    for fetch in fetches:
+        fetch.start()
+
+    def wait():
+        for fetch in fetches:
+            fetch.wait()
+
     beside = up[...] + down[...]
-    out = next_field(parts, (c0, c1, c2, c3), field, None, diag, beside, fetch.wait)
+    out = next_field(parts, (c0, c1, c2, c3), field, None, diag, beside, wait)
     field_out[...] = out
     store_parts(send, out, row_ref[0] % NY)
 
@@ -276,7 +287,7 @@
                 first_step, (*outs, shape((H, NZ * W), BF16)), row, own, parts, *blocks[1:], diag, up, down, field,
                 smem=1,
                 hbm=1,
-                scratch=[pltpu.SemaphoreType.DMA],
+                scratch=[pltpu.SemaphoreType.DMA((FETCHES,))],
             )
         else:
             field, send = call(

time: 137 us -> 138 us (level)
  no operation moved by 1% of the time
where the time goes in v14:
time: 138 us; the launch traced here: 137 us
  starting transfers between devices  53.4 us (39%)
  blocking collectives  42.4 us (31%)
  waiting for transfers between devices  31.3 us (23%)
  Pallas kernels  7.79 us (6%)
    all_to_all x3, waiting for transfers between devices, on_device(): parts = lax.all_to_all(send, 'z', 0, 0, tiled=True)  27.1 us
    all_to_all x3, starting transfers between devices, on_device(): parts = lax.all_to_all(send, 'z', 0, 0, tiled=True)  24.2 us
    all_to_all x1, blocking collectives, on_device(): parts = lax.all_to_all(send, 'z', 0, 0, tiled=True)  16.9 us
    all_to_all x1, blocking collectives, on_device(): table = lax.all_to_all(table, 'z', 0, 0, tiled=True)  15.5 us
    ppermute x2, starting transfers between devices, even(): return lax.ppermute(field, ('x', 'c'), [(i, i ^ 1) for i in range(NX * NC)])  10.5 us
    all_to_all x1, blocking collectives, on_device(): packed = lax.all_to_all(packed, ('x', 'c'), 0, 0, tiled=True)  9.99 us
    ppermute x3, starting transfers between devices, swapped(): return lax.ppermute(array, 'y', [(y, y ^ mask) for y in range(NY)])  8.61 us
    all_to_all x1, starting transfers between devices, on_device(): packed = lax.all_to_all(packed, ('c', 'y'), 0, 0, tiled=True)  8.15 us
  transfers between devices with their start and end apart: 12, of which 6 were waited for; matrix products, arithmetic and copies ran while one was open for 1% of the time, Pallas kernels for 1%

profile of v14, /device:TPU:24, one launch (start us, length us, event | category | flops | bytes accessed | tf_op | source)
XLA Modules:
  0.0 137.0 jit_solution(9268567727686146017)
XLA Ops:
  0.6 0.0 copy-start
  0.6 2.7 %collective-permute-start = (bf16[64,4096]{1,0:T(8,128)(2,1)}, bf16[64,4096]{1,0:T(8,128)(2,1)S(1)}, u32[]{:S(2)}, u32[]{:S(2)}) collective-permute-start(bf16[64,4096]{1,0:T(8,128)(2,1)} %bitcast.6), channel_id=1, source_target_pairs={{0,1},{1,0},{2,3},{3,2},{4,5},{5,4},{6,7},{7,6},{8,9},{9,8},{10,11... | collective-permute-start | bytes 1572872 | tf_op jit(solution)/shard_map/ppermute | solution.py:252
  3.3 0.7 pad.1.clone
  4.0 0.0 copy-done
  4.0 0.6 broadcast_in_dim.21
  4.7 8.2 %all-to-all-start = ((f32[8,8,128]{2,1,0:T(8,128)}), f32[8,8,128]{2,1,0:T(8,128)S(1)}, u32[]{:S(2)}, u32[]{:S(2)}) async-start(f32[8,8,128]{2,1,0:T(8,128)} %broadcast_in_dim.21), calls=%async_computation | async-start | bytes 65536 | tf_op jit(solution)/shard_map/all_to_all | solution.py:269
  12.8 2.0 %collective-permute-start.2 = (bf16[64,4096]{1,0:T(8,128)(2,1)}, bf16[64,4096]{1,0:T(8,128)(2,1)S(1)}, u32[]{:S(2)}, u32[]{:S(2)}) collective-permute-start(bf16[64,4096]{1,0:T(8,128)(2,1)} %bitcast.7), channel_id=1, source_target_pairs={{0,3},{1,2},{2,1},{3,0},{4,7},{5,6},{6,5},{7,4},{8,11},{9,10},{10,... | collective-permute-start | bytes 1572872 | tf_op jit(solution)/shard_map/ppermute | solution.py:252
  14.8 2.5 %all-to-all-done.packed = f32[8,8,128]{2,1,0:T(8,128)S(1)} async-done(((f32[8,8,128]{2,1,0:T(8,128)}), f32[8,8,128]{2,1,0:T(8,128)S(1)}, u32[]{:S(2)}, u32[]{:S(2)}) %all-to-all-start) | async-done | bytes 32800 | tf_op jit(solution)/shard_map/all_to_all | solution.py:269
  17.3 0.0 collective-permute-done.c1
  17.3 4.0 %collective-permute-start.1 = (bf16[64,4096]{1,0:T(8,128)(2,1)S(1)}, bf16[64,4096]{1,0:T(8,128)(2,1)S(1)}, u32[]{:S(2)}, u32[]{:S(2)}) collective-permute-start(bf16[64,4096]{1,0:T(8,128)(2,1)S(1)} %collective-permute-done.c1), channel_id=1, source_target_pairs={{0,3},{1,2},{2,1},{3,0},{4,7},{5,6},{6,5},{7,4},{8,11},{9,10},{10,... | collective-permute-start | bytes 1572872 | tf_op jit(solution)/shard_map/ppermute | solution.py:252
  21.3 0.9 shard_map.50
  22.2 15.2 %all-to-all-start.1 = ((bf16[16,8,256]{2,1,0:T(8,128)(2,1)}), bf16[16,8,256]{2,1,0:T(8,128)(2,1)S(1)}, u32[]{:S(2)}, u32[]{:S(2)}) async-start(bf16[16,8,256]{2,1,0:T(8,128)(2,1)} %get-tuple-element.20), calls=%async_computation.1 | async-start | bytes 131072 | tf_op jit(solution)/shard_map/all_to_all | solution.py:283
  37.4 0.7 collective-permute-start.3
  38.1 0.0 collective-permute-done.2.c3
  38.1 0.0 collective-permute-done.3.down.d0
  38.1 12.0 %all-to-all-done.1.parts = bf16[16,8,256]{2,1,0:T(8,128)(2,1)S(1)} async-done(((bf16[16,8,256]{2,1,0:T(8,128)(2,1)}), bf16[16,8,256]{2,1,0:T(8,128)(2,1)S(1)}, u32[]{:S(2)}, u32[]{:S(2)}) %all-to-all-start.1) | async-done | bytes 65568 | tf_op jit(solution)/shard_map/all_to_all | solution.py:283
  50.1 0.0 collective-permute-done.1.c2
  50.1 2.7 %shard_map.51 = (f32[8,256]{1,0:T(8,128)S(1)}, bf16[16,16,256]{2,1,0:T(8,128)(2,1)}, bf16[64,4096]{1,0:T(8,128)(2,1)S(1)}) custom-call(s32[1]{0:T(128)} %bitcast.row_ref.plane_ref, bf16[64,4096]{1,0:T(8,128)(2,1)} %bitcast.8, bf16[16,8,256]{2,1,0:T(8,128)(2,1)S(1)} %all-to-all-done.1.parts, bf16[64,4096]{1,0:T(8,128)(2,1)S(1)} %collective-permute-done.c1, ...), custom_call_target="tpu_custom_call" | custom-call | tf_op jit(solution)/shard_map/pallas_call | solution.py:33
  52.8 3.6 %all-to-all-start.2 = ((bf16[16,16,256]{2,1,0:T(8,128)(2,1)}), bf16[16,16,256]{2,1,0:T(8,128)(2,1)S(1)}, u32[]{:S(2)}, u32[]{:S(2)}) async-start(bf16[16,16,256]{2,1,0:T(8,128)(2,1)} %get-tuple-element.25), calls=%async_computation.2 | async-start | bytes 262144 | tf_op jit(solution)/shard_map/all_to_all | solution.py:283
  56.4 0.7 collective-permute-start.5
  57.0 5.5 %collective-permute-start.4 = (f32[8,256]{1,0:T(8,128)S(1)}, f32[8,256]{1,0:T(8,128)S(1)}, u32[]{:S(2)}, u32[]{:S(2)}) collective-permute-start(f32[8,256]{1,0:T(8,128)S(1)} %get-tuple-element.27.field.previous.f1), channel_id=1, source_target_pairs={{0,64},{64,0},{128,192},{192,128},{256,320},{320,256},{384,448},{4... | collective-permute-start | bytes 24584 | tf_op jit(solution)/shard_map/ppermute | solution.py:256
  62.5 0.0 collective-permute-done.5.down.d1
  62.5 0.8 collective-permute-done.4.up.u1
  63.3 6.9 %all-to-all-done.2.parts = bf16[16,16,256]{2,1,0:T(8,128)(2,1)S(1)} async-done(((bf16[16,16,256]{2,1,0:T(8,128)(2,1)}), bf16[16,16,256]{2,1,0:T(8,128)(2,1)S(1)}, u32[]{:S(2)}, u32[]{:S(2)}) %all-to-all-start.2) | async-done | bytes 131104 | tf_op jit(solution)/shard_map/all_to_all | solution.py:283
  70.2 1.5 %shard_map.52 = (f32[8,256]{1,0:T(8,128)S(1)}, bf16[16,16,256]{2,1,0:T(8,128)(2,1)}) custom-call(s32[1]{0:T(128)} %bitcast.row_ref.plane_ref, bf16[16,16,256]{2,1,0:T(8,128)(2,1)S(1)} %all-to-all-done.2.parts, bf16[64,4096]{1,0:T(8,128)(2,1)S(1)} %get-tuple-element.26.c0, bf16[64,4096]{1,0:T(8,128)(2,1)S(1)} %collective-permute-done.c1, ...), custom_call_target="tpu_custom_call" | custom-call | tf_op jit(solution)/shard_map/pallas_call | solution.py:33
  71.6 5.5 %all-to-all-start.3 = ((bf16[16,16,256]{2,1,0:T(8,128)(2,1)}), bf16[16,16,256]{2,1,0:T(8,128)(2,1)S(1)}, u32[]{:S(2)}, u32[]{:S(2)}) async-start(bf16[16,16,256]{2,1,0:T(8,128)(2,1)} %get-tuple-element.28), calls=%async_computation.3 | async-start | bytes 262144 | tf_op jit(solution)/shard_map/all_to_all | solution.py:283
  77.1 0.7 collective-permute-start.7
  77.8 5.0 %collective-permute-start.6 = (f32[8,256]{1,0:T(8,128)S(1)}, f32[8,256]{1,0:T(8,128)S(1)}, u32[]{:S(2)}, u32[]{:S(2)}) collective-permute-start(f32[8,256]{1,0:T(8,128)S(1)} %get-tuple-element.29.field.f2), channel_id=1, source_target_pairs={{0,64},{64,0},{128,192},{192,128},{256,320},{320,256},{384,448},{4... | collective-permute-start | bytes 24584 | tf_op jit(solution)/shard_map/ppermute | solution.py:256
  82.8 0.0 collective-permute-done.7.down.d2
  82.8 0.8 collective-permute-done.6.up.u2
  83.6 8.2 %all-to-all-done.3.parts = bf16[16,16,256]{2,1,0:T(8,128)(2,1)S(1)} async-done(((bf16[16,16,256]{2,1,0:T(8,128)(2,1)}), bf16[16,16,256]{2,1,0:T(8,128)(2,1)S(1)}, u32[]{:S(2)}, u32[]{:S(2)}) %all-to-all-start.3) | async-done | bytes 131104 | tf_op jit(solution)/shard_map/all_to_all | solution.py:283
  91.8 0.8 shard_map.53
  92.6 16.9 %all_to_all.35.parts = bf16[16,8,256]{2,1,0:T(8,128)(2,1)S(1)} all-to-all(bf16[16,8,256]{2,1,0:T(8,128)(2,1)S(1)} %get-tuple-element.30), channel_id=1, replica_groups=mesh['x'=4,'c'=2,'z'=16,'y'=4] {'z'}, dimensions={0} | all-to-all | bytes 131072 | tf_op jit(solution)/shard_map/all_to_all | solution.py:297
  109.5 0.8 shard_map.54
  110.3 10.0 %all_to_all.36.packed = f32[8,8,640]{2,1,0:T(8,128)S(1)} all-to-all(f32[8,8,640]{2,1,0:T(8,128)S(1)} %shard_map.54), channel_id=1, replica_groups=mesh['x'=4,'c'=2,'z'=16,'y'=4] {'x','c'}, dimensions={0} | all-to-all | bytes 327680 | tf_op jit(solution)/shard_map/all_to_all | solution.py:303
  120.3 0.1 shard_map.55
  120.4 15.5 %all_to_all.37.tables = f32[16,8,128]{2,1,0:T(8,128)S(1)} all-to-all(f32[16,8,128]{2,1,0:T(8,128)S(1)} %get-tuple-element.32), channel_id=1, replica_groups=mesh['x'=4,'c'=2,'z'=16,'y'=4] {'z'}, dimensions={0} | all-to-all | bytes 131072 | tf_op jit(solution)/shard_map/all_to_all | solution.py:305
  135.9 1.1 shard_map.56
  (1 shorter events, 0.0 us)
Async XLA Ops:
  0.6 3.4 %copy-start = (f32[1,8,64]{2,1,0:T(8,128)S(1)}, f32[1,8,64]{2,1,0:T(8,128)}, u32[]{:S(2)}) copy-start(f32[1,8,64]{2,1,0:T(8,128)} %param.3) | copy-start | bytes 6148
  0.6 16.7 %collective-permute-start = (bf16[64,4096]{1,0:T(8,128)(2,1)}, bf16[64,4096]{1,0:T(8,128)(2,1)S(1)}, u32[]{:S(2)}, u32[]{:S(2)}) collective-permute-start(bf16[64,4096]{1,0:T(8,128)(2,1)} %bitcast.6), channel_id=1, source_target_pairs={{0,1},{1,0},{2,3},{3,2},{4,5},{5,4},{6,7},{7,6},{8,9},{9,8},{10,11... | collective-permute-start | bytes 1572872 | tf_op jit(solution)/shard_map/ppermute | solution.py:252
  4.7 12.7 %all-to-all-start = ((f32[8,8,128]{2,1,0:T(8,128)}), f32[8,8,128]{2,1,0:T(8,128)S(1)}, u32[]{:S(2)}, u32[]{:S(2)}) async-start(f32[8,8,128]{2,1,0:T(8,128)} %broadcast_in_dim.21), calls=%async_computation | async-start | bytes 65536 | tf_op jit(solution)/shard_map/all_to_all | solution.py:269
  12.8 25.3 %collective-permute-start.2 = (bf16[64,4096]{1,0:T(8,128)(2,1)}, bf16[64,4096]{1,0:T(8,128)(2,1)S(1)}, u32[]{:S(2)}, u32[]{:S(2)}) collective-permute-start(bf16[64,4096]{1,0:T(8,128)(2,1)} %bitcast.7), channel_id=1, source_target_pairs={{0,3},{1,2},{2,1},{3,0},{4,7},{5,6},{6,5},{7,4},{8,11},{9,10},{10,... | collective-permute-start | bytes 1572872 | tf_op jit(solution)/shard_map/ppermute | solution.py:252
  17.3 32.8 %collective-permute-start.1 = (bf16[64,4096]{1,0:T(8,128)(2,1)S(1)}, bf16[64,4096]{1,0:T(8,128)(2,1)S(1)}, u32[]{:S(2)}, u32[]{:S(2)}) collective-permute-start(bf16[64,4096]{1,0:T(8,128)(2,1)S(1)} %collective-permute-done.c1), channel_id=1, source_target_pairs={{0,3},{1,2},{2,1},{3,0},{4,7},{5,6},{6,5},{7,4},{8,11},{9,10},{10,... | collective-permute-start | bytes 1572872 | tf_op jit(solution)/shard_map/ppermute | solution.py:252
  22.2 27.9 %all-to-all-start.1 = ((bf16[16,8,256]{2,1,0:T(8,128)(2,1)}), bf16[16,8,256]{2,1,0:T(8,128)(2,1)S(1)}, u32[]{:S(2)}, u32[]{:S(2)}) async-start(bf16[16,8,256]{2,1,0:T(8,128)(2,1)} %get-tuple-element.20), calls=%async_computation.1 | async-start | bytes 131072 | tf_op jit(solution)/shard_map/all_to_all | solution.py:283
  37.4 0.7 collective-permute-start.3
  52.8 17.4 %all-to-all-start.2 = ((bf16[16,16,256]{2,1,0:T(8,128)(2,1)}), bf16[16,16,256]{2,1,0:T(8,128)(2,1)S(1)}, u32[]{:S(2)}, u32[]{:S(2)}) async-start(bf16[16,16,256]{2,1,0:T(8,128)(2,1)} %get-tuple-element.25), calls=%async_computation.2 | async-start | bytes 262144 | tf_op jit(solution)/shard_map/all_to_all | solution.py:283
  56.4 6.1 %collective-permute-start.5 = (f32[8,256]{1,0:T(8,128)S(1)}, f32[8,256]{1,0:T(8,128)S(1)}, u32[]{:S(2)}, u32[]{:S(2)}) collective-permute-start(f32[8,256]{1,0:T(8,128)S(1)} %get-tuple-element.27.field.previous.f1), channel_id=1, source_target_pairs={{64,128},{192,256},{320,384},{128,64},{256,192},{384,320},{65,129}... | collective-permute-start | bytes 24584 | tf_op jit(solution)/shard_map/ppermute | solution.py:261
  57.0 6.3 %collective-permute-start.4 = (f32[8,256]{1,0:T(8,128)S(1)}, f32[8,256]{1,0:T(8,128)S(1)}, u32[]{:S(2)}, u32[]{:S(2)}) collective-permute-start(f32[8,256]{1,0:T(8,128)S(1)} %get-tuple-element.27.field.previous.f1), channel_id=1, source_target_pairs={{0,64},{64,0},{128,192},{192,128},{256,320},{320,256},{384,448},{4... | collective-permute-start | bytes 24584 | tf_op jit(solution)/shard_map/ppermute | solution.py:256
  71.6 20.2 %all-to-all-start.3 = ((bf16[16,16,256]{2,1,0:T(8,128)(2,1)}), bf16[16,16,256]{2,1,0:T(8,128)(2,1)S(1)}, u32[]{:S(2)}, u32[]{:S(2)}) async-start(bf16[16,16,256]{2,1,0:T(8,128)(2,1)} %get-tuple-element.28), calls=%async_computation.3 | async-start | bytes 262144 | tf_op jit(solution)/shard_map/all_to_all | solution.py:283
  77.1 5.7 %collective-permute-start.7 = (f32[8,256]{1,0:T(8,128)S(1)}, f32[8,256]{1,0:T(8,128)S(1)}, u32[]{:S(2)}, u32[]{:S(2)}) collective-permute-start(f32[8,256]{1,0:T(8,128)S(1)} %get-tuple-element.29.field.f2), channel_id=1, source_target_pairs={{64,128},{192,256},{320,384},{128,64},{256,192},{384,320},{65,129}... | collective-permute-start | bytes 24584 | tf_op jit(solution)/shard_map/ppermute | solution.py:261
  77.8 5.8 %collective-permute-start.6 = (f32[8,256]{1,0:T(8,128)S(1)}, f32[8,256]{1,0:T(8,128)S(1)}, u32[]{:S(2)}, u32[]{:S(2)}) collective-permute-start(f32[8,256]{1,0:T(8,128)S(1)} %get-tuple-element.29.field.f2), channel_id=1, source_target_pairs={{0,64},{64,0},{128,192},{192,128},{256,320},{320,256},{384,448},{4... | collective-permute-start | bytes 24584 | tf_op jit(solution)/shard_map/ppermute | solution.py:256

commit v15 on v13

--- a/solution.py
+++ b/solution.py
@@ -56,19 +56,21 @@
         send[z] = parts
 
 
-def unpack(row_ref, packed, field_out, even_out, diag_out, send):
+def unpack(row_ref, packed, field_out, up_out, down_out, diag_out, send):
     row = row_ref[0] % NY
-    core = row_ref[0] // NY % NC
+    plane = row_ref[0] // NY
+    top = NX * NC - 1
 
     def wide(which, columns):
         return reorder(
             jnp.concatenate([packed[which * NY + y][:, columns] for y in range(NY)], axis=1), row
         )
 
-    field = wide(core, slice(0, H))
+    field = wide(plane, slice(0, H))
     field_out[...] = field
-    even_out[...] = wide(1 - core, slice(0, H))
-    diag_out[...] = wide(core, slice(H, 2 * H))
+    up_out[...] = jnp.where(plane > 0, wide(jnp.maximum(plane - 1, 0), slice(0, H)), 0.0)
+    down_out[...] = jnp.where(plane < top, wide(jnp.minimum(plane + 1, top), slice(0, H)), 0.0)
+    diag_out[...] = wide(plane, slice(H, 2 * H))
     store_parts(send, field, row)
 
 
@@ -254,20 +256,21 @@
     own = coupling[0]
     row = lax.axis_index(("x", "c", "y")).astype(jnp.int32).reshape(1)
     packed = jnp.concatenate([source[0], jnp.broadcast_to(diagonal, (B, H))], axis=1)
-    packed = jnp.broadcast_to(packed[None], (NC * NY, B, 128))
-    packed = lax.all_to_all(packed, ("c", "y"), 0, 0, tiled=True)
+    packed = jnp.broadcast_to(packed[None], (NX * NC * NY, B, 128))
+    packed = lax.all_to_all(packed, ("x", "c", "y"), 0, 0, tiled=True)
     by_1, by_3 = swapped(own, 1), swapped(own, 3)
     by_1, packed = lax.optimization_barrier((by_1, packed))
     blocks = [own, by_1, swapped(by_1, 3), by_3]
     shape = jax.ShapeDtypeStruct
     wide = shape((B, W), F32)
     sends = [shape((NZ, 2 * B if low else B, W), BF16) for low in WITH_LOW]
-    field, up, diag, send = call(unpack, (wide, wide, wide, sends[0]), row, packed, smem=1)
+    field, up, down, diag, send = call(
+        unpack, (wide, wide, wide, wide, sends[0]), row, packed, smem=1
+    )
     fields, beside = [field], []
     for k in range(STEPS - 1):
-        down = odd(field)
         if k > 0:
-            up = even(field)
+            up, down = even(field), odd(field)
         beside += [up, down]
         parts = lax.all_to_all(send, "z", 0, 0, tiled=True)
         outs = (wide, sends[k + 1])

time: 137 us -> 139 us (1.015)
  waiting for transfers between devices: 31.2 us -> 34.7 us
  starting transfers between devices: 53.4 us -> 51.2 us
    all_to_all x3, waiting for transfers between devices: 27.1 us -> 29 us  [on_device(): parts = lax.all_to_all(send, 'z', 0, 0, tiled=True)]
    all_to_all x1, waiting for transfers between devices: 2.54 us -> 4.14 us  [on_device(): packed = lax.all_to_all(packed, ('x', 'c', 'y'), 0, 0, tiled=True)]
  transfers between devices with their start and end apart: 12 -> 11, of which waited for: 6 -> 6; matrix products, arithmetic and copies ran while one was open for 1% -> 1% of each run, Pallas kernels for 1% -> 1%
where the time goes in v15:
time: 139 us; the launch traced here: 138 us
  starting transfers between devices  51.2 us (37%)
  blocking collectives  43.1 us (31%)
  waiting for transfers between devices  34.7 us (25%)
  Pallas kernels  7.3 us (5%)
    all_to_all x3, waiting for transfers between devices, on_device(): parts = lax.all_to_all(send, 'z', 0, 0, tiled=True)  29 us
    all_to_all x3, starting transfers between devices, on_device(): parts = lax.all_to_all(send, 'z', 0, 0, tiled=True)  23.5 us
    all_to_all x1, blocking collectives, on_device(): parts = lax.all_to_all(send, 'z', 0, 0, tiled=True)  17.2 us
    all_to_all x1, blocking collectives, on_device(): table = lax.all_to_all(table, 'z', 0, 0, tiled=True)  15.6 us
    all_to_all x1, blocking collectives, on_device(): packed = lax.all_to_all(packed, ('x', 'c'), 0, 0, tiled=True)  10.3 us
    ppermute x2, starting transfers between devices, even(): return lax.ppermute(field, ('x', 'c'), [(i, i ^ 1) for i in range(NX * NC)])  9.44 us
    ppermute x3, starting transfers between devices, swapped(): return lax.ppermute(array, 'y', [(y, y ^ mask) for y in range(NY)])  8.58 us
    all_to_all x1, starting transfers between devices, on_device(): packed = lax.all_to_all(packed, ('x', 'c', 'y'), 0, 0, tiled=True)  8.37 us
  transfers between devices with their start and end apart: 11, of which 6 were waited for; matrix products, arithmetic and copies ran while one was open for 1% of the time, Pallas kernels for 1%

profile of v15, /device:TPU:24, one launch (start us, length us, event | category | flops | bytes accessed | tf_op | source)
XLA Modules:
  0.0 138.5 jit_solution(15025225994010311039)
XLA Ops:
  0.6 0.0 copy-start
  0.6 2.7 %collective-permute-start = (bf16[64,4096]{1,0:T(8,128)(2,1)}, bf16[64,4096]{1,0:T(8,128)(2,1)S(1)}, u32[]{:S(2)}, u32[]{:S(2)}) collective-permute-start(bf16[64,4096]{1,0:T(8,128)(2,1)} %bitcast.6), channel_id=1, source_target_pairs={{0,1},{1,0},{2,3},{3,2},{4,5},{5,4},{6,7},{7,6},{8,9},{9,8},{10,11... | collective-permute-start | bytes 1572872 | tf_op jit(solution)/shard_map/ppermute | solution.py:243
  3.3 0.7 pad.1.clone
  4.0 0.0 copy-done
  4.0 0.7 broadcast_in_dim.21
  4.7 8.4 %all-to-all-start = ((f32[32,8,128]{2,1,0:T(8,128)}), f32[32,8,128]{2,1,0:T(8,128)S(1)}, u32[]{:S(2)}, u32[]{:S(2)}) async-start(f32[32,8,128]{2,1,0:T(8,128)} %broadcast_in_dim.21), calls=%async_computation | async-start | bytes 262144 | tf_op jit(solution)/shard_map/all_to_all | solution.py:260
  13.1 2.2 %collective-permute-start.2 = (bf16[64,4096]{1,0:T(8,128)(2,1)}, bf16[64,4096]{1,0:T(8,128)(2,1)S(1)}, u32[]{:S(2)}, u32[]{:S(2)}) collective-permute-start(bf16[64,4096]{1,0:T(8,128)(2,1)} %bitcast.7), channel_id=1, source_target_pairs={{0,3},{1,2},{2,1},{3,0},{4,7},{5,6},{6,5},{7,4},{8,11},{9,10},{10,... | collective-permute-start | bytes 1572872 | tf_op jit(solution)/shard_map/ppermute | solution.py:243
  15.3 4.1 %all-to-all-done.packed = f32[32,8,128]{2,1,0:T(8,128)S(1)} async-done(((f32[32,8,128]{2,1,0:T(8,128)}), f32[32,8,128]{2,1,0:T(8,128)S(1)}, u32[]{:S(2)}, u32[]{:S(2)}) %all-to-all-start) | async-done | bytes 131104 | tf_op jit(solution)/shard_map/all_to_all | solution.py:260
  19.5 0.0 collective-permute-done.c1
  19.5 3.7 %collective-permute-start.1 = (bf16[64,4096]{1,0:T(8,128)(2,1)S(1)}, bf16[64,4096]{1,0:T(8,128)(2,1)S(1)}, u32[]{:S(2)}, u32[]{:S(2)}) collective-permute-start(bf16[64,4096]{1,0:T(8,128)(2,1)S(1)} %collective-permute-done.c1), channel_id=1, source_target_pairs={{0,3},{1,2},{2,1},{3,0},{4,7},{5,6},{6,5},{7,4},{8,11},{9,10},{10,... | collective-permute-start | bytes 1572872 | tf_op jit(solution)/shard_map/ppermute | solution.py:243
  23.2 0.9 shard_map.50
  24.0 14.6 %all-to-all-start.1 = ((bf16[16,8,256]{2,1,0:T(8,128)(2,1)}), bf16[16,8,256]{2,1,0:T(8,128)(2,1)S(1)}, u32[]{:S(2)}, u32[]{:S(2)}) async-start(bf16[16,8,256]{2,1,0:T(8,128)(2,1)} %get-tuple-element.21), calls=%async_computation.1 | async-start | bytes 131072 | tf_op jit(solution)/shard_map/all_to_all | solution.py:275
  38.6 0.0 collective-permute-done.2.c3
  38.6 12.7 %all-to-all-done.1.parts = bf16[16,8,256]{2,1,0:T(8,128)(2,1)S(1)} async-done(((bf16[16,8,256]{2,1,0:T(8,128)(2,1)}), bf16[16,8,256]{2,1,0:T(8,128)(2,1)S(1)}, u32[]{:S(2)}, u32[]{:S(2)}) %all-to-all-start.1) | async-done | bytes 65568 | tf_op jit(solution)/shard_map/all_to_all | solution.py:275
  51.3 0.0 collective-permute-done.1.c2
  51.3 2.2 %shard_map.51 = (f32[8,256]{1,0:T(8,128)S(1)}, bf16[16,16,256]{2,1,0:T(8,128)(2,1)}, bf16[64,4096]{1,0:T(8,128)(2,1)S(1)}) custom-call(s32[1]{0:T(128)} %bitcast.row_ref.plane_ref, bf16[64,4096]{1,0:T(8,128)(2,1)} %bitcast.8, bf16[16,8,256]{2,1,0:T(8,128)(2,1)S(1)} %all-to-all-done.1.parts, bf16[64,4096]{1,0:T(8,128)(2,1)S(1)} %collective-permute-done.c1, ...), custom_call_target="tpu_custom_call" | custom-call | tf_op jit(solution)/shard_map/pallas_call | solution.py:32
  53.5 5.0 %all-to-all-start.2 = ((bf16[16,16,256]{2,1,0:T(8,128)(2,1)}), bf16[16,16,256]{2,1,0:T(8,128)(2,1)S(1)}, u32[]{:S(2)}, u32[]{:S(2)}) async-start(bf16[16,16,256]{2,1,0:T(8,128)(2,1)} %get-tuple-element.27), calls=%async_computation.2 | async-start | bytes 262144 | tf_op jit(solution)/shard_map/all_to_all | solution.py:275
  58.5 0.7 collective-permute-start.4
  59.2 4.7 %collective-permute-start.3 = (f32[8,256]{1,0:T(8,128)S(1)}, f32[8,256]{1,0:T(8,128)S(1)}, u32[]{:S(2)}, u32[]{:S(2)}) collective-permute-start(f32[8,256]{1,0:T(8,128)S(1)} %get-tuple-element.29.field.previous.f1), channel_id=1, source_target_pairs={{0,64},{64,0},{128,192},{192,128},{256,320},{320,256},{384,448},{4... | collective-permute-start | bytes 24584 | tf_op jit(solution)/shard_map/ppermute | solution.py:247
  63.9 0.0 collective-permute-done.4.down.d1
  63.9 0.8 collective-permute-done.3.up.u1
  64.7 8.1 %all-to-all-done.2.parts = bf16[16,16,256]{2,1,0:T(8,128)(2,1)S(1)} async-done(((bf16[16,16,256]{2,1,0:T(8,128)(2,1)}), bf16[16,16,256]{2,1,0:T(8,128)(2,1)S(1)}, u32[]{:S(2)}, u32[]{:S(2)}) %all-to-all-start.2) | async-done | bytes 131104 | tf_op jit(solution)/shard_map/all_to_all | solution.py:275
  72.8 1.5 %shard_map.52 = (f32[8,256]{1,0:T(8,128)S(1)}, bf16[16,16,256]{2,1,0:T(8,128)(2,1)}) custom-call(s32[1]{0:T(128)} %bitcast.row_ref.plane_ref, bf16[16,16,256]{2,1,0:T(8,128)(2,1)S(1)} %all-to-all-done.2.parts, bf16[64,4096]{1,0:T(8,128)(2,1)S(1)} %get-tuple-element.28.c0, bf16[64,4096]{1,0:T(8,128)(2,1)S(1)} %collective-permute-done.c1, ...), custom_call_target="tpu_custom_call" | custom-call | tf_op jit(solution)/shard_map/pallas_call | solution.py:32
  74.3 3.9 %all-to-all-start.3 = ((bf16[16,16,256]{2,1,0:T(8,128)(2,1)}), bf16[16,16,256]{2,1,0:T(8,128)(2,1)S(1)}, u32[]{:S(2)}, u32[]{:S(2)}) async-start(bf16[16,16,256]{2,1,0:T(8,128)(2,1)} %get-tuple-element.30), calls=%async_computation.3 | async-start | bytes 262144 | tf_op jit(solution)/shard_map/all_to_all | solution.py:275
  78.2 0.7 collective-permute-start.6
  78.9 4.7 %collective-permute-start.5 = (f32[8,256]{1,0:T(8,128)S(1)}, f32[8,256]{1,0:T(8,128)S(1)}, u32[]{:S(2)}, u32[]{:S(2)}) collective-permute-start(f32[8,256]{1,0:T(8,128)S(1)} %get-tuple-element.31.field.f2), channel_id=1, source_target_pairs={{0,64},{64,0},{128,192},{192,128},{256,320},{320,256},{384,448},{4... | collective-permute-start | bytes 24584 | tf_op jit(solution)/shard_map/ppermute | solution.py:247
  83.6 0.0 collective-permute-done.6.down.d2
  83.6 0.8 collective-permute-done.5.up.u2
  84.4 8.2 %all-to-all-done.3.parts = bf16[16,16,256]{2,1,0:T(8,128)(2,1)S(1)} async-done(((bf16[16,16,256]{2,1,0:T(8,128)(2,1)}), bf16[16,16,256]{2,1,0:T(8,128)(2,1)S(1)}, u32[]{:S(2)}, u32[]{:S(2)}) %all-to-all-start.3) | async-done | bytes 131104 | tf_op jit(solution)/shard_map/all_to_all | solution.py:275
  92.6 0.8 shard_map.53
  93.4 17.2 %all_to_all.35.parts = bf16[16,8,256]{2,1,0:T(8,128)(2,1)S(1)} all-to-all(bf16[16,8,256]{2,1,0:T(8,128)(2,1)S(1)} %get-tuple-element.32), channel_id=1, replica_groups=mesh['x'=4,'c'=2,'z'=16,'y'=4] {'z'}, dimensions={0} | all-to-all | bytes 131072 | tf_op jit(solution)/shard_map/all_to_all | solution.py:289
  110.6 0.8 shard_map.54
  111.4 10.3 %all_to_all.36.packed = f32[8,8,640]{2,1,0:T(8,128)S(1)} all-to-all(f32[8,8,640]{2,1,0:T(8,128)S(1)} %shard_map.54), channel_id=1, replica_groups=mesh['x'=4,'c'=2,'z'=16,'y'=4] {'x','c'}, dimensions={0} | all-to-all | bytes 327680 | tf_op jit(solution)/shard_map/all_to_all | solution.py:295
  121.7 0.1 shard_map.55
  121.8 15.6 %all_to_all.37.tables = f32[16,8,128]{2,1,0:T(8,128)S(1)} all-to-all(f32[16,8,128]{2,1,0:T(8,128)S(1)} %get-tuple-element.34), channel_id=1, replica_groups=mesh['x'=4,'c'=2,'z'=16,'y'=4] {'z'}, dimensions={0} | all-to-all | bytes 131072 | tf_op jit(solution)/shard_map/all_to_all | solution.py:297
  137.3 1.1 shard_map.56
  (1 shorter events, 0.0 us)
Async XLA Ops:
  0.6 3.4 %copy-start = (f32[1,8,64]{2,1,0:T(8,128)S(1)}, f32[1,8,64]{2,1,0:T(8,128)}, u32[]{:S(2)}) copy-start(f32[1,8,64]{2,1,0:T(8,128)} %param.3) | copy-start | bytes 6148
  0.6 18.8 %collective-permute-start = (bf16[64,4096]{1,0:T(8,128)(2,1)}, bf16[64,4096]{1,0:T(8,128)(2,1)S(1)}, u32[]{:S(2)}, u32[]{:S(2)}) collective-permute-start(bf16[64,4096]{1,0:T(8,128)(2,1)} %bitcast.6), channel_id=1, source_target_pairs={{0,1},{1,0},{2,3},{3,2},{4,5},{5,4},{6,7},{7,6},{8,9},{9,8},{10,11... | collective-permute-start | bytes 1572872 | tf_op jit(solution)/shard_map/ppermute | solution.py:243
  4.7 14.8 %all-to-all-start = ((f32[32,8,128]{2,1,0:T(8,128)}), f32[32,8,128]{2,1,0:T(8,128)S(1)}, u32[]{:S(2)}, u32[]{:S(2)}) async-start(f32[32,8,128]{2,1,0:T(8,128)} %broadcast_in_dim.21), calls=%async_computation | async-start | bytes 262144 | tf_op jit(solution)/shard_map/all_to_all | solution.py:260
  13.1 25.5 %collective-permute-start.2 = (bf16[64,4096]{1,0:T(8,128)(2,1)}, bf16[64,4096]{1,0:T(8,128)(2,1)S(1)}, u32[]{:S(2)}, u32[]{:S(2)}) collective-permute-start(bf16[64,4096]{1,0:T(8,128)(2,1)} %bitcast.7), channel_id=1, source_target_pairs={{0,3},{1,2},{2,1},{3,0},{4,7},{5,6},{6,5},{7,4},{8,11},{9,10},{10,... | collective-permute-start | bytes 1572872 | tf_op jit(solution)/shard_map/ppermute | solution.py:243
  19.5 31.9 %collective-permute-start.1 = (bf16[64,4096]{1,0:T(8,128)(2,1)S(1)}, bf16[64,4096]{1,0:T(8,128)(2,1)S(1)}, u32[]{:S(2)}, u32[]{:S(2)}) collective-permute-start(bf16[64,4096]{1,0:T(8,128)(2,1)S(1)} %collective-permute-done.c1), channel_id=1, source_target_pairs={{0,3},{1,2},{2,1},{3,0},{4,7},{5,6},{6,5},{7,4},{8,11},{9,10},{10,... | collective-permute-start | bytes 1572872 | tf_op jit(solution)/shard_map/ppermute | solution.py:243
  24.0 27.3 %all-to-all-start.1 = ((bf16[16,8,256]{2,1,0:T(8,128)(2,1)}), bf16[16,8,256]{2,1,0:T(8,128)(2,1)S(1)}, u32[]{:S(2)}, u32[]{:S(2)}) async-start(bf16[16,8,256]{2,1,0:T(8,128)(2,1)} %get-tuple-element.21), calls=%async_computation.1 | async-start | bytes 131072 | tf_op jit(solution)/shard_map/all_to_all | solution.py:275
  53.5 19.3 %all-to-all-start.2 = ((bf16[16,16,256]{2,1,0:T(8,128)(2,1)}), bf16[16,16,256]{2,1,0:T(8,128)(2,1)S(1)}, u32[]{:S(2)}, u32[]{:S(2)}) async-start(bf16[16,16,256]{2,1,0:T(8,128)(2,1)} %get-tuple-element.27), calls=%async_computation.2 | async-start | bytes 262144 | tf_op jit(solution)/shard_map/all_to_all | solution.py:275
  58.5 5.4 %collective-permute-start.4 = (f32[8,256]{1,0:T(8,128)S(1)}, f32[8,256]{1,0:T(8,128)S(1)}, u32[]{:S(2)}, u32[]{:S(2)}) collective-permute-start(f32[8,256]{1,0:T(8,128)S(1)} %get-tuple-element.29.field.previous.f1), channel_id=1, source_target_pairs={{64,128},{192,256},{320,384},{128,64},{256,192},{384,320},{65,129}... | collective-permute-start | bytes 24584 | tf_op jit(solution)/shard_map/ppermute | solution.py:252
  59.2 5.5 %collective-permute-start.3 = (f32[8,256]{1,0:T(8,128)S(1)}, f32[8,256]{1,0:T(8,128)S(1)}, u32[]{:S(2)}, u32[]{:S(2)}) collective-permute-start(f32[8,256]{1,0:T(8,128)S(1)} %get-tuple-element.29.field.previous.f1), channel_id=1, source_target_pairs={{0,64},{64,0},{128,192},{192,128},{256,320},{320,256},{384,448},{4... | collective-permute-start | bytes 24584 | tf_op jit(solution)/shard_map/ppermute | solution.py:247
  74.3 18.3 %all-to-all-start.3 = ((bf16[16,16,256]{2,1,0:T(8,128)(2,1)}), bf16[16,16,256]{2,1,0:T(8,128)(2,1)S(1)}, u32[]{:S(2)}, u32[]{:S(2)}) async-start(bf16[16,16,256]{2,1,0:T(8,128)(2,1)} %get-tuple-element.30), calls=%async_computation.3 | async-start | bytes 262144 | tf_op jit(solution)/shard_map/all_to_all | solution.py:275
  78.2 5.4 %collective-permute-start.6 = (f32[8,256]{1,0:T(8,128)S(1)}, f32[8,256]{1,0:T(8,128)S(1)}, u32[]{:S(2)}, u32[]{:S(2)}) collective-permute-start(f32[8,256]{1,0:T(8,128)S(1)} %get-tuple-element.31.field.f2), channel_id=1, source_target_pairs={{64,128},{192,256},{320,384},{128,64},{256,192},{384,320},{65,129}... | collective-permute-start | bytes 24584 | tf_op jit(solution)/shard_map/ppermute | solution.py:252
  78.9 5.6 %collective-permute-start.5 = (f32[8,256]{1,0:T(8,128)S(1)}, f32[8,256]{1,0:T(8,128)S(1)}, u32[]{:S(2)}, u32[]{:S(2)}) collective-permute-start(f32[8,256]{1,0:T(8,128)S(1)} %get-tuple-element.31.field.f2), channel_id=1, source_target_pairs={{0,64},{64,0},{128,192},{192,128},{256,320},{320,256},{384,448},{4... | collective-permute-start | bytes 24584 | tf_op jit(solution)/shard_map/ppermute | solution.py:247

commit v16 on v13

--- a/solution.py
+++ b/solution.py
@@ -9,7 +9,7 @@
 CENTRE = 6.75
 SCALE = 32.0
 LINK = (6.5**2 / 12 + 2.0) / SCALE
-WITH_LOW = (False, True, True, False)
+WITH_LOW = (False, True, False, False)
 PAIRS = [(i, j) for j in range(STEPS + 1) for i in range(j + 1)]
 NZ, NY, NX, NC = 16, 4, 4, 2
 B = 8

time: 137 us -> 136 us (level)
  waiting for transfers between devices: 31.2 us -> 29.6 us
    all_to_all x3, waiting for transfers between devices: 27.1 us -> 25.4 us  [on_device(): parts = lax.all_to_all(send, 'z', 0, 0, tiled=True)]
    all_to_all x1, blocking collectives: 16.9 us -> 18.4 us  [on_device(): parts = lax.all_to_all(send, 'z', 0, 0, tiled=True)]
where the time goes in v16:
time: 136 us; the launch traced here: 135 us
  starting transfers between devices  53.4 us (39%)
  blocking collectives  42.9 us (32%)
  waiting for transfers between devices  29.6 us (22%)
  Pallas kernels  7.29 us (5%)
    all_to_all x3, waiting for transfers between devices, on_device(): parts = lax.all_to_all(send, 'z', 0, 0, tiled=True)  25.4 us
    all_to_all x3, starting transfers between devices, on_device(): parts = lax.all_to_all(send, 'z', 0, 0, tiled=True)  24.2 us
    all_to_all x1, blocking collectives, on_device(): parts = lax.all_to_all(send, 'z', 0, 0, tiled=True)  18.4 us
    all_to_all x1, blocking collectives, on_device(): table = lax.all_to_all(table, 'z', 0, 0, tiled=True)  15.6 us
    ppermute x2, starting transfers between devices, even(): return lax.ppermute(field, ('x', 'c'), [(i, i ^ 1) for i in range(NX * NC)])  10.5 us
    all_to_all x1, blocking collectives, on_device(): packed = lax.all_to_all(packed, ('x', 'c'), 0, 0, tiled=True)  8.89 us
    ppermute x3, starting transfers between devices, swapped(): return lax.ppermute(array, 'y', [(y, y ^ mask) for y in range(NY)])  8.61 us
    all_to_all x1, starting transfers between devices, on_device(): packed = lax.all_to_all(packed, ('c', 'y'), 0, 0, tiled=True)  8.15 us
  transfers between devices with their start and end apart: 12, of which 6 were waited for; matrix products, arithmetic and copies ran while one was open for 1% of the time, Pallas kernels for 1%

profile of v16, /device:TPU:24, one launch (start us, length us, event | category | flops | bytes accessed | tf_op | source)
XLA Modules:
  0.0 135.4 jit_solution(17067447683514111315)
XLA Ops:
  0.6 0.0 copy-start
  0.6 2.7 %collective-permute-start = (bf16[64,4096]{1,0:T(8,128)(2,1)}, bf16[64,4096]{1,0:T(8,128)(2,1)S(1)}, u32[]{:S(2)}, u32[]{:S(2)}) collective-permute-start(bf16[64,4096]{1,0:T(8,128)(2,1)} %bitcast.6), channel_id=1, source_target_pairs={{0,1},{1,0},{2,3},{3,2},{4,5},{5,4},{6,7},{7,6},{8,9},{9,8},{10,11... | collective-permute-start | bytes 1572872 | tf_op jit(solution)/shard_map/ppermute | solution.py:241
  3.3 0.7 pad.1.clone
  4.0 0.0 copy-done
  4.0 0.6 broadcast_in_dim.21
  4.7 8.2 %all-to-all-start = ((f32[8,8,128]{2,1,0:T(8,128)}), f32[8,8,128]{2,1,0:T(8,128)S(1)}, u32[]{:S(2)}, u32[]{:S(2)}) async-start(f32[8,8,128]{2,1,0:T(8,128)} %broadcast_in_dim.21), calls=%async_computation | async-start | bytes 65536 | tf_op jit(solution)/shard_map/all_to_all | solution.py:258
  12.8 2.0 %collective-permute-start.2 = (bf16[64,4096]{1,0:T(8,128)(2,1)}, bf16[64,4096]{1,0:T(8,128)(2,1)S(1)}, u32[]{:S(2)}, u32[]{:S(2)}) collective-permute-start(bf16[64,4096]{1,0:T(8,128)(2,1)} %bitcast.7), channel_id=1, source_target_pairs={{0,3},{1,2},{2,1},{3,0},{4,7},{5,6},{6,5},{7,4},{8,11},{9,10},{10,... | collective-permute-start | bytes 1572872 | tf_op jit(solution)/shard_map/ppermute | solution.py:241
  14.8 2.5 %all-to-all-done.packed = f32[8,8,128]{2,1,0:T(8,128)S(1)} async-done(((f32[8,8,128]{2,1,0:T(8,128)}), f32[8,8,128]{2,1,0:T(8,128)S(1)}, u32[]{:S(2)}, u32[]{:S(2)}) %all-to-all-start) | async-done | bytes 32800 | tf_op jit(solution)/shard_map/all_to_all | solution.py:258
  17.3 0.0 collective-permute-done.c1
  17.3 4.0 %collective-permute-start.1 = (bf16[64,4096]{1,0:T(8,128)(2,1)S(1)}, bf16[64,4096]{1,0:T(8,128)(2,1)S(1)}, u32[]{:S(2)}, u32[]{:S(2)}) collective-permute-start(bf16[64,4096]{1,0:T(8,128)(2,1)S(1)} %collective-permute-done.c1), channel_id=1, source_target_pairs={{0,3},{1,2},{2,1},{3,0},{4,7},{5,6},{6,5},{7,4},{8,11},{9,10},{10,... | collective-permute-start | bytes 1572872 | tf_op jit(solution)/shard_map/ppermute | solution.py:241
  21.3 0.9 shard_map.50
  22.2 15.2 %all-to-all-start.1 = ((bf16[16,8,256]{2,1,0:T(8,128)(2,1)}), bf16[16,8,256]{2,1,0:T(8,128)(2,1)S(1)}, u32[]{:S(2)}, u32[]{:S(2)}) async-start(bf16[16,8,256]{2,1,0:T(8,128)(2,1)} %get-tuple-element.20), calls=%async_computation.1 | async-start | bytes 131072 | tf_op jit(solution)/shard_map/all_to_all | solution.py:272
  37.4 0.7 collective-permute-start.3
  38.1 0.0 collective-permute-done.2.c3
  38.1 0.0 collective-permute-done.3.down.d0
  38.1 12.0 %all-to-all-done.1.parts = bf16[16,8,256]{2,1,0:T(8,128)(2,1)S(1)} async-done(((bf16[16,8,256]{2,1,0:T(8,128)(2,1)}), bf16[16,8,256]{2,1,0:T(8,128)(2,1)S(1)}, u32[]{:S(2)}, u32[]{:S(2)}) %all-to-all-start.1) | async-done | bytes 65568 | tf_op jit(solution)/shard_map/all_to_all | solution.py:272
  50.1 0.0 collective-permute-done.1.c2
  50.1 2.2 %shard_map.51 = (f32[8,256]{1,0:T(8,128)S(1)}, bf16[16,16,256]{2,1,0:T(8,128)(2,1)}, bf16[64,4096]{1,0:T(8,128)(2,1)S(1)}) custom-call(s32[1]{0:T(128)} %bitcast.row_ref.plane_ref, bf16[64,4096]{1,0:T(8,128)(2,1)} %bitcast.8, bf16[16,8,256]{2,1,0:T(8,128)(2,1)S(1)} %all-to-all-done.1.parts, bf16[64,4096]{1,0:T(8,128)(2,1)S(1)} %collective-permute-done.c1, ...), custom_call_target="tpu_custom_call" | custom-call | tf_op jit(solution)/shard_map/pallas_call | solution.py:32
  52.3 3.6 %all-to-all-start.2 = ((bf16[16,16,256]{2,1,0:T(8,128)(2,1)}), bf16[16,16,256]{2,1,0:T(8,128)(2,1)S(1)}, u32[]{:S(2)}, u32[]{:S(2)}) async-start(bf16[16,16,256]{2,1,0:T(8,128)(2,1)} %get-tuple-element.25), calls=%async_computation.2 | async-start | bytes 262144 | tf_op jit(solution)/shard_map/all_to_all | solution.py:272
  55.9 0.7 collective-permute-start.5
  56.6 5.5 %collective-permute-start.4 = (f32[8,256]{1,0:T(8,128)S(1)}, f32[8,256]{1,0:T(8,128)S(1)}, u32[]{:S(2)}, u32[]{:S(2)}) collective-permute-start(f32[8,256]{1,0:T(8,128)S(1)} %get-tuple-element.27.field.previous.f1), channel_id=1, source_target_pairs={{0,64},{64,0},{128,192},{192,128},{256,320},{320,256},{384,448},{4... | collective-permute-start | bytes 24584 | tf_op jit(solution)/shard_map/ppermute | solution.py:245
  62.0 0.0 collective-permute-done.5.down.d1
  62.0 0.8 collective-permute-done.4.up.u1
  62.8 6.9 %all-to-all-done.2.parts = bf16[16,16,256]{2,1,0:T(8,128)(2,1)S(1)} async-done(((bf16[16,16,256]{2,1,0:T(8,128)(2,1)}), bf16[16,16,256]{2,1,0:T(8,128)(2,1)S(1)}, u32[]{:S(2)}, u32[]{:S(2)}) %all-to-all-start.2) | async-done | bytes 131104 | tf_op jit(solution)/shard_map/all_to_all | solution.py:272
  69.7 1.4 %shard_map.52 = (f32[8,256]{1,0:T(8,128)S(1)}, bf16[16,8,256]{2,1,0:T(8,128)(2,1)}) custom-call(s32[1]{0:T(128)} %bitcast.row_ref.plane_ref, bf16[16,16,256]{2,1,0:T(8,128)(2,1)S(1)} %all-to-all-done.2.parts, bf16[64,4096]{1,0:T(8,128)(2,1)S(1)} %get-tuple-element.26.c0, bf16[64,4096]{1,0:T(8,128)(2,1)S(1)} %collective-permute-done.c1, ...), custom_call_target="tpu_custom_call" | custom-call | tf_op jit(solution)/shard_map/pallas_call | solution.py:32
  71.1 5.5 %all-to-all-start.3 = ((bf16[16,8,256]{2,1,0:T(8,128)(2,1)}), bf16[16,8,256]{2,1,0:T(8,128)(2,1)S(1)}, u32[]{:S(2)}, u32[]{:S(2)}) async-start(bf16[16,8,256]{2,1,0:T(8,128)(2,1)} %get-tuple-element.28), calls=%async_computation.3 | async-start | bytes 131072 | tf_op jit(solution)/shard_map/all_to_all | solution.py:272
  76.6 0.7 collective-permute-start.7
  77.3 5.0 %collective-permute-start.6 = (f32[8,256]{1,0:T(8,128)S(1)}, f32[8,256]{1,0:T(8,128)S(1)}, u32[]{:S(2)}, u32[]{:S(2)}) collective-permute-start(f32[8,256]{1,0:T(8,128)S(1)} %get-tuple-element.29.field.f2), channel_id=1, source_target_pairs={{0,64},{64,0},{128,192},{192,128},{256,320},{320,256},{384,448},{4... | collective-permute-start | bytes 24584 | tf_op jit(solution)/shard_map/ppermute | solution.py:245
  82.3 0.0 collective-permute-done.7.down.d2
  82.3 0.8 collective-permute-done.6.up.u2
  83.1 6.5 %all-to-all-done.3.parts = bf16[16,8,256]{2,1,0:T(8,128)(2,1)S(1)} async-done(((bf16[16,8,256]{2,1,0:T(8,128)(2,1)}), bf16[16,8,256]{2,1,0:T(8,128)(2,1)S(1)}, u32[]{:S(2)}, u32[]{:S(2)}) %all-to-all-start.3) | async-done | bytes 65568 | tf_op jit(solution)/shard_map/all_to_all | solution.py:272
  89.6 0.8 shard_map.53
  90.4 18.4 %all_to_all.35.parts = bf16[16,8,256]{2,1,0:T(8,128)(2,1)S(1)} all-to-all(bf16[16,8,256]{2,1,0:T(8,128)(2,1)S(1)} %get-tuple-element.30), channel_id=1, replica_groups=mesh['x'=4,'c'=2,'z'=16,'y'=4] {'z'}, dimensions={0} | all-to-all | bytes 131072 | tf_op jit(solution)/shard_map/all_to_all | solution.py:286
  108.8 0.8 shard_map.54
  109.6 8.9 %all_to_all.36.packed = f32[8,8,640]{2,1,0:T(8,128)S(1)} all-to-all(f32[8,8,640]{2,1,0:T(8,128)S(1)} %shard_map.54), channel_id=1, replica_groups=mesh['x'=4,'c'=2,'z'=16,'y'=4] {'x','c'}, dimensions={0} | all-to-all | bytes 327680 | tf_op jit(solution)/shard_map/all_to_all | solution.py:292
  118.5 0.1 shard_map.55
  118.6 15.6 %all_to_all.37.tables = f32[16,8,128]{2,1,0:T(8,128)S(1)} all-to-all(f32[16,8,128]{2,1,0:T(8,128)S(1)} %get-tuple-element.32), channel_id=1, replica_groups=mesh['x'=4,'c'=2,'z'=16,'y'=4] {'z'}, dimensions={0} | all-to-all | bytes 131072 | tf_op jit(solution)/shard_map/all_to_all | solution.py:294
  134.3 1.1 shard_map.56
  (1 shorter events, 0.0 us)
Async XLA Ops:
  0.6 3.4 %copy-start = (f32[1,8,64]{2,1,0:T(8,128)S(1)}, f32[1,8,64]{2,1,0:T(8,128)}, u32[]{:S(2)}) copy-start(f32[1,8,64]{2,1,0:T(8,128)} %param.3) | copy-start | bytes 6148
  0.6 16.7 %collective-permute-start = (bf16[64,4096]{1,0:T(8,128)(2,1)}, bf16[64,4096]{1,0:T(8,128)(2,1)S(1)}, u32[]{:S(2)}, u32[]{:S(2)}) collective-permute-start(bf16[64,4096]{1,0:T(8,128)(2,1)} %bitcast.6), channel_id=1, source_target_pairs={{0,1},{1,0},{2,3},{3,2},{4,5},{5,4},{6,7},{7,6},{8,9},{9,8},{10,11... | collective-permute-start | bytes 1572872 | tf_op jit(solution)/shard_map/ppermute | solution.py:241
  4.7 12.7 %all-to-all-start = ((f32[8,8,128]{2,1,0:T(8,128)}), f32[8,8,128]{2,1,0:T(8,128)S(1)}, u32[]{:S(2)}, u32[]{:S(2)}) async-start(f32[8,8,128]{2,1,0:T(8,128)} %broadcast_in_dim.21), calls=%async_computation | async-start | bytes 65536 | tf_op jit(solution)/shard_map/all_to_all | solution.py:258
  12.8 25.3 %collective-permute-start.2 = (bf16[64,4096]{1,0:T(8,128)(2,1)}, bf16[64,4096]{1,0:T(8,128)(2,1)S(1)}, u32[]{:S(2)}, u32[]{:S(2)}) collective-permute-start(bf16[64,4096]{1,0:T(8,128)(2,1)} %bitcast.7), channel_id=1, source_target_pairs={{0,3},{1,2},{2,1},{3,0},{4,7},{5,6},{6,5},{7,4},{8,11},{9,10},{10,... | collective-permute-start | bytes 1572872 | tf_op jit(solution)/shard_map/ppermute | solution.py:241
  17.3 32.8 %collective-permute-start.1 = (bf16[64,4096]{1,0:T(8,128)(2,1)S(1)}, bf16[64,4096]{1,0:T(8,128)(2,1)S(1)}, u32[]{:S(2)}, u32[]{:S(2)}) collective-permute-start(bf16[64,4096]{1,0:T(8,128)(2,1)S(1)} %collective-permute-done.c1), channel_id=1, source_target_pairs={{0,3},{1,2},{2,1},{3,0},{4,7},{5,6},{6,5},{7,4},{8,11},{9,10},{10,... | collective-permute-start | bytes 1572872 | tf_op jit(solution)/shard_map/ppermute | solution.py:241
  22.2 27.9 %all-to-all-start.1 = ((bf16[16,8,256]{2,1,0:T(8,128)(2,1)}), bf16[16,8,256]{2,1,0:T(8,128)(2,1)S(1)}, u32[]{:S(2)}, u32[]{:S(2)}) async-start(bf16[16,8,256]{2,1,0:T(8,128)(2,1)} %get-tuple-element.20), calls=%async_computation.1 | async-start | bytes 131072 | tf_op jit(solution)/shard_map/all_to_all | solution.py:272
  37.4 0.7 collective-permute-start.3
  52.3 17.4 %all-to-all-start.2 = ((bf16[16,16,256]{2,1,0:T(8,128)(2,1)}), bf16[16,16,256]{2,1,0:T(8,128)(2,1)S(1)}, u32[]{:S(2)}, u32[]{:S(2)}) async-start(bf16[16,16,256]{2,1,0:T(8,128)(2,1)} %get-tuple-element.25), calls=%async_computation.2 | async-start | bytes 262144 | tf_op jit(solution)/shard_map/all_to_all | solution.py:272
  55.9 6.1 %collective-permute-start.5 = (f32[8,256]{1,0:T(8,128)S(1)}, f32[8,256]{1,0:T(8,128)S(1)}, u32[]{:S(2)}, u32[]{:S(2)}) collective-permute-start(f32[8,256]{1,0:T(8,128)S(1)} %get-tuple-element.27.field.previous.f1), channel_id=1, source_target_pairs={{64,128},{192,256},{320,384},{128,64},{256,192},{384,320},{65,129}... | collective-permute-start | bytes 24584 | tf_op jit(solution)/shard_map/ppermute | solution.py:250
  56.6 6.3 %collective-permute-start.4 = (f32[8,256]{1,0:T(8,128)S(1)}, f32[8,256]{1,0:T(8,128)S(1)}, u32[]{:S(2)}, u32[]{:S(2)}) collective-permute-start(f32[8,256]{1,0:T(8,128)S(1)} %get-tuple-element.27.field.previous.f1), channel_id=1, source_target_pairs={{0,64},{64,0},{128,192},{192,128},{256,320},{320,256},{384,448},{4... | collective-permute-start | bytes 24584 | tf_op jit(solution)/shard_map/ppermute | solution.py:245
  71.1 18.5 %all-to-all-start.3 = ((bf16[16,8,256]{2,1,0:T(8,128)(2,1)}), bf16[16,8,256]{2,1,0:T(8,128)(2,1)S(1)}, u32[]{:S(2)}, u32[]{:S(2)}) async-start(bf16[16,8,256]{2,1,0:T(8,128)(2,1)} %get-tuple-element.28), calls=%async_computation.3 | async-start | bytes 131072 | tf_op jit(solution)/shard_map/all_to_all | solution.py:272
  76.6 5.7 %collective-permute-start.7 = (f32[8,256]{1,0:T(8,128)S(1)}, f32[8,256]{1,0:T(8,128)S(1)}, u32[]{:S(2)}, u32[]{:S(2)}) collective-permute-start(f32[8,256]{1,0:T(8,128)S(1)} %get-tuple-element.29.field.f2), channel_id=1, source_target_pairs={{64,128},{192,256},{320,384},{128,64},{256,192},{384,320},{65,129}... | collective-permute-start | bytes 24584 | tf_op jit(solution)/shard_map/ppermute | solution.py:250
  77.3 5.8 %collective-permute-start.6 = (f32[8,256]{1,0:T(8,128)S(1)}, f32[8,256]{1,0:T(8,128)S(1)}, u32[]{:S(2)}, u32[]{:S(2)}) collective-permute-start(f32[8,256]{1,0:T(8,128)S(1)} %get-tuple-element.29.field.f2), channel_id=1, source_target_pairs={{0,64},{64,0},{128,192},{192,128},{256,320},{320,256},{384,448},{4... | collective-permute-start | bytes 24584 | tf_op jit(solution)/shard_map/ppermute | solution.py:245
